TPU v7x, 256 devices: a whole 4x4x8 slice. The times are simulated.
256 devices in a mesh: group: 32 (over y, z_hi, core), tensor: 8 (over z_lo, x).
Axes of the slice: x: 4, y: 4, z: 8 (z_hi: 4, z_lo: 2; z = z_hi * 2 + z_lo), core: 2. Of those that a mesh axis runs over, the one named last changes fastest.
Arguments:
- span_rows: bfloat16 [49152, 2048], P('group', 'tensor'), may hold values from -80 to 80
- norm_gain: float32 [2048], replicated, may hold values from 0.1 to 1.9
- q_weight: bfloat16 [2048, 2048], P(None, 'tensor'), may hold values from -0.125 to 0.125
- gate_weight: bfloat16 [2048, 2048], P(None, 'tensor'), may hold values from -0.125 to 0.125
- k_weight: bfloat16 [2048, 1024], P(None, 'tensor'), may hold values from -0.125 to 0.125
- v_weight: bfloat16 [2048, 1024], P(None, 'tensor'), may hold values from -0.125 to 0.125
- q_norm_gain: float32 [128], replicated, may hold values from 1 to 150
- k_norm_gain: float32 [128], replicated, may hold values from 1 to 2.5
- o_weight: bfloat16 [2048, 2048], P('tensor'), may hold values from -0.125 to 0.125
- key_cache: bfloat16 [32, 64, 128, 1024], P('group', None, None, 'tensor'), may hold values from -6 to 6
- value_cache: bfloat16 [32, 64, 128, 1024], P('group', None, None, 'tensor'), may hold values from -6 to 6
- holders: int32 [768, 1], replicated, may hold values from 0 to 31; in each aligned block of 24 rows (0 to 23, 24 to 47, ...) at most 2 rows name the same one
- prefix_lengths: int32 [768], replicated, may hold values from 1 to 128, 49152 in all
Outputs:
- attn_out: bfloat16 [49152, 2048], P(('group', 'tensor'))
Inputs may be any that keep to these rules, and one draw needn't show every extreme that they name: `holders`: among the 24 requests of one group no holder is named more than 2 times; in some groups one holder is named exactly 2 times. `prefix_lengths`: some request has a prefix of exactly 128 positions.
All inputs are finite; a program needn't handle non-finite values.
Results may differ from a plain program's by a relative error of at most 0.03.
Values may be sent and summed in bfloat16 or wider, within the bound.
No kernel may reach another device: no remote copies, remote signals or barrier semaphores. Data moves between devices by JAX's collectives and lax.ppermute only.
A program may use at most 128 MiB of HBM per device.

v0:
```python
import math

import jax
import jax.numpy as jnp
from jax import lax
from jax.sharding import PartitionSpec as P

EPSILON = 1e-06
ROPE_BASE = 1000000.0


def rms_scale(values, gain_vector):
    mean_sq = jnp.mean(values * values, axis=-1, keepdims=True)
    return values * lax.rsqrt(mean_sq + EPSILON) * gain_vector


def rotate(values, positions):
    half_dim = values.shape[-1] // 2
    frequency = ROPE_BASE ** (-jnp.arange(half_dim, dtype=jnp.float32) * 2.0 / values.shape[-1])
    angles = positions.astype(jnp.float32)[:, :, None, None] * frequency
    cosine = jnp.cos(angles)
    sine_part = jnp.sin(angles)
    front_half = values[..., :half_dim]
    back_half = values[..., half_dim:]
    return jnp.concatenate(
        [front_half * cosine - back_half * sine_part, back_half * cosine + front_half * sine_part],
        axis=-1,
    )


def softmax_parts(scores, valid_keys):
    scores = jnp.where(valid_keys, scores, -jnp.inf)
    row_max = jnp.max(scores, axis=-1)
    raw_weights = jnp.exp(scores - row_max[..., None])
    row_total = jnp.sum(raw_weights, axis=-1)
    return (raw_weights.astype(jnp.bfloat16), row_max, row_total)


def local(
    span_rows,
    norm_gain,
    q_weight,
    gate_weight,
    k_weight,
    v_weight,
    q_norm_gain,
    k_norm_gain,
    o_weight,
    key_cache,
    value_cache,
    holders,
    prefix_lengths,
):
    groups = lax.axis_size("group")
    group_id = lax.axis_index("group")
    requests = prefix_lengths.shape[0] // groups
    span_len = span_rows.shape[0] // requests
    head_dim = q_norm_gain.shape[0]
    query_heads = q_weight.shape[1] // head_dim
    key_heads = k_weight.shape[1] // head_dim
    group_share = query_heads // key_heads
    capacity = key_cache.shape[1] // groups
    window = key_cache.shape[2]
    score_scale = 1.0 / math.sqrt(head_dim)
    all_holders = holders.reshape(groups, requests)
    same_holder = all_holders[:, :, None] == all_holders[:, None, :]
    request_order = jnp.arange(requests)
    earlier = request_order[None, :] < request_order[:, None]
    all_ranks = jnp.sum(jnp.logical_and(same_holder, earlier[None]), axis=2)
    all_lengths = prefix_lengths.reshape(groups, requests)
    my_holders = lax.dynamic_index_in_dim(all_holders, group_id, 0, keepdims=False)
    my_ranks = lax.dynamic_index_in_dim(all_ranks, group_id, 0, keepdims=False)
    my_lengths = lax.dynamic_index_in_dim(all_lengths, group_id, 0, keepdims=False)
    my_slots = my_holders * capacity + my_ranks
    positions = my_lengths[:, None] + jnp.arange(span_len, dtype=jnp.int32)[None, :]
    whole_rows = lax.all_gather(span_rows, "tensor", axis=1, tiled=True)
    normed = rms_scale(whole_rows.astype(jnp.float32), norm_gain).astype(jnp.bfloat16)
    queries = jnp.dot(normed, q_weight, preferred_element_type=jnp.float32).reshape(
        requests, span_len, query_heads, head_dim
    )
    queries = rotate(rms_scale(queries, q_norm_gain), positions).astype(jnp.bfloat16)
    new_keys = jnp.dot(normed, k_weight, preferred_element_type=jnp.float32).reshape(
        requests, span_len, key_heads, head_dim
    )
    new_keys = rotate(rms_scale(new_keys, k_norm_gain), positions).astype(jnp.bfloat16)
    new_values = (
        jnp.dot(normed, v_weight, preferred_element_type=jnp.float32)
        .astype(jnp.bfloat16)
        .reshape(requests, span_len, key_heads, head_dim)
    )
    gate_logits = jnp.dot(normed, gate_weight, preferred_element_type=jnp.float32)
    grouped = queries.reshape(requests, span_len, key_heads, group_share, head_dim)
    local_keys = key_cache.reshape(groups, capacity, window, key_heads * head_dim)
    local_values = value_cache.reshape(groups, capacity, window, key_heads * head_dim)
    got_keys, got_values = (
        lax.all_to_all(local_keys, "group", split_axis=0, concat_axis=0, tiled=True),
        lax.all_to_all(local_values, "group", split_axis=0, concat_axis=0, tiled=True),
    )
    prefix_keys = got_keys.reshape(groups * capacity, window, key_heads, head_dim)[my_slots]
    prefix_values = got_values.reshape(groups * capacity, window, key_heads, head_dim)[my_slots]
    all_keys = jnp.concatenate([prefix_keys, new_keys], axis=1)
    all_values = jnp.concatenate([prefix_values, new_values], axis=1)
    scores = (
        jnp.einsum("rqkgd,rlkd->rkgql", grouped, all_keys, preferred_element_type=jnp.float32)
        * score_scale
    )
    key_index = jnp.arange(window + span_len)[None, None, :]
    query_index = jnp.arange(span_len)[None, :, None]
    valid_keys = jnp.where(
        key_index < window, key_index < my_lengths[:, None, None], key_index - window <= query_index
    )
    weights, row_max, row_total = softmax_parts(scores, valid_keys[:, None, None])
    mixed_heads = (
        jnp.einsum("rkgql,rlkd->rkgqd", weights, all_values, preferred_element_type=jnp.float32)
        / row_total[..., None]
    )
    mixed_heads = jnp.transpose(mixed_heads, (0, 3, 1, 2, 4)).reshape(
        requests * span_len, query_heads * head_dim
    )
    attended = (mixed_heads * jax.nn.sigmoid(gate_logits)).astype(jnp.bfloat16)
    return lax.psum_scatter(
        jnp.dot(attended, o_weight, preferred_element_type=jnp.float32).astype(jnp.bfloat16),
        "tensor",
        scatter_dimension=0,
        tiled=True,
    )


def solution(mesh):
    placed = (
        P("group", "tensor"),
        P(),
        P(None, "tensor"),
        P(None, "tensor"),
        P(None, "tensor"),
        P(None, "tensor"),
        P(),
        P(),
        P("tensor", None),
        P("group", None, None, "tensor"),
        P("group", None, None, "tensor"),
        P(),
        P(),
    )
    return jax.shard_map(
        local, mesh=mesh, in_specs=placed, out_specs=P(("group", "tensor"), None), check_vma=False
    )
```

profile of v0, /device:TPU:8, one launch (start us, length us, event | category | flops | bytes accessed | tf_op | source)
XLA Modules:
  0.0 309.9 jit_solution(1799825172396202955)
XLA Ops:
  6.5 0.0 copy-start
  6.5 0.0 all-gather.2.cloned.1.call-start
  6.5 0.7 all-gather.2.cloned.1.call-update
  7.3 79.4 %all_to_all.10 = bf16[32,2,128,128]{3,2,1,0:T(8,128)(2,1)} all-to-all(bf16[32,2,128,128]{3,2,1,0:T(8,128)(2,1)} %bitcast.72), channel_id=1, replica_groups=mesh['group'=32,'tensor'=8] {'group'}, dimensions={0} | all-to-all | bytes 4194304 | tf_op jit(solution)/shard_map/all_to_all | solution.py:96
  86.7 0.0 copy-start.10
  86.7 6.5 %all-to-all-start.1 = ((bf16[32,2,128,128]{3,2,1,0:T(8,128)(2,1)}), bf16[32,2,128,128]{3,2,1,0:T(8,128)(2,1)S(1)}, u32[]{:S(2)}, u32[]{:S(2)}) async-start(bf16[32,2,128,128]{3,2,1,0:T(8,128)(2,1)} %bitcast.73), calls=%async_computation.1 | async-start | bytes 4194304 | tf_op jit(solution)/shard_map/all_to_all | solution.py:97
  93.2 0.0 reduce-scatter.2.cloned.1.call-start
  93.2 0.0 copy-done.9
  93.2 0.1 reshape.306
  93.3 0.0 copy-done.10
  93.3 0.1 reshape.309
  93.4 0.1 copy.32
  93.5 0.2 convert_reduce_fusion
  93.7 0.2 add_reduce_fusion
  94.0 0.1 iota_compare_fusion.1
  94.0 0.1 add_convert_fusion.1
  94.1 1.0 broadcast_select_fusion
  95.1 4.3 %multiply_cosine_fusion = (f32[24,64,64]{2,1,0:T(8,128)}, f32[24,64,64]{2,1,0:T(8,128)}) fusion(f32[64]{0:T(128)S(1)} %multiply_power_fusion, f32[24,64]{1,0:T(8,128)S(1)} %add_convert_fusion.1), kind=kLoop, calls=%fused_computation.42 | loop fusion | flops 98304 | bytes 792832 | tf_op jit(solution)/shard_map/cos | solution.py:21
  99.4 3.2 %gather_fusion = bf16[24,128,128]{2,1,0:T(8,128)(2,1)} fusion(bf16[64,128,128]{2,1,0:T(8,128)(2,1)} %bitcast.71, s32[1024]{0:T(1024)S(1)} %pad_clamp_fusion), kind=kCustom, calls=%fused_computation | custom fusion | bytes 1572960 | tf_op jit(solution)/shard_map/gather | solution.py:99
  102.6 63.2 %all-to-all-done.1 = bf16[32,2,128,128]{3,2,1,0:T(8,128)(2,1)S(1)} async-done(((bf16[32,2,128,128]{3,2,1,0:T(8,128)(2,1)}), bf16[32,2,128,128]{3,2,1,0:T(8,128)(2,1)S(1)}, u32[]{:S(2)}, u32[]{:S(2)}) %all-to-all-start.1) | async-done | bytes 2097184 | tf_op jit(solution)/shard_map/all_to_all | solution.py:97
  165.8 1.6 gather_fusion.1
  167.4 0.0 copy-start.8
  167.4 5.2 %all-gather.2.cloned.1.call-done = bf16[1536,2048]{1,0:T(8,128)(2,1)} async-done(((bf16[1536,256]{1,0:T(8,128)(2,1)}), bf16[1536,2048]{1,0:T(8,128)(2,1)}) %all-gather.2.cloned.1.call-update) | async-done | bytes 6291472 | tf_op jit(solution)/shard_map/all_gather | solution.py:76
  172.6 0.0 copy-start.1
  172.6 4.2 %fusion = f32[1536]{0:T(1024)S(1)} fusion(bf16[1536,2048]{1,0:T(8,128)(2,1)} %all-gather.2.cloned.1.call-done), kind=kLoop, calls=%fused_computation.4 | loop fusion | flops 9435648 | bytes 6297600 | tf_op jit(solution)/shard_map/reduce_sum | solution.py:13
  176.8 0.0 copy-done.8
  176.8 0.3 copy-done.1
  177.2 0.0 copy-start.13
  177.2 1.5 fusion.2
  178.7 0.0 copy-start.2
  178.7 2.6 copy-done.2
  181.3 0.0 copy-done.13
  181.3 3.0 fusion.47
  184.4 2.1 reshape.312
  186.4 1.7 multiply_reduce_fusion
  188.1 0.3 copy.35
  188.5 0.0 copy-start.11
  188.5 4.7 %multiply_reduce_fusion.1 = (f32[1536]{0:T(1024)S(1)}, f32[1536,128]{1,0:T(8,128)S(1)}) fusion(bf16[1536,2048]{1,0:T(8,128)(2,1)} %copy-done.2, bf16[2048,128]{1,0:T(8,128)(2,1)} %param.17), kind=kOutput, calls=%fused_computation.58 | convolution fusion | flops 805698048 | bytes 7608320 | tf_op jit(solution)/shard_map/dot_general | solution.py:82
  193.2 0.1 rsqrt.29
  193.3 0.0 copy-done.11
  193.3 0.3 multiply_multiply_fusion
  193.6 3.7 %fusion.33 = (bf16[24,64,1,64]{3,1,0,2:T(8,128)(2,1)S(1)}, bf16[24,64,1,64]{3,1,0,2:T(8,128)(2,1)S(1)}) fusion(f32[24,64,1,128]{3,1,0,2:T(8,128)S(1)} %multiply_multiply_fusion, f32[64]{0:T(128)S(1)} %multiply_power_fusion, f32[24,64]{1,0:T(8,128)S(1)} %add_convert_fusion.1), kind=kLoop, calls=%fused_computation.50 | loop fusion | flops 884736 | bytes 1186048 | tf_op jit(solution)/shard_map/convert.2
  197.3 0.0 copy-done.14
  197.3 0.0 copy-start.12
  197.4 4.6 %convolution_convert_fusion.1 = bf16[1536,128]{1,0:T(8,128)(2,1)S(1)} fusion(bf16[1536,2048]{1,0:T(8,128)(2,1)} %copy-done.2, bf16[2048,128]{1,0:T(8,128)(2,1)S(1)} %copy-done.14), kind=kOutput, calls=%fused_computation.18 | convolution fusion | flops 805502976 | bytes 7208960 | tf_op jit(solution)/shard_map/dot_general | solution.py:87
  202.0 0.0 copy-done.12
  202.0 0.0 copy-start.3
  202.0 0.0 copy-start.4
  202.0 0.5 fusion.14
  202.5 0.6 copy-done.3
  203.1 0.2 copy-done.4
  203.3 0.8 subtract_convert_fusion
  204.1 0.2 copy-done.5
  204.3 0.3 copy-done.7
  204.6 1.6 fusion.10
  206.2 0.0 copy-start.6
  206.2 1.3 fusion.3
  207.6 0.0 copy-done.6
  207.6 1.8 divide_bitcast_fusion
  209.4 1.2 copy.38
  210.6 0.0 copy-done
  210.6 12.1 %convolution_convert_fusion = bf16[1536,2048]{1,0:T(8,128)(2,1)} fusion(bf16[256,2048]{1,0:T(8,128)(2,1)S(1)} %copy-done, bf16[1536,2048]{1,0:T(8,128)(2,1)} %copy-done.2, bf16[2048,256]{1,0:T(8,128)(2,1)} %param.16, f32[192,8,2,128]{3,2,1,0:T(2,128)S(1)} %bitcast.74), kind=kOutput, calls=%fused_computation.7 | convolution fusion | flops 3226337280 | bytes 16252928 | tf_op jit(solution)/shard_map/dot_general | solution.py:122
  222.7 0.0 reduce-scatter.2.cloned.1.call-update
  222.8 80.3 %reduce-scatter.2.cloned.1.call-done = bf16[192,2048]{1,0:T(8,128)(2,1)} async-done(((bf16[1536,2048]{1,0:T(8,128)(2,1)}), bf16[192,2048]{1,0:T(8,128)(2,1)}) %reduce-scatter.2.cloned.1.call-update) | async-done | bytes 786448 | tf_op jit(solution)/shard_map/reduce_scatter | solution.py:121
  (17 shorter events, 0.1 us)
Async XLA Ops:
  6.5 204.1 %copy-start = (bf16[256,2048]{1,0:T(8,128)(2,1)S(1)}, bf16[256,2048]{1,0:T(8,128)(2,1)}, u32[]{:S(2)}) copy-start(bf16[256,2048]{1,0:T(8,128)(2,1)} %param.21) | copy-start | bytes 3145732
  6.5 166.0 %all-gather.2.cloned.1.call-start = ((), (), s32[]{:S(2)}) async-start(), calls=%async_computation.3 | async-start | bytes 7077888 | tf_op jit(solution)/shard_map/all_gather | solution.py:76
  86.7 6.6 %copy-start.9 = (s32[768]{0:T(1024)S(1)}, s32[768]{0:T(1024)}, u32[]{:S(2)}) copy-start(s32[768]{0:T(1024)} %param.25) | copy-start | bytes 9220
  86.7 6.7 %copy-start.10 = (s32[768,1]{0,1:T(1,128)S(1)}, s32[768,1]{0,1:T(1,128)}, u32[]{:S(2)}) copy-start(s32[768,1]{0,1:T(1,128)} %param.24) | copy-start | bytes 9220
  86.7 79.1 %all-to-all-start.1 = ((bf16[32,2,128,128]{3,2,1,0:T(8,128)(2,1)}), bf16[32,2,128,128]{3,2,1,0:T(8,128)(2,1)S(1)}, u32[]{:S(2)}, u32[]{:S(2)}) async-start(bf16[32,2,128,128]{3,2,1,0:T(8,128)(2,1)} %bitcast.73), calls=%async_computation.1 | async-start | bytes 4194304 | tf_op jit(solution)/shard_map/all_to_all | solution.py:97
  93.2 209.9 %reduce-scatter.2.cloned.1.call-start = ((), (), s32[]{:S(2)}) async-start(), calls=%async_computation.4 | async-start | bytes 7077888 | tf_op jit(solution)/shard_map/reduce_scatter | solution.py:121
  167.4 9.5 %copy-start.8 = (f32[2048]{0:T(1024)S(1)}, f32[2048]{0:T(1024)}, u32[]{:S(2)}) copy-start(f32[2048]{0:T(1024)} %param.14) | copy-start | bytes 24580
  172.6 4.6 %copy-start.1 = (bf16[1536,2048]{1,0:T(8,128)(2,1)S(1)}, bf16[1536,2048]{1,0:T(8,128)(2,1)}, u32[]{:S(2)}) copy-start(bf16[1536,2048]{1,0:T(8,128)(2,1)} %all-gather.2.cloned.1.call-done) | copy-start | bytes 18874372
  177.2 4.2 %copy-start.13 = (bf16[2048,256]{1,0:T(8,128)(2,1)S(1)}, bf16[2048,256]{1,0:T(8,128)(2,1)}, u32[]{:S(2)}) copy-start(bf16[2048,256]{1,0:T(8,128)(2,1)} %param.15) | copy-start | bytes 3145732
  178.7 2.7 copy-start.2
  188.5 4.8 %copy-start.11 = (f32[128]{0:T(128)S(1)}, f32[128]{0:T(128)}, u32[]{:S(2)}) copy-start(f32[128]{0:T(128)} %param.20) | copy-start | bytes 1540
  193.3 4.0 %copy-start.14 = (bf16[2048,128]{1,0:T(8,128)(2,1)S(1)}, bf16[2048,128]{1,0:T(8,128)(2,1)}, u32[]{:S(2)}) copy-start(bf16[2048,128]{1,0:T(8,128)(2,1)} %param.18) | copy-start | bytes 1572868
  197.3 4.6 %copy-start.12 = (f32[128]{0:T(128)S(1)}, f32[128]{0:T(128)}, u32[]{:S(2)}) copy-start(f32[128]{0:T(128)} %param.19) | copy-start | bytes 1540
  202.0 1.1 copy-start.3
  202.0 1.4 copy-start.4
  203.3 1.0 copy-start.5
  203.3 1.3 copy-start.7
  206.2 1.3 copy-start.6
Sparse Core Ops, SparseCore 0:
  9.1 163.4 all-gather.1
  222.9 80.1 reduce-scatter.1
where the time goes:
time: 311 us; the launch traced here: 310 us
  waiting for transfers between devices  149 us (48%)
  blocking collectives  79.4 us (26%)
  matrix products  27.9 us (9%)
  other arithmetic  19.9 us (6%)
  between operations  13.7 us (4%)
  local copies, waits for them, and re-layouts  13 us (4%)
  starting transfers between devices  6.54 us (2%)
    reduce_scatter x1, waiting for transfers between devices, local(): lax.psum_scatter(jnp.dot(attended, o_weight, preferred_element_type=jnp.f...  80.3 us
    all_to_all x1, blocking collectives, local(): lax.all_to_all(local_keys, 'group', split_axis=0, concat_axis=0, tiled=True)  79.4 us
    all_to_all x1, waiting for transfers between devices, local(): lax.all_to_all(local_values, 'group', split_axis=0, concat_axis=0, tiled=...  63.2 us
    dot_general x1, matrix products, local(): jnp.dot(attended, o_weight, preferred_element_type=jnp.float32)  12.1 us
    all_to_all x1, starting transfers between devices, local(): lax.all_to_all(local_values, 'group', split_axis=0, concat_axis=0, tiled=...  6.49 us
  transfers between devices with their start and end apart: 3, of which 3 were waited for; matrix products, arithmetic and copies ran while one was open for 3% of the time, Pallas kernels for 0%

commit v1 on v0

v1 whole, which is shorter than its diff:
```python
import functools
import math

import jax
import jax.numpy as jnp
from jax import lax
from jax.experimental import pallas as pl
from jax.experimental.pallas import tpu as pltpu
from jax.sharding import Mesh
from jax.sharding import PartitionSpec as P

EPSILON = 1e-06
ROPE_BASE = 1000000.0
GROUP = ("y", "zh", "c")
TENSOR = ("zl", "x")
ROW_TILE = 256
BATCH = 4


def ring(size, step):
    return [(i, (i + step) % size) for i in range(size)]


def shift(value, axis, step):
    return lax.ppermute(value, axis, ring(lax.axis_size(axis), step))


def spread(block):
    twin = shift(block, "zl", 1)
    below, above = shift(block, "x", 1), shift(block, "x", -1)
    twin_below, twin_above = shift(twin, "x", 1), shift(twin, "x", -1)
    far = shift(below, "x", 1)
    twin_far = shift(twin_above, "x", -1)
    return [block, twin, below, above, twin_below, twin_above, far, twin_far]


def block_ids():
    zl, x = lax.axis_index("zl"), lax.axis_index("x")
    pairs = [(0, 0), (1, 0), (0, 3), (0, 1), (1, 3), (1, 1), (0, 2), (1, 2)]
    return jnp.stack([((zl + dz) % 2) * 4 + (x + dx) % 4 for dz, dx in pairs]).astype(jnp.int32)


def head_norm_rotate(values, gain, cosine, sine):
    scale = lax.rsqrt(jnp.mean(values * values, axis=-1, keepdims=True) + EPSILON)
    scaled = values * scale * gain
    half = values.shape[-1] // 2
    return scaled * cosine + pltpu.roll(scaled, half, 1) * sine


def project_kernel(ids, *refs):
    pieces, rest = refs[:8], refs[8:]
    (gain, wq, wg, wk, wv, q_gain, k_gain, cosine, sine, q_out, g_out, k_out, v_out, normed) = rest
    width = pieces[0].shape[1]
    head = wk.shape[1]
    total = jnp.zeros((pieces[0].shape[0], 1), jnp.float32)
    for piece in pieces:
        value = piece[...].astype(jnp.float32)
        total = total + jnp.sum(value * value, axis=-1, keepdims=True)
    scale = lax.rsqrt(total / (8 * width) + EPSILON)
    for j, piece in enumerate(pieces):
        block = ids[j]
        value = piece[...].astype(jnp.float32) * scale * gain[pl.ds(block, 1), :]
        normed[:, pl.ds(pl.multiple_of(block * width, width), width)] = value.astype(jnp.bfloat16)
    x = normed[...]
    cos, sin = cosine[...], sine[...]
    q = jnp.dot(x, wq[...], preferred_element_type=jnp.float32)
    for h in range(q.shape[1] // head):
        part = head_norm_rotate(q[:, h * head : (h + 1) * head], q_gain[...], cos, sin)
        q_out[:, h * head : (h + 1) * head] = part.astype(jnp.bfloat16)
    k = jnp.dot(x, wk[...], preferred_element_type=jnp.float32)
    k_out[...] = head_norm_rotate(k, k_gain[...], cos, sin).astype(jnp.bfloat16)
    v_out[...] = jnp.dot(x, wv[...], preferred_element_type=jnp.float32).astype(jnp.bfloat16)
    gate = jnp.dot(x, wg[...], preferred_element_type=jnp.float32)
    g_out[...] = jax.nn.sigmoid(gate)


def project(ids, pieces, gain, wq, wg, wk, wv, q_gain, k_gain, cosine, sine):
    rows, width = pieces[0].shape
    depth = gain.shape[0]
    head = q_gain.shape[0]
    tile = lambda columns: pl.BlockSpec((ROW_TILE, columns), lambda i, _: (i, 0))
    whole = lambda a: pl.BlockSpec(a.shape, lambda i, _: (0, 0))
    gain = gain.reshape(depth // width, width)
    q_gain, k_gain = q_gain.reshape(1, head), k_gain.reshape(1, head)
    constants = (gain, wq, wg, wk, wv, q_gain, k_gain)
    return pl.pallas_call(
        project_kernel,
        out_shape=(
            jax.ShapeDtypeStruct((rows, wq.shape[1]), jnp.bfloat16),
            jax.ShapeDtypeStruct((rows, wg.shape[1]), jnp.float32),
            jax.ShapeDtypeStruct((rows, head), jnp.bfloat16),
            jax.ShapeDtypeStruct((rows, head), jnp.bfloat16),
        ),
        grid_spec=pltpu.PrefetchScalarGridSpec(
            num_scalar_prefetch=1,
            grid=(rows // ROW_TILE,),
            in_specs=[tile(width)] * 8 + [whole(a) for a in constants] + [tile(head)] * 2,
            out_specs=[tile(wq.shape[1]), tile(wg.shape[1]), tile(head), tile(head)],
            scratch_shapes=[pltpu.VMEM((ROW_TILE, depth), jnp.bfloat16)],
        ),
        compiler_params=pltpu.CompilerParams(vmem_limit_bytes=40 << 20),
        cost_estimate=pl.CostEstimate(
            flops=2 * rows * depth * 6 * head, bytes_accessed=14 << 20, transcendentals=rows * 256
        ),
        name="project",
    )(ids, *pieces, *constants, cosine, sine)


def attend_kernel(starts, lengths, q, g, k, v, keys, values, out):
    head = k.shape[1]
    span = q.shape[0] // BATCH
    window = 128
    shares = q.shape[1] // head
    score_scale = 1.0 / math.sqrt(head)
    contract = (((1,), (1,)), ((), ()))
    column = lax.broadcasted_iota(jnp.int32, (shares * span, window), 1)
    old_row = lax.broadcasted_iota(jnp.int32, (window, head), 0)
    token = lax.broadcasted_iota(jnp.int32, (shares, span, span), 1).reshape(shares * span, span)
    causal = lax.broadcasted_iota(jnp.int32, (shares * span, span), 1) <= token
    for b in range(BATCH):
        r = pl.program_id(0) * BATCH + b
        length = lengths[r]
        rows = slice(b * span, (b + 1) * span)
        query = jnp.concatenate([q[rows, s * head : (s + 1) * head] for s in range(shares)], axis=0)
        place = pl.ds(pl.multiple_of(starts[r], 16), window)
        old_keys, old_values = keys[place, :], values[place, :]
        old_values = jnp.where(old_row < length, old_values, jnp.zeros_like(old_values))
        old = lax.dot_general(query, old_keys, contract, preferred_element_type=jnp.float32)
        new = lax.dot_general(query, k[rows, :], contract, preferred_element_type=jnp.float32)
        old = jnp.where(column < length, old * score_scale, -jnp.inf)
        new = jnp.where(causal, new * score_scale, -jnp.inf)
        row_max = jnp.maximum(
            jnp.max(old, axis=-1, keepdims=True), jnp.max(new, axis=-1, keepdims=True)
        )
        old, new = jnp.exp(old - row_max), jnp.exp(new - row_max)
        row_total = jnp.sum(old, axis=-1, keepdims=True) + jnp.sum(new, axis=-1, keepdims=True)
        mixed = jnp.dot(old.astype(jnp.bfloat16), old_values, preferred_element_type=jnp.float32)
        mixed += jnp.dot(new.astype(jnp.bfloat16), v[rows, :], preferred_element_type=jnp.float32)
        mixed = mixed / row_total
        for s in range(shares):
            columns = slice(s * head, (s + 1) * head)
            part = mixed[s * span : (s + 1) * span] * g[rows, columns]
            out[rows, columns] = part.astype(jnp.bfloat16)


def attend(starts, lengths, q, g, k, v, keys, values):
    rows, columns = q.shape
    head = k.shape[1]
    step = rows // lengths.shape[0] * BATCH
    tile = lambda width: pl.BlockSpec((step, width), lambda i, *_: (i, 0))
    whole = lambda a: pl.BlockSpec(a.shape, lambda i, *_: (0, 0))
    return pl.pallas_call(
        attend_kernel,
        out_shape=jax.ShapeDtypeStruct((rows, columns), jnp.bfloat16),
        grid_spec=pltpu.PrefetchScalarGridSpec(
            num_scalar_prefetch=2,
            grid=(rows // step,),
            in_specs=[tile(columns)] * 2 + [tile(head)] * 2 + [whole(keys), whole(values)],
            out_specs=tile(columns),
        ),
        compiler_params=pltpu.CompilerParams(vmem_limit_bytes=40 << 20),
        cost_estimate=pl.CostEstimate(
            flops=4 * rows * columns * 192, bytes_accessed=8 << 20, transcendentals=rows * 2 * 192
        ),
        name="attend",
    )(starts, lengths, q, g, k, v, keys, values)


def assemble_kernel(places, *refs):
    pieces, out, sems = refs[:-2], refs[-2], refs[-1]
    depth = pieces[0].shape[0]
    copies = []
    for j, piece in enumerate(pieces):
        start = pl.multiple_of(places[j] * depth, depth)
        copies.append(pltpu.make_async_copy(piece, out.at[pl.ds(start, depth)], sems.at[j]))
    for copy in copies:
        copy.start()
    for copy in copies:
        copy.wait()


def assemble(places, pieces):
    depth, columns = pieces[0].shape
    count = len(pieces)
    return pl.pallas_call(
        assemble_kernel,
        out_shape=jax.ShapeDtypeStruct((depth * count, columns), pieces[0].dtype),
        grid_spec=pltpu.PrefetchScalarGridSpec(
            num_scalar_prefetch=1,
            grid=(1,),
            in_specs=[pl.BlockSpec(memory_space=pl.ANY)] * count,
            out_specs=pl.BlockSpec(memory_space=pl.ANY),
            scratch_shapes=[pltpu.SemaphoreType.DMA((count,))],
        ),
        cost_estimate=pl.CostEstimate(flops=0, bytes_accessed=16 << 20, transcendentals=0),
        name="assemble",
    )(places, *pieces)


def output_kernel(heads, weight, out, joined):
    width = heads.shape[2]

    @pl.when(pl.program_id(0) == 0)
    def _():
        for j in range(heads.shape[0]):
            joined[:, j * width : (j + 1) * width] = heads[j]

    total = jnp.dot(joined[...], weight[...], preferred_element_type=jnp.float32)
    out[...] = total.astype(jnp.bfloat16)


def project_out(heads, weight):
    blocks, rows, width = heads.shape
    depth, columns = weight.shape
    tile = 512
    return pl.pallas_call(
        output_kernel,
        out_shape=jax.ShapeDtypeStruct((rows, columns), jnp.bfloat16),
        grid=(columns // tile,),
        in_specs=[
            pl.BlockSpec(heads.shape, lambda i: (0, 0, 0)),
            pl.BlockSpec((depth, tile), lambda i: (0, i)),
        ],
        out_specs=pl.BlockSpec((rows, tile), lambda i: (0, i)),
        scratch_shapes=[pltpu.VMEM((rows, depth), jnp.bfloat16)],
        compiler_params=pltpu.CompilerParams(vmem_limit_bytes=30 << 20),
        cost_estimate=pl.CostEstimate(
            flops=2 * rows * depth * columns, bytes_accessed=10 << 20, transcendentals=0
        ),
        name="project_out",
    )(heads, weight)


def local(
    span_rows,
    norm_gain,
    q_weight,
    gate_weight,
    k_weight,
    v_weight,
    q_norm_gain,
    k_norm_gain,
    o_weight,
    key_cache,
    value_cache,
    holders,
    prefix_lengths,
):
    groups = 32
    group_id = lax.axis_index(GROUP)
    requests = prefix_lengths.shape[0] // groups
    rows = span_rows.shape[0]
    span_len = rows // requests
    head_dim = q_norm_gain.shape[0]
    capacity = key_cache.shape[1] // groups
    window = key_cache.shape[2]
    blocks = lax.axis_size(TENSOR)

    all_holders = holders.reshape(groups, requests)
    my_holders = lax.dynamic_index_in_dim(all_holders, group_id, 0, keepdims=False)
    my_lengths = lax.dynamic_index_in_dim(
        prefix_lengths.reshape(groups, requests), group_id, 0, keepdims=False
    )
    order = jnp.arange(requests)
    earlier = order[None, :] < order[:, None]
    my_ranks = jnp.sum((my_holders[:, None] == my_holders[None, :]) & earlier, axis=1)
    starts = ((my_holders * capacity + my_ranks) * window).astype(jnp.int32)

    positions = my_lengths[:, None] + jnp.arange(span_len, dtype=jnp.int32)[None, :]
    half = head_dim // 2
    frequency = ROPE_BASE ** (-jnp.arange(half, dtype=jnp.float32) * 2.0 / head_dim)
    angles = positions.reshape(-1).astype(jnp.float32)[:, None] * frequency
    cosine, sine = jnp.cos(angles), jnp.sin(angles)
    cosine = jnp.concatenate([cosine, cosine], axis=-1)
    sine = jnp.concatenate([-sine, sine], axis=-1)

    ids = block_ids()
    pieces = spread(span_rows)

    local_keys = key_cache.reshape(groups, capacity * window, head_dim)
    local_values = value_cache.reshape(groups, capacity * window, head_dim)
    keys = lax.all_to_all(local_keys, GROUP, 0, 0, tiled=True).reshape(-1, head_dim)
    values = lax.all_to_all(local_values, GROUP, 0, 0, tiled=True).reshape(-1, head_dim)

    q, g, k, v = project(
        ids, pieces, norm_gain, q_weight, gate_weight, k_weight, v_weight,
        q_norm_gain, k_norm_gain, cosine, sine,
    )

    core = lax.axis_index("c")
    depth = o_weight.shape[0] // 2
    mine = lax.dynamic_slice_in_dim(o_weight, core * depth, depth, 0)
    half_pieces = spread(mine)
    other_pieces = [shift(p, "c", 1) for p in half_pieces]
    places = jnp.concatenate([ids * 2 + core, ids * 2 + 1 - core]).astype(jnp.int32)
    whole_weight = assemble(places, half_pieces + other_pieces)

    attended = attend(starts, my_lengths, q, g, k, v, keys, values)
    heads = lax.all_to_all(
        attended.reshape(blocks, rows // blocks, attended.shape[1]), TENSOR, 0, 0, tiled=True
    )
    return project_out(heads, whole_weight)


def solution(mesh):
    mesh = Mesh(mesh.devices.reshape(4, 4, 2, 2, 4), GROUP + TENSOR)
    placed = (
        P(GROUP, TENSOR),
        P(),
        P(None, TENSOR),
        P(None, TENSOR),
        P(None, TENSOR),
        P(None, TENSOR),
        P(),
        P(),
        P(TENSOR, None),
        P(GROUP, None, None, TENSOR),
        P(GROUP, None, None, TENSOR),
        P(),
        P(),
    )
    return jax.shard_map(
        local, mesh=mesh, in_specs=placed, out_specs=P(GROUP + TENSOR, None), check_vma=False
    )
```

time: 311 us -> 517 us (1.66)
  Pallas kernels: 0 us -> 283 us
  waiting for transfers between devices: 149 us -> 109 us
  starting transfers between devices: 6.54 us -> 36.7 us
  matrix products: 27.9 us -> 0 us
  blocking collectives: 79.4 us -> 60.2 us
  between operations: 13.7 us -> 0.32 us
  other arithmetic: 19.9 us -> 9.36 us
    pallas_call x0 -> x4, Pallas kernels: none -> 283 us  [the longest x1 256 us: assemble(): pl.pallas_call(assemble_kernel, out_shape=jax.ShapeDtypeStruct((depth * c...]
    ppermute x0 -> x22, waiting for transfers between devices: none -> 109 us  [shift(): return lax.ppermute(value, axis, ring(lax.axis_size(axis), step))]
    reduce_scatter x1 -> x0, waiting for transfers between devices: 80.3 us -> none  [local(): lax.psum_scatter(jnp.dot(attended, o_weight, preferred_element_type=jnp.f...]
    all_to_all x1 -> x2, waiting for transfers between devices: 63.2 us -> 0.01 us  [the longest x1 0.01 us: local(): lax.all_to_all(local_values, GROUP, 0, 0, tiled=True).reshape(-1, head_dim)]
    dot_general x6 -> x0, matrix products: 27.9 us -> none  [the longest x1 12.1 us: local(): jnp.dot(attended, o_weight, preferred_element_type=jnp.float32)]
    ppermute x0 -> x22, starting transfers between devices: none -> 22.7 us  [shift(): return lax.ppermute(value, axis, ring(lax.axis_size(axis), step))]
    all_to_all x1, blocking collectives: 79.4 us -> 60.2 us  [local(): lax.all_to_all(local_keys, GROUP, 0, 0, tiled=True).reshape(-1, head_dim)]
    unnamed x30 -> x58, local copies, waits for them, and re-layouts: 4.4 us -> 14.9 us
  transfers between devices with their start and end apart: 3 -> 24, of which waited for: 3 -> 6; matrix products, arithmetic and copies ran while one was open for 3% -> 2% of each run, Pallas kernels for 0% -> 54%
where the time goes in v1:
time: 517 us; the launch traced here: 515 us
  Pallas kernels  283 us (55%)
  waiting for transfers between devices  109 us (21%)
  blocking collectives  60.2 us (12%)
  starting transfers between devices  36.7 us (7%)
  local copies, waits for them, and re-layouts  16.1 us (3%)
  other arithmetic  9.36 us (2%)
    pallas_call x1, Pallas kernels, assemble(): pl.pallas_call(assemble_kernel, out_shape=jax.ShapeDtypeStruct((depth * c...  256 us
    ppermute x22, waiting for transfers between devices, shift(): return lax.ppermute(value, axis, ring(lax.axis_size(axis), step))  109 us
    all_to_all x1, blocking collectives, local(): lax.all_to_all(local_keys, GROUP, 0, 0, tiled=True).reshape(-1, head_dim)  60.2 us
    ppermute x22, starting transfers between devices, shift(): return lax.ppermute(value, axis, ring(lax.axis_size(axis), step))  22.7 us
    unnamed x58, local copies, waits for them, and re-layouts  14.9 us
    pallas_call x1, Pallas kernels, project(): pl.pallas_call(project_kernel, out_shape=(jax.ShapeDtypeStruct((rows, wq....  14.2 us
  transfers between devices with their start and end apart: 24, of which 6 were waited for; matrix products, arithmetic and copies ran while one was open for 2% of the time, Pallas kernels for 54%

profile of v1, /device:TPU:8, one launch (start us, length us, event | category | flops | bytes accessed | tf_op | source)
XLA Modules:
  0.0 514.6 jit_solution(17017108682817971704)
XLA Ops:
  0.0 60.2 %all_to_all.15 = bf16[32,256,128]{2,1,0:T(8,128)(2,1)S(1)} all-to-all(bf16[32,256,128]{2,1,0:T(8,128)(2,1)} %bitcast.23), channel_id=1, replica_groups=mesh['y'=4,'zh'=4,'c'=2,'zl'=2,'x'=4] {'y','zh','c'}, dimensions={0} | all-to-all | bytes 4194304 | tf_op jit(solution)/shard_map/all_to_all | solution.py:282
  60.2 9.2 %all-to-all-start.1 = ((bf16[32,256,128]{2,1,0:T(8,128)(2,1)}), bf16[32,256,128]{2,1,0:T(8,128)(2,1)}, u32[]{:S(2)}, u32[]{:S(2)}) async-start(bf16[32,256,128]{2,1,0:T(8,128)(2,1)} %bitcast.24), calls=%async_computation.1 | async-start | bytes 4194304 | tf_op jit(solution)/shard_map/all_to_all | solution.py:283
  69.4 0.0 copy-start.26
  69.4 0.1 collective-permute-start
  69.5 1.6 collective-permute-start.1
  71.1 1.7 collective-permute-start.2
  72.8 0.8 constant_dynamic-slice_fusion.refs_0_
  73.7 1.9 collective-permute-start.7
  75.6 0.1 reshape.55
  75.7 0.1 reshape.56
  75.8 56.9 %collective-permute-done.refs_1_ = bf16[1536,256]{1,0:T(8,128)(2,1)} collective-permute-done((bf16[1536,256]{1,0:T(8,128)(2,1)}, bf16[1536,256]{1,0:T(8,128)(2,1)}, u32[]{:S(2)}, u32[]{:S(2)}) %collective-permute-start) | collective-permute-done | bytes 786464 | tf_op jit(solution)/shard_map/ppermute | solution.py:25
  132.8 2.8 collective-permute-start.4
  135.5 0.1 add_convert_fusion
  135.6 0.1 convert_element_type.15
  135.7 4.5 fusion
  140.1 0.8 collective-permute-start.5
  140.9 11.1 %collective-permute-done.4.refs_5_ = bf16[1536,256]{1,0:T(8,128)(2,1)} collective-permute-done((bf16[1536,256]{1,0:T(8,128)(2,1)}, bf16[1536,256]{1,0:T(8,128)(2,1)}, u32[]{:S(2)}, u32[]{:S(2)}) %collective-permute-start.4) | collective-permute-done | bytes 786464 | tf_op jit(solution)/shard_map/ppermute | solution.py:25
  152.0 3.7 collective-permute-start.6
  155.7 0.2 convert_reduce_fusion
  155.8 0.6 add_multiply_fusion.starts
  156.4 0.1 stack.35.ids
  156.5 0.0 copy-start.12
  156.5 0.0 copy-start.13
  156.5 0.0 copy-start.14
  156.6 1.8 pad_maximum_fusion.refs_15_
  158.4 1.6 pad_maximum_fusion.1.refs_16_
  160.0 0.1 collective-permute-start.8
  160.1 3.2 collective-permute-start.9
  163.3 15.7 %collective-permute-done.5.refs_6_ = bf16[1536,256]{1,0:T(8,128)(2,1)} collective-permute-done((bf16[1536,256]{1,0:T(8,128)(2,1)}, bf16[1536,256]{1,0:T(8,128)(2,1)}, u32[]{:S(2)}, u32[]{:S(2)}) %collective-permute-start.5) | collective-permute-done | bytes 786464 | tf_op jit(solution)/shard_map/ppermute | solution.py:25
  179.0 0.0 collective-permute-start.11
  179.0 0.0 copy-start.15
  179.1 0.6 copy-done.15
  179.7 0.7 copy-done.16
  180.4 14.2 %project.1 = (bf16[1536,256]{1,0:T(8,128)(2,1)S(1)}, f32[1536,256]{1,0:T(8,128)S(1)}, bf16[1536,128]{1,0:T(8,128)(2,1)S(1)}, bf16[1536,128]{1,0:T(8,128)(2,1)S(1)}) custom-call(s32[8]{0:T(128)S(1)} %stack.35.ids, bf16[1536,256]{1,0:T(8,128)(2,1)S(1)} %copy-done.12, bf16[1536,256]{1,0:T(8,128)(2,1)} %collective-permute-done.refs_1_, ...), custom_call_target="tpu_custom_call" | custom-call | flops 4831838208 | bytes 14680064 | tf_op jit(solution)/shard_map/project/pallas_call | solution.py:86
  194.6 1.2 copy-done.3
  195.7 0.9 copy-done.5
  196.6 0.8 copy-done.7
  197.4 1.4 copy-done.4
  198.8 1.1 copy-done.6
  199.9 1.0 copy-done.8
  200.9 0.7 copy-done.9
  201.6 9.0 %attend.1 = bf16[1536,256]{1,0:T(8,128)(2,1)S(1)} custom-call(s32[24]{0:T(128)S(1)} %copy-done.9, s32[24]{0:T(128)S(1)} %get-tuple-element.19.lengths, bf16[1536,256]{1,0:T(8,128)(2,1)S(1)} %copy-done.6, f32[1536,256]{1,0:T(8,128)S(1)} %copy-done.4, bf16[1536,128]{1,0:T(8,128)(2,1)S(1)} %get-tuple-element.11.k, bf16[1536,128]{1,0:T(8,128)(2,1)S(1)} %copy-done.8, ...), custom_call_target="tpu_custom_call" | custom-call | flops 301989888 | bytes 8388608 | tf_op jit(solution)/shard_map/attend/pallas_call | solution.py:152
  210.6 0.0 copy-start.2
  210.6 0.9 copy-done.2
  211.5 4.9 all-to-all-start.2
  216.3 2.0 collective-permute-start.10
  218.4 1.5 collective-permute-start.12
  219.8 0.5 collective-permute-start.16
  220.4 1.8 collective-permute-start.13
  222.1 15.8 %collective-permute-done.10.refs_4_ = bf16[128,2048]{1,0:T(8,128)(2,1)S(1)} collective-permute-done((bf16[128,2048]{1,0:T(8,128)(2,1)}, bf16[128,2048]{1,0:T(8,128)(2,1)S(1)}, u32[]{:S(2)}, u32[]{:S(2)}) %collective-permute-start.10) | collective-permute-done | bytes 524320 | tf_op jit(solution)/shard_map/ppermute | solution.py:25
  237.9 8.6 %collective-permute-done.12.refs_6_ = bf16[128,2048]{1,0:T(8,128)(2,1)S(1)} collective-permute-done((bf16[128,2048]{1,0:T(8,128)(2,1)}, bf16[128,2048]{1,0:T(8,128)(2,1)S(1)}, u32[]{:S(2)}, u32[]{:S(2)}) %collective-permute-start.12) | collective-permute-done | bytes 524320 | tf_op jit(solution)/shard_map/ppermute | solution.py:25
  246.5 0.5 collective-permute-start.18
  247.0 0.3 copy-done.19
  247.3 0.8 copy-done.20
  248.1 0.5 collective-permute-start.20
  248.6 0.1 collective-permute-start.21
  248.7 0.6 pad_add_fusion.places
  249.4 0.8 collective-permute-done.20.refs_14_
  250.1 0.2 copy-done.24
  250.3 0.2 copy-done.23
  250.5 0.8 copy-done.25
  251.3 256.0 %assemble.1.weight = bf16[2048,2048]{1,0:T(8,128)(2,1)} custom-call(s32[16]{0:T(128)} %pad_add_fusion.places, bf16[128,2048]{1,0:T(8,128)(2,1)} %constant_dynamic-slice_fusion.refs_0_, bf16[128,2048]{1,0:T(8,128)(2,1)} %collective-permute-done.7.refs_1_, bf16[128,2048]{1,0:T(8,128)(2,1)} %collective-permute-done.8.refs_2_, ...), custom_call_target="tpu_custom_call" | custom-call | bytes 16777216 | tf_op jit(solution)/shard_map/assemble/pallas_call | solution.py:185
  507.4 3.4 copy-done.1
  510.8 3.8 project_out.1
  (64 shorter events, 0.2 us)
Async XLA Ops:
  0.0 72.8 %copy-start = (bf16[256,2048]{1,0:T(8,128)(2,1)S(1)}, bf16[256,2048]{1,0:T(8,128)(2,1)}, u32[]{:S(2)}) copy-start(bf16[256,2048]{1,0:T(8,128)(2,1)} %param.21) | copy-start | bytes 3145732
  60.2 15.4 %copy-start.28 = (s32[768,1]{0,1:T(1,128)S(1)}, s32[768,1]{0,1:T(1,128)}, u32[]{:S(2)}) copy-start(s32[768,1]{0,1:T(1,128)} %param.24) | copy-start | bytes 9220
  60.2 15.5 %copy-start.27 = (s32[768]{0:T(1024)S(1)}, s32[768]{0:T(1024)}, u32[]{:S(2)}) copy-start(s32[768]{0:T(1024)} %param.25) | copy-start | bytes 9220
  60.2 137.1 %all-to-all-start.1 = ((bf16[32,256,128]{2,1,0:T(8,128)(2,1)}), bf16[32,256,128]{2,1,0:T(8,128)(2,1)}, u32[]{:S(2)}, u32[]{:S(2)}) async-start(bf16[32,256,128]{2,1,0:T(8,128)(2,1)} %bitcast.24), calls=%async_computation.1 | async-start | bytes 4194304 | tf_op jit(solution)/shard_map/all_to_all | solution.py:283
  69.4 87.0 %copy-start.26 = (f32[2048]{0:T(1024)S(1)}, f32[2048]{0:T(1024)}, u32[]{:S(2)}) copy-start(f32[2048]{0:T(1024)} %param.14) | copy-start | bytes 24580
  69.4 63.3 %collective-permute-start = (bf16[1536,256]{1,0:T(8,128)(2,1)}, bf16[1536,256]{1,0:T(8,128)(2,1)}, u32[]{:S(2)}, u32[]{:S(2)}) collective-permute-start(bf16[1536,256]{1,0:T(8,128)(2,1)} %refs_0_.1), channel_id=1, source_target_pairs={{0,4},{4,0},{1,5},{5,1},{2,6},{6,2},{3,7},{7,3},{8,12},{12,8},{9,1... | collective-permute-start | bytes 2359304 | tf_op jit(solution)/shard_map/ppermute | solution.py:25
  69.5 70.6 %collective-permute-start.1 = (bf16[1536,256]{1,0:T(8,128)(2,1)}, bf16[1536,256]{1,0:T(8,128)(2,1)}, u32[]{:S(2)}, u32[]{:S(2)}) collective-permute-start(bf16[1536,256]{1,0:T(8,128)(2,1)} %refs_0_.1), channel_id=1, source_target_pairs={{0,1},{1,2},{2,3},{3,0},{4,5},{5,6},{6,7},{7,4},{8,9},{9,10},{10,1... | collective-permute-start | bytes 2359304 | tf_op jit(solution)/shard_map/ppermute | solution.py:25
  71.1 89.0 %collective-permute-start.2 = (bf16[1536,256]{1,0:T(8,128)(2,1)}, bf16[1536,256]{1,0:T(8,128)(2,1)}, u32[]{:S(2)}, u32[]{:S(2)}) collective-permute-start(bf16[1536,256]{1,0:T(8,128)(2,1)} %refs_0_.1), channel_id=1, source_target_pairs={{0,3},{1,0},{2,1},{3,2},{4,7},{5,4},{6,5},{7,6},{8,11},{9,8},{10,9... | collective-permute-start | bytes 2359304 | tf_op jit(solution)/shard_map/ppermute | solution.py:25
  73.7 86.3 %collective-permute-start.7 = (bf16[128,2048]{1,0:T(8,128)(2,1)}, bf16[128,2048]{1,0:T(8,128)(2,1)}, u32[]{:S(2)}, u32[]{:S(2)}) collective-permute-start(bf16[128,2048]{1,0:T(8,128)(2,1)} %constant_dynamic-slice_fusion.refs_0_), channel_id=1, source_target_pairs={{0,4},{4,0},{1,5},{5,1},{2,6},{6,2},{3,7},{7,3},{8,12},{12,8},{9,1... | collective-permute-start | bytes 1572872 | tf_op jit(solution)/shard_map/ppermute | solution.py:25
  132.8 19.2 %collective-permute-start.4 = (bf16[1536,256]{1,0:T(8,128)(2,1)}, bf16[1536,256]{1,0:T(8,128)(2,1)}, u32[]{:S(2)}, u32[]{:S(2)}) collective-permute-start(bf16[1536,256]{1,0:T(8,128)(2,1)} %collective-permute-done.refs_1_), channel_id=1, source_target_pairs={{0,3},{1,0},{2,1},{3,2},{4,7},{5,4},{6,5},{7,6},{8,11},{9,8},{10,9... | collective-permute-start | bytes 2359304 | tf_op jit(solution)/shard_map/ppermute | solution.py:25
  140.1 23.2 %collective-permute-start.3 = (bf16[1536,256]{1,0:T(8,128)(2,1)}, bf16[1536,256]{1,0:T(8,128)(2,1)}, u32[]{:S(2)}, u32[]{:S(2)}) collective-permute-start(bf16[1536,256]{1,0:T(8,128)(2,1)} %collective-permute-done.refs_1_), channel_id=1, source_target_pairs={{0,1},{1,2},{2,3},{3,0},{4,5},{5,6},{6,7},{7,4},{8,9},{9,10},{10,1... | collective-permute-start | bytes 2359304 | tf_op jit(solution)/shard_map/ppermute | solution.py:25
  140.1 38.9 %collective-permute-start.5 = (bf16[1536,256]{1,0:T(8,128)(2,1)}, bf16[1536,256]{1,0:T(8,128)(2,1)}, u32[]{:S(2)}, u32[]{:S(2)}) collective-permute-start(bf16[1536,256]{1,0:T(8,128)(2,1)} %collective-permute-done.1.refs_2_), channel_id=1, source_target_pairs={{0,1},{1,2},{2,3},{3,0},{4,5},{5,6},{6,7},{7,4},{8,9},{9,10},{10,1... | collective-permute-start | bytes 2359304 | tf_op jit(solution)/shard_map/ppermute | solution.py:25
  152.0 27.0 %collective-permute-start.6 = (bf16[1536,256]{1,0:T(8,128)(2,1)}, bf16[1536,256]{1,0:T(8,128)(2,1)}, u32[]{:S(2)}, u32[]{:S(2)}) collective-permute-start(bf16[1536,256]{1,0:T(8,128)(2,1)} %collective-permute-done.4.refs_5_), channel_id=1, source_target_pairs={{0,3},{1,0},{2,1},{3,2},{4,7},{5,4},{6,5},{7,6},{8,11},{9,8},{10,9... | collective-permute-start | bytes 2359304 | tf_op jit(solution)/shard_map/ppermute | solution.py:25
  156.5 22.5 %copy-start.10 = (bf16[2048,256]{1,0:T(8,128)(2,1)S(1)}, bf16[2048,256]{1,0:T(8,128)(2,1)}, u32[]{:S(2)}) copy-start(bf16[2048,256]{1,0:T(8,128)(2,1)} %refs_9_.1) | copy-start | bytes 3145732
  156.5 22.5 %copy-start.11 = (bf16[2048,256]{1,0:T(8,128)(2,1)S(1)}, bf16[2048,256]{1,0:T(8,128)(2,1)}, u32[]{:S(2)}) copy-start(bf16[2048,256]{1,0:T(8,128)(2,1)} %refs_10_.1) | copy-start | bytes 3145732
  156.5 22.5 %copy-start.12 = (bf16[1536,256]{1,0:T(8,128)(2,1)S(1)}, bf16[1536,256]{1,0:T(8,128)(2,1)}, u32[]{:S(2)}) copy-start(bf16[1536,256]{1,0:T(8,128)(2,1)} %refs_0_.1) | copy-start | bytes 2359300
  156.5 22.5 %copy-start.13 = (bf16[2048,128]{1,0:T(8,128)(2,1)S(1)}, bf16[2048,128]{1,0:T(8,128)(2,1)}, u32[]{:S(2)}) copy-start(bf16[2048,128]{1,0:T(8,128)(2,1)} %refs_11_.1) | copy-start | bytes 1572868
  156.5 22.5 %copy-start.14 = (bf16[2048,128]{1,0:T(8,128)(2,1)S(1)}, bf16[2048,128]{1,0:T(8,128)(2,1)}, u32[]{:S(2)}) copy-start(bf16[2048,128]{1,0:T(8,128)(2,1)} %refs_12_.1) | copy-start | bytes 1572868
  160.0 58.4 %collective-permute-start.8 = (bf16[128,2048]{1,0:T(8,128)(2,1)}, bf16[128,2048]{1,0:T(8,128)(2,1)}, u32[]{:S(2)}, u32[]{:S(2)}) collective-permute-start(bf16[128,2048]{1,0:T(8,128)(2,1)} %constant_dynamic-slice_fusion.refs_0_), channel_id=1, source_target_pairs={{0,1},{1,2},{2,3},{3,0},{4,5},{5,6},{6,7},{7,4},{8,9},{9,10},{10,1... | collective-permute-start | bytes 1572872 | tf_op jit(solution)/shard_map/ppermute | solution.py:25
  160.1 59.7 %collective-permute-start.9 = (bf16[128,2048]{1,0:T(8,128)(2,1)}, bf16[128,2048]{1,0:T(8,128)(2,1)}, u32[]{:S(2)}, u32[]{:S(2)}) collective-permute-start(bf16[128,2048]{1,0:T(8,128)(2,1)} %constant_dynamic-slice_fusion.refs_0_), channel_id=1, source_target_pairs={{0,3},{1,0},{2,1},{3,2},{4,7},{5,4},{6,5},{7,6},{8,11},{9,8},{10,9... | collective-permute-start | bytes 1572872 | tf_op jit(solution)/shard_map/ppermute | solution.py:25
  163.3 56.5 %collective-permute-start.14 = (bf16[128,2048]{1,0:T(8,128)(2,1)}, bf16[128,2048]{1,0:T(8,128)(2,1)}, u32[]{:S(2)}, u32[]{:S(2)}) collective-permute-start(bf16[128,2048]{1,0:T(8,128)(2,1)} %constant_dynamic-slice_fusion.refs_0_), channel_id=1, source_target_pairs={{0,8},{8,0},{1,9},{9,1},{2,10},{10,2},{3,11},{11,3},{4,12},{12,4},... | collective-permute-start | bytes 1572872 | tf_op jit(solution)/shard_map/ppermute | solution.py:25
  179.0 41.4 %collective-permute-start.11 = (bf16[128,2048]{1,0:T(8,128)(2,1)}, bf16[128,2048]{1,0:T(8,128)(2,1)}, u32[]{:S(2)}, u32[]{:S(2)}) collective-permute-start(bf16[128,2048]{1,0:T(8,128)(2,1)} %collective-permute-done.7.refs_1_), channel_id=1, source_target_pairs={{0,3},{1,0},{2,1},{3,2},{4,7},{5,4},{6,5},{7,6},{8,11},{9,8},{10,9... | collective-permute-start | bytes 1572872 | tf_op jit(solution)/shard_map/ppermute | solution.py:25
  179.0 0.7 copy-start.15
  179.7 0.7 copy-start.16
  194.6 1.2 copy-start.3
  195.7 0.9 copy-start.5
  196.6 0.8 copy-start.7
  197.4 1.4 copy-start.4
  198.8 1.1 copy-start.6
  199.9 1.0 copy-start.8
  200.9 0.7 copy-start.9
  210.6 0.9 copy-start.2
  211.5 295.9 %all-to-all-start.2 = ((bf16[8,192,256]{2,1,0:T(8,128)(2,1)}), bf16[8,192,256]{2,1,0:T(8,128)(2,1)S(1)}, u32[]{:S(2)}, u32[]{:S(2)}) async-start(bf16[8,192,256]{2,1,0:T(8,128)(2,1)} %bitcast.20), calls=%async_computation.2 | async-start | bytes 1572864 | tf_op jit(solution)/shard_map/all_to_all | solution.py:299
  216.3 21.5 %collective-permute-start.10 = (bf16[128,2048]{1,0:T(8,128)(2,1)}, bf16[128,2048]{1,0:T(8,128)(2,1)S(1)}, u32[]{:S(2)}, u32[]{:S(2)}) collective-permute-start(bf16[128,2048]{1,0:T(8,128)(2,1)} %collective-permute-done.7.refs_1_), channel_id=1, source_target_pairs={{0,1},{1,2},{2,3},{3,0},{4,5},{5,6},{6,7},{7,4},{8,9},{9,10},{10,1... | collective-permute-start | bytes 1572872 | tf_op jit(solution)/shard_map/ppermute | solution.py:25
  218.4 28.1 %collective-permute-start.12 = (bf16[128,2048]{1,0:T(8,128)(2,1)}, bf16[128,2048]{1,0:T(8,128)(2,1)S(1)}, u32[]{:S(2)}, u32[]{:S(2)}) collective-permute-start(bf16[128,2048]{1,0:T(8,128)(2,1)} %collective-permute-done.8.refs_2_), channel_id=1, source_target_pairs={{0,1},{1,2},{2,3},{3,0},{4,5},{5,6},{6,7},{7,4},{8,9},{9,10},{10,1... | collective-permute-start | bytes 1572872 | tf_op jit(solution)/shard_map/ppermute | solution.py:25
  219.8 26.7 %collective-permute-start.15 = (bf16[128,2048]{1,0:T(8,128)(2,1)}, bf16[128,2048]{1,0:T(8,128)(2,1)S(1)}, u32[]{:S(2)}, u32[]{:S(2)}) collective-permute-start(bf16[128,2048]{1,0:T(8,128)(2,1)} %collective-permute-done.7.refs_1_), channel_id=1, source_target_pairs={{0,8},{8,0},{1,9},{9,1},{2,10},{10,2},{3,11},{11,3},{4,12},{12,4},... | collective-permute-start | bytes 1572872 | tf_op jit(solution)/shard_map/ppermute | solution.py:25
  219.8 27.5 %collective-permute-start.16 = (bf16[128,2048]{1,0:T(8,128)(2,1)}, bf16[128,2048]{1,0:T(8,128)(2,1)S(1)}, u32[]{:S(2)}, u32[]{:S(2)}) collective-permute-start(bf16[128,2048]{1,0:T(8,128)(2,1)} %collective-permute-done.8.refs_2_), channel_id=1, source_target_pairs={{0,8},{8,0},{1,9},{9,1},{2,10},{10,2},{3,11},{11,3},{4,12},{12,4},... | collective-permute-start | bytes 1572872 | tf_op jit(solution)/shard_map/ppermute | solution.py:25
  220.4 28.2 %collective-permute-start.13 = (bf16[128,2048]{1,0:T(8,128)(2,1)}, bf16[128,2048]{1,0:T(8,128)(2,1)S(1)}, u32[]{:S(2)}, u32[]{:S(2)}) collective-permute-start(bf16[128,2048]{1,0:T(8,128)(2,1)} %collective-permute-done.11.refs_5_), channel_id=1, source_target_pairs={{0,3},{1,0},{2,1},{3,2},{4,7},{5,4},{6,5},{7,6},{8,11},{9,8},{10,9... | collective-permute-start | bytes 1572872 | tf_op jit(solution)/shard_map/ppermute | solution.py:25
  237.9 13.4 %copy-start.17 = (bf16[128,2048]{1,0:T(8,128)(2,1)}, bf16[128,2048]{1,0:T(8,128)(2,1)S(1)}, u32[]{:S(2)}) copy-start(bf16[128,2048]{1,0:T(8,128)(2,1)S(1)} %collective-permute-done.10.refs_4_) | copy-start | bytes 1572868
  237.9 11.4 %collective-permute-start.17 = (bf16[128,2048]{1,0:T(8,128)(2,1)}, bf16[128,2048]{1,0:T(8,128)(2,1)S(1)}, u32[]{:S(2)}, u32[]{:S(2)}) collective-permute-start(bf16[128,2048]{1,0:T(8,128)(2,1)} %collective-permute-done.9.refs_3_), channel_id=1, source_target_pairs={{0,8},{8,0},{1,9},{9,1},{2,10},{10,2},{3,11},{11,3},{4,12},{12,4},... | collective-permute-start | bytes 1572872 | tf_op jit(solution)/shard_map/ppermute | solution.py:25
  246.5 4.8 copy-start.18
  246.5 2.8 collective-permute-start.19
  246.5 0.8 copy-start.19
  246.5 2.8 collective-permute-start.18
  247.3 0.8 copy-start.20
  248.1 2.0 collective-permute-start.20
  248.6 1.5 copy-start.21
  248.6 2.7 collective-permute-start.21
  249.3 0.8 copy-start.22
  249.3 1.0 copy-start.24
  249.4 1.2 copy-start.23
  250.5 0.8 copy-start.25
  507.4 3.4 copy-start.1

commit v2 on v1

--- a/solution.py
+++ b/solution.py
@@ -15,6 +15,8 @@
 TENSOR = ("zl", "x")
 ROW_TILE = 256
 BATCH = 4
+UNIT = 16
+PACKED = 72 * UNIT
 
 
 def ring(size, step):
@@ -106,13 +108,25 @@
     )(ids, *pieces, *constants, cosine, sine)
 
 
-def attend_kernel(starts, lengths, q, g, k, v, keys, values, out):
+def attend_kernel(starts, lengths, q, g, k, v, *refs):
+    key_parts, value_parts = refs[:4], refs[4:8]
+    out, keys, values = refs[8:]
     head = k.shape[1]
     span = q.shape[0] // BATCH
-    window = 128
     shares = q.shape[1] // head
+    size = key_parts[0].shape[0]
+    window = keys.shape[0] - 4 * size
     score_scale = 1.0 / math.sqrt(head)
     contract = (((1,), (1,)), ((), ()))
+
+    @pl.when(pl.program_id(0) == 0)
+    def _():
+        for j in range(4):
+            keys[j * size : (j + 1) * size, :] = key_parts[j][...]
+            values[j * size : (j + 1) * size, :] = value_parts[j][...]
+        keys[4 * size :, :] = jnp.zeros((window, head), keys.dtype)
+        values[4 * size :, :] = jnp.zeros((window, head), values.dtype)
+
     column = lax.broadcasted_iota(jnp.int32, (shares * span, window), 1)
     old_row = lax.broadcasted_iota(jnp.int32, (window, head), 0)
     token = lax.broadcasted_iota(jnp.int32, (shares, span, span), 1).reshape(shares * span, span)
@@ -122,7 +136,7 @@
         length = lengths[r]
         rows = slice(b * span, (b + 1) * span)
         query = jnp.concatenate([q[rows, s * head : (s + 1) * head] for s in range(shares)], axis=0)
-        place = pl.ds(pl.multiple_of(starts[r], 16), window)
+        place = pl.ds(pl.multiple_of(starts[r], UNIT), window)
         old_keys, old_values = keys[place, :], values[place, :]
         old_values = jnp.where(old_row < length, old_values, jnp.zeros_like(old_values))
         old = lax.dot_general(query, old_keys, contract, preferred_element_type=jnp.float32)
@@ -143,92 +157,120 @@
             out[rows, columns] = part.astype(jnp.bfloat16)
 
 
-def attend(starts, lengths, q, g, k, v, keys, values):
+def attend(starts, lengths, q, g, k, v, keys, values, window):
     rows, columns = q.shape
     head = k.shape[1]
     step = rows // lengths.shape[0] * BATCH
     tile = lambda width: pl.BlockSpec((step, width), lambda i, *_: (i, 0))
     whole = lambda a: pl.BlockSpec(a.shape, lambda i, *_: (0, 0))
+    store = pltpu.VMEM((4 * keys[0].shape[0] + window, head), keys[0].dtype)
     return pl.pallas_call(
         attend_kernel,
         out_shape=jax.ShapeDtypeStruct((rows, columns), jnp.bfloat16),
         grid_spec=pltpu.PrefetchScalarGridSpec(
             num_scalar_prefetch=2,
             grid=(rows // step,),
-            in_specs=[tile(columns)] * 2 + [tile(head)] * 2 + [whole(keys), whole(values)],
+            in_specs=[tile(columns)] * 2 + [tile(head)] * 2 + [whole(a) for a in keys + values],
             out_specs=tile(columns),
+            scratch_shapes=[store, store],
         ),
         compiler_params=pltpu.CompilerParams(vmem_limit_bytes=40 << 20),
         cost_estimate=pl.CostEstimate(
             flops=4 * rows * columns * 192, bytes_accessed=8 << 20, transcendentals=rows * 2 * 192
         ),
         name="attend",
-    )(starts, lengths, q, g, k, v, keys, values)
-
-
-def assemble_kernel(places, *refs):
-    pieces, out, sems = refs[:-2], refs[-2], refs[-1]
-    depth = pieces[0].shape[0]
-    copies = []
-    for j, piece in enumerate(pieces):
-        start = pl.multiple_of(places[j] * depth, depth)
-        copies.append(pltpu.make_async_copy(piece, out.at[pl.ds(start, depth)], sems.at[j]))
-    for copy in copies:
-        copy.start()
-    for copy in copies:
-        copy.wait()
-
-
-def assemble(places, pieces):
-    depth, columns = pieces[0].shape
-    count = len(pieces)
+    )(starts, lengths, q, g, k, v, *keys, *values)
+
+
+def pack_kernel(offsets, *refs):
+    pieces, outs, store = refs[:4], refs[4:8], refs[8]
+    slots, window = pieces[0].shape[2], pieces[0].shape[3]
+    size = outs[0].shape[0]
+    for k, out in enumerate(outs):
+        for j in range(4 * 2 * slots):
+            p, q, rank = j // (2 * slots), j // slots % 2, j % slots
+            block = offsets[4 * 4 * 2 * slots + k]
+            place = pl.multiple_of(offsets[k * 4 * 2 * slots + j], UNIT)
+            store[pl.ds(place, window), :] = pieces[p][q, block, rank]
+        out[...] = store[:size, :]
+
+
+def pack(offsets, pieces, size):
+    window, head = pieces[0].shape[3:]
     return pl.pallas_call(
-        assemble_kernel,
-        out_shape=jax.ShapeDtypeStruct((depth * count, columns), pieces[0].dtype),
+        pack_kernel,
+        out_shape=[jax.ShapeDtypeStruct((size, head), pieces[0].dtype)] * 4,
         grid_spec=pltpu.PrefetchScalarGridSpec(
             num_scalar_prefetch=1,
             grid=(1,),
-            in_specs=[pl.BlockSpec(memory_space=pl.ANY)] * count,
-            out_specs=pl.BlockSpec(memory_space=pl.ANY),
-            scratch_shapes=[pltpu.SemaphoreType.DMA((count,))],
-        ),
-        cost_estimate=pl.CostEstimate(flops=0, bytes_accessed=16 << 20, transcendentals=0),
-        name="assemble",
-    )(places, *pieces)
-
-
-def output_kernel(heads, weight, out, joined):
-    width = heads.shape[2]
+            in_specs=[pl.BlockSpec(a.shape, lambda i, _: (0,) * 5) for a in pieces],
+            out_specs=[pl.BlockSpec((size, head), lambda i, _: (0, 0))] * 4,
+            scratch_shapes=[pltpu.VMEM((size + window, head), pieces[0].dtype)],
+        ),
+        compiler_params=pltpu.CompilerParams(vmem_limit_bytes=30 << 20),
+        cost_estimate=pl.CostEstimate(flops=0, bytes_accessed=4 << 20, transcendentals=0),
+        name="pack",
+    )(offsets, *pieces)
+
+
+def output_kernel(places, heads, mine, other, out, joined):
+    count, depth = mine.shape[:2]
 
     @pl.when(pl.program_id(0) == 0)
     def _():
-        for j in range(heads.shape[0]):
-            joined[:, j * width : (j + 1) * width] = heads[j]
-
-    total = jnp.dot(joined[...], weight[...], preferred_element_type=jnp.float32)
+        for j in range(count):
+            for h in range(2):
+                first = pl.multiple_of((places[count] + h) % 2 * depth, depth)
+                columns = slice((2 * j + h) * depth, (2 * j + h + 1) * depth)
+                joined[:, columns] = heads[places[j], :, pl.ds(first, depth)]
+
+    total = jnp.zeros(out.shape, jnp.float32)
+    for j in range(count):
+        weight = jnp.concatenate([mine[j], other[j]], axis=0)
+        part = joined[:, 2 * j * depth : 2 * (j + 1) * depth]
+        total = total + jnp.dot(part, weight, preferred_element_type=jnp.float32)
     out[...] = total.astype(jnp.bfloat16)
 
 
-def project_out(heads, weight):
+def project_out(places, heads, mine, other):
     blocks, rows, width = heads.shape
-    depth, columns = weight.shape
+    depth, columns = mine.shape[1:]
     tile = 512
+    half = pl.BlockSpec((blocks, depth, tile), lambda i, _: (0, 0, i))
     return pl.pallas_call(
         output_kernel,
         out_shape=jax.ShapeDtypeStruct((rows, columns), jnp.bfloat16),
-        grid=(columns // tile,),
-        in_specs=[
-            pl.BlockSpec(heads.shape, lambda i: (0, 0, 0)),
-            pl.BlockSpec((depth, tile), lambda i: (0, i)),
-        ],
-        out_specs=pl.BlockSpec((rows, tile), lambda i: (0, i)),
-        scratch_shapes=[pltpu.VMEM((rows, depth), jnp.bfloat16)],
+        grid_spec=pltpu.PrefetchScalarGridSpec(
+            num_scalar_prefetch=1,
+            grid=(columns // tile,),
+            in_specs=[pl.BlockSpec(heads.shape, lambda i, _: (0, 0, 0)), half, half],
+            out_specs=pl.BlockSpec((rows, tile), lambda i, _: (0, i)),
+            scratch_shapes=[pltpu.VMEM((rows, blocks * width), jnp.bfloat16)],
+        ),
         compiler_params=pltpu.CompilerParams(vmem_limit_bytes=30 << 20),
         cost_estimate=pl.CostEstimate(
-            flops=2 * rows * depth * columns, bytes_accessed=10 << 20, transcendentals=0
+            flops=2 * rows * blocks * width * columns, bytes_accessed=10 << 20, transcendentals=0
         ),
         name="project_out",
-    )(heads, weight)
+    )(places, heads, mine, other)
+
+
+def take(array, index):
+    return lax.dynamic_index_in_dim(array, index, 0, keepdims=False)
+
+
+def across_y(cache, groups, capacity):
+    window, head = cache.shape[1:]
+    y, c = lax.axis_index("y"), lax.axis_index("c")
+    sides = cache.reshape(4, 4, 2, capacity, window, head)
+    own = lax.dynamic_index_in_dim(sides, c, 2, keepdims=False)
+    twin = shift(lax.dynamic_index_in_dim(sides, 1 - c, 2, keepdims=False), "c", 1)
+    parts = [jnp.stack([take(own, (y + k) % 4), take(twin, (y + k) % 4)]) for k in range(4)]
+    return [parts[0]] + [shift(parts[k], "y", k) for k in (1, 3, 2)]
+
+
+def across_z(parts):
+    return [parts[0]] + [shift(parts[k], "zh", k) for k in range(1, 4)]
 
 
 def local(
@@ -246,7 +288,7 @@
     holders,
     prefix_lengths,
 ):
-    groups = 32
+    groups = lax.axis_size(GROUP)
     group_id = lax.axis_index(GROUP)
     requests = prefix_lengths.shape[0] // groups
     rows = span_rows.shape[0]
@@ -256,15 +298,51 @@
     window = key_cache.shape[2]
     blocks = lax.axis_size(TENSOR)
 
+    y, zh, core = lax.axis_index("y"), lax.axis_index("zh"), lax.axis_index("c")
     all_holders = holders.reshape(groups, requests)
-    my_holders = lax.dynamic_index_in_dim(all_holders, group_id, 0, keepdims=False)
-    my_lengths = lax.dynamic_index_in_dim(
-        prefix_lengths.reshape(groups, requests), group_id, 0, keepdims=False
-    )
+    all_lengths = prefix_lengths.reshape(groups, requests)
     order = jnp.arange(requests)
     earlier = order[None, :] < order[:, None]
-    my_ranks = jnp.sum((my_holders[:, None] == my_holders[None, :]) & earlier, axis=1)
-    starts = ((my_holders * capacity + my_ranks) * window).astype(jnp.int32)
+    same = all_holders[:, :, None] == all_holders[:, None, :]
+    all_ranks = jnp.sum(same & earlier[None], axis=2)
+    all_units = (all_lengths + UNIT - 1) // UNIT
+    plane = all_holders // 2 % 4
+    per_plane = jnp.sum(
+        jnp.where(plane[:, :, None] == jnp.arange(4), all_units[:, :, None], 0), axis=1
+    )
+    fits = jnp.max(per_plane) * UNIT <= PACKED
+
+    seen_y, seen_c = jnp.array([0, 3, 1, 2]), jnp.array([0, 1])
+    slot_y = (y + seen_y[:, None, None]) % 4
+    slot_c = (core + seen_c[None, :, None]) % 2
+    slot_rank = jnp.arange(capacity)[None, None, :]
+    z_ids = (zh + jnp.arange(4)) % 4
+    served = (y * 4 + z_ids) * 2 + core
+    slot_holder = (slot_y * 4 + zh) * 2 + slot_c
+    slot_key = (slot_holder * capacity + slot_rank).reshape(-1)
+    served_key = (all_holders * capacity + all_ranks)[served]
+    hit = served_key[:, :, None] == slot_key[None, None, :]
+    slot_units = jnp.sum(jnp.where(hit, all_units[served][:, :, None], 0), axis=1)
+    offsets = (jnp.cumsum(slot_units, axis=1) - slot_units) * UNIT
+    z_ids = z_ids.astype(jnp.int32)
+
+    mine = lambda a: lax.dynamic_index_in_dim(a, group_id, 0, keepdims=False)
+    my_holders, my_ranks, my_lengths, my_units = map(
+        mine, (all_holders, all_ranks, all_lengths, all_units)
+    )
+    from_y = (my_holders // 8 - y) % 4
+    from_y = jnp.where(from_y == 3, 1, jnp.where(from_y == 1, 2, jnp.where(from_y == 2, 3, 0)))
+    from_z = (zh - my_holders // 2 % 4) % 4
+    from_c = (my_holders - core) % 2
+    my_order = (from_y * 2 + from_c) * capacity + my_ranks
+    ahead = (from_z[:, None] == from_z[None, :]) & (my_order[None, :] < my_order[:, None])
+    my_start = jnp.sum(jnp.where(ahead, my_units[None, :], 0), axis=1) * UNIT
+
+    def packing(size):
+        limit = jnp.minimum(offsets, size).reshape(-1)
+        places = jnp.concatenate([limit, z_ids]).astype(jnp.int32)
+        starts = jnp.minimum(from_z * size + my_start, 4 * size)
+        return places, starts.astype(jnp.int32)
 
     positions = my_lengths[:, None] + jnp.arange(span_len, dtype=jnp.int32)[None, :]
     half = head_dim // 2
@@ -277,29 +355,44 @@
     ids = block_ids()
     pieces = spread(span_rows)
 
-    local_keys = key_cache.reshape(groups, capacity * window, head_dim)
-    local_values = value_cache.reshape(groups, capacity * window, head_dim)
-    keys = lax.all_to_all(local_keys, GROUP, 0, 0, tiled=True).reshape(-1, head_dim)
-    values = lax.all_to_all(local_values, GROUP, 0, 0, tiled=True).reshape(-1, head_dim)
+    key_parts = across_y(key_cache[0], groups, capacity)
+    value_parts = across_y(value_cache[0], groups, capacity)
+    places, starts = packing(PACKED)
+    keys = across_z(pack(places, key_parts, PACKED))
+    values = across_z(pack(places, value_parts, PACKED))
+
+    depth = o_weight.shape[0] // 2
+    half, pieces[6], pieces[7] = lax.optimization_barrier(
+        (lax.dynamic_slice_in_dim(o_weight, core * depth, depth, 0), pieces[6], pieces[7])
+    )
+    pair = jnp.stack([half, shift(half, "zl", 1)])
+    below, above = shift(pair, "x", 1), shift(pair, "x", -1)
+    far, twin_far = shift(below[0], "x", 1), shift(above[1], "x", -1)
+    halves = jnp.stack(
+        [pair[0], pair[1], below[0], above[0], below[1], above[1], far, twin_far]
+    )
+    other_halves = shift(halves, "c", 1)
 
     q, g, k, v = project(
         ids, pieces, norm_gain, q_weight, gate_weight, k_weight, v_weight,
         q_norm_gain, k_norm_gain, cosine, sine,
     )
 
-    core = lax.axis_index("c")
-    depth = o_weight.shape[0] // 2
-    mine = lax.dynamic_slice_in_dim(o_weight, core * depth, depth, 0)
-    half_pieces = spread(mine)
-    other_pieces = [shift(p, "c", 1) for p in half_pieces]
-    places = jnp.concatenate([ids * 2 + core, ids * 2 + 1 - core]).astype(jnp.int32)
-    whole_weight = assemble(places, half_pieces + other_pieces)
-
-    attended = attend(starts, my_lengths, q, g, k, v, keys, values)
+    def packed(keys, values, key_parts, value_parts, q, g, k, v):
+        return attend(starts, my_lengths, q, g, k, v, keys, values, window)
+
+    def full(keys, values, key_parts, value_parts, q, g, k, v):
+        size = 8 * capacity * window
+        places, starts = packing(size)
+        keys, values = (across_z(pack(places, a, size)) for a in (key_parts, value_parts))
+        return attend(starts, my_lengths, q, g, k, v, keys, values, window)
+
+    attended = lax.cond(fits, packed, full, keys, values, key_parts, value_parts, q, g, k, v)
     heads = lax.all_to_all(
         attended.reshape(blocks, rows // blocks, attended.shape[1]), TENSOR, 0, 0, tiled=True
     )
-    return project_out(heads, whole_weight)
+    out_places = jnp.concatenate([ids, core[None]]).astype(jnp.int32)
+    return project_out(out_places, heads, halves, other_halves)
 
 
 def solution(mesh):

time: 517 us -> 249 us (0.48)
  Pallas kernels: 283 us -> 36.7 us
  blocking collectives: 60.2 us -> 0 us
  starting transfers between devices: 36.7 us -> 51.7 us
  other arithmetic: 9.36 us -> 20.5 us
  local copies, waits for them, and re-layouts: 16.1 us -> 21.9 us
    pallas_call x1 -> x2, Pallas kernels: 256 us -> 5.84 us  [pack(): pl.pallas_call(pack_kernel, out_shape=[jax.ShapeDtypeStruct((size, head),...]
    all_to_all x1 -> x0, blocking collectives: 60.2 us -> none  [local(): lax.all_to_all(local_keys, GROUP, 0, 0, tiled=True).reshape(-1, head_dim)]
    ppermute x22 -> x27, starting transfers between devices: 22.7 us -> 46.4 us  [shift(): return lax.ppermute(value, axis, ring(lax.axis_size(axis), step))]
    all_to_all x1, waiting for transfers between devices: 0.01 us -> 12.6 us  [local(): lax.all_to_all(attended.reshape(blocks, rows // blocks, attended.shape[1]...]
    another operation x0 -> x10, other arithmetic: none -> 11.7 us  [the longest x8 11.4 us: across_y(): jnp.stack([take(own, (y + k) % 4), take(twin, (y + k) % 4)])]
    unnamed x58 -> x43, local copies, waits for them, and re-layouts: 14.9 us -> 4.42 us
    all_to_all x1 -> x0, starting transfers between devices: 9.16 us -> none  [local(): lax.all_to_all(local_values, GROUP, 0, 0, tiled=True).reshape(-1, head_dim)]
    ppermute x22 -> x27, waiting for transfers between devices: 109 us -> 100 us  [shift(): return lax.ppermute(value, axis, ring(lax.axis_size(axis), step))]
  transfers between devices with their start and end apart: 24 -> 28, of which waited for: 6 -> 12; matrix products, arithmetic and copies ran while one was open for 2% -> 17% of each run, Pallas kernels for 54% -> 8%
where the time goes in v2:
time: 249 us; the launch traced here: 245 us
  waiting for transfers between devices  113 us (45%)
  starting transfers between devices  51.7 us (21%)
  Pallas kernels  36.7 us (15%)
  local copies, waits for them, and re-layouts  21.9 us (9%)
  other arithmetic  20.5 us (8%)
    ppermute x27, waiting for transfers between devices, shift(): return lax.ppermute(value, axis, ring(lax.axis_size(axis), step))  100 us
    ppermute x27, starting transfers between devices, shift(): return lax.ppermute(value, axis, ring(lax.axis_size(axis), step))  46.4 us
    pallas_call x1, Pallas kernels, project(): pl.pallas_call(project_kernel, out_shape=(jax.ShapeDtypeStruct((rows, wq....  14.4 us
    all_to_all x1, waiting for transfers between devices, local(): lax.all_to_all(attended.reshape(blocks, rows // blocks, attended.shape[1]...  12.6 us
    another operation x8, other arithmetic, across_y(): jnp.stack([take(own, (y + k) % 4), take(twin, (y + k) % 4)])  11.4 us
    pallas_call x1, Pallas kernels, attend(): pl.pallas_call(attend_kernel, out_shape=jax.ShapeDtypeStruct((rows, colum...  9.82 us
    dynamic_slice x3, local copies, waits for them, and re-layouts, take(): return lax.dynamic_index_in_dim(array, index, 0, keepdims=False)  7.21 us
    pallas_call x1, Pallas kernels, project_out(): pl.pallas_call(output_kernel, out_shape=jax.ShapeDtypeStruct((rows, colum...  6.64 us
  transfers between devices with their start and end apart: 28, of which 12 were waited for; matrix products, arithmetic and copies ran while one was open for 17% of the time, Pallas kernels for 8%

profile of v2, /device:TPU:8, one launch (start us, length us, event | category | flops | bytes accessed | tf_op | source)
XLA Modules:
  0.0 244.5 jit_solution(4630297591420172889)
XLA Ops:
  0.0 1.9 collective-permute-start.14
  1.9 1.5 collective-permute-start.15
  3.4 2.4 dynamic-slice_bitcast_fusion
  5.8 2.3 dynamic-slice_bitcast_fusion.1
  8.1 0.5 collective-permute-start.6
  8.7 2.2 dynamic-slice_bitcast_fusion.6
  10.9 2.2 dynamic-slice_bitcast_fusion.2
  14.1 0.6 gather_fusion.1
  14.6 0.6 gather_fusion
  16.1 4.4 %fusion = (f32[1536,64]{1,0:T(8,128)}, f32[1536,64]{1,0:T(8,128)}, f32[1536,64]{1,0:T(8,128)}) fusion(f32[64]{0:T(128)S(1)} %multiply_power_fusion, f32[1536]{0:T(1024)S(1)} %convert_element_type.19), kind=kLoop, calls=%fused_computation.38 | loop fusion | flops 196608 | bytes 1186048 | tf_op jit(solution)/shard_map/neg | solution.py:353
  20.5 2.8 %constant_dynamic-slice_fusion.2 = (bf16[1,4,2,128,128]{4,3,2,1,0:T(8,128)(2,1)}, bf16[1,4,2,128,128]{4,3,2,1,0:T(8,128)(2,1)}, bf16[1,4,2,128,128]{4,3,2,1,0:T(...) fusion(bf16[4,4,2,128,128]{4,3,2,1,0:T(8,128)(2,1)} %collective, ...), kind=kLoop, calls=%fused_computation.105 | loop fusion | bytes 4194320 | tf_op jit(solution)/shard_map/jit(dynamic_index_in_dim)/dynamic_slice | solution.py:259
  23.3 0.8 pad_maximum_fusion.4
  24.2 1.6 collective-permute-start.7
  26.1 1.8 collective-permute-start.18
  27.8 1.9 pad_maximum_fusion.5
  30.1 1.9 pad_maximum_fusion.6
  32.0 2.3 collective-permute-start.9
  34.3 1.9 pad_maximum_fusion.8
  36.2 1.9 pad_maximum_fusion.9
  38.1 0.8 collective-permute-start.11
  39.3 0.9 collective-permute-start.12
  40.2 0.9 constant_dynamic-slice_fusion
  41.1 1.9 pad_maximum_fusion.10
  43.0 12.4 %collective-permute-done.8.refs_2_ = bf16[2,4,2,128,128]{4,3,2,1,0:T(8,128)(2,1)} collective-permute-done((bf16[2,4,2,128,128]{4,3,2,1,0:T(8,128)(2,1)}, bf16[2,4,2,128,128]{4,3,2,1,0:T(8,128)(2,1)}, u32[]{:S(2)}, u32[]{:S(2)}) %collective-permute-start.8) | collective-permute-done | bytes 524320 | tf_op jit(solution)/shard_map/ppermute | solution.py:27
  55.3 2.9 %collective-permute-start.13 = (bf16[2,4,2,128,128]{4,3,2,1,0:T(8,128)(2,1)}, bf16[2,4,2,128,128]{4,3,2,1,0:T(8,128)(2,1)}, u32[]{:S(2)}, u32[]{:S(2)}) collective-permute-start(bf16[2,4,2,128,128]{4,3,2,1,0:T(8,128)(2,1)} %pad_maximum_fusion.10), channel_id=1, source_target_pairs={{0,128},{64,192},{128,0},{192,64},{1,129},{65,193},{129,1},{193,65... | collective-permute-start | bytes 1572872 | tf_op jit(solution)/shard_map/ppermute | solution.py:27
  58.4 1.6 collective-permute-start.16
  60.0 1.8 collective-permute-done.11.refs_1_
  61.8 1.5 collective-permute-start.17
  63.3 3.3 %collective-permute-done.12.refs_2_ = bf16[2,4,2,128,128]{4,3,2,1,0:T(8,128)(2,1)} collective-permute-done((bf16[2,4,2,128,128]{4,3,2,1,0:T(8,128)(2,1)}, bf16[2,4,2,128,128]{4,3,2,1,0:T(8,128)(2,1)}, u32[]{:S(2)}, u32[]{:S(2)}) %collective-permute-start.12) | collective-permute-done | bytes 524320 | tf_op jit(solution)/shard_map/ppermute | solution.py:27
  66.9 3.0 %collective-permute-start.20 = (bf16[1536,256]{1,0:T(8,128)(2,1)}, bf16[1536,256]{1,0:T(8,128)(2,1)}, u32[]{:S(2)}, u32[]{:S(2)}) collective-permute-start(bf16[1536,256]{1,0:T(8,128)(2,1)} %collective-permute-done.18.refs_5_), channel_id=1, source_target_pairs={{0,3},{1,0},{2,1},{3,2},{4,7},{5,4},{6,5},{7,6},{8,11},{9,8},{10,9... | collective-permute-start | bytes 2359304 | tf_op jit(solution)/shard_map/ppermute | solution.py:27
  69.9 0.6 reduce_max.9
  71.3 2.5 %pad_maximum_fusion.1 = (f32[1536,128]{1,0:T(8,128)S(1)}, f32[1536,128]{1,0:T(8,128)S(1)}) fusion(f32[1536,64]{1,0:T(8,128)} %get-tuple-element.184, f32[1536,64]{1,0:T(8,128)} %get-tuple-element.183, f32[1536,64]{1,0:T(8,128)} %get-tuple-element.182), kind=kLoop, calls=%fused_computation.11 | loop fusion | flops 393216 | bytes 2752512 | tf_op jit(solution)/shard_map/concatenate | solution.py:352
  73.8 1.1 pad_maximum_fusion.3.refs_0_
  74.9 2.9 %pack.6 = (bf16[1152,128]{1,0:T(8,128)(2,1)}, bf16[1152,128]{1,0:T(8,128)(2,1)S(1)}, bf16[1152,128]{1,0:T(8,128)(2,1)S(1)}, bf16[1152,128]{1,0:T(8,128)(2,1)S(1)}) custom-call(s32[68]{0:T(128)S(1)} %pad_add_fusion.1.offsets, bf16[2,4,2,128,128]{4,3,2,1,0:T(8,128)(2,1)S(1)} %pad_maximum_fusion.3.refs_0_, ...), custom_call_target="tpu_custom_call" | custom-call | bytes 4194304 | tf_op jit(solution)/shard_map/pack/pallas_call | solution.py:200
  77.8 3.3 %collective-permute-start.21 = (bf16[1152,128]{1,0:T(8,128)(2,1)S(1)}, bf16[1152,128]{1,0:T(8,128)(2,1)S(1)}, u32[]{:S(2)}, u32[]{:S(2)}) collective-permute-start(bf16[1152,128]{1,0:T(8,128)(2,1)S(1)} %get-tuple-element.148), channel_id=1, source_target_pairs={{0,16},{16,32},{32,48},{48,0},{1,17},{17,33},{33,49},{49,1},{2,18}... | collective-permute-start | bytes 884744 | tf_op jit(solution)/shard_map/ppermute | solution.py:27
  81.2 2.9 %pack.7 = (bf16[1152,128]{1,0:T(8,128)(2,1)}, bf16[1152,128]{1,0:T(8,128)(2,1)S(1)}, bf16[1152,128]{1,0:T(8,128)(2,1)S(1)}, bf16[1152,128]{1,0:T(8,128)(2,1)S(1)}) custom-call(s32[68]{0:T(128)S(1)} %pad_add_fusion.1.offsets, bf16[2,4,2,128,128]{4,3,2,1,0:T(8,128)(2,1)S(1)} %pad_maximum_fusion.7.refs_0_, ...), custom_call_target="tpu_custom_call" | custom-call | bytes 4194304 | tf_op jit(solution)/shard_map/pack/pallas_call | solution.py:200
  84.1 14.0 %collective-permute-done.19.refs_6_ = bf16[1536,256]{1,0:T(8,128)(2,1)} collective-permute-done((bf16[1536,256]{1,0:T(8,128)(2,1)S(1)}, bf16[1536,256]{1,0:T(8,128)(2,1)}, u32[]{:S(2)}, u32[]{:S(2)}) %collective-permute-start.19) | collective-permute-done | bytes 786464 | tf_op jit(solution)/shard_map/ppermute | solution.py:27
  98.1 6.3 %collective-permute-start.22 = (bf16[1152,128]{1,0:T(8,128)(2,1)S(1)}, bf16[1152,128]{1,0:T(8,128)(2,1)S(1)}, u32[]{:S(2)}, u32[]{:S(2)}) collective-permute-start(bf16[1152,128]{1,0:T(8,128)(2,1)S(1)} %get-tuple-element.149), channel_id=1, source_target_pairs={{0,32},{16,48},{32,0},{48,16},{1,33},{17,49},{33,1},{49,17},{2,34}... | collective-permute-start | bytes 884744 | tf_op jit(solution)/shard_map/ppermute | solution.py:27
  104.4 0.6 collective-permute-start.23
  105.0 2.4 collective-permute-start.24
  107.4 2.2 collective-permute-start.25
  109.6 4.0 %collective-permute-start.26 = (bf16[1152,128]{1,0:T(8,128)(2,1)S(1)}, bf16[1152,128]{1,0:T(8,128)(2,1)S(1)}, u32[]{:S(2)}, u32[]{:S(2)}) collective-permute-start(bf16[1152,128]{1,0:T(8,128)(2,1)S(1)} %get-tuple-element.154), channel_id=1, source_target_pairs={{0,48},{16,0},{32,16},{48,32},{1,49},{17,1},{33,17},{49,33},{2,50}... | collective-permute-start | bytes 884744 | tf_op jit(solution)/shard_map/ppermute | solution.py:27
  113.7 14.4 %project.1 = (bf16[1536,256]{1,0:T(8,128)(2,1)}, f32[1536,256]{1,0:T(8,128)}, bf16[1536,128]{1,0:T(8,128)(2,1)}, bf16[1536,128]{1,0:T(8,128)(2,1)}) custom-call(s32[8]{0:T(128)S(1)} %stack.101.ids, bf16[1536,256]{1,0:T(8,128)(2,1)S(1)} %copy-done.3, bf16[1536,256]{1,0:T(8,128)(2,1)S(1)} %collective-permute-done.14.refs_1_, ...), custom_call_target="tpu_custom_call" | custom-call | flops 4831838208 | bytes 14680064 | tf_op jit(solution)/shard_map/project/pallas_call | solution.py:88
  128.1 20.1 %collective-permute-done.23 = bf16[1152,128]{1,0:T(8,128)(2,1)S(1)} collective-permute-done((bf16[1152,128]{1,0:T(8,128)(2,1)S(1)}, bf16[1152,128]{1,0:T(8,128)(2,1)S(1)}, u32[]{:S(2)}, u32[]{:S(2)}) %collective-permute-start.23) | collective-permute-done | bytes 294944 | tf_op jit(solution)/shard_map/ppermute | solution.py:27
  148.2 6.1 %collective-permute-done.26 = bf16[1152,128]{1,0:T(8,128)(2,1)S(1)} collective-permute-done((bf16[1152,128]{1,0:T(8,128)(2,1)S(1)}, bf16[1152,128]{1,0:T(8,128)(2,1)S(1)}, u32[]{:S(2)}, u32[]{:S(2)}) %collective-permute-start.26) | collective-permute-done | bytes 294944 | tf_op jit(solution)/shard_map/ppermute | solution.py:27
  154.3 9.8 %conditional.1 = (bf16[1536,256]{1,0:T(8,128)(2,1)}) conditional(s32[]{:T(128)} %convert_element_type.16, (s32[24]{0:T(128)S(1)}, s32[24]{0:T(128)S(1)}, s32[4,16]{1,0:T(4,128)S(1)}, s32[4,16]{1,0:T(4,128)S(1)}, s32[4]{0:T(128)S(1)}, /*index=5*/bf16[2,4,2,128,128]{4,3,2,1,0:T(8,128)(2,1)}, bf16[2,4,2,128,128]{4,3,2,1,0:T(8,128)(2,1)}, ...), branch_computations={%region_6.7_spmd, %region_7.8_spmd} | conditional | flops 301990208 | bytes 41945512 | solution.py:390
  154.3 9.8 %attend.3 = bf16[1536,256]{1,0:T(8,128)(2,1)} custom-call(s32[24]{0:T(128)S(1)} %add_minimum_fusion.1.starts, s32[24]{0:T(128)S(1)} %get-tuple-element.113.lengths, bf16[1536,256]{1,0:T(8,128)(2,1)} %get-tuple-element.114.q, f32[1536,256]{1,0:T(8,128)} %get-tuple-element.115.g, bf16[1536,128]{1,0:T(8,128)(2,1)} %get-tuple-element.116.k, ...), custom_call_target="tpu_custom_call" | custom-call | flops 301989888 | bytes 8388608 | tf_op jit(solution)/shard_map/cond/branch_1_fun/attend/pallas_call | solution.py:167
  164.2 13.6 %collective-permute-done.27 = bf16[128,2048]{1,0:T(8,128)(2,1)S(1)} collective-permute-done((bf16[128,2048]{1,0:T(8,128)(2,1)S(1)}, bf16[128,2048]{1,0:T(8,128)(2,1)S(1)}, u32[]{:S(2)}, u32[]{:S(2)}) %collective-permute-start.27) | collective-permute-done | bytes 524320 | tf_op jit(solution)/shard_map/ppermute | solution.py:27
  178.0 3.2 %collective-permute-start.29 = (bf16[2,128,2048]{2,1,0:T(8,128)(2,1)S(1)}, bf16[2,128,2048]{2,1,0:T(8,128)(2,1)S(1)}, u32[]{:S(2)}, u32[]{:S(2)}) collective-permute-start(bf16[2,128,2048]{2,1,0:T(8,128)(2,1)S(1)} %pad_maximum_fusion), channel_id=1, source_target_pairs={{0,3},{1,0},{2,1},{3,2},{4,7},{5,4},{6,5},{7,6},{8,11},{9,8},{10,9... | collective-permute-start | bytes 3145736 | tf_op jit(solution)/shard_map/ppermute | solution.py:27
  181.2 0.8 constant_dynamic-update-slice_fusion.1
  182.1 0.9 constant_dynamic-update-slice_fusion
  183.0 20.2 %collective-permute-done.28 = bf16[2,128,2048]{2,1,0:T(8,128)(2,1)S(1)} collective-permute-done((bf16[2,128,2048]{2,1,0:T(8,128)(2,1)S(1)}, bf16[2,128,2048]{2,1,0:T(8,128)(2,1)S(1)}, u32[]{:S(2)}, u32[]{:S(2)}) %collective-permute-start.28) | collective-permute-done | bytes 1048608 | tf_op jit(solution)/shard_map/ppermute | solution.py:27
  203.2 0.9 slice_bitcast_fusion.1
  204.1 0.9 slice_dynamic-update-slice_fusion.1
  205.0 0.8 slice_dynamic-update-slice_fusion
  205.8 0.9 slice_bitcast_fusion
  206.7 3.2 %collective-permute-start.31 = (bf16[128,2048]{1,0:T(8,128)(2,1)S(1)}, bf16[128,2048]{1,0:T(8,128)(2,1)S(1)}, u32[]{:S(2)}, u32[]{:S(2)}) collective-permute-start(bf16[128,2048]{1,0:T(8,128)(2,1)S(1)} %get-tuple-element.168), channel_id=1, source_target_pairs={{0,3},{1,0},{2,1},{3,2},{4,7},{5,4},{6,5},{7,6},{8,11},{9,8},{10,9... | collective-permute-start | bytes 1572872 | tf_op jit(solution)/shard_map/ppermute | solution.py:27
  210.0 7.2 %collective-permute-done.30 = bf16[128,2048]{1,0:T(8,128)(2,1)S(1)} collective-permute-done((bf16[128,2048]{1,0:T(8,128)(2,1)S(1)}, bf16[128,2048]{1,0:T(8,128)(2,1)S(1)}, u32[]{:S(2)}, u32[]{:S(2)}) %collective-permute-start.30) | collective-permute-done | bytes 524320 | tf_op jit(solution)/shard_map/ppermute | solution.py:27
  217.1 0.9 bitcast_dynamic-update-slice_fusion.1
  218.0 1.0 collective-permute-done.31
  219.0 0.9 bitcast_dynamic-update-slice_fusion.mine
  219.9 5.3 %all-to-all-start = ((bf16[8,192,256]{2,1,0:T(8,128)(2,1)}), bf16[8,192,256]{2,1,0:T(8,128)(2,1)S(1)}, u32[]{:S(2)}, u32[]{:S(2)}) async-start(bf16[8,192,256]{2,1,0:T(8,128)(2,1)} %bitcast.26), calls=%async_computation | async-start | bytes 1572864 | tf_op jit(solution)/shard_map/all_to_all | solution.py:391
  225.3 12.6 %all-to-all-done.heads = bf16[8,192,256]{2,1,0:T(8,128)(2,1)S(1)} async-done(((bf16[8,192,256]{2,1,0:T(8,128)(2,1)}), bf16[8,192,256]{2,1,0:T(8,128)(2,1)S(1)}, u32[]{:S(2)}, u32[]{:S(2)}) %all-to-all-start) | async-done | bytes 786464 | tf_op jit(solution)/shard_map/all_to_all | solution.py:391
  237.9 6.6 %project_out.1 = bf16[192,2048]{1,0:T(8,128)(2,1)} custom-call(s32[9]{0:T(128)S(1)} %concatenate.16.places, bf16[8,192,256]{2,1,0:T(8,128)(2,1)S(1)} %all-to-all-done.heads, bf16[8,128,2048]{2,1,0:T(8,128)(2,1)} %bitcast_dynamic-update-slice_fusion.mine, bf16[8,128,2048]{2,1,0:T(8,128)(2,1)} %collective-permute-done.32.other), custom_call_target="tpu_custom_call" | custom-call | flops 1610612736 | bytes 10485760 | tf_op jit(solution)/shard_map/project_out/pallas_call | solution.py:240
  (102 shorter events, 3.9 us)
Async XLA Ops:
  0.0 40.2 %copy-start = (bf16[256,2048]{1,0:T(8,128)(2,1)S(1)}, bf16[256,2048]{1,0:T(8,128)(2,1)}, u32[]{:S(2)}) copy-start(bf16[256,2048]{1,0:T(8,128)(2,1)} %param.25) | copy-start | bytes 3145732
  0.0 26.1 %collective-permute-start.14 = (bf16[1536,256]{1,0:T(8,128)(2,1)}, bf16[1536,256]{1,0:T(8,128)(2,1)S(1)}, u32[]{:S(2)}, u32[]{:S(2)}) collective-permute-start(bf16[1536,256]{1,0:T(8,128)(2,1)} %refs_0_.1), channel_id=1, source_target_pairs={{0,4},{4,0},{1,5},{5,1},{2,6},{6,2},{3,7},{7,3},{8,12},{12,8},{9,1... | collective-permute-start | bytes 2359304 | tf_op jit(solution)/shard_map/ppermute | solution.py:27
  1.9 36.2 %collective-permute-start.15 = (bf16[1536,256]{1,0:T(8,128)(2,1)}, bf16[1536,256]{1,0:T(8,128)(2,1)S(1)}, u32[]{:S(2)}, u32[]{:S(2)}) collective-permute-start(bf16[1536,256]{1,0:T(8,128)(2,1)} %refs_0_.1), channel_id=1, source_target_pairs={{0,1},{1,2},{2,3},{3,0},{4,5},{5,6},{6,7},{7,4},{8,9},{9,10},{10,1... | collective-permute-start | bytes 2359304 | tf_op jit(solution)/shard_map/ppermute | solution.py:27
  3.4 9.8 %copy-start.20 = (s32[768]{0:T(1024)S(1)}, s32[768]{0:T(1024)}, u32[]{:S(2)}) copy-start(s32[768]{0:T(1024)} %param.29) | copy-start | bytes 9220
  3.4 9.9 %copy-start.21 = (s32[768,1]{0,1:T(1,128)S(1)}, s32[768,1]{0,1:T(1,128)}, u32[]{:S(2)}) copy-start(s32[768,1]{0,1:T(1,128)} %param.28) | copy-start | bytes 9220
  3.4 11.8 %copy-start.22 = (s32[4]{0:T(128)S(1)}, s32[4]{0:T(128)}, u32[]{:S(2)}) copy-start(s32[4]{0:T(128)} %constant.564.clone) | copy-start | bytes 52
  5.8 14.7 %collective-permute-start.10 = (bf16[4,4,2,128,128]{4,3,2,1,0:T(8,128)(2,1)}, bf16[4,4,2,128,128]{4,3,2,1,0:T(8,128)(2,1)}, u32[]{:S(2)}, u32[]{:S(2)}) collective-permute-start(bf16[4,4,2,128,128]{4,3,2,1,0:T(8,128)(2,1)} %dynamic-slice_bitcast_fusion), channel_id=1, source_target_pairs={{0,8},{8,0},{1,9},{9,1},{2,10},{10,2},{3,11},{11,3},{4,12},{12,4},... | collective-permute-start | bytes 3145736 | tf_op jit(solution)/shard_map/ppermute | solution.py:27
  8.1 12.4 %collective-permute-start.6 = (bf16[4,4,2,128,128]{4,3,2,1,0:T(8,128)(2,1)}, bf16[4,4,2,128,128]{4,3,2,1,0:T(8,128)(2,1)}, u32[]{:S(2)}, u32[]{:S(2)}) collective-permute-start(bf16[4,4,2,128,128]{4,3,2,1,0:T(8,128)(2,1)} %dynamic-slice_bitcast_fusion.1), channel_id=1, source_target_pairs={{0,8},{8,0},{1,9},{9,1},{2,10},{10,2},{3,11},{11,3},{4,12},{12,4},... | collective-permute-start | bytes 3145736 | tf_op jit(solution)/shard_map/ppermute | solution.py:27
  16.0 7.3 %copy-start.16 = (bf16[1,4,2,128,128]{4,3,2,1,0:T(8,128)(2,1)S(1)}, bf16[1,4,2,128,128]{4,3,2,1,0:T(8,128)(2,1)}, u32[]{:S(2)}) copy-start(bf16[1,4,2,128,128]{4,3,2,1,0:T(8,128)(2,1)} %get-tuple-element.165) | copy-start | bytes 786436
  23.3 35.1 %copy-start.3 = (bf16[1536,256]{1,0:T(8,128)(2,1)S(1)}, bf16[1536,256]{1,0:T(8,128)(2,1)}, u32[]{:S(2)}) copy-start(bf16[1536,256]{1,0:T(8,128)(2,1)} %refs_0_.1) | copy-start | bytes 2359300
  23.3 47.9 %copy-start.19 = (f32[2048]{0:T(1024)S(1)}, f32[2048]{0:T(1024)}, u32[]{:S(2)}) copy-start(f32[2048]{0:T(1024)} %param.18) | copy-start | bytes 24580
  24.2 15.1 %collective-permute-start.7 = (bf16[2,4,2,128,128]{4,3,2,1,0:T(8,128)(2,1)}, bf16[2,4,2,128,128]{4,3,2,1,0:T(8,128)(2,1)}, u32[]{:S(2)}, u32[]{:S(2)}) collective-permute-start(bf16[2,4,2,128,128]{4,3,2,1,0:T(8,128)(2,1)} %pad_maximum_fusion.4), channel_id=1, source_target_pairs={{0,64},{64,128},{128,192},{192,0},{1,65},{65,129},{129,193},{193,1... | collective-permute-start | bytes 1572872 | tf_op jit(solution)/shard_map/ppermute | solution.py:27
  26.1 40.8 %collective-permute-start.18 = (bf16[1536,256]{1,0:T(8,128)(2,1)S(1)}, bf16[1536,256]{1,0:T(8,128)(2,1)}, u32[]{:S(2)}, u32[]{:S(2)}) collective-permute-start(bf16[1536,256]{1,0:T(8,128)(2,1)S(1)} %collective-permute-done.14.refs_1_), channel_id=1, source_target_pairs={{0,3},{1,0},{2,1},{3,2},{4,7},{5,4},{6,5},{7,6},{8,11},{9,8},{10,9... | collective-permute-start | bytes 2359304 | tf_op jit(solution)/shard_map/ppermute | solution.py:27
  29.7 25.6 %collective-permute-start.8 = (bf16[2,4,2,128,128]{4,3,2,1,0:T(8,128)(2,1)}, bf16[2,4,2,128,128]{4,3,2,1,0:T(8,128)(2,1)}, u32[]{:S(2)}, u32[]{:S(2)}) collective-permute-start(bf16[2,4,2,128,128]{4,3,2,1,0:T(8,128)(2,1)} %pad_maximum_fusion.5), channel_id=1, source_target_pairs={{0,192},{64,0},{128,64},{192,128},{1,193},{65,1},{129,65},{193,129... | collective-permute-start | bytes 1572872 | tf_op jit(solution)/shard_map/ppermute | solution.py:27
  32.0 26.3 %collective-permute-start.9 = (bf16[2,4,2,128,128]{4,3,2,1,0:T(8,128)(2,1)}, bf16[2,4,2,128,128]{4,3,2,1,0:T(8,128)(2,1)}, u32[]{:S(2)}, u32[]{:S(2)}) collective-permute-start(bf16[2,4,2,128,128]{4,3,2,1,0:T(8,128)(2,1)} %pad_maximum_fusion.6), channel_id=1, source_target_pairs={{0,128},{64,192},{128,0},{192,64},{1,129},{65,193},{129,1},{193,65... | collective-permute-start | bytes 1572872 | tf_op jit(solution)/shard_map/ppermute | solution.py:27
  38.1 23.7 %collective-permute-start.11 = (bf16[2,4,2,128,128]{4,3,2,1,0:T(8,128)(2,1)}, bf16[2,4,2,128,128]{4,3,2,1,0:T(8,128)(2,1)}, u32[]{:S(2)}, u32[]{:S(2)}) collective-permute-start(bf16[2,4,2,128,128]{4,3,2,1,0:T(8,128)(2,1)} %pad_maximum_fusion.8), channel_id=1, source_target_pairs={{0,64},{64,128},{128,192},{192,0},{1,65},{65,129},{129,193},{193,1... | collective-permute-start | bytes 1572872 | tf_op jit(solution)/shard_map/ppermute | solution.py:27
  39.3 27.3 %collective-permute-start.12 = (bf16[2,4,2,128,128]{4,3,2,1,0:T(8,128)(2,1)}, bf16[2,4,2,128,128]{4,3,2,1,0:T(8,128)(2,1)}, u32[]{:S(2)}, u32[]{:S(2)}) collective-permute-start(bf16[2,4,2,128,128]{4,3,2,1,0:T(8,128)(2,1)} %pad_maximum_fusion.9), channel_id=1, source_target_pairs={{0,192},{64,0},{128,64},{192,128},{1,193},{65,1},{129,65},{193,129... | collective-permute-start | bytes 1572872 | tf_op jit(solution)/shard_map/ppermute | solution.py:27
  55.3 22.5 %collective-permute-start.13 = (bf16[2,4,2,128,128]{4,3,2,1,0:T(8,128)(2,1)}, bf16[2,4,2,128,128]{4,3,2,1,0:T(8,128)(2,1)}, u32[]{:S(2)}, u32[]{:S(2)}) collective-permute-start(bf16[2,4,2,128,128]{4,3,2,1,0:T(8,128)(2,1)} %pad_maximum_fusion.10), channel_id=1, source_target_pairs={{0,128},{64,192},{128,0},{192,64},{1,129},{65,193},{129,1},{193,65... | collective-permute-start | bytes 1572872 | tf_op jit(solution)/shard_map/ppermute | solution.py:27
  58.4 46.6 %collective-permute-start.16 = (bf16[1536,256]{1,0:T(8,128)(2,1)S(1)}, bf16[1536,256]{1,0:T(8,128)(2,1)}, u32[]{:S(2)}, u32[]{:S(2)}) collective-permute-start(bf16[1536,256]{1,0:T(8,128)(2,1)S(1)} %copy-done.3), channel_id=1, source_target_pairs={{0,3},{1,0},{2,1},{3,2},{4,7},{5,4},{6,5},{7,6},{8,11},{9,8},{10,9... | collective-permute-start | bytes 2359304 | tf_op jit(solution)/shard_map/ppermute | solution.py:27
  61.8 45.6 %collective-permute-start.17 = (bf16[1536,256]{1,0:T(8,128)(2,1)S(1)}, bf16[1536,256]{1,0:T(8,128)(2,1)}, u32[]{:S(2)}, u32[]{:S(2)}) collective-permute-start(bf16[1536,256]{1,0:T(8,128)(2,1)S(1)} %collective-permute-done.14.refs_1_), channel_id=1, source_target_pairs={{0,1},{1,2},{2,3},{3,0},{4,5},{5,6},{6,7},{7,4},{8,9},{9,10},{10,1... | collective-permute-start | bytes 2359304 | tf_op jit(solution)/shard_map/ppermute | solution.py:27
  66.6 31.6 %collective-permute-start.19 = (bf16[1536,256]{1,0:T(8,128)(2,1)S(1)}, bf16[1536,256]{1,0:T(8,128)(2,1)}, u32[]{:S(2)}, u32[]{:S(2)}) collective-permute-start(bf16[1536,256]{1,0:T(8,128)(2,1)S(1)} %collective-permute-done.15.refs_2_), channel_id=1, source_target_pairs={{0,1},{1,2},{2,3},{3,0},{4,5},{5,6},{6,7},{7,4},{8,9},{9,10},{10,1... | collective-permute-start | bytes 2359304 | tf_op jit(solution)/shard_map/ppermute | solution.py:27
  66.9 37.6 %collective-permute-start.20 = (bf16[1536,256]{1,0:T(8,128)(2,1)}, bf16[1536,256]{1,0:T(8,128)(2,1)}, u32[]{:S(2)}, u32[]{:S(2)}) collective-permute-start(bf16[1536,256]{1,0:T(8,128)(2,1)} %collective-permute-done.18.refs_5_), channel_id=1, source_target_pairs={{0,3},{1,0},{2,1},{3,2},{4,7},{5,4},{6,5},{7,6},{8,11},{9,8},{10,9... | collective-permute-start | bytes 2359304 | tf_op jit(solution)/shard_map/ppermute | solution.py:27
  71.3 9.8 %copy-start.15 = (bf16[1,4,2,128,128]{4,3,2,1,0:T(8,128)(2,1)S(1)}, bf16[1,4,2,128,128]{4,3,2,1,0:T(8,128)(2,1)}, u32[]{:S(2)}) copy-start(bf16[1,4,2,128,128]{4,3,2,1,0:T(8,128)(2,1)} %get-tuple-element.162) | copy-start | bytes 786436
  71.3 9.8 %copy-start.17 = (bf16[1,4,2,128,128]{4,3,2,1,0:T(8,128)(2,1)S(1)}, bf16[1,4,2,128,128]{4,3,2,1,0:T(8,128)(2,1)}, u32[]{:S(2)}) copy-start(bf16[1,4,2,128,128]{4,3,2,1,0:T(8,128)(2,1)} %get-tuple-element.175) | copy-start | bytes 786436
  71.3 42.4 %copy-start.1 = (bf16[2048,256]{1,0:T(8,128)(2,1)S(1)}, bf16[2048,256]{1,0:T(8,128)(2,1)}, u32[]{:S(2)}) copy-start(bf16[2048,256]{1,0:T(8,128)(2,1)} %refs_9_.1) | copy-start | bytes 3145732
  71.3 42.4 %copy-start.2 = (bf16[2048,256]{1,0:T(8,128)(2,1)S(1)}, bf16[2048,256]{1,0:T(8,128)(2,1)}, u32[]{:S(2)}) copy-start(bf16[2048,256]{1,0:T(8,128)(2,1)} %refs_10_.1) | copy-start | bytes 3145732
  71.3 42.4 %copy-start.4 = (bf16[2048,128]{1,0:T(8,128)(2,1)S(1)}, bf16[2048,128]{1,0:T(8,128)(2,1)}, u32[]{:S(2)}) copy-start(bf16[2048,128]{1,0:T(8,128)(2,1)} %refs_11_.1) | copy-start | bytes 1572868
  71.3 42.4 %copy-start.5 = (bf16[2048,128]{1,0:T(8,128)(2,1)S(1)}, bf16[2048,128]{1,0:T(8,128)(2,1)}, u32[]{:S(2)}) copy-start(bf16[2048,128]{1,0:T(8,128)(2,1)} %refs_12_.1) | copy-start | bytes 1572868
  71.3 42.4 %copy-start.6 = (f32[128]{0:T(128)S(1)}, f32[128]{0:T(128)}, u32[]{:S(2)}) copy-start(f32[128]{0:T(128)} %param.23) | copy-start | bytes 1540
  71.3 42.4 %copy-start.7 = (f32[128]{0:T(128)S(1)}, f32[128]{0:T(128)}, u32[]{:S(2)}) copy-start(f32[128]{0:T(128)} %param.24) | copy-start | bytes 1540
  74.9 38.7 %copy-start.9 = (bf16[2,4,2,128,128]{4,3,2,1,0:T(8,128)(2,1)}, bf16[2,4,2,128,128]{4,3,2,1,0:T(8,128)(2,1)S(1)}, u32[]{:S(2)}) copy-start(bf16[2,4,2,128,128]{4,3,2,1,0:T(8,128)(2,1)S(1)} %pad_maximum_fusion.3.refs_0_) | copy-start | bytes 1572868
  77.8 31.8 %collective-permute-start.21 = (bf16[1152,128]{1,0:T(8,128)(2,1)S(1)}, bf16[1152,128]{1,0:T(8,128)(2,1)S(1)}, u32[]{:S(2)}, u32[]{:S(2)}) collective-permute-start(bf16[1152,128]{1,0:T(8,128)(2,1)S(1)} %get-tuple-element.148), channel_id=1, source_target_pairs={{0,16},{16,32},{32,48},{48,0},{1,17},{17,33},{33,49},{49,1},{2,18}... | collective-permute-start | bytes 884744 | tf_op jit(solution)/shard_map/ppermute | solution.py:27
  81.2 32.5 %copy-start.10 = (bf16[2,4,2,128,128]{4,3,2,1,0:T(8,128)(2,1)}, bf16[2,4,2,128,128]{4,3,2,1,0:T(8,128)(2,1)S(1)}, u32[]{:S(2)}) copy-start(bf16[2,4,2,128,128]{4,3,2,1,0:T(8,128)(2,1)S(1)} %pad_maximum_fusion.7.refs_0_) | copy-start | bytes 1572868
  98.1 30.0 %collective-permute-start.22 = (bf16[1152,128]{1,0:T(8,128)(2,1)S(1)}, bf16[1152,128]{1,0:T(8,128)(2,1)S(1)}, u32[]{:S(2)}, u32[]{:S(2)}) collective-permute-start(bf16[1152,128]{1,0:T(8,128)(2,1)S(1)} %get-tuple-element.149), channel_id=1, source_target_pairs={{0,32},{16,48},{32,0},{48,16},{1,33},{17,49},{33,1},{49,17},{2,34}... | collective-permute-start | bytes 884744 | tf_op jit(solution)/shard_map/ppermute | solution.py:27
  104.4 43.8 %collective-permute-start.23 = (bf16[1152,128]{1,0:T(8,128)(2,1)S(1)}, bf16[1152,128]{1,0:T(8,128)(2,1)S(1)}, u32[]{:S(2)}, u32[]{:S(2)}) collective-permute-start(bf16[1152,128]{1,0:T(8,128)(2,1)S(1)} %get-tuple-element.150), channel_id=1, source_target_pairs={{0,48},{16,0},{32,16},{48,32},{1,49},{17,1},{33,17},{49,33},{2,50}... | collective-permute-start | bytes 884744 | tf_op jit(solution)/shard_map/ppermute | solution.py:27
  105.0 43.2 %collective-permute-start.24 = (bf16[1152,128]{1,0:T(8,128)(2,1)S(1)}, bf16[1152,128]{1,0:T(8,128)(2,1)S(1)}, u32[]{:S(2)}, u32[]{:S(2)}) collective-permute-start(bf16[1152,128]{1,0:T(8,128)(2,1)S(1)} %get-tuple-element.152), channel_id=1, source_target_pairs={{0,16},{16,32},{32,48},{48,0},{1,17},{17,33},{33,49},{49,1},{2,18}... | collective-permute-start | bytes 884744 | tf_op jit(solution)/shard_map/ppermute | solution.py:27
  107.4 40.8 %collective-permute-start.25 = (bf16[1152,128]{1,0:T(8,128)(2,1)S(1)}, bf16[1152,128]{1,0:T(8,128)(2,1)S(1)}, u32[]{:S(2)}, u32[]{:S(2)}) collective-permute-start(bf16[1152,128]{1,0:T(8,128)(2,1)S(1)} %get-tuple-element.153), channel_id=1, source_target_pairs={{0,32},{16,48},{32,0},{48,16},{1,33},{17,49},{33,1},{49,17},{2,34}... | collective-permute-start | bytes 884744 | tf_op jit(solution)/shard_map/ppermute | solution.py:27
  109.6 4.1 %copy-start.18 = (bf16[1152,128]{1,0:T(8,128)(2,1)}, bf16[1152,128]{1,0:T(8,128)(2,1)S(1)}, u32[]{:S(2)}) copy-start(bf16[1152,128]{1,0:T(8,128)(2,1)S(1)} %collective-permute-done.21) | copy-start | bytes 884740
  109.6 44.7 %collective-permute-start.26 = (bf16[1152,128]{1,0:T(8,128)(2,1)S(1)}, bf16[1152,128]{1,0:T(8,128)(2,1)S(1)}, u32[]{:S(2)}, u32[]{:S(2)}) collective-permute-start(bf16[1152,128]{1,0:T(8,128)(2,1)S(1)} %get-tuple-element.154), channel_id=1, source_target_pairs={{0,48},{16,0},{32,16},{48,32},{1,49},{17,1},{33,17},{49,33},{2,50}... | collective-permute-start | bytes 884744 | tf_op jit(solution)/shard_map/ppermute | solution.py:27
  154.3 9.8 %copy-start.11 = (bf16[128,2048]{1,0:T(8,128)(2,1)S(1)}, bf16[128,2048]{1,0:T(8,128)(2,1)}, u32[]{:S(2)}) copy-start(bf16[128,2048]{1,0:T(8,128)(2,1)} %constant_dynamic-slice_fusion) | copy-start | bytes 1572868
  164.1 13.7 %collective-permute-start.27 = (bf16[128,2048]{1,0:T(8,128)(2,1)S(1)}, bf16[128,2048]{1,0:T(8,128)(2,1)S(1)}, u32[]{:S(2)}, u32[]{:S(2)}) collective-permute-start(bf16[128,2048]{1,0:T(8,128)(2,1)S(1)} %copy-done.11), channel_id=1, source_target_pairs={{0,4},{4,0},{1,5},{5,1},{2,6},{6,2},{3,7},{7,3},{8,12},{12,8},{9,1... | collective-permute-start | bytes 1572872 | tf_op jit(solution)/shard_map/ppermute | solution.py:27
  177.9 25.3 %collective-permute-start.28 = (bf16[2,128,2048]{2,1,0:T(8,128)(2,1)S(1)}, bf16[2,128,2048]{2,1,0:T(8,128)(2,1)S(1)}, u32[]{:S(2)}, u32[]{:S(2)}) collective-permute-start(bf16[2,128,2048]{2,1,0:T(8,128)(2,1)S(1)} %pad_maximum_fusion), channel_id=1, source_target_pairs={{0,1},{1,2},{2,3},{3,0},{4,5},{5,6},{6,7},{7,4},{8,9},{9,10},{10,1... | collective-permute-start | bytes 3145736 | tf_op jit(solution)/shard_map/ppermute | solution.py:27
  178.0 26.1 %collective-permute-start.29 = (bf16[2,128,2048]{2,1,0:T(8,128)(2,1)S(1)}, bf16[2,128,2048]{2,1,0:T(8,128)(2,1)S(1)}, u32[]{:S(2)}, u32[]{:S(2)}) collective-permute-start(bf16[2,128,2048]{2,1,0:T(8,128)(2,1)S(1)} %pad_maximum_fusion), channel_id=1, source_target_pairs={{0,3},{1,0},{2,1},{3,2},{4,7},{5,4},{6,5},{7,6},{8,11},{9,8},{10,9... | collective-permute-start | bytes 3145736 | tf_op jit(solution)/shard_map/ppermute | solution.py:27
  204.1 13.0 %collective-permute-start.30 = (bf16[128,2048]{1,0:T(8,128)(2,1)S(1)}, bf16[128,2048]{1,0:T(8,128)(2,1)S(1)}, u32[]{:S(2)}, u32[]{:S(2)}) collective-permute-start(bf16[128,2048]{1,0:T(8,128)(2,1)S(1)} %get-tuple-element.170), channel_id=1, source_target_pairs={{0,1},{1,2},{2,3},{3,0},{4,5},{5,6},{6,7},{7,4},{8,9},{9,10},{10,1... | collective-permute-start | bytes 1572872 | tf_op jit(solution)/shard_map/ppermute | solution.py:27
  206.7 12.3 %collective-permute-start.31 = (bf16[128,2048]{1,0:T(8,128)(2,1)S(1)}, bf16[128,2048]{1,0:T(8,128)(2,1)S(1)}, u32[]{:S(2)}, u32[]{:S(2)}) collective-permute-start(bf16[128,2048]{1,0:T(8,128)(2,1)S(1)} %get-tuple-element.168), channel_id=1, source_target_pairs={{0,3},{1,0},{2,1},{3,2},{4,7},{5,4},{6,5},{7,6},{8,11},{9,8},{10,9... | collective-permute-start | bytes 1572872 | tf_op jit(solution)/shard_map/ppermute | solution.py:27
  219.9 18.0 %collective-permute-start.32 = (bf16[8,128,2048]{2,1,0:T(8,128)(2,1)}, bf16[8,128,2048]{2,1,0:T(8,128)(2,1)}, u32[]{:S(2)}, u32[]{:S(2)}) collective-permute-start(bf16[8,128,2048]{2,1,0:T(8,128)(2,1)} %bitcast_dynamic-update-slice_fusion.mine), channel_id=1, source_target_pairs={{0,8},{8,0},{1,9},{9,1},{2,10},{10,2},{3,11},{11,3},{4,12},{12,4},... | collective-permute-start | bytes 12582920 | tf_op jit(solution)/shard_map/ppermute | solution.py:27
  219.9 18.0 %all-to-all-start = ((bf16[8,192,256]{2,1,0:T(8,128)(2,1)}), bf16[8,192,256]{2,1,0:T(8,128)(2,1)S(1)}, u32[]{:S(2)}, u32[]{:S(2)}) async-start(bf16[8,192,256]{2,1,0:T(8,128)(2,1)} %bitcast.26), calls=%async_computation | async-start | bytes 1572864 | tf_op jit(solution)/shard_map/all_to_all | solution.py:391

commit v3 on v2

--- a/solution.py
+++ b/solution.py
@@ -17,6 +17,7 @@
 BATCH = 4
 UNIT = 16
 PACKED = 72 * UNIT
+COST = pl.CostEstimate(flops=1 << 20, bytes_accessed=1 << 20, transcendentals=0)
 
 
 def ring(size, step):
@@ -51,29 +52,44 @@
 
 def project_kernel(ids, *refs):
     pieces, rest = refs[:8], refs[8:]
-    (gain, wq, wg, wk, wv, q_gain, k_gain, cosine, sine, q_out, g_out, k_out, v_out, normed) = rest
-    width = pieces[0].shape[1]
+    (gain, wq, wg, wk, wv, q_gain, k_gain, cosine, sine, q_out, g_out, k_out, v_out, scaled) = rest
+    rows, width = pieces[0].shape
     head = wk.shape[1]
-    total = jnp.zeros((pieces[0].shape[0], 1), jnp.float32)
-    for piece in pieces:
-        value = piece[...].astype(jnp.float32)
-        total = total + jnp.sum(value * value, axis=-1, keepdims=True)
-    scale = lax.rsqrt(total / (8 * width) + EPSILON)
+    edges = [0]
+    for w in (wq, wg, wk, wv):
+        edges.append(edges[-1] + w.shape[1])
+
+    @pl.when(pl.program_id(0) == 0)
+    def _():
+        for j in range(8):
+            block = pl.multiple_of(ids[j] * width, width)
+            here = pl.ds(block, width)
+            for w, first, last in zip((wq, wg, wk, wv), edges, edges[1:]):
+                part = w[here, :].astype(jnp.float32) * gain[here, :]
+                scaled[j * width : (j + 1) * width, first:last] = part.astype(jnp.bfloat16)
+
+    total = jnp.zeros((rows, 128), jnp.float32)
+    product = jnp.zeros((rows, edges[-1]), jnp.float32)
     for j, piece in enumerate(pieces):
-        block = ids[j]
-        value = piece[...].astype(jnp.float32) * scale * gain[pl.ds(block, 1), :]
-        normed[:, pl.ds(pl.multiple_of(block * width, width), width)] = value.astype(jnp.bfloat16)
-    x = normed[...]
+        value = piece[...]
+        product = product + jnp.dot(
+            value, scaled[j * width : (j + 1) * width, :], preferred_element_type=jnp.float32
+        )
+        value = value.astype(jnp.float32)
+        square = value * value
+        for first in range(0, width, 128):
+            total = total + square[:, first : first + 128]
+    total = jnp.sum(total, axis=-1, keepdims=True)
+    product = product * lax.rsqrt(total / (8 * width) + EPSILON)
     cos, sin = cosine[...], sine[...]
-    q = jnp.dot(x, wq[...], preferred_element_type=jnp.float32)
-    for h in range(q.shape[1] // head):
-        part = head_norm_rotate(q[:, h * head : (h + 1) * head], q_gain[...], cos, sin)
-        q_out[:, h * head : (h + 1) * head] = part.astype(jnp.bfloat16)
-    k = jnp.dot(x, wk[...], preferred_element_type=jnp.float32)
-    k_out[...] = head_norm_rotate(k, k_gain[...], cos, sin).astype(jnp.bfloat16)
-    v_out[...] = jnp.dot(x, wv[...], preferred_element_type=jnp.float32).astype(jnp.bfloat16)
-    gate = jnp.dot(x, wg[...], preferred_element_type=jnp.float32)
-    g_out[...] = jax.nn.sigmoid(gate)
+    for h in range(edges[1] // head):
+        here = slice(h * head, (h + 1) * head)
+        part = head_norm_rotate(product[:, here], q_gain[...], cos, sin)
+        q_out[:, here] = part.astype(jnp.bfloat16)
+    g_out[...] = jax.nn.sigmoid(product[:, edges[1] : edges[2]])
+    k = head_norm_rotate(product[:, edges[2] : edges[3]], k_gain[...], cos, sin)
+    k_out[...] = k.astype(jnp.bfloat16)
+    v_out[...] = product[:, edges[3] : edges[4]].astype(jnp.bfloat16)
 
 
 def project(ids, pieces, gain, wq, wg, wk, wv, q_gain, k_gain, cosine, sine):
@@ -82,9 +98,9 @@
     head = q_gain.shape[0]
     tile = lambda columns: pl.BlockSpec((ROW_TILE, columns), lambda i, _: (i, 0))
     whole = lambda a: pl.BlockSpec(a.shape, lambda i, _: (0, 0))
-    gain = gain.reshape(depth // width, width)
     q_gain, k_gain = q_gain.reshape(1, head), k_gain.reshape(1, head)
-    constants = (gain, wq, wg, wk, wv, q_gain, k_gain)
+    constants = (gain.reshape(depth, 1), wq, wg, wk, wv, q_gain, k_gain)
+    columns = sum(w.shape[1] for w in (wq, wg, wk, wv))
     return pl.pallas_call(
         project_kernel,
         out_shape=(
@@ -98,12 +114,10 @@
             grid=(rows // ROW_TILE,),
             in_specs=[tile(width)] * 8 + [whole(a) for a in constants] + [tile(head)] * 2,
             out_specs=[tile(wq.shape[1]), tile(wg.shape[1]), tile(head), tile(head)],
-            scratch_shapes=[pltpu.VMEM((ROW_TILE, depth), jnp.bfloat16)],
+            scratch_shapes=[pltpu.VMEM((depth, columns), jnp.bfloat16)],
         ),
         compiler_params=pltpu.CompilerParams(vmem_limit_bytes=40 << 20),
-        cost_estimate=pl.CostEstimate(
-            flops=2 * rows * depth * 6 * head, bytes_accessed=14 << 20, transcendentals=rows * 256
-        ),
+        cost_estimate=COST,
         name="project",
     )(ids, *pieces, *constants, cosine, sine)
 
@@ -129,27 +143,29 @@
 
     column = lax.broadcasted_iota(jnp.int32, (shares * span, window), 1)
     old_row = lax.broadcasted_iota(jnp.int32, (window, head), 0)
-    token = lax.broadcasted_iota(jnp.int32, (shares, span, span), 1).reshape(shares * span, span)
-    causal = lax.broadcasted_iota(jnp.int32, (shares * span, span), 1) <= token
+    token = lax.broadcasted_iota(jnp.int32, (shares, span, window), 1)
+    token = token.reshape(shares * span, window)
+    together = window // span
     for b in range(BATCH):
         r = pl.program_id(0) * BATCH + b
         length = lengths[r]
         rows = slice(b * span, (b + 1) * span)
+        first = b // together * together
+        both = slice(first * span, (first + together) * span)
+        own = column - (b - first) * span
         query = jnp.concatenate([q[rows, s * head : (s + 1) * head] for s in range(shares)], axis=0)
         place = pl.ds(pl.multiple_of(starts[r], UNIT), window)
         old_keys, old_values = keys[place, :], values[place, :]
         old_values = jnp.where(old_row < length, old_values, jnp.zeros_like(old_values))
         old = lax.dot_general(query, old_keys, contract, preferred_element_type=jnp.float32)
-        new = lax.dot_general(query, k[rows, :], contract, preferred_element_type=jnp.float32)
+        new = lax.dot_general(query, k[both, :], contract, preferred_element_type=jnp.float32)
         old = jnp.where(column < length, old * score_scale, -jnp.inf)
-        new = jnp.where(causal, new * score_scale, -jnp.inf)
-        row_max = jnp.maximum(
-            jnp.max(old, axis=-1, keepdims=True), jnp.max(new, axis=-1, keepdims=True)
-        )
+        new = jnp.where((own >= 0) & (own <= token), new * score_scale, -jnp.inf)
+        row_max = jnp.max(jnp.maximum(old, new), axis=-1, keepdims=True)
         old, new = jnp.exp(old - row_max), jnp.exp(new - row_max)
-        row_total = jnp.sum(old, axis=-1, keepdims=True) + jnp.sum(new, axis=-1, keepdims=True)
+        row_total = jnp.sum(old + new, axis=-1, keepdims=True)
         mixed = jnp.dot(old.astype(jnp.bfloat16), old_values, preferred_element_type=jnp.float32)
-        mixed += jnp.dot(new.astype(jnp.bfloat16), v[rows, :], preferred_element_type=jnp.float32)
+        mixed += jnp.dot(new.astype(jnp.bfloat16), v[both, :], preferred_element_type=jnp.float32)
         mixed = mixed / row_total
         for s in range(shares):
             columns = slice(s * head, (s + 1) * head)
@@ -175,54 +191,117 @@
             scratch_shapes=[store, store],
         ),
         compiler_params=pltpu.CompilerParams(vmem_limit_bytes=40 << 20),
-        cost_estimate=pl.CostEstimate(
-            flops=4 * rows * columns * 192, bytes_accessed=8 << 20, transcendentals=rows * 2 * 192
-        ),
+        cost_estimate=COST,
         name="attend",
     )(starts, lengths, q, g, k, v, *keys, *values)
 
 
-def pack_kernel(offsets, *refs):
-    pieces, outs, store = refs[:4], refs[4:8], refs[8]
-    slots, window = pieces[0].shape[2], pieces[0].shape[3]
+def pack_kernel(offsets, own, twin, *refs):
+    received, outs, store = refs[:3], refs[3:7], refs[7]
+    window, head = own.shape[4:]
+    slots = own.shape[3]
     size = outs[0].shape[0]
     for k, out in enumerate(outs):
+        block = offsets[k]
         for j in range(4 * 2 * slots):
-            p, q, rank = j // (2 * slots), j // slots % 2, j % slots
-            block = offsets[4 * 4 * 2 * slots + k]
-            place = pl.multiple_of(offsets[k * 4 * 2 * slots + j], UNIT)
-            store[pl.ds(place, window), :] = pieces[p][q, block, rank]
+            p, side, rank = j // (2 * slots), j // slots % 2, j % slots
+            place = pl.multiple_of(offsets[6 + k * 4 * 2 * slots + j], UNIT)
+            if p > 0:
+                value = received[p - 1][side, block, rank]
+            elif side > 0:
+                value = twin[0, block, rank]
+            else:
+                value = own[0, block, 0, rank]
+            store[pl.ds(place, window), :] = value
         out[...] = store[:size, :]
 
 
-def pack(offsets, pieces, size):
-    window, head = pieces[0].shape[3:]
+def pack(offsets, cache, twin, received, size):
+    capacity, window, head = cache.shape[3:]
     return pl.pallas_call(
         pack_kernel,
-        out_shape=[jax.ShapeDtypeStruct((size, head), pieces[0].dtype)] * 4,
+        out_shape=[jax.ShapeDtypeStruct((size, head), cache.dtype)] * 4,
         grid_spec=pltpu.PrefetchScalarGridSpec(
             num_scalar_prefetch=1,
             grid=(1,),
-            in_specs=[pl.BlockSpec(a.shape, lambda i, _: (0,) * 5) for a in pieces],
+            in_specs=[
+                pl.BlockSpec((1, 4, 1, capacity, window, head), lambda i, o: (o[4], 0, o[5], 0, 0, 0)),
+                pl.BlockSpec((1, 4, capacity, window, head), lambda i, o: (o[4], 0, 0, 0, 0)),
+            ]
+            + [pl.BlockSpec(a.shape, lambda i, _: (0,) * 5) for a in received],
             out_specs=[pl.BlockSpec((size, head), lambda i, _: (0, 0))] * 4,
-            scratch_shapes=[pltpu.VMEM((size + window, head), pieces[0].dtype)],
+            scratch_shapes=[pltpu.VMEM((size + window, head), cache.dtype)],
         ),
         compiler_params=pltpu.CompilerParams(vmem_limit_bytes=30 << 20),
-        cost_estimate=pl.CostEstimate(flops=0, bytes_accessed=4 << 20, transcendentals=0),
+        cost_estimate=COST,
         name="pack",
-    )(offsets, *pieces)
-
-
-def output_kernel(places, heads, mine, other, out, joined):
+    )(offsets, cache, twin, *received)
+
+
+def copy_kernel(_, *refs):
+    for source, target in zip(refs, refs[len(refs) // 2 :]):
+        target[...] = source[...].reshape(target.shape)
+
+
+def for_twin(place, caches):
+    _, _, _, capacity, window, head = caches[0].shape
+    return pl.pallas_call(
+        copy_kernel,
+        out_shape=[jax.ShapeDtypeStruct((4, 4, capacity, window, head), caches[0].dtype)] * 2,
+        grid_spec=pltpu.PrefetchScalarGridSpec(
+            num_scalar_prefetch=1,
+            grid=(4,),
+            in_specs=[
+                pl.BlockSpec((1, 4, 1, capacity, window, head), lambda i, o: (i, 0, 1 - o[1], 0, 0, 0))
+            ]
+            * 2,
+            out_specs=[pl.BlockSpec((1, 4, capacity, window, head), lambda i, _: (i, 0, 0, 0, 0))] * 2,
+        ),
+        cost_estimate=COST,
+        name="for_twin",
+    )(place, *caches)
+
+
+def arrange_kernel(_, *refs):
+    for own, twin, out in zip(refs[:3], refs[3:6], refs[6:]):
+        out[0] = own[0, :, 0]
+        out[1] = twin[0]
+
+
+def arrange(place, cache, twin):
+    capacity, window, head = cache.shape[3:]
+    own = lambda k: pl.BlockSpec(
+        (1, 4, 1, capacity, window, head), lambda i, o: ((o[0] + k) % 4, 0, o[1], 0, 0, 0)
+    )
+    other = lambda k: pl.BlockSpec(
+        (1, 4, capacity, window, head), lambda i, o: ((o[0] + k) % 4, 0, 0, 0, 0)
+    )
+    shape = (2, 4, capacity, window, head)
+    return pl.pallas_call(
+        arrange_kernel,
+        out_shape=[jax.ShapeDtypeStruct(shape, cache.dtype)] * 3,
+        grid_spec=pltpu.PrefetchScalarGridSpec(
+            num_scalar_prefetch=1,
+            grid=(1,),
+            in_specs=[own(k) for k in (1, 3, 2)] + [other(k) for k in (1, 3, 2)],
+            out_specs=[pl.BlockSpec(shape, lambda i, _: (0,) * 5)] * 3,
+        ),
+        compiler_params=pltpu.CompilerParams(vmem_limit_bytes=20 << 20),
+        cost_estimate=COST,
+        name="arrange",
+    )(place, cache, cache, cache, twin, twin, twin)
+
+
+def output_kernel(place, heads, mine, other, out, joined):
     count, depth = mine.shape[:2]
 
     @pl.when(pl.program_id(0) == 0)
     def _():
         for j in range(count):
             for h in range(2):
-                first = pl.multiple_of((places[count] + h) % 2 * depth, depth)
+                first = pl.multiple_of((place[1] + h) % 2 * depth, depth)
                 columns = slice((2 * j + h) * depth, (2 * j + h + 1) * depth)
-                joined[:, columns] = heads[places[j], :, pl.ds(first, depth)]
+                joined[:, columns] = heads[j, :, pl.ds(first, depth)]
 
     total = jnp.zeros(out.shape, jnp.float32)
     for j in range(count):
@@ -232,7 +311,7 @@
     out[...] = total.astype(jnp.bfloat16)
 
 
-def project_out(places, heads, mine, other):
+def project_out(place, heads, mine, other):
     blocks, rows, width = heads.shape
     depth, columns = mine.shape[1:]
     tile = 512
@@ -248,25 +327,13 @@
             scratch_shapes=[pltpu.VMEM((rows, blocks * width), jnp.bfloat16)],
         ),
         compiler_params=pltpu.CompilerParams(vmem_limit_bytes=30 << 20),
-        cost_estimate=pl.CostEstimate(
-            flops=2 * rows * blocks * width * columns, bytes_accessed=10 << 20, transcendentals=0
-        ),
+        cost_estimate=COST,
         name="project_out",
-    )(places, heads, mine, other)
-
-
-def take(array, index):
-    return lax.dynamic_index_in_dim(array, index, 0, keepdims=False)
-
-
-def across_y(cache, groups, capacity):
-    window, head = cache.shape[1:]
-    y, c = lax.axis_index("y"), lax.axis_index("c")
-    sides = cache.reshape(4, 4, 2, capacity, window, head)
-    own = lax.dynamic_index_in_dim(sides, c, 2, keepdims=False)
-    twin = shift(lax.dynamic_index_in_dim(sides, 1 - c, 2, keepdims=False), "c", 1)
-    parts = [jnp.stack([take(own, (y + k) % 4), take(twin, (y + k) % 4)]) for k in range(4)]
-    return [parts[0]] + [shift(parts[k], "y", k) for k in (1, 3, 2)]
+    )(place, heads, mine, other)
+
+
+def across_y(place, cache, twin):
+    return [shift(a, "y", k) for a, k in zip(arrange(place, cache, twin), (1, 3, 2))]
 
 
 def across_z(parts):
@@ -324,7 +391,7 @@
     hit = served_key[:, :, None] == slot_key[None, None, :]
     slot_units = jnp.sum(jnp.where(hit, all_units[served][:, :, None], 0), axis=1)
     offsets = (jnp.cumsum(slot_units, axis=1) - slot_units) * UNIT
-    z_ids = z_ids.astype(jnp.int32)
+    place = jnp.stack([y, core]).astype(jnp.int32)
 
     mine = lambda a: lax.dynamic_index_in_dim(a, group_id, 0, keepdims=False)
     my_holders, my_ranks, my_lengths, my_units = map(
@@ -340,7 +407,7 @@
 
     def packing(size):
         limit = jnp.minimum(offsets, size).reshape(-1)
-        places = jnp.concatenate([limit, z_ids]).astype(jnp.int32)
+        places = jnp.concatenate([z_ids, place, limit]).astype(jnp.int32)
         starts = jnp.minimum(from_z * size + my_start, 4 * size)
         return places, starts.astype(jnp.int32)
 
@@ -353,24 +420,20 @@
     sine = jnp.concatenate([-sine, sine], axis=-1)
 
     ids = block_ids()
+    sides = (4, 4, 2, capacity, window, head_dim)
+    caches = [key_cache.reshape(sides), value_cache.reshape(sides)]
+    twins = [shift(a, "c", 1) for a in for_twin(place, caches)]
+    places, starts = packing(PACKED)
     pieces = spread(span_rows)
 
-    key_parts = across_y(key_cache[0], groups, capacity)
-    value_parts = across_y(value_cache[0], groups, capacity)
-    places, starts = packing(PACKED)
-    keys = across_z(pack(places, key_parts, PACKED))
-    values = across_z(pack(places, value_parts, PACKED))
+    key_parts = across_y(place, caches[0], twins[0])
+    value_parts = across_y(place, caches[1], twins[1])
+    keys = across_z(pack(places, caches[0], twins[0], key_parts, PACKED))
+    values = across_z(pack(places, caches[1], twins[1], value_parts, PACKED))
 
     depth = o_weight.shape[0] // 2
-    half, pieces[6], pieces[7] = lax.optimization_barrier(
-        (lax.dynamic_slice_in_dim(o_weight, core * depth, depth, 0), pieces[6], pieces[7])
-    )
-    pair = jnp.stack([half, shift(half, "zl", 1)])
-    below, above = shift(pair, "x", 1), shift(pair, "x", -1)
-    far, twin_far = shift(below[0], "x", 1), shift(above[1], "x", -1)
-    halves = jnp.stack(
-        [pair[0], pair[1], below[0], above[0], below[1], above[1], far, twin_far]
-    )
+    half = lax.dynamic_slice_in_dim(o_weight, core * depth, depth, 0)
+    halves = lax.all_gather(half, TENSOR)
     other_halves = shift(halves, "c", 1)
 
     q, g, k, v = project(
@@ -378,21 +441,22 @@
         q_norm_gain, k_norm_gain, cosine, sine,
     )
 
-    def packed(keys, values, key_parts, value_parts, q, g, k, v):
+    def packed(keys, values, twins, key_parts, value_parts, q, g, k, v):
         return attend(starts, my_lengths, q, g, k, v, keys, values, window)
 
-    def full(keys, values, key_parts, value_parts, q, g, k, v):
+    def full(keys, values, twins, key_parts, value_parts, q, g, k, v):
         size = 8 * capacity * window
         places, starts = packing(size)
-        keys, values = (across_z(pack(places, a, size)) for a in (key_parts, value_parts))
+        keys = across_z(pack(places, caches[0], twins[0], key_parts, size))
+        values = across_z(pack(places, caches[1], twins[1], value_parts, size))
         return attend(starts, my_lengths, q, g, k, v, keys, values, window)
 
-    attended = lax.cond(fits, packed, full, keys, values, key_parts, value_parts, q, g, k, v)
+    q, other_halves = lax.optimization_barrier((q, other_halves))
+    attended = lax.cond(fits, packed, full, keys, values, twins, key_parts, value_parts, q, g, k, v)
     heads = lax.all_to_all(
         attended.reshape(blocks, rows // blocks, attended.shape[1]), TENSOR, 0, 0, tiled=True
     )
-    out_places = jnp.concatenate([ids, core[None]]).astype(jnp.int32)
-    return project_out(out_places, heads, halves, other_halves)
+    return project_out(place, heads, halves, other_halves)
 
 
 def solution(mesh):

time: 249 us -> 260 us (1.044); the launches traced: 245 us -> 259 us
  blocking collectives: 0 us -> 42 us
  waiting for transfers between devices: 113 us -> 95.1 us
  starting transfers between devices: 51.7 us -> 37.7 us
  between operations: 1.05 us -> 14.3 us
  other arithmetic: 20.5 us -> 9.14 us
  Pallas kernels: 36.7 us -> 43.2 us
  local copies, waits for them, and re-layouts: 21.9 us -> 17.7 us
    ppermute x27 -> x22, waiting for transfers between devices: 100 us -> 36.5 us  [shift(): return lax.ppermute(value, axis, ring(lax.axis_size(axis), step))]
    all_gather x0 -> x1, waiting for transfers between devices: none -> 58.6 us  [local(): halves = lax.all_gather(half, TENSOR)]
    all_to_all x0 -> x1, blocking collectives: none -> 42 us  [local(): lax.all_to_all(attended.reshape(blocks, rows // blocks, attended.shape[1]...]
    all_to_all x1 -> x0, waiting for transfers between devices: 12.6 us -> none  [local(): lax.all_to_all(attended.reshape(blocks, rows // blocks, attended.shape[1]...]
    another operation x9 -> x1, other arithmetic: 11.5 us -> 0.07 us  [local(): place = jnp.stack([y, core]).astype(jnp.int32)]
    unnamed x43 -> x66, local copies, waits for them, and re-layouts: 4.42 us -> 13.9 us
    pallas_call x0 -> x3, Pallas kernels: none -> 9.34 us  [the longest x2 4.98 us: arrange(): pl.pallas_call(arrange_kernel, out_shape=[jax.ShapeDtypeStruct(shape, cac...]
    ppermute x27 -> x22, starting transfers between devices: 46.4 us -> 37.7 us  [shift(): return lax.ppermute(value, axis, ring(lax.axis_size(axis), step))]
  transfers between devices with their start and end apart: 28 -> 23, of which waited for: 12 -> 10; matrix products, arithmetic and copies ran while one was open for 17% -> 4% of each run, Pallas kernels for 8% -> 10%
where the time goes in v3:
time: 260 us; the launch traced here: 259 us
  waiting for transfers between devices  95.1 us (37%)
  Pallas kernels  43.2 us (17%)
  blocking collectives  42 us (16%)
  starting transfers between devices  37.7 us (15%)
  local copies, waits for them, and re-layouts  17.7 us (7%)
  between operations  14.3 us (6%)
  other arithmetic  9.14 us (4%)
    all_gather x1, waiting for transfers between devices, local(): halves = lax.all_gather(half, TENSOR)  58.6 us
    all_to_all x1, blocking collectives, local(): lax.all_to_all(attended.reshape(blocks, rows // blocks, attended.shape[1]...  42 us
    ppermute x22, starting transfers between devices, shift(): return lax.ppermute(value, axis, ring(lax.axis_size(axis), step))  37.7 us
    ppermute x22, waiting for transfers between devices, shift(): return lax.ppermute(value, axis, ring(lax.axis_size(axis), step))  36.5 us
    unnamed x66, local copies, waits for them, and re-layouts  13.9 us
    pallas_call x1, Pallas kernels, project(): pl.pallas_call(project_kernel, out_shape=(jax.ShapeDtypeStruct((rows, wq....  12 us
    pallas_call x1, Pallas kernels, attend(): pl.pallas_call(attend_kernel, out_shape=jax.ShapeDtypeStruct((rows, colum...  9.97 us
    pallas_call x1, Pallas kernels, project_out(): pl.pallas_call(output_kernel, out_shape=jax.ShapeDtypeStruct((rows, colum...  5.99 us
  transfers between devices with their start and end apart: 23, of which 10 were waited for; matrix products, arithmetic and copies ran while one was open for 4% of the time, Pallas kernels for 10%

profile of v3, /device:TPU:8, one launch (start us, length us, event | category | flops | bytes accessed | tf_op | source)
XLA Modules:
  0.0 259.3 jit_solution(6945111812510381510)
XLA Ops:
  6.5 1.2 copy-done
  7.8 0.8 constant_dynamic-slice_fusion
  8.6 58.6 %all-gather.3.cloned.1.call-done = bf16[1024,2048]{1,0:T(8,128)(2,1)} async-done(((bf16[128,2048]{1,0:T(8,128)(2,1)}), bf16[1024,2048]{1,0:T(8,128)(2,1)}) %all-gather.3.cloned.1.call-update) | async-done | bytes 4194320 | tf_op jit(solution)/shard_map/all_gather | solution.py:436
  67.3 0.8 collective-permute-start.14
  68.1 4.4 %for_twin.1 = (bf16[4,4,2,128,128]{4,3,2,1,0:T(8,128)(2,1)}, bf16[4,4,2,128,128]{4,3,2,1,0:T(8,128)(2,1)}) custom-call(s32[2]{0:T(128)S(1)} %pad_add_fusion.1._.place, bf16[4,4,2,2,128,128]{5,4,3,2,1,0:T(8,128)(2,1)} %bitcast.27, bf16[4,4,2,2,128,128]{5,4,3,2,1,0:T(8,128)(2,1)} %bitcast.33), custom_call_target="tpu_custom_call" | custom-call | flops 1048576 | bytes 1048576 | tf_op jit(solution)/shard_map/for_twin/pallas_call | solution.py:248
  72.5 0.5 collective-permute-start.10
  73.3 0.2 convert_reduce_fusion
  73.8 0.6 gather_fusion
  74.4 0.6 gather_fusion.1
  75.0 2.8 %collective-permute-done.10.refs_3_.refs_4_.refs_5_.twin = bf16[4,4,2,128,128]{4,3,2,1,0:T(8,128)(2,1)} collective-permute-done((bf16[4,4,2,128,128]{4,3,2,1,0:T(8,128)(2,1)}, bf16[4,4,2,128,128]{4,3,2,1,0:T(8,128)(2,1)}, u32[]{:S(2)}, u32[]{:S(2)}) %collective-permute-start.10) | collective-permute-done | bytes 1048608 | tf_op jit(solution)/shard_map/ppermute | solution.py:28
  77.8 2.2 collective-permute-start.16
  79.9 0.2 select_reduce_fusion.1
  80.1 0.2 reduce_window_sum.11
  80.3 3.0 %arrange.3 = (bf16[2,4,2,128,128]{4,3,2,1,0:T(8,128)(2,1)}, bf16[2,4,2,128,128]{4,3,2,1,0:T(8,128)(2,1)}, bf16[2,4,2,128,128]{4,3,2,1,0:T(8,128)(2,1)S(1)}) custom-call(s32[2]{0:T(128)S(1)} %pad_add_fusion.1._.place, bf16[4,4,2,2,128,128]{5,4,3,2,1,0:T(8,128)(2,1)} %bitcast.34, bf16[4,4,2,2,128,128]{5,4,3,2,1,0:T(8,128)(2,1)} %bitcast.35, ...), custom_call_target="tpu_custom_call" | custom-call | flops 1048576 | bytes 1048576 | tf_op jit(solution)/shard_map/arrange/pallas_call | solution.py:280
  83.3 0.8 copy-done.20
  84.1 4.5 %collective-permute-done.15.refs_2_ = bf16[1536,256]{1,0:T(8,128)(2,1)S(1)} collective-permute-done((bf16[1536,256]{1,0:T(8,128)(2,1)}, bf16[1536,256]{1,0:T(8,128)(2,1)S(1)}, u32[]{:S(2)}, u32[]{:S(2)}) %collective-permute-start.15) | collective-permute-done | bytes 786464 | tf_op jit(solution)/shard_map/ppermute | solution.py:28
  88.6 1.5 collective-permute-start.11
  90.1 0.5 collective-permute-start.12
  90.7 0.3 collective-permute-start.18
  91.3 0.3 fusion.10
  91.6 2.0 arrange.2
  93.6 4.6 %collective-permute-done.16.refs_3_ = bf16[1536,256]{1,0:T(8,128)(2,1)} collective-permute-done((bf16[1536,256]{1,0:T(8,128)(2,1)S(1)}, bf16[1536,256]{1,0:T(8,128)(2,1)}, u32[]{:S(2)}, u32[]{:S(2)}) %collective-permute-start.16) | collective-permute-done | bytes 786464 | tf_op jit(solution)/shard_map/ppermute | solution.py:28
  98.2 2.1 collective-permute-start.13
  100.4 3.4 %collective-permute-done.11.refs_0_ = bf16[2,4,2,128,128]{4,3,2,1,0:T(8,128)(2,1)} collective-permute-done((bf16[2,4,2,128,128]{4,3,2,1,0:T(8,128)(2,1)}, bf16[2,4,2,128,128]{4,3,2,1,0:T(8,128)(2,1)}, u32[]{:S(2)}, u32[]{:S(2)}) %collective-permute-start.11) | collective-permute-done | bytes 524320 | tf_op jit(solution)/shard_map/ppermute | solution.py:28
  103.8 1.5 collective-permute-start.7
  105.3 8.0 %collective-permute-start.8 = (bf16[2,4,2,128,128]{4,3,2,1,0:T(8,128)(2,1)S(1)}, bf16[2,4,2,128,128]{4,3,2,1,0:T(8,128)(2,1)S(1)}, u32[]{:S(2)}, u32[]{:S(2)}) collective-permute-start(bf16[2,4,2,128,128]{4,3,2,1,0:T(8,128)(2,1)S(1)} %get-tuple-element.159), channel_id=1, source_target_pairs={{0,192},{64,0},{128,64},{192,128},{1,193},{65,1},{129,65},{193,129... | collective-permute-start | bytes 1572872 | tf_op jit(solution)/shard_map/ppermute | solution.py:28
  113.4 3.7 %collective-permute-done.13.refs_2_ = bf16[2,4,2,128,128]{4,3,2,1,0:T(8,128)(2,1)S(1)} collective-permute-done((bf16[2,4,2,128,128]{4,3,2,1,0:T(8,128)(2,1)S(1)}, bf16[2,4,2,128,128]{4,3,2,1,0:T(8,128)(2,1)S(1)}, u32[]{:S(2)}, u32[]{:S(2)}) %collective-permute-start.13) | collective-permute-done | bytes 524320 | tf_op jit(solution)/shard_map/ppermute | solution.py:28
  117.1 7.8 %collective-permute-done.7.refs_0_ = bf16[2,4,2,128,128]{4,3,2,1,0:T(8,128)(2,1)S(1)} collective-permute-done((bf16[2,4,2,128,128]{4,3,2,1,0:T(8,128)(2,1)S(1)}, bf16[2,4,2,128,128]{4,3,2,1,0:T(8,128)(2,1)S(1)}, u32[]{:S(2)}, u32[]{:S(2)}) %collective-permute-start.7) | collective-permute-done | bytes 524320 | tf_op jit(solution)/shard_map/ppermute | solution.py:28
  124.9 1.5 collective-permute-done.8.refs_1_
  126.4 2.0 collective-permute-start.9
  128.4 1.9 collective-permute-start.20
  130.3 4.5 %fusion = (f32[1536,64]{1,0:T(8,128)}, f32[1536,64]{1,0:T(8,128)}, f32[1536,64]{1,0:T(8,128)}) fusion(f32[64]{0:T(128)S(1)} %multiply_power_fusion, f32[1536]{0:T(1024)S(1)} %convert_element_type.19), kind=kLoop, calls=%fused_computation.11 | loop fusion | flops 196608 | bytes 1186048 | tf_op jit(solution)/shard_map/neg | solution.py:420
  134.8 3.1 %pack.7 = (bf16[1152,128]{1,0:T(8,128)(2,1)}, bf16[1152,128]{1,0:T(8,128)(2,1)S(1)}, bf16[1152,128]{1,0:T(8,128)(2,1)}, bf16[1152,128]{1,0:T(8,128)(2,1)}) custom-call(s32[70]{0:T(128)S(1)} %pad_add_fusion.2.offsets, bf16[4,4,2,2,128,128]{5,4,3,2,1,0:T(8,128)(2,1)S(1)} %bitcast.38, ...), custom_call_target="tpu_custom_call" | custom-call | flops 1048576 | bytes 1048576 | tf_op jit(solution)/shard_map/pack/pallas_call | solution.py:221
  137.9 3.5 %collective-permute-done.9.refs_2_ = bf16[2,4,2,128,128]{4,3,2,1,0:T(8,128)(2,1)S(1)} collective-permute-done((bf16[2,4,2,128,128]{4,3,2,1,0:T(8,128)(2,1)S(1)}, bf16[2,4,2,128,128]{4,3,2,1,0:T(8,128)(2,1)S(1)}, u32[]{:S(2)}, u32[]{:S(2)}) %collective-permute-start.9) | collective-permute-done | bytes 524320 | tf_op jit(solution)/shard_map/ppermute | solution.py:28
  141.3 2.5 collective-permute-start.25
  143.9 0.2 select_reduce_fusion.2
  144.1 2.8 %pack.6 = (bf16[1152,128]{1,0:T(8,128)(2,1)}, bf16[1152,128]{1,0:T(8,128)(2,1)}, bf16[1152,128]{1,0:T(8,128)(2,1)}, bf16[1152,128]{1,0:T(8,128)(2,1)}) custom-call(s32[70]{0:T(128)S(1)} %pad_add_fusion.2.offsets, bf16[4,4,2,2,128,128]{5,4,3,2,1,0:T(8,128)(2,1)S(1)} %bitcast.32, ...), custom_call_target="tpu_custom_call" | custom-call | flops 1048576 | bytes 1048576 | tf_op jit(solution)/shard_map/pack/pallas_call | solution.py:221
  146.9 4.7 %collective-permute-done.19.refs_6_ = bf16[1536,256]{1,0:T(8,128)(2,1)S(1)} collective-permute-done((bf16[1536,256]{1,0:T(8,128)(2,1)S(1)}, bf16[1536,256]{1,0:T(8,128)(2,1)S(1)}, u32[]{:S(2)}, u32[]{:S(2)}) %collective-permute-start.19) | collective-permute-done | bytes 786464 | tf_op jit(solution)/shard_map/ppermute | solution.py:28
  151.6 0.9 copy-done.12
  152.4 4.8 %collective-permute-start.26 = (bf16[1152,128]{1,0:T(8,128)(2,1)}, bf16[1152,128]{1,0:T(8,128)(2,1)S(1)}, u32[]{:S(2)}, u32[]{:S(2)}) collective-permute-start(bf16[1152,128]{1,0:T(8,128)(2,1)} %get-tuple-element.176), channel_id=1, source_target_pairs={{0,32},{16,48},{32,0},{48,16},{1,33},{17,49},{33,1},{49,17},{2,34}... | collective-permute-start | bytes 884744 | tf_op jit(solution)/shard_map/ppermute | solution.py:28
  157.3 0.9 copy-done.10
  158.2 1.3 collective-permute-start.27
  159.5 1.6 collective-permute-start.22
  161.1 0.9 copy-done.14
  162.0 2.7 %collective-permute-start.23 = (bf16[1152,128]{1,0:T(8,128)(2,1)}, bf16[1152,128]{1,0:T(8,128)(2,1)}, u32[]{:S(2)}, u32[]{:S(2)}) collective-permute-start(bf16[1152,128]{1,0:T(8,128)(2,1)} %get-tuple-element.172), channel_id=1, source_target_pairs={{0,32},{16,48},{32,0},{48,16},{1,33},{17,49},{33,1},{49,17},{2,34}... | collective-permute-start | bytes 884744 | tf_op jit(solution)/shard_map/ppermute | solution.py:28
  164.7 3.4 %collective-permute-start.24 = (bf16[1152,128]{1,0:T(8,128)(2,1)}, bf16[1152,128]{1,0:T(8,128)(2,1)}, u32[]{:S(2)}, u32[]{:S(2)}) collective-permute-start(bf16[1152,128]{1,0:T(8,128)(2,1)} %get-tuple-element.173), channel_id=1, source_target_pairs={{0,48},{16,0},{32,16},{48,32},{1,49},{17,1},{33,17},{49,33},{2,50}... | collective-permute-start | bytes 884744 | tf_op jit(solution)/shard_map/ppermute | solution.py:28
  168.2 0.6 reduce_max.9
  169.4 0.4 copy.30.refs_8_
  169.9 2.5 pad_maximum_fusion
  172.5 0.1 copy-done.5
  172.6 0.2 copy-done.7
  172.8 1.1 copy-done.9
  174.0 1.1 copy-done.11
  175.1 1.1 copy-done.13
  176.2 1.1 copy-done.15
  177.4 1.0 copy-done.16
  178.4 1.0 copy-done.17
  179.4 12.0 %project.1 = (bf16[1536,256]{1,0:T(8,128)(2,1)}, f32[1536,256]{1,0:T(8,128)}, bf16[1536,128]{1,0:T(8,128)(2,1)}, bf16[1536,128]{1,0:T(8,128)(2,1)}) custom-call(s32[8]{0:T(128)S(1)} %stack.47.ids, bf16[1536,256]{1,0:T(8,128)(2,1)S(1)} %copy-done.5, bf16[1536,256]{1,0:T(8,128)(2,1)S(1)} %copy-done.9, bf16[1536,256]{1,0:T(8,128)(2,1)S(1)} %copy-done.7, ...), custom_call_target="tpu_custom_call" | custom-call | flops 1048576 | bytes 1048576 | tf_op jit(solution)/shard_map/project/pallas_call | solution.py:104
  191.5 10.7 %conditional.1 = (bf16[1536,256]{1,0:T(8,128)(2,1)S(1)}) conditional(s32[]{:T(128)} %convert_element_type.16, (s32[24]{0:T(128)S(1)}, s32[24]{0:T(128)S(1)}, s32[4,16]{1,0:T(4,128)S(1)}, s32[4,16]{1,0:T(4,128)S(1)}, s32[4]{0:T(128)S(1)}, /*index=5*/s32[2]{0:T(128)S(1)}, bf16[4,4,2,2,128,128]{5,4,3,2,1,0:T(8,128)(2,1)}, ...), branch_computations={%region_6.7_spmd, %region_7.8_spmd} | conditional | flops 3146132 | bytes 42994216 | solution.py:455
  191.5 0.7 copy-done.37
  192.2 10.0 %attend.3 = bf16[1536,256]{1,0:T(8,128)(2,1)S(1)} custom-call(s32[24]{0:T(128)S(1)} %add_minimum_fusion.1.starts, s32[24]{0:T(128)S(1)} %get-tuple-element.122.lengths, bf16[1536,256]{1,0:T(8,128)(2,1)} %get-tuple-element.123.q, f32[1536,256]{1,0:T(8,128)} %get-tuple-element.124.g, bf16[1536,128]{1,0:T(8,128)(2,1)} %get-tuple-element.125.k, ...), custom_call_target="tpu_custom_call" | custom-call | flops 1048576 | bytes 1048576 | tf_op jit(solution)/shard_map/cond/branch_1_fun/attend/pallas_call | solution.py:183
  202.2 42.0 %all_to_all.5.heads = bf16[8,192,256]{2,1,0:T(8,128)(2,1)S(1)} all-to-all(bf16[8,192,256]{2,1,0:T(8,128)(2,1)S(1)} %bitcast.39), channel_id=1, replica_groups=mesh['y'=4,'zh'=4,'c'=2,'zl'=2,'x'=4] {'zl','x'}, dimensions={0} | all-to-all | bytes 1572864 | tf_op jit(solution)/shard_map/all_to_all | solution.py:456
  244.2 2.2 copy-done.1
  246.4 6.0 %project_out.1 = bf16[192,2048]{1,0:T(8,128)(2,1)} custom-call(s32[2]{0:T(128)S(1)} %pad_add_fusion.1._.place, bf16[8,192,256]{2,1,0:T(8,128)(2,1)S(1)} %all_to_all.5.heads, bf16[8,128,2048]{2,1,0:T(8,128)(2,1)S(1)} %bitcast.24, bf16[8,128,2048]{2,1,0:T(8,128)(2,1)} %collective-permute-done.21.other), custom_call_target="tpu_custom_call" | custom-call | flops 1048576 | bytes 1048576 | tf_op jit(solution)/shard_map/project_out/pallas_call | solution.py:319
  (105 shorter events, 1.5 us)
Async XLA Ops:
  6.5 1.2 copy-start
  6.5 60.7 %all-gather.3.cloned.1.call-start = ((), (), s32[]{:S(2)}) async-start(), calls=%async_computation.1 | async-start | bytes 4718592 | tf_op jit(solution)/shard_map/all_gather | solution.py:436
  67.2 97.5 %collective-permute-start.21 = (bf16[8,128,2048]{2,1,0:T(8,128)(2,1)}, bf16[8,128,2048]{2,1,0:T(8,128)(2,1)}, u32[]{:S(2)}, u32[]{:S(2)}) collective-permute-start(bf16[8,128,2048]{2,1,0:T(8,128)(2,1)} %bitcast.23), channel_id=1, source_target_pairs={{0,8},{8,0},{1,9},{9,1},{2,10},{10,2},{3,11},{11,3},{4,12},{12,4},... | collective-permute-start | bytes 12582920 | tf_op jit(solution)/shard_map/ppermute | solution.py:28
  67.3 21.4 %collective-permute-start.15 = (bf16[1536,256]{1,0:T(8,128)(2,1)}, bf16[1536,256]{1,0:T(8,128)(2,1)S(1)}, u32[]{:S(2)}, u32[]{:S(2)}) collective-permute-start(bf16[1536,256]{1,0:T(8,128)(2,1)} %refs_0_.1), channel_id=1, source_target_pairs={{0,1},{1,2},{2,3},{3,0},{4,5},{5,6},{6,7},{7,4},{8,9},{9,10},{10,1... | collective-permute-start | bytes 2359304 | tf_op jit(solution)/shard_map/ppermute | solution.py:28
  67.3 22.9 %collective-permute-start.14 = (bf16[1536,256]{1,0:T(8,128)(2,1)}, bf16[1536,256]{1,0:T(8,128)(2,1)S(1)}, u32[]{:S(2)}, u32[]{:S(2)}) collective-permute-start(bf16[1536,256]{1,0:T(8,128)(2,1)} %refs_0_.1), channel_id=1, source_target_pairs={{0,4},{4,0},{1,5},{5,1},{2,6},{6,2},{3,7},{7,3},{8,12},{12,8},{9,1... | collective-permute-start | bytes 2359304 | tf_op jit(solution)/shard_map/ppermute | solution.py:28
  68.1 4.9 %copy-start.41 = (s32[4]{0:T(128)S(1)}, s32[4]{0:T(128)}, u32[]{:S(2)}) copy-start(s32[4]{0:T(128)} %constant.255.clone) | copy-start | bytes 52
  68.1 5.0 %copy-start.40 = (s32[768,1]{0,1:T(1,128)S(1)}, s32[768,1]{0,1:T(1,128)}, u32[]{:S(2)}) copy-start(s32[768,1]{0,1:T(1,128)} %param.28) | copy-start | bytes 9220
  68.1 5.6 %copy-start.39 = (s32[768]{0:T(1024)S(1)}, s32[768]{0:T(1024)}, u32[]{:S(2)}) copy-start(s32[768]{0:T(1024)} %param.29) | copy-start | bytes 9220
  68.1 9.6 %copy-start.4 = (bf16[1536,256]{1,0:T(8,128)(2,1)S(1)}, bf16[1536,256]{1,0:T(8,128)(2,1)}, u32[]{:S(2)}) copy-start(bf16[1536,256]{1,0:T(8,128)(2,1)} %refs_0_.1) | copy-start | bytes 2359300
  72.5 18.3 %collective-permute-start.6 = (bf16[4,4,2,128,128]{4,3,2,1,0:T(8,128)(2,1)}, bf16[4,4,2,128,128]{4,3,2,1,0:T(8,128)(2,1)}, u32[]{:S(2)}, u32[]{:S(2)}) collective-permute-start(bf16[4,4,2,128,128]{4,3,2,1,0:T(8,128)(2,1)} %get-tuple-element.157), channel_id=1, source_target_pairs={{0,8},{8,0},{1,9},{9,1},{2,10},{10,2},{3,11},{11,3},{4,12},{12,4},... | collective-permute-start | bytes 3145736 | tf_op jit(solution)/shard_map/ppermute | solution.py:28
  72.5 5.3 %collective-permute-start.10 = (bf16[4,4,2,128,128]{4,3,2,1,0:T(8,128)(2,1)}, bf16[4,4,2,128,128]{4,3,2,1,0:T(8,128)(2,1)}, u32[]{:S(2)}, u32[]{:S(2)}) collective-permute-start(bf16[4,4,2,128,128]{4,3,2,1,0:T(8,128)(2,1)} %get-tuple-element.161), channel_id=1, source_target_pairs={{0,8},{8,0},{1,9},{9,1},{2,10},{10,2},{3,11},{11,3},{4,12},{12,4},... | collective-permute-start | bytes 3145736 | tf_op jit(solution)/shard_map/ppermute | solution.py:28
  77.8 20.5 %collective-permute-start.16 = (bf16[1536,256]{1,0:T(8,128)(2,1)S(1)}, bf16[1536,256]{1,0:T(8,128)(2,1)}, u32[]{:S(2)}, u32[]{:S(2)}) collective-permute-start(bf16[1536,256]{1,0:T(8,128)(2,1)S(1)} %copy-done.4), channel_id=1, source_target_pairs={{0,3},{1,0},{2,1},{3,2},{4,7},{5,4},{6,5},{7,6},{8,11},{9,8},{10,9... | collective-permute-start | bytes 2359304 | tf_op jit(solution)/shard_map/ppermute | solution.py:28
  83.3 0.8 copy-start.20
  88.6 36.3 %copy-start.6 = (bf16[1536,256]{1,0:T(8,128)(2,1)}, bf16[1536,256]{1,0:T(8,128)(2,1)S(1)}, u32[]{:S(2)}) copy-start(bf16[1536,256]{1,0:T(8,128)(2,1)S(1)} %collective-permute-done.15.refs_2_) | copy-start | bytes 2359300
  88.6 15.1 %collective-permute-start.11 = (bf16[2,4,2,128,128]{4,3,2,1,0:T(8,128)(2,1)}, bf16[2,4,2,128,128]{4,3,2,1,0:T(8,128)(2,1)}, u32[]{:S(2)}, u32[]{:S(2)}) collective-permute-start(bf16[2,4,2,128,128]{4,3,2,1,0:T(8,128)(2,1)} %get-tuple-element.162), channel_id=1, source_target_pairs={{0,64},{64,128},{128,192},{192,0},{1,65},{65,129},{129,193},{193,1... | collective-permute-start | bytes 1572872 | tf_op jit(solution)/shard_map/ppermute | solution.py:28
  90.1 27.0 %copy-start.8 = (bf16[1536,256]{1,0:T(8,128)(2,1)}, bf16[1536,256]{1,0:T(8,128)(2,1)S(1)}, u32[]{:S(2)}) copy-start(bf16[1536,256]{1,0:T(8,128)(2,1)S(1)} %collective-permute-done.14.refs_1_) | copy-start | bytes 2359300
  90.1 15.2 %collective-permute-start.12 = (bf16[2,4,2,128,128]{4,3,2,1,0:T(8,128)(2,1)}, bf16[2,4,2,128,128]{4,3,2,1,0:T(8,128)(2,1)}, u32[]{:S(2)}, u32[]{:S(2)}) collective-permute-start(bf16[2,4,2,128,128]{4,3,2,1,0:T(8,128)(2,1)} %get-tuple-element.163), channel_id=1, source_target_pairs={{0,192},{64,0},{128,64},{192,128},{1,193},{65,1},{129,65},{193,129... | collective-permute-start | bytes 1572872 | tf_op jit(solution)/shard_map/ppermute | solution.py:28
  90.7 37.7 %collective-permute-start.18 = (bf16[1536,256]{1,0:T(8,128)(2,1)S(1)}, bf16[1536,256]{1,0:T(8,128)(2,1)}, u32[]{:S(2)}, u32[]{:S(2)}) collective-permute-start(bf16[1536,256]{1,0:T(8,128)(2,1)S(1)} %collective-permute-done.14.refs_1_), channel_id=1, source_target_pairs={{0,3},{1,0},{2,1},{3,2},{4,7},{5,4},{6,5},{7,6},{8,11},{9,8},{10,9... | collective-permute-start | bytes 2359304 | tf_op jit(solution)/shard_map/ppermute | solution.py:28
  91.6 6.7 %copy-start.21 = (bf16[2,4,2,128,128]{4,3,2,1,0:T(8,128)(2,1)S(1)}, bf16[2,4,2,128,128]{4,3,2,1,0:T(8,128)(2,1)}, u32[]{:S(2)}) copy-start(bf16[2,4,2,128,128]{4,3,2,1,0:T(8,128)(2,1)} %copy-done.20) | copy-start | bytes 1572868
  93.6 41.2 %copy-start.24 = (bf16[1,64,128,128]{3,2,1,0:T(8,128)(2,1)S(1)}, bf16[1,64,128,128]{3,2,1,0:T(8,128)(2,1)}, u32[]{:S(2)}) copy-start(bf16[1,64,128,128]{3,2,1,0:T(8,128)(2,1)} %param.27) | copy-start | bytes 6291460
  98.2 18.9 %collective-permute-start.13 = (bf16[2,4,2,128,128]{4,3,2,1,0:T(8,128)(2,1)S(1)}, bf16[2,4,2,128,128]{4,3,2,1,0:T(8,128)(2,1)S(1)}, u32[]{:S(2)}, u32[]{:S(2)}) collective-permute-start(bf16[2,4,2,128,128]{4,3,2,1,0:T(8,128)(2,1)S(1)} %copy-done.21), channel_id=1, source_target_pairs={{0,128},{64,192},{128,0},{192,64},{1,129},{65,193},{129,1},{193,65... | collective-permute-start | bytes 1572872 | tf_op jit(solution)/shard_map/ppermute | solution.py:28
  103.8 21.1 %collective-permute-start.7 = (bf16[2,4,2,128,128]{4,3,2,1,0:T(8,128)(2,1)S(1)}, bf16[2,4,2,128,128]{4,3,2,1,0:T(8,128)(2,1)S(1)}, u32[]{:S(2)}, u32[]{:S(2)}) collective-permute-start(bf16[2,4,2,128,128]{4,3,2,1,0:T(8,128)(2,1)S(1)} %get-tuple-element.158), channel_id=1, source_target_pairs={{0,64},{64,128},{128,192},{192,0},{1,65},{65,129},{129,193},{193,1... | collective-permute-start | bytes 1572872 | tf_op jit(solution)/shard_map/ppermute | solution.py:28
  105.3 21.1 %collective-permute-start.8 = (bf16[2,4,2,128,128]{4,3,2,1,0:T(8,128)(2,1)S(1)}, bf16[2,4,2,128,128]{4,3,2,1,0:T(8,128)(2,1)S(1)}, u32[]{:S(2)}, u32[]{:S(2)}) collective-permute-start(bf16[2,4,2,128,128]{4,3,2,1,0:T(8,128)(2,1)S(1)} %get-tuple-element.159), channel_id=1, source_target_pairs={{0,192},{64,0},{128,64},{192,128},{1,193},{65,1},{129,65},{193,129... | collective-permute-start | bytes 1572872 | tf_op jit(solution)/shard_map/ppermute | solution.py:28
  117.1 20.8 %copy-start.27 = (bf16[2,4,2,128,128]{4,3,2,1,0:T(8,128)(2,1)}, bf16[2,4,2,128,128]{4,3,2,1,0:T(8,128)(2,1)S(1)}, u32[]{:S(2)}) copy-start(bf16[2,4,2,128,128]{4,3,2,1,0:T(8,128)(2,1)S(1)} %collective-permute-done.13.refs_2_) | copy-start | bytes 1572868
  117.1 40.2 %collective-permute-start.17 = (bf16[1536,256]{1,0:T(8,128)(2,1)S(1)}, bf16[1536,256]{1,0:T(8,128)(2,1)S(1)}, u32[]{:S(2)}, u32[]{:S(2)}) collective-permute-start(bf16[1536,256]{1,0:T(8,128)(2,1)S(1)} %collective-permute-done.14.refs_1_), channel_id=1, source_target_pairs={{0,1},{1,2},{2,3},{3,0},{4,5},{5,6},{6,7},{7,4},{8,9},{9,10},{10,1... | collective-permute-start | bytes 2359304 | tf_op jit(solution)/shard_map/ppermute | solution.py:28
  124.9 19.1 %copy-start.28 = (bf16[2,4,2,128,128]{4,3,2,1,0:T(8,128)(2,1)}, bf16[2,4,2,128,128]{4,3,2,1,0:T(8,128)(2,1)S(1)}, u32[]{:S(2)}) copy-start(bf16[2,4,2,128,128]{4,3,2,1,0:T(8,128)(2,1)S(1)} %collective-permute-done.7.refs_0_) | copy-start | bytes 1572868
  124.9 26.6 %collective-permute-start.19 = (bf16[1536,256]{1,0:T(8,128)(2,1)S(1)}, bf16[1536,256]{1,0:T(8,128)(2,1)S(1)}, u32[]{:S(2)}, u32[]{:S(2)}) collective-permute-start(bf16[1536,256]{1,0:T(8,128)(2,1)S(1)} %collective-permute-done.15.refs_2_), channel_id=1, source_target_pairs={{0,1},{1,2},{2,3},{3,0},{4,5},{5,6},{6,7},{7,4},{8,9},{9,10},{10,1... | collective-permute-start | bytes 2359304 | tf_op jit(solution)/shard_map/ppermute | solution.py:28
  126.4 17.7 %copy-start.30 = (bf16[2,4,2,128,128]{4,3,2,1,0:T(8,128)(2,1)}, bf16[2,4,2,128,128]{4,3,2,1,0:T(8,128)(2,1)S(1)}, u32[]{:S(2)}) copy-start(bf16[2,4,2,128,128]{4,3,2,1,0:T(8,128)(2,1)S(1)} %collective-permute-done.8.refs_1_) | copy-start | bytes 1572868
  126.4 14.9 %collective-permute-start.9 = (bf16[2,4,2,128,128]{4,3,2,1,0:T(8,128)(2,1)S(1)}, bf16[2,4,2,128,128]{4,3,2,1,0:T(8,128)(2,1)S(1)}, u32[]{:S(2)}, u32[]{:S(2)}) collective-permute-start(bf16[2,4,2,128,128]{4,3,2,1,0:T(8,128)(2,1)S(1)} %get-tuple-element.160), channel_id=1, source_target_pairs={{0,128},{64,192},{128,0},{192,64},{1,129},{65,193},{129,1},{193,65... | collective-permute-start | bytes 1572872 | tf_op jit(solution)/shard_map/ppermute | solution.py:28
  128.4 32.7 %collective-permute-start.20 = (bf16[1536,256]{1,0:T(8,128)(2,1)}, bf16[1536,256]{1,0:T(8,128)(2,1)S(1)}, u32[]{:S(2)}, u32[]{:S(2)}) collective-permute-start(bf16[1536,256]{1,0:T(8,128)(2,1)} %collective-permute-done.18.refs_5_), channel_id=1, source_target_pairs={{0,3},{1,0},{2,1},{3,2},{4,7},{5,4},{6,5},{7,6},{8,11},{9,8},{10,9... | collective-permute-start | bytes 2359304 | tf_op jit(solution)/shard_map/ppermute | solution.py:28
  134.8 9.3 %copy-start.22 = (bf16[1,64,128,128]{3,2,1,0:T(8,128)(2,1)S(1)}, bf16[1,64,128,128]{3,2,1,0:T(8,128)(2,1)}, u32[]{:S(2)}) copy-start(bf16[1,64,128,128]{3,2,1,0:T(8,128)(2,1)} %param.26) | copy-start | bytes 6291460
  141.3 5.5 %copy-start.32 = (bf16[2,4,2,128,128]{4,3,2,1,0:T(8,128)(2,1)}, bf16[2,4,2,128,128]{4,3,2,1,0:T(8,128)(2,1)S(1)}, u32[]{:S(2)}) copy-start(bf16[2,4,2,128,128]{4,3,2,1,0:T(8,128)(2,1)S(1)} %collective-permute-done.9.refs_2_) | copy-start | bytes 1572868
  141.3 18.1 %collective-permute-start.25 = (bf16[1152,128]{1,0:T(8,128)(2,1)S(1)}, bf16[1152,128]{1,0:T(8,128)(2,1)S(1)}, u32[]{:S(2)}, u32[]{:S(2)}) collective-permute-start(bf16[1152,128]{1,0:T(8,128)(2,1)S(1)} %get-tuple-element.175), channel_id=1, source_target_pairs={{0,16},{16,32},{32,48},{48,0},{1,17},{17,33},{33,49},{49,1},{2,18}... | collective-permute-start | bytes 884744 | tf_op jit(solution)/shard_map/ppermute | solution.py:28
  144.1 25.3 %copy-start.38 = (f32[2048]{0:T(1024)S(1)}, f32[2048]{0:T(1024)}, u32[]{:S(2)}) copy-start(f32[2048]{0:T(1024)} %param.18) | copy-start | bytes 24580
  151.6 0.9 copy-start.12
  152.4 39.0 %collective-permute-start.26 = (bf16[1152,128]{1,0:T(8,128)(2,1)}, bf16[1152,128]{1,0:T(8,128)(2,1)S(1)}, u32[]{:S(2)}, u32[]{:S(2)}) collective-permute-start(bf16[1152,128]{1,0:T(8,128)(2,1)} %get-tuple-element.176), channel_id=1, source_target_pairs={{0,32},{16,48},{32,0},{48,16},{1,33},{17,49},{33,1},{49,17},{2,34}... | collective-permute-start | bytes 884744 | tf_op jit(solution)/shard_map/ppermute | solution.py:28
  157.3 0.9 copy-start.10
  158.2 33.3 %collective-permute-start.27 = (bf16[1152,128]{1,0:T(8,128)(2,1)}, bf16[1152,128]{1,0:T(8,128)(2,1)}, u32[]{:S(2)}, u32[]{:S(2)}) collective-permute-start(bf16[1152,128]{1,0:T(8,128)(2,1)} %get-tuple-element.177), channel_id=1, source_target_pairs={{0,48},{16,0},{32,16},{48,32},{1,49},{17,1},{33,17},{49,33},{2,50}... | collective-permute-start | bytes 884744 | tf_op jit(solution)/shard_map/ppermute | solution.py:28
  159.5 1.7 copy-start.36
  159.5 32.0 %collective-permute-start.22 = (bf16[1152,128]{1,0:T(8,128)(2,1)}, bf16[1152,128]{1,0:T(8,128)(2,1)}, u32[]{:S(2)}, u32[]{:S(2)}) collective-permute-start(bf16[1152,128]{1,0:T(8,128)(2,1)} %get-tuple-element.171), channel_id=1, source_target_pairs={{0,16},{16,32},{32,48},{48,0},{1,17},{17,33},{33,49},{49,1},{2,18}... | collective-permute-start | bytes 884744 | tf_op jit(solution)/shard_map/ppermute | solution.py:28
  161.1 0.9 copy-start.14
  162.0 29.5 %collective-permute-start.23 = (bf16[1152,128]{1,0:T(8,128)(2,1)}, bf16[1152,128]{1,0:T(8,128)(2,1)}, u32[]{:S(2)}, u32[]{:S(2)}) collective-permute-start(bf16[1152,128]{1,0:T(8,128)(2,1)} %get-tuple-element.172), channel_id=1, source_target_pairs={{0,32},{16,48},{32,0},{48,16},{1,33},{17,49},{33,1},{49,17},{2,34}... | collective-permute-start | bytes 884744 | tf_op jit(solution)/shard_map/ppermute | solution.py:28
  164.7 26.8 %collective-permute-start.24 = (bf16[1152,128]{1,0:T(8,128)(2,1)}, bf16[1152,128]{1,0:T(8,128)(2,1)}, u32[]{:S(2)}, u32[]{:S(2)}) collective-permute-start(bf16[1152,128]{1,0:T(8,128)(2,1)} %get-tuple-element.173), channel_id=1, source_target_pairs={{0,48},{16,0},{32,16},{48,32},{1,49},{17,1},{33,17},{49,33},{2,50}... | collective-permute-start | bytes 884744 | tf_op jit(solution)/shard_map/ppermute | solution.py:28
  169.8 2.6 %copy-start.2 = (bf16[2048,256]{1,0:T(8,128)(2,1)S(1)}, bf16[2048,256]{1,0:T(8,128)(2,1)}, u32[]{:S(2)}) copy-start(bf16[2048,256]{1,0:T(8,128)(2,1)} %refs_9_.1) | copy-start | bytes 3145732
  169.8 2.6 %copy-start.18 = (f32[128]{0:T(128)S(1)}, f32[128]{0:T(128)}, u32[]{:S(2)}) copy-start(f32[128]{0:T(128)} %param.23) | copy-start | bytes 1540
  169.8 2.6 %copy-start.19 = (f32[128]{0:T(128)S(1)}, f32[128]{0:T(128)}, u32[]{:S(2)}) copy-start(f32[128]{0:T(128)} %param.24) | copy-start | bytes 1540
  169.9 2.5 copy-start.3
  169.9 2.6 %copy-start.5 = (bf16[1536,256]{1,0:T(8,128)(2,1)S(1)}, bf16[1536,256]{1,0:T(8,128)(2,1)}, u32[]{:S(2)}) copy-start(bf16[1536,256]{1,0:T(8,128)(2,1)} %refs_0_.1) | copy-start | bytes 2359300
  169.9 2.9 %copy-start.7 = (bf16[1536,256]{1,0:T(8,128)(2,1)S(1)}, bf16[1536,256]{1,0:T(8,128)(2,1)}, u32[]{:S(2)}) copy-start(bf16[1536,256]{1,0:T(8,128)(2,1)} %copy-done.6) | copy-start | bytes 2359300
  172.8 1.1 copy-start.9
  173.9 1.1 copy-start.11
  175.1 1.1 copy-start.13
  176.2 1.1 copy-start.15
  177.4 1.0 copy-start.16
  178.4 1.0 copy-start.17
  191.5 0.7 copy-start.37
  244.2 2.2 copy-start.1
Sparse Core Ops, SparseCore 0:
  9.1 58.0 all-gather.2

commit v4 on v3

--- a/solution.py
+++ b/solution.py
@@ -196,144 +196,89 @@
     )(starts, lengths, q, g, k, v, *keys, *values)
 
 
-def pack_kernel(offsets, own, twin, *refs):
-    received, outs, store = refs[:3], refs[3:7], refs[7]
-    window, head = own.shape[4:]
-    slots = own.shape[3]
+def pack_kernel(offsets, cache, *refs):
+    outs, store = refs[:4], refs[4]
+    sources, _, slots, window, head = cache.shape
     size = outs[0].shape[0]
     for k, out in enumerate(outs):
-        block = offsets[k]
-        for j in range(4 * 2 * slots):
-            p, side, rank = j // (2 * slots), j // slots % 2, j % slots
-            place = pl.multiple_of(offsets[6 + k * 4 * 2 * slots + j], UNIT)
-            if p > 0:
-                value = received[p - 1][side, block, rank]
-            elif side > 0:
-                value = twin[0, block, rank]
-            else:
-                value = own[0, block, 0, rank]
-            store[pl.ds(place, window), :] = value
+        for j in range(sources * slots):
+            place = pl.multiple_of(offsets[4 + k * sources * slots + j], UNIT)
+            store[pl.ds(place, window), :] = cache[j // slots, offsets[k], j % slots]
         out[...] = store[:size, :]
 
 
-def pack(offsets, cache, twin, received, size):
-    capacity, window, head = cache.shape[3:]
+def pack(offsets, cache, size):
+    window, head = cache.shape[3:]
     return pl.pallas_call(
         pack_kernel,
         out_shape=[jax.ShapeDtypeStruct((size, head), cache.dtype)] * 4,
         grid_spec=pltpu.PrefetchScalarGridSpec(
             num_scalar_prefetch=1,
             grid=(1,),
-            in_specs=[
-                pl.BlockSpec((1, 4, 1, capacity, window, head), lambda i, o: (o[4], 0, o[5], 0, 0, 0)),
-                pl.BlockSpec((1, 4, capacity, window, head), lambda i, o: (o[4], 0, 0, 0, 0)),
-            ]
-            + [pl.BlockSpec(a.shape, lambda i, _: (0,) * 5) for a in received],
+            in_specs=[pl.BlockSpec(cache.shape, lambda i, _: (0,) * 5)],
             out_specs=[pl.BlockSpec((size, head), lambda i, _: (0, 0))] * 4,
             scratch_shapes=[pltpu.VMEM((size + window, head), cache.dtype)],
         ),
         compiler_params=pltpu.CompilerParams(vmem_limit_bytes=30 << 20),
         cost_estimate=COST,
         name="pack",
-    )(offsets, cache, twin, *received)
-
-
-def copy_kernel(_, *refs):
-    for source, target in zip(refs, refs[len(refs) // 2 :]):
-        target[...] = source[...].reshape(target.shape)
-
-
-def for_twin(place, caches):
-    _, _, _, capacity, window, head = caches[0].shape
+    )(offsets, cache)
+
+
+def by_target_kernel(source, target):
+    for c in range(2):
+        target[0, c] = source[0, :, c]
+
+
+def by_target(cache):
+    ny, nz, nc, capacity, window, head = cache.shape
     return pl.pallas_call(
-        copy_kernel,
-        out_shape=[jax.ShapeDtypeStruct((4, 4, capacity, window, head), caches[0].dtype)] * 2,
-        grid_spec=pltpu.PrefetchScalarGridSpec(
-            num_scalar_prefetch=1,
-            grid=(4,),
-            in_specs=[
-                pl.BlockSpec((1, 4, 1, capacity, window, head), lambda i, o: (i, 0, 1 - o[1], 0, 0, 0))
-            ]
-            * 2,
-            out_specs=[pl.BlockSpec((1, 4, capacity, window, head), lambda i, _: (i, 0, 0, 0, 0))] * 2,
-        ),
+        by_target_kernel,
+        out_shape=jax.ShapeDtypeStruct((ny, nc, nz, capacity, window, head), cache.dtype),
+        grid=(ny,),
+        in_specs=[pl.BlockSpec((1, nz, nc, capacity, window, head), lambda i: (i, 0, 0, 0, 0, 0))],
+        out_specs=pl.BlockSpec((1, nc, nz, capacity, window, head), lambda i: (i, 0, 0, 0, 0, 0)),
         cost_estimate=COST,
-        name="for_twin",
-    )(place, *caches)
-
-
-def arrange_kernel(_, *refs):
-    for own, twin, out in zip(refs[:3], refs[3:6], refs[6:]):
-        out[0] = own[0, :, 0]
-        out[1] = twin[0]
-
-
-def arrange(place, cache, twin):
-    capacity, window, head = cache.shape[3:]
-    own = lambda k: pl.BlockSpec(
-        (1, 4, 1, capacity, window, head), lambda i, o: ((o[0] + k) % 4, 0, o[1], 0, 0, 0)
-    )
-    other = lambda k: pl.BlockSpec(
-        (1, 4, capacity, window, head), lambda i, o: ((o[0] + k) % 4, 0, 0, 0, 0)
-    )
-    shape = (2, 4, capacity, window, head)
-    return pl.pallas_call(
-        arrange_kernel,
-        out_shape=[jax.ShapeDtypeStruct(shape, cache.dtype)] * 3,
-        grid_spec=pltpu.PrefetchScalarGridSpec(
-            num_scalar_prefetch=1,
-            grid=(1,),
-            in_specs=[own(k) for k in (1, 3, 2)] + [other(k) for k in (1, 3, 2)],
-            out_specs=[pl.BlockSpec(shape, lambda i, _: (0,) * 5)] * 3,
-        ),
-        compiler_params=pltpu.CompilerParams(vmem_limit_bytes=20 << 20),
-        cost_estimate=COST,
-        name="arrange",
-    )(place, cache, cache, cache, twin, twin, twin)
-
-
-def output_kernel(place, heads, mine, other, out, joined):
-    count, depth = mine.shape[:2]
+        name="by_target",
+    )(cache)
+
+
+def output_kernel(heads, weight, out, joined):
+    width = heads.shape[2]
 
     @pl.when(pl.program_id(0) == 0)
     def _():
-        for j in range(count):
-            for h in range(2):
-                first = pl.multiple_of((place[1] + h) % 2 * depth, depth)
-                columns = slice((2 * j + h) * depth, (2 * j + h + 1) * depth)
-                joined[:, columns] = heads[j, :, pl.ds(first, depth)]
-
-    total = jnp.zeros(out.shape, jnp.float32)
-    for j in range(count):
-        weight = jnp.concatenate([mine[j], other[j]], axis=0)
-        part = joined[:, 2 * j * depth : 2 * (j + 1) * depth]
-        total = total + jnp.dot(part, weight, preferred_element_type=jnp.float32)
+        for j in range(heads.shape[0]):
+            joined[:, j * width : (j + 1) * width] = heads[j]
+
+    total = jnp.dot(joined[...], weight[...], preferred_element_type=jnp.float32)
     out[...] = total.astype(jnp.bfloat16)
 
 
-def project_out(place, heads, mine, other):
+def project_out(heads, weight):
     blocks, rows, width = heads.shape
-    depth, columns = mine.shape[1:]
+    depth, columns = weight.shape
     tile = 512
-    half = pl.BlockSpec((blocks, depth, tile), lambda i, _: (0, 0, i))
     return pl.pallas_call(
         output_kernel,
         out_shape=jax.ShapeDtypeStruct((rows, columns), jnp.bfloat16),
-        grid_spec=pltpu.PrefetchScalarGridSpec(
-            num_scalar_prefetch=1,
-            grid=(columns // tile,),
-            in_specs=[pl.BlockSpec(heads.shape, lambda i, _: (0, 0, 0)), half, half],
-            out_specs=pl.BlockSpec((rows, tile), lambda i, _: (0, i)),
-            scratch_shapes=[pltpu.VMEM((rows, blocks * width), jnp.bfloat16)],
-        ),
+        grid=(columns // tile,),
+        in_specs=[
+            pl.BlockSpec(heads.shape, lambda i: (0, 0, 0)),
+            pl.BlockSpec((depth, tile), lambda i: (0, i)),
+        ],
+        out_specs=pl.BlockSpec((rows, tile), lambda i: (0, i)),
+        scratch_shapes=[pltpu.VMEM((rows, depth), jnp.bfloat16)],
         compiler_params=pltpu.CompilerParams(vmem_limit_bytes=30 << 20),
         cost_estimate=COST,
         name="project_out",
-    )(place, heads, mine, other)
-
-
-def across_y(place, cache, twin):
-    return [shift(a, "y", k) for a, k in zip(arrange(place, cache, twin), (1, 3, 2))]
+    )(heads, weight)
+
+
+def across_y(cache):
+    _, nz, _, capacity, window, head = cache.shape
+    flat = by_target(cache).reshape(8, nz * capacity * window, head)
+    return lax.all_to_all(flat, ("y", "c"), 0, 0, tiled=True).reshape(8, nz, capacity, window, head)
 
 
 def across_z(parts):
@@ -379,9 +324,8 @@
     )
     fits = jnp.max(per_plane) * UNIT <= PACKED
 
-    seen_y, seen_c = jnp.array([0, 3, 1, 2]), jnp.array([0, 1])
-    slot_y = (y + seen_y[:, None, None]) % 4
-    slot_c = (core + seen_c[None, :, None]) % 2
+    slot_y = jnp.arange(4)[:, None, None]
+    slot_c = jnp.arange(2)[None, :, None]
     slot_rank = jnp.arange(capacity)[None, None, :]
     z_ids = (zh + jnp.arange(4)) % 4
     served = (y * 4 + z_ids) * 2 + core
@@ -391,72 +335,58 @@
     hit = served_key[:, :, None] == slot_key[None, None, :]
     slot_units = jnp.sum(jnp.where(hit, all_units[served][:, :, None], 0), axis=1)
     offsets = (jnp.cumsum(slot_units, axis=1) - slot_units) * UNIT
-    place = jnp.stack([y, core]).astype(jnp.int32)
 
     mine = lambda a: lax.dynamic_index_in_dim(a, group_id, 0, keepdims=False)
     my_holders, my_ranks, my_lengths, my_units = map(
         mine, (all_holders, all_ranks, all_lengths, all_units)
     )
-    from_y = (my_holders // 8 - y) % 4
-    from_y = jnp.where(from_y == 3, 1, jnp.where(from_y == 1, 2, jnp.where(from_y == 2, 3, 0)))
     from_z = (zh - my_holders // 2 % 4) % 4
-    from_c = (my_holders - core) % 2
-    my_order = (from_y * 2 + from_c) * capacity + my_ranks
+    my_order = (my_holders // 8 * 2 + my_holders % 2) * capacity + my_ranks
     ahead = (from_z[:, None] == from_z[None, :]) & (my_order[None, :] < my_order[:, None])
     my_start = jnp.sum(jnp.where(ahead, my_units[None, :], 0), axis=1) * UNIT
 
     def packing(size):
         limit = jnp.minimum(offsets, size).reshape(-1)
-        places = jnp.concatenate([z_ids, place, limit]).astype(jnp.int32)
+        places = jnp.concatenate([z_ids, limit]).astype(jnp.int32)
         starts = jnp.minimum(from_z * size + my_start, 4 * size)
         return places, starts.astype(jnp.int32)
 
     positions = my_lengths[:, None] + jnp.arange(span_len, dtype=jnp.int32)[None, :]
+    channel = jnp.arange(head_dim)
     half = head_dim // 2
-    frequency = ROPE_BASE ** (-jnp.arange(half, dtype=jnp.float32) * 2.0 / head_dim)
+    frequency = ROPE_BASE ** (-(channel % half).astype(jnp.float32) * 2.0 / head_dim)
     angles = positions.reshape(-1).astype(jnp.float32)[:, None] * frequency
-    cosine, sine = jnp.cos(angles), jnp.sin(angles)
-    cosine = jnp.concatenate([cosine, cosine], axis=-1)
-    sine = jnp.concatenate([-sine, sine], axis=-1)
+    cosine = jnp.cos(angles)
+    sine = jnp.sin(angles) * jnp.where(channel < half, -1.0, 1.0)
 
     ids = block_ids()
     sides = (4, 4, 2, capacity, window, head_dim)
-    caches = [key_cache.reshape(sides), value_cache.reshape(sides)]
-    twins = [shift(a, "c", 1) for a in for_twin(place, caches)]
     places, starts = packing(PACKED)
+    whole_weight = lax.all_gather(o_weight, TENSOR, axis=0, tiled=True)
     pieces = spread(span_rows)
-
-    key_parts = across_y(place, caches[0], twins[0])
-    value_parts = across_y(place, caches[1], twins[1])
-    keys = across_z(pack(places, caches[0], twins[0], key_parts, PACKED))
-    values = across_z(pack(places, caches[1], twins[1], value_parts, PACKED))
-
-    depth = o_weight.shape[0] // 2
-    half = lax.dynamic_slice_in_dim(o_weight, core * depth, depth, 0)
-    halves = lax.all_gather(half, TENSOR)
-    other_halves = shift(halves, "c", 1)
+    key_part, value_part = across_y(key_cache.reshape(sides)), across_y(value_cache.reshape(sides))
+    keys = across_z(pack(places, key_part, PACKED))
+    values = across_z(pack(places, value_part, PACKED))
 
     q, g, k, v = project(
         ids, pieces, norm_gain, q_weight, gate_weight, k_weight, v_weight,
         q_norm_gain, k_norm_gain, cosine, sine,
     )
 
-    def packed(keys, values, twins, key_parts, value_parts, q, g, k, v):
+    def packed(keys, values, key_part, value_part, q, g, k, v):
         return attend(starts, my_lengths, q, g, k, v, keys, values, window)
 
-    def full(keys, values, twins, key_parts, value_parts, q, g, k, v):
+    def full(keys, values, key_part, value_part, q, g, k, v):
         size = 8 * capacity * window
         places, starts = packing(size)
-        keys = across_z(pack(places, caches[0], twins[0], key_parts, size))
-        values = across_z(pack(places, caches[1], twins[1], value_parts, size))
+        keys, values = (across_z(pack(places, a, size)) for a in (key_part, value_part))
         return attend(starts, my_lengths, q, g, k, v, keys, values, window)
 
-    q, other_halves = lax.optimization_barrier((q, other_halves))
-    attended = lax.cond(fits, packed, full, keys, values, twins, key_parts, value_parts, q, g, k, v)
+    attended = lax.cond(fits, packed, full, keys, values, key_part, value_part, q, g, k, v)
     heads = lax.all_to_all(
         attended.reshape(blocks, rows // blocks, attended.shape[1]), TENSOR, 0, 0, tiled=True
     )
-    return project_out(place, heads, halves, other_halves)
+    return project_out(heads, whole_weight)
 
 
 def solution(mesh):

time: 260 us -> 238 us (0.915)
  blocking collectives: 42 us -> 15.9 us
  waiting for transfers between devices: 95.1 us -> 116 us
  local copies, waits for them, and re-layouts: 17.7 us -> 9.22 us
  other arithmetic: 9.14 us -> 4.92 us
  Pallas kernels: 43.2 us -> 39.8 us
    ppermute x22 -> x13, waiting for transfers between devices: 36.5 us -> 99.4 us  [shift(): return lax.ppermute(value, axis, ring(lax.axis_size(axis), step))]
    all_gather x1, waiting for transfers between devices: 58.6 us -> 0.01 us  [local(): whole_weight = lax.all_gather(o_weight, TENSOR, axis=0, tiled=True)]
    all_to_all x1, blocking collectives: 42 us -> 15.9 us  [local(): lax.all_to_all(attended.reshape(blocks, rows // blocks, attended.shape[1]...]
    all_to_all x0 -> x2, waiting for transfers between devices: none -> 15.9 us  [across_y(): lax.all_to_all(flat, ('y', 'c'), 0, 0, tiled=True)]
    ppermute x22 -> x13, starting transfers between devices: 37.7 us -> 24.6 us  [shift(): return lax.ppermute(value, axis, ring(lax.axis_size(axis), step))]
    all_to_all x0 -> x2, starting transfers between devices: none -> 12.2 us  [across_y(): lax.all_to_all(flat, ('y', 'c'), 0, 0, tiled=True)]
    unnamed x66 -> x26, local copies, waits for them, and re-layouts: 13.9 us -> 6.94 us
    neg x1 -> x0, other arithmetic: 4.48 us -> none  [local(): sine = jnp.concatenate([-sine, sine], axis=-1)]
  transfers between devices with their start and end apart: 23 -> 16, of which waited for: 10 -> 9; matrix products, arithmetic and copies ran while one was open for 4% -> 3% of each run, Pallas kernels for 10% -> 15%
where the time goes in v4:
time: 238 us; the launch traced here: 237 us
  waiting for transfers between devices  116 us (49%)
  Pallas kernels  39.8 us (17%)
  starting transfers between devices  36.8 us (15%)
  blocking collectives  15.9 us (7%)
  between operations  14.3 us (6%)
  local copies, waits for them, and re-layouts  9.22 us (4%)
  other arithmetic  4.92 us (2%)
    ppermute x13, waiting for transfers between devices, shift(): return lax.ppermute(value, axis, ring(lax.axis_size(axis), step))  99.4 us
    ppermute x13, starting transfers between devices, shift(): return lax.ppermute(value, axis, ring(lax.axis_size(axis), step))  24.6 us
    all_to_all x1, blocking collectives, local(): lax.all_to_all(attended.reshape(blocks, rows // blocks, attended.shape[1]...  15.9 us
    all_to_all x2, waiting for transfers between devices, across_y(): lax.all_to_all(flat, ('y', 'c'), 0, 0, tiled=True)  15.9 us
    pallas_call x1, Pallas kernels, project(): pl.pallas_call(project_kernel, out_shape=(jax.ShapeDtypeStruct((rows, wq....  12.3 us
    all_to_all x2, starting transfers between devices, across_y(): lax.all_to_all(flat, ('y', 'c'), 0, 0, tiled=True)  12.2 us
    pallas_call x1, Pallas kernels, attend(): pl.pallas_call(attend_kernel, out_shape=jax.ShapeDtypeStruct((rows, colum...  9.47 us
    pallas_call x2, Pallas kernels, by_target(): pl.pallas_call(by_target_kernel, out_shape=jax.ShapeDtypeStruct((ny, nc,...  7.73 us
  transfers between devices with their start and end apart: 16, of which 9 were waited for; matrix products, arithmetic and copies ran while one was open for 3% of the time, Pallas kernels for 15%

profile of v4, /device:TPU:8, one launch (start us, length us, event | category | flops | bytes accessed | tf_op | source)
XLA Modules:
  0.0 236.9 jit_solution(2208428137268770763)
XLA Ops:
  6.5 0.7 all-gather.2.cloned.1.call-update
  7.3 3.8 %by_target.2 = bf16[4,2,4,2,128,128]{5,4,3,2,1,0:T(8,128)(2,1)} custom-call(bf16[4,4,2,2,128,128]{5,4,3,2,1,0:T(8,128)(2,1)} %bitcast.29), custom_call_target="tpu_custom_call" | custom-call | flops 1048576 | bytes 1048576 | tf_op jit(solution)/shard_map/by_target/pallas_call | solution.py:235
  11.1 6.6 %all-to-all-start = ((bf16[8,1024,128]{2,1,0:T(8,128)(2,1)}), bf16[8,1024,128]{2,1,0:T(8,128)(2,1)}, u32[]{:S(2)}, u32[]{:S(2)}) async-start(bf16[8,1024,128]{2,1,0:T(8,128)(2,1)} %bitcast.26), calls=%async_computation | async-start | bytes 4194304 | tf_op jit(solution)/shard_map/all_to_all | solution.py:281
  17.6 0.4 collective-permute-start.6
  18.1 1.5 collective-permute-start.7
  19.6 1.7 collective-permute-start.8
  21.3 0.1 reshape.363
  21.4 0.1 add_convert_fusion
  21.5 0.1 convert_element_type.26
  21.6 0.4 copy.28.refs_8_
  22.0 0.1 reshape.362
  22.0 0.1 copy.24
  22.1 0.2 convert_reduce_fusion
  22.3 0.1 copy.27
  22.4 0.1 copy.23
  22.5 0.6 gather_fusion.1
  23.1 0.6 gather_fusion
  23.6 3.9 %by_target.3 = bf16[4,2,4,2,128,128]{5,4,3,2,1,0:T(8,128)(2,1)} custom-call(bf16[4,4,2,2,128,128]{5,4,3,2,1,0:T(8,128)(2,1)} %bitcast.30), custom_call_target="tpu_custom_call" | custom-call | flops 1048576 | bytes 1048576 | tf_op jit(solution)/shard_map/by_target/pallas_call | solution.py:235
  27.6 0.1 add_multiply_fusion
  27.6 15.9 %all-to-all-done = bf16[8,1024,128]{2,1,0:T(8,128)(2,1)} async-done(((bf16[8,1024,128]{2,1,0:T(8,128)(2,1)}), bf16[8,1024,128]{2,1,0:T(8,128)(2,1)}, u32[]{:S(2)}, u32[]{:S(2)}) %all-to-all-start) | async-done | bytes 2097184 | tf_op jit(solution)/shard_map/all_to_all | solution.py:281
  43.5 5.7 %all-to-all-start.1 = ((bf16[8,1024,128]{2,1,0:T(8,128)(2,1)}), bf16[8,1024,128]{2,1,0:T(8,128)(2,1)}, u32[]{:S(2)}, u32[]{:S(2)}) async-start(bf16[8,1024,128]{2,1,0:T(8,128)(2,1)} %bitcast.27), calls=%async_computation.1 | async-start | bytes 4194304 | tf_op jit(solution)/shard_map/all_to_all | solution.py:281
  49.2 0.1 iota_add_fusion
  49.3 0.1 add.369
  49.4 0.7 collective-permute-done.6.refs_1_
  50.1 0.6 collective-permute-start.10
  50.7 0.2 select_reduce_fusion.1
  50.9 0.2 reduce_window_sum.11
  51.1 0.1 min.22
  51.2 0.1 copy.22
  51.3 0.6 reduce_max.9
  52.6 0.1 stack.35.ids
  52.7 0.3 fusion.9
  52.9 0.1 pad_add_fusion.1.offsets
  53.0 1.5 collective-permute-start.9
  54.5 18.3 %collective-permute-done.7.refs_2_ = bf16[1536,256]{1,0:T(8,128)(2,1)} collective-permute-done((bf16[1536,256]{1,0:T(8,128)(2,1)S(1)}, bf16[1536,256]{1,0:T(8,128)(2,1)}, u32[]{:S(2)}, u32[]{:S(2)}) %collective-permute-start.7) | collective-permute-done | bytes 786464 | tf_op jit(solution)/shard_map/ppermute | solution.py:28
  72.8 49.5 %collective-permute-done.10.refs_5_ = bf16[1536,256]{1,0:T(8,128)(2,1)} collective-permute-done((bf16[1536,256]{1,0:T(8,128)(2,1)}, bf16[1536,256]{1,0:T(8,128)(2,1)}, u32[]{:S(2)}, u32[]{:S(2)}) %collective-permute-start.10) | collective-permute-done | bytes 786464 | tf_op jit(solution)/shard_map/ppermute | solution.py:28
  122.3 3.7 %collective-permute-start.12 = (bf16[1536,256]{1,0:T(8,128)(2,1)}, bf16[1536,256]{1,0:T(8,128)(2,1)}, u32[]{:S(2)}, u32[]{:S(2)}) collective-permute-start(bf16[1536,256]{1,0:T(8,128)(2,1)} %collective-permute-done.10.refs_5_), channel_id=1, source_target_pairs={{0,3},{1,0},{2,1},{3,2},{4,7},{5,4},{6,5},{7,6},{8,11},{9,8},{10,9... | collective-permute-start | bytes 2359304 | tf_op jit(solution)/shard_map/ppermute | solution.py:28
  125.9 2.8 %fusion = (f32[1536,128]{1,0:T(8,128)S(1)}, f32[1536,128]{1,0:T(8,128)S(1)}) fusion(f32[128]{0:T(128)S(1)} %get-tuple-element.142, f32[128]{0:T(128)S(1)} %get-tuple-element.143, f32[1536]{0:T(1024)S(1)} %convert_element_type.26), kind=kLoop, calls=%fused_computation.8 | loop fusion | flops 393216 | bytes 1580032 | tf_op jit(solution)/shard_map/mul | solution.py:360
  128.7 0.0 copy-start.6
  128.7 0.0 copy-start.7
  128.8 3.2 %pack.6 = (bf16[1152,128]{1,0:T(8,128)(2,1)}, bf16[1152,128]{1,0:T(8,128)(2,1)}, bf16[1152,128]{1,0:T(8,128)(2,1)S(1)}, bf16[1152,128]{1,0:T(8,128)(2,1)S(1)}) custom-call(s32[68]{0:T(128)S(1)} %pad_add_fusion.1.offsets, bf16[8,4,2,128,128]{4,3,2,1,0:T(8,128)(2,1)} %bitcast.4.cache), custom_call_target="tpu_custom_call" | custom-call | flops 1048576 | bytes 1048576 | tf_op jit(solution)/shard_map/pack/pallas_call | solution.py:212
  131.9 0.7 copy-done.8
  132.6 0.7 copy-done.9
  133.3 3.3 %collective-permute-start.13 = (bf16[1152,128]{1,0:T(8,128)(2,1)}, bf16[1152,128]{1,0:T(8,128)(2,1)}, u32[]{:S(2)}, u32[]{:S(2)}) collective-permute-start(bf16[1152,128]{1,0:T(8,128)(2,1)} %get-tuple-element.125), channel_id=1, source_target_pairs={{0,16},{16,32},{32,48},{48,0},{1,17},{17,33},{33,49},{49,1},{2,18}... | collective-permute-start | bytes 884744 | tf_op jit(solution)/shard_map/ppermute | solution.py:28
  136.7 3.3 %pack.7 = (bf16[1152,128]{1,0:T(8,128)(2,1)}, bf16[1152,128]{1,0:T(8,128)(2,1)S(1)}, bf16[1152,128]{1,0:T(8,128)(2,1)S(1)}, bf16[1152,128]{1,0:T(8,128)(2,1)S(1)}) custom-call(s32[68]{0:T(128)S(1)} %pad_add_fusion.1.offsets, bf16[8,4,2,128,128]{4,3,2,1,0:T(8,128)(2,1)} %bitcast.7.cache), custom_call_target="tpu_custom_call" | custom-call | flops 1048576 | bytes 1048576 | tf_op jit(solution)/shard_map/pack/pallas_call | solution.py:212
  140.0 4.5 %collective-permute-start.14 = (bf16[1152,128]{1,0:T(8,128)(2,1)}, bf16[1152,128]{1,0:T(8,128)(2,1)S(1)}, u32[]{:S(2)}, u32[]{:S(2)}) collective-permute-start(bf16[1152,128]{1,0:T(8,128)(2,1)} %copy-done.9), channel_id=1, source_target_pairs={{0,32},{16,48},{32,0},{48,16},{1,33},{17,49},{33,1},{49,17},{2,34}... | collective-permute-start | bytes 884744 | tf_op jit(solution)/shard_map/ppermute | solution.py:28
  144.4 2.7 %collective-permute-start.15 = (bf16[1152,128]{1,0:T(8,128)(2,1)}, bf16[1152,128]{1,0:T(8,128)(2,1)S(1)}, u32[]{:S(2)}, u32[]{:S(2)}) collective-permute-start(bf16[1152,128]{1,0:T(8,128)(2,1)} %copy-done.8), channel_id=1, source_target_pairs={{0,48},{16,0},{32,16},{48,32},{1,49},{17,1},{33,17},{49,33},{2,50}... | collective-permute-start | bytes 884744 | tf_op jit(solution)/shard_map/ppermute | solution.py:28
  147.2 3.8 %collective-permute-done.11.refs_6_ = bf16[1536,256]{1,0:T(8,128)(2,1)} collective-permute-done((bf16[1536,256]{1,0:T(8,128)(2,1)}, bf16[1536,256]{1,0:T(8,128)(2,1)}, u32[]{:S(2)}, u32[]{:S(2)}) %collective-permute-start.11) | collective-permute-done | bytes 786464 | tf_op jit(solution)/shard_map/ppermute | solution.py:28
  151.0 1.2 collective-permute-start.16
  152.1 13.0 %collective-permute-done.13 = bf16[1152,128]{1,0:T(8,128)(2,1)} collective-permute-done((bf16[1152,128]{1,0:T(8,128)(2,1)}, bf16[1152,128]{1,0:T(8,128)(2,1)}, u32[]{:S(2)}, u32[]{:S(2)}) %collective-permute-start.13) | collective-permute-done | bytes 294944 | tf_op jit(solution)/shard_map/ppermute | solution.py:28
  165.1 3.0 %collective-permute-start.17 = (bf16[1152,128]{1,0:T(8,128)(2,1)S(1)}, bf16[1152,128]{1,0:T(8,128)(2,1)S(1)}, u32[]{:S(2)}, u32[]{:S(2)}) collective-permute-start(bf16[1152,128]{1,0:T(8,128)(2,1)S(1)} %get-tuple-element.130), channel_id=1, source_target_pairs={{0,32},{16,48},{32,0},{48,16},{1,33},{17,49},{33,1},{49,17},{2,34}... | collective-permute-start | bytes 884744 | tf_op jit(solution)/shard_map/ppermute | solution.py:28
  168.2 0.5 collective-permute-start.18
  168.7 0.2 select_reduce_fusion.2
  168.9 1.0 copy-done.4
  170.0 1.0 copy-done.5
  171.0 12.3 %project.1 = (bf16[1536,256]{1,0:T(8,128)(2,1)}, f32[1536,256]{1,0:T(8,128)}, bf16[1536,128]{1,0:T(8,128)(2,1)}, bf16[1536,128]{1,0:T(8,128)(2,1)}) custom-call(s32[8]{0:T(128)S(1)} %stack.35.ids, bf16[1536,256]{1,0:T(8,128)(2,1)S(1)} %copy-done.3, bf16[1536,256]{1,0:T(8,128)(2,1)} %collective-permute-done.6.refs_1_, ...), custom_call_target="tpu_custom_call" | custom-call | flops 1048576 | bytes 1048576 | tf_op jit(solution)/shard_map/project/pallas_call | solution.py:104
  183.4 0.5 collective-permute-done.16
  183.8 13.3 %collective-permute-done.17 = bf16[1152,128]{1,0:T(8,128)(2,1)S(1)} collective-permute-done((bf16[1152,128]{1,0:T(8,128)(2,1)S(1)}, bf16[1152,128]{1,0:T(8,128)(2,1)S(1)}, u32[]{:S(2)}, u32[]{:S(2)}) %collective-permute-start.17) | collective-permute-done | bytes 294944 | tf_op jit(solution)/shard_map/ppermute | solution.py:28
  197.2 0.3 collective-permute-done.18
  197.5 9.5 %conditional.1 = (bf16[1536,256]{1,0:T(8,128)(2,1)S(1)}) conditional(s32[]{:T(128)} %convert_element_type.23, (s32[24]{0:T(128)S(1)}, s32[24]{0:T(128)S(1)}, s32[4,16]{1,0:T(4,128)S(1)}, s32[4,16]{1,0:T(4,128)S(1)}, s32[4]{0:T(128)S(1)}, /*index=5*/bf16[8,4,2,128,128]{4,3,2,1,0:T(8,128)(2,1)}, bf16[8,4,2,128,128]{4,3,2,1,0:T(8,128)(2,1)}, ...), branch_computations={%region_6.7_spmd, %region_7.8_spmd} | conditional | flops 3146060 | bytes 28314024 | solution.py:385
  197.5 9.5 %attend.3 = bf16[1536,256]{1,0:T(8,128)(2,1)S(1)} custom-call(s32[24]{0:T(128)S(1)} %add_minimum_fusion.1.starts, s32[24]{0:T(128)S(1)} %get-tuple-element.95.lengths, bf16[1536,256]{1,0:T(8,128)(2,1)} %get-tuple-element.96.q, f32[1536,256]{1,0:T(8,128)} %get-tuple-element.97.g, bf16[1536,128]{1,0:T(8,128)(2,1)} %get-tuple-element.98.k, ...), custom_call_target="tpu_custom_call" | custom-call | flops 1048576 | bytes 1048576 | tf_op jit(solution)/shard_map/cond/branch_1_fun/attend/pallas_call | solution.py:183
  206.9 15.9 %all_to_all.15.heads = bf16[8,192,256]{2,1,0:T(8,128)(2,1)S(1)} all-to-all(bf16[8,192,256]{2,1,0:T(8,128)(2,1)S(1)} %bitcast.28), channel_id=1, replica_groups=mesh['y'=4,'zh'=4,'c'=2,'zl'=2,'x'=4] {'zl','x'}, dimensions={0} | all-to-all | bytes 1572864 | tf_op jit(solution)/shard_map/all_to_all | solution.py:386
  222.8 3.4 %copy-done = bf16[2048,2048]{1,0:T(8,128)(2,1)S(1)} copy-done((bf16[2048,2048]{1,0:T(8,128)(2,1)S(1)}, bf16[2048,2048]{1,0:T(8,128)(2,1)}, u32[]{:S(2)}) %copy-start) | copy-done | bytes 8388632
  226.2 3.8 %project_out.1 = bf16[192,2048]{1,0:T(8,128)(2,1)} custom-call(bf16[8,192,256]{2,1,0:T(8,128)(2,1)S(1)} %all_to_all.15.heads, bf16[2048,2048]{1,0:T(8,128)(2,1)S(1)} %copy-done), custom_call_target="tpu_custom_call" | custom-call | flops 1048576 | bytes 1048576 | tf_op jit(solution)/shard_map/project_out/pallas_call | solution.py:262
  (44 shorter events, 0.3 us)
Async XLA Ops:
  6.5 216.3 %all-gather.2.cloned.1.call-start = ((), (), s32[]{:S(2)}) async-start(), calls=%async_computation.3 | async-start | bytes 9437184 | tf_op jit(solution)/shard_map/all_gather | solution.py:365
  11.1 6.6 %copy-start.3 = (bf16[1536,256]{1,0:T(8,128)(2,1)S(1)}, bf16[1536,256]{1,0:T(8,128)(2,1)}, u32[]{:S(2)}) copy-start(bf16[1536,256]{1,0:T(8,128)(2,1)} %refs_0_.1) | copy-start | bytes 2359300
  11.1 10.2 %copy-start.15 = (s32[768]{0:T(1024)S(1)}, s32[768]{0:T(1024)}, u32[]{:S(2)}) copy-start(s32[768]{0:T(1024)} %param.27) | copy-start | bytes 9220
  11.1 10.5 %copy-start.14 = (f32[2048]{0:T(1024)S(1)}, f32[2048]{0:T(1024)}, u32[]{:S(2)}) copy-start(f32[2048]{0:T(1024)} %param.16) | copy-start | bytes 24580
  11.1 10.9 %copy-start.16 = (s32[768,1]{0,1:T(1,128)S(1)}, s32[768,1]{0,1:T(1,128)}, u32[]{:S(2)}) copy-start(s32[768,1]{0,1:T(1,128)} %param.26) | copy-start | bytes 9220
  11.1 32.4 %all-to-all-start = ((bf16[8,1024,128]{2,1,0:T(8,128)(2,1)}), bf16[8,1024,128]{2,1,0:T(8,128)(2,1)}, u32[]{:S(2)}, u32[]{:S(2)}) async-start(bf16[8,1024,128]{2,1,0:T(8,128)(2,1)} %bitcast.26), calls=%async_computation | async-start | bytes 4194304 | tf_op jit(solution)/shard_map/all_to_all | solution.py:281
  17.6 32.4 %collective-permute-start.6 = (bf16[1536,256]{1,0:T(8,128)(2,1)S(1)}, bf16[1536,256]{1,0:T(8,128)(2,1)}, u32[]{:S(2)}, u32[]{:S(2)}) collective-permute-start(bf16[1536,256]{1,0:T(8,128)(2,1)S(1)} %copy-done.3), channel_id=1, source_target_pairs={{0,4},{4,0},{1,5},{5,1},{2,6},{6,2},{3,7},{7,3},{8,12},{12,8},{9,1... | collective-permute-start | bytes 2359304 | tf_op jit(solution)/shard_map/ppermute | solution.py:28
  18.1 54.7 %collective-permute-start.7 = (bf16[1536,256]{1,0:T(8,128)(2,1)S(1)}, bf16[1536,256]{1,0:T(8,128)(2,1)}, u32[]{:S(2)}, u32[]{:S(2)}) collective-permute-start(bf16[1536,256]{1,0:T(8,128)(2,1)S(1)} %copy-done.3), channel_id=1, source_target_pairs={{0,1},{1,2},{2,3},{3,0},{4,5},{5,6},{6,7},{7,4},{8,9},{9,10},{10,1... | collective-permute-start | bytes 2359304 | tf_op jit(solution)/shard_map/ppermute | solution.py:28
  19.6 120.4 %collective-permute-start.8 = (bf16[1536,256]{1,0:T(8,128)(2,1)S(1)}, bf16[1536,256]{1,0:T(8,128)(2,1)}, u32[]{:S(2)}, u32[]{:S(2)}) collective-permute-start(bf16[1536,256]{1,0:T(8,128)(2,1)S(1)} %copy-done.3), channel_id=1, source_target_pairs={{0,3},{1,0},{2,1},{3,2},{4,7},{5,4},{6,5},{7,6},{8,11},{9,8},{10,9... | collective-permute-start | bytes 2359304 | tf_op jit(solution)/shard_map/ppermute | solution.py:28
  43.5 93.1 %all-to-all-start.1 = ((bf16[8,1024,128]{2,1,0:T(8,128)(2,1)}), bf16[8,1024,128]{2,1,0:T(8,128)(2,1)}, u32[]{:S(2)}, u32[]{:S(2)}) async-start(bf16[8,1024,128]{2,1,0:T(8,128)(2,1)} %bitcast.27), calls=%async_computation.1 | async-start | bytes 4194304 | tf_op jit(solution)/shard_map/all_to_all | solution.py:281
  50.1 72.2 %collective-permute-start.10 = (bf16[1536,256]{1,0:T(8,128)(2,1)}, bf16[1536,256]{1,0:T(8,128)(2,1)}, u32[]{:S(2)}, u32[]{:S(2)}) collective-permute-start(bf16[1536,256]{1,0:T(8,128)(2,1)} %collective-permute-done.6.refs_1_), channel_id=1, source_target_pairs={{0,3},{1,0},{2,1},{3,2},{4,7},{5,4},{6,5},{7,6},{8,11},{9,8},{10,9... | collective-permute-start | bytes 2359304 | tf_op jit(solution)/shard_map/ppermute | solution.py:28
  53.0 91.4 %collective-permute-start.9 = (bf16[1536,256]{1,0:T(8,128)(2,1)}, bf16[1536,256]{1,0:T(8,128)(2,1)}, u32[]{:S(2)}, u32[]{:S(2)}) collective-permute-start(bf16[1536,256]{1,0:T(8,128)(2,1)} %collective-permute-done.6.refs_1_), channel_id=1, source_target_pairs={{0,1},{1,2},{2,3},{3,0},{4,5},{5,6},{6,7},{7,4},{8,9},{9,10},{10,1... | collective-permute-start | bytes 2359304 | tf_op jit(solution)/shard_map/ppermute | solution.py:28
  72.8 78.2 %collective-permute-start.11 = (bf16[1536,256]{1,0:T(8,128)(2,1)}, bf16[1536,256]{1,0:T(8,128)(2,1)}, u32[]{:S(2)}, u32[]{:S(2)}) collective-permute-start(bf16[1536,256]{1,0:T(8,128)(2,1)} %collective-permute-done.7.refs_2_), channel_id=1, source_target_pairs={{0,1},{1,2},{2,3},{3,0},{4,5},{5,6},{6,7},{7,4},{8,9},{9,10},{10,1... | collective-permute-start | bytes 2359304 | tf_op jit(solution)/shard_map/ppermute | solution.py:28
  122.3 45.9 %collective-permute-start.12 = (bf16[1536,256]{1,0:T(8,128)(2,1)}, bf16[1536,256]{1,0:T(8,128)(2,1)}, u32[]{:S(2)}, u32[]{:S(2)}) collective-permute-start(bf16[1536,256]{1,0:T(8,128)(2,1)} %collective-permute-done.10.refs_5_), channel_id=1, source_target_pairs={{0,3},{1,0},{2,1},{3,2},{4,7},{5,4},{6,5},{7,6},{8,11},{9,8},{10,9... | collective-permute-start | bytes 2359304 | tf_op jit(solution)/shard_map/ppermute | solution.py:28
  128.7 40.2 %copy-start.6 = (f32[128]{0:T(128)S(1)}, f32[128]{0:T(128)}, u32[]{:S(2)}) copy-start(f32[128]{0:T(128)} %param.21) | copy-start | bytes 1540
  128.7 40.2 %copy-start.7 = (f32[128]{0:T(128)S(1)}, f32[128]{0:T(128)}, u32[]{:S(2)}) copy-start(f32[128]{0:T(128)} %param.22) | copy-start | bytes 1540
  131.9 0.7 copy-start.8
  132.6 0.7 copy-start.9
  133.3 31.8 %collective-permute-start.13 = (bf16[1152,128]{1,0:T(8,128)(2,1)}, bf16[1152,128]{1,0:T(8,128)(2,1)}, u32[]{:S(2)}, u32[]{:S(2)}) collective-permute-start(bf16[1152,128]{1,0:T(8,128)(2,1)} %get-tuple-element.125), channel_id=1, source_target_pairs={{0,16},{16,32},{32,48},{48,0},{1,17},{17,33},{33,49},{49,1},{2,18}... | collective-permute-start | bytes 884744 | tf_op jit(solution)/shard_map/ppermute | solution.py:28
  136.7 32.3 %copy-start.1 = (bf16[2048,256]{1,0:T(8,128)(2,1)S(1)}, bf16[2048,256]{1,0:T(8,128)(2,1)}, u32[]{:S(2)}) copy-start(bf16[2048,256]{1,0:T(8,128)(2,1)} %refs_9_.1) | copy-start | bytes 3145732
  136.7 32.3 %copy-start.2 = (bf16[2048,256]{1,0:T(8,128)(2,1)S(1)}, bf16[2048,256]{1,0:T(8,128)(2,1)}, u32[]{:S(2)}) copy-start(bf16[2048,256]{1,0:T(8,128)(2,1)} %refs_10_.1) | copy-start | bytes 3145732
  140.0 43.4 %collective-permute-start.14 = (bf16[1152,128]{1,0:T(8,128)(2,1)}, bf16[1152,128]{1,0:T(8,128)(2,1)S(1)}, u32[]{:S(2)}, u32[]{:S(2)}) collective-permute-start(bf16[1152,128]{1,0:T(8,128)(2,1)} %copy-done.9), channel_id=1, source_target_pairs={{0,32},{16,48},{32,0},{48,16},{1,33},{17,49},{33,1},{49,17},{2,34}... | collective-permute-start | bytes 884744 | tf_op jit(solution)/shard_map/ppermute | solution.py:28
  144.4 39.0 %collective-permute-start.15 = (bf16[1152,128]{1,0:T(8,128)(2,1)}, bf16[1152,128]{1,0:T(8,128)(2,1)S(1)}, u32[]{:S(2)}, u32[]{:S(2)}) collective-permute-start(bf16[1152,128]{1,0:T(8,128)(2,1)} %copy-done.8), channel_id=1, source_target_pairs={{0,48},{16,0},{32,16},{48,32},{1,49},{17,1},{33,17},{49,33},{2,50}... | collective-permute-start | bytes 884744 | tf_op jit(solution)/shard_map/ppermute | solution.py:28
  151.0 32.9 %collective-permute-start.16 = (bf16[1152,128]{1,0:T(8,128)(2,1)S(1)}, bf16[1152,128]{1,0:T(8,128)(2,1)S(1)}, u32[]{:S(2)}, u32[]{:S(2)}) collective-permute-start(bf16[1152,128]{1,0:T(8,128)(2,1)S(1)} %get-tuple-element.129), channel_id=1, source_target_pairs={{0,16},{16,32},{32,48},{48,0},{1,17},{17,33},{33,49},{49,1},{2,18}... | collective-permute-start | bytes 884744 | tf_op jit(solution)/shard_map/ppermute | solution.py:28
  165.1 32.0 %collective-permute-start.17 = (bf16[1152,128]{1,0:T(8,128)(2,1)S(1)}, bf16[1152,128]{1,0:T(8,128)(2,1)S(1)}, u32[]{:S(2)}, u32[]{:S(2)}) collective-permute-start(bf16[1152,128]{1,0:T(8,128)(2,1)S(1)} %get-tuple-element.130), channel_id=1, source_target_pairs={{0,32},{16,48},{32,0},{48,16},{1,33},{17,49},{33,1},{49,17},{2,34}... | collective-permute-start | bytes 884744 | tf_op jit(solution)/shard_map/ppermute | solution.py:28
  168.2 29.3 %collective-permute-start.18 = (bf16[1152,128]{1,0:T(8,128)(2,1)S(1)}, bf16[1152,128]{1,0:T(8,128)(2,1)S(1)}, u32[]{:S(2)}, u32[]{:S(2)}) collective-permute-start(bf16[1152,128]{1,0:T(8,128)(2,1)S(1)} %get-tuple-element.131), channel_id=1, source_target_pairs={{0,48},{16,0},{32,16},{48,32},{1,49},{17,1},{33,17},{49,33},{2,50}... | collective-permute-start | bytes 884744 | tf_op jit(solution)/shard_map/ppermute | solution.py:28
  168.9 1.0 copy-start.4
  170.0 1.0 copy-start.5
  222.8 3.4 %copy-start = (bf16[2048,2048]{1,0:T(8,128)(2,1)S(1)}, bf16[2048,2048]{1,0:T(8,128)(2,1)}, u32[]{:S(2)}) copy-start(bf16[2048,2048]{1,0:T(8,128)(2,1)} %all-gather.2.cloned.1.call-done.weight) | copy-start | bytes 25165828
Sparse Core Ops, SparseCore 0:
  9.1 151.7 all-gather.1

commit v5 on v4

--- a/solution.py
+++ b/solution.py
@@ -243,42 +243,51 @@
     )(cache)
 
 
-def output_kernel(heads, weight, out, joined):
-    width = heads.shape[2]
+def output_kernel(place, heads, mine, other, out, joined):
+    count, depth = mine.shape[:2]
 
     @pl.when(pl.program_id(0) == 0)
     def _():
-        for j in range(heads.shape[0]):
-            joined[:, j * width : (j + 1) * width] = heads[j]
-
-    total = jnp.dot(joined[...], weight[...], preferred_element_type=jnp.float32)
+        for j in range(count):
+            for h in range(2):
+                first = pl.multiple_of((place[1] + h) % 2 * depth, depth)
+                columns = slice((2 * j + h) * depth, (2 * j + h + 1) * depth)
+                joined[:, columns] = heads[j, :, pl.ds(first, depth)]
+
+    total = jnp.zeros(out.shape, jnp.float32)
+    for j in range(count):
+        weight = jnp.concatenate([mine[j], other[j]], axis=0)
+        part = joined[:, 2 * j * depth : 2 * (j + 1) * depth]
+        total = total + jnp.dot(part, weight, preferred_element_type=jnp.float32)
     out[...] = total.astype(jnp.bfloat16)
 
 
-def project_out(heads, weight):
+def project_out(place, heads, mine, other):
     blocks, rows, width = heads.shape
-    depth, columns = weight.shape
+    depth, columns = mine.shape[1:]
     tile = 512
+    half = pl.BlockSpec((blocks, depth, tile), lambda i, _: (0, 0, i))
     return pl.pallas_call(
         output_kernel,
         out_shape=jax.ShapeDtypeStruct((rows, columns), jnp.bfloat16),
-        grid=(columns // tile,),
-        in_specs=[
-            pl.BlockSpec(heads.shape, lambda i: (0, 0, 0)),
-            pl.BlockSpec((depth, tile), lambda i: (0, i)),
-        ],
-        out_specs=pl.BlockSpec((rows, tile), lambda i: (0, i)),
-        scratch_shapes=[pltpu.VMEM((rows, depth), jnp.bfloat16)],
+        grid_spec=pltpu.PrefetchScalarGridSpec(
+            num_scalar_prefetch=1,
+            grid=(columns // tile,),
+            in_specs=[pl.BlockSpec(heads.shape, lambda i, _: (0, 0, 0)), half, half],
+            out_specs=pl.BlockSpec((rows, tile), lambda i, _: (0, i)),
+            scratch_shapes=[pltpu.VMEM((rows, blocks * width), jnp.bfloat16)],
+        ),
         compiler_params=pltpu.CompilerParams(vmem_limit_bytes=30 << 20),
         cost_estimate=COST,
         name="project_out",
-    )(heads, weight)
-
-
-def across_y(cache):
-    _, nz, _, capacity, window, head = cache.shape
-    flat = by_target(cache).reshape(8, nz * capacity * window, head)
-    return lax.all_to_all(flat, ("y", "c"), 0, 0, tiled=True).reshape(8, nz, capacity, window, head)
+    )(place, heads, mine, other)
+
+
+def across_y(slots):
+    ny, nc, nz, capacity, window, head = slots.shape
+    flat = slots.reshape(ny * nc, nz * capacity * window, head)
+    flat = lax.all_to_all(flat, ("y", "c"), 0, 0, tiled=True)
+    return flat.reshape(ny * nc, nz, capacity, window, head)
 
 
 def across_z(parts):
@@ -362,10 +371,23 @@
     ids = block_ids()
     sides = (4, 4, 2, capacity, window, head_dim)
     places, starts = packing(PACKED)
-    whole_weight = lax.all_gather(o_weight, TENSOR, axis=0, tiled=True)
     pieces = spread(span_rows)
-    key_part, value_part = across_y(key_cache.reshape(sides)), across_y(value_cache.reshape(sides))
+    key_part = across_y(by_target(key_cache.reshape(sides)))
+    value_slots, key_part, pieces[1:4] = lax.optimization_barrier(
+        (by_target(value_cache.reshape(sides)), key_part, pieces[1:4])
+    )
+    value_part = across_y(value_slots)
     keys = across_z(pack(places, key_part, PACKED))
+
+    depth = o_weight.shape[0] // 2
+    half = lax.dynamic_slice_in_dim(o_weight, core * depth, depth, 0)
+    half, value_part, keys, pieces[4:] = lax.optimization_barrier(
+        (half, value_part, keys, pieces[4:])
+    )
+    copies = jnp.broadcast_to(half, (blocks,) + half.shape)
+    halves = lax.all_to_all(copies, TENSOR, 0, 0, tiled=True)
+    other_halves = shift(halves, "c", 1)
+
     values = across_z(pack(places, value_part, PACKED))
 
     q, g, k, v = project(
@@ -386,7 +408,8 @@
     heads = lax.all_to_all(
         attended.reshape(blocks, rows // blocks, attended.shape[1]), TENSOR, 0, 0, tiled=True
     )
-    return project_out(heads, whole_weight)
+    place = jnp.stack([y, core]).astype(jnp.int32)
+    return project_out(place, heads, halves, other_halves)
 
 
 def solution(mesh):

time: 238 us -> 220 us (0.924)
  blocking collectives: 15.9 us -> 0 us
  starting transfers between devices: 36.8 us -> 51.1 us
  between operations: 14.3 us -> 1.01 us
  waiting for transfers between devices: 116 us -> 108 us
  Pallas kernels: 39.8 us -> 43.3 us
    all_to_all x1 -> x0, blocking collectives: 15.9 us -> none  [local(): lax.all_to_all(attended.reshape(blocks, rows // blocks, attended.shape[1]...]
    all_to_all x2 -> x4, starting transfers between devices: 12.2 us -> 22.9 us  [the longest x2 12.4 us: across_y(): flat = lax.all_to_all(flat, ('y', 'c'), 0, 0, tiled=True)]
    ppermute x13 -> x14, waiting for transfers between devices: 99.4 us -> 90.7 us  [shift(): return lax.ppermute(value, axis, ring(lax.axis_size(axis), step))]
    ppermute x13 -> x14, starting transfers between devices: 24.6 us -> 28.2 us  [shift(): return lax.ppermute(value, axis, ring(lax.axis_size(axis), step))]
    pallas_call x1, Pallas kernels: 3.8 us -> 6.62 us  [project_out(): pl.pallas_call(output_kernel, out_shape=jax.ShapeDtypeStruct((rows, colum...]
    broadcast_in_dim x0 -> x1, local copies, waits for them, and re-layouts: none -> 2.56 us  [local(): copies = jnp.broadcast_to(half, (blocks,) + half.shape)]
    unnamed x26 -> x36, local copies, waits for them, and re-layouts: 6.94 us -> 4.4 us
    all_to_all x2 -> x4, waiting for transfers between devices: 15.9 us -> 17.4 us  [the longest x1 12.6 us: local(): lax.all_to_all(attended.reshape(blocks, rows // blocks, attended.shape[1]...]
  transfers between devices with their start and end apart: 16 -> 18, of which waited for: 9 -> 11; matrix products, arithmetic and copies ran while one was open for 3% -> 3% of each run, Pallas kernels for 15% -> 15%
where the time goes in v5:
time: 220 us; the launch traced here: 218 us
  waiting for transfers between devices  108 us (49%)
  starting transfers between devices  51.1 us (23%)
  Pallas kernels  43.3 us (20%)
  local copies, waits for them, and re-layouts  9.28 us (4%)
  other arithmetic  5.06 us (2%)
    ppermute x14, waiting for transfers between devices, shift(): return lax.ppermute(value, axis, ring(lax.axis_size(axis), step))  90.7 us
    ppermute x14, starting transfers between devices, shift(): return lax.ppermute(value, axis, ring(lax.axis_size(axis), step))  28.2 us
    all_to_all x1, waiting for transfers between devices, local(): lax.all_to_all(attended.reshape(blocks, rows // blocks, attended.shape[1]...  12.6 us
    all_to_all x2, starting transfers between devices, across_y(): flat = lax.all_to_all(flat, ('y', 'c'), 0, 0, tiled=True)  12.4 us
    pallas_call x1, Pallas kernels, project(): pl.pallas_call(project_kernel, out_shape=(jax.ShapeDtypeStruct((rows, wq....  12.2 us
    pallas_call x1, Pallas kernels, attend(): pl.pallas_call(attend_kernel, out_shape=jax.ShapeDtypeStruct((rows, colum...  10.3 us
    pallas_call x2, Pallas kernels, by_target(): pl.pallas_call(by_target_kernel, out_shape=jax.ShapeDtypeStruct((ny, nc,...  7.7 us
    pallas_call x1, Pallas kernels, project_out(): pl.pallas_call(output_kernel, out_shape=jax.ShapeDtypeStruct((rows, colum...  6.62 us
  transfers between devices with their start and end apart: 18, of which 11 were waited for; matrix products, arithmetic and copies ran while one was open for 3% of the time, Pallas kernels for 15%

profile of v5, /device:TPU:8, one launch (start us, length us, event | category | flops | bytes accessed | tf_op | source)
XLA Modules:
  0.0 217.9 jit_solution(5533300464893214894)
XLA Ops:
  0.0 3.9 %by_target.3 = bf16[4,2,4,2,128,128]{5,4,3,2,1,0:T(8,128)(2,1)} custom-call(bf16[4,4,2,2,128,128]{5,4,3,2,1,0:T(8,128)(2,1)} %bitcast.30), custom_call_target="tpu_custom_call" | custom-call | flops 1048576 | bytes 1048576 | tf_op jit(solution)/shard_map/by_target/pallas_call | solution.py:235
  3.9 6.6 %all-to-all-start = ((bf16[8,1024,128]{2,1,0:T(8,128)(2,1)}), bf16[8,1024,128]{2,1,0:T(8,128)(2,1)}, u32[]{:S(2)}, u32[]{:S(2)}) async-start(bf16[8,1024,128]{2,1,0:T(8,128)(2,1)} %bitcast.29), calls=%async_computation | async-start | bytes 4194304 | tf_op jit(solution)/shard_map/all_to_all | solution.py:289
  10.5 1.9 collective-permute-start.6
  12.4 1.7 collective-permute-start.8
  14.1 3.8 %by_target.2 = bf16[4,2,4,2,128,128]{5,4,3,2,1,0:T(8,128)(2,1)} custom-call(bf16[4,4,2,2,128,128]{5,4,3,2,1,0:T(8,128)(2,1)} %bitcast.31), custom_call_target="tpu_custom_call" | custom-call | flops 1048576 | bytes 1048576 | tf_op jit(solution)/shard_map/by_target/pallas_call | solution.py:235
  17.9 0.1 add_multiply_fusion
  18.0 13.3 %collective-permute-done.7.refs_2_ = bf16[1536,256]{1,0:T(8,128)(2,1)S(1)} collective-permute-done((bf16[1536,256]{1,0:T(8,128)(2,1)S(1)}, bf16[1536,256]{1,0:T(8,128)(2,1)S(1)}, u32[]{:S(2)}, u32[]{:S(2)}) %collective-permute-start.7) | collective-permute-done | bytes 786464 | tf_op jit(solution)/shard_map/ppermute | solution.py:28
  31.3 0.2 collective-permute-done.8.refs_3_
  31.5 4.8 %all-to-all-done = bf16[8,1024,128]{2,1,0:T(8,128)(2,1)} async-done(((bf16[8,1024,128]{2,1,0:T(8,128)(2,1)}), bf16[8,1024,128]{2,1,0:T(8,128)(2,1)}, u32[]{:S(2)}, u32[]{:S(2)}) %all-to-all-start) | async-done | bytes 2097184 | tf_op jit(solution)/shard_map/all_to_all | solution.py:289
  36.3 5.8 %all-to-all-start.1 = ((bf16[8,1024,128]{2,1,0:T(8,128)(2,1)}), bf16[8,1024,128]{2,1,0:T(8,128)(2,1)}, u32[]{:S(2)}, u32[]{:S(2)}) async-start(bf16[8,1024,128]{2,1,0:T(8,128)(2,1)} %bitcast.28), calls=%async_computation.1 | async-start | bytes 4194304 | tf_op jit(solution)/shard_map/all_to_all | solution.py:289
  42.2 0.1 iota_add_fusion
  42.2 0.1 add.372
  42.4 0.1 reshape.362
  42.4 0.1 copy.24
  42.5 1.3 collective-permute-start.13
  43.8 0.2 convert_reduce_fusion
  44.0 0.1 copy.27
  44.0 0.1 reshape.363
  44.2 0.6 gather_fusion
  44.8 0.9 collective-permute-start.14
  45.7 0.6 gather_fusion.1
  46.2 0.1 collective-permute-start.12
  46.3 15.8 %collective-permute-done.13.refs_5_ = bf16[1536,256]{1,0:T(8,128)(2,1)S(1)} collective-permute-done((bf16[1536,256]{1,0:T(8,128)(2,1)S(1)}, bf16[1536,256]{1,0:T(8,128)(2,1)S(1)}, u32[]{:S(2)}, u32[]{:S(2)}) %collective-permute-start.13) | collective-permute-done | bytes 786464 | tf_op jit(solution)/shard_map/ppermute | solution.py:28
  62.2 2.4 %collective-permute-start.15 = (bf16[1536,256]{1,0:T(8,128)(2,1)S(1)}, bf16[1536,256]{1,0:T(8,128)(2,1)}, u32[]{:S(2)}, u32[]{:S(2)}) collective-permute-start(bf16[1536,256]{1,0:T(8,128)(2,1)S(1)} %collective-permute-done.13.refs_5_), channel_id=1, source_target_pairs={{0,3},{1,0},{2,1},{3,2},{4,7},{5,4},{6,5},{7,6},{8,11},{9,8},{10,9... | collective-permute-start | bytes 2359304 | tf_op jit(solution)/shard_map/ppermute | solution.py:28
  64.6 0.2 select_reduce_fusion.1
  64.8 0.2 reduce_window_sum.11
  65.0 0.1 min.22
  65.1 0.1 pad_add_fusion.2.offsets
  65.2 3.3 %pack.6 = (bf16[1152,128]{1,0:T(8,128)(2,1)}, bf16[1152,128]{1,0:T(8,128)(2,1)}, bf16[1152,128]{1,0:T(8,128)(2,1)}, bf16[1152,128]{1,0:T(8,128)(2,1)}) custom-call(s32[68]{0:T(128)S(1)} %pad_add_fusion.2.offsets, bf16[8,4,2,128,128]{4,3,2,1,0:T(8,128)(2,1)} %bitcast.7.cache), custom_call_target="tpu_custom_call" | custom-call | flops 1048576 | bytes 1048576 | tf_op jit(solution)/shard_map/pack/pallas_call | solution.py:212
  68.6 3.3 %collective-permute-start.9 = (bf16[1152,128]{1,0:T(8,128)(2,1)}, bf16[1152,128]{1,0:T(8,128)(2,1)}, u32[]{:S(2)}, u32[]{:S(2)}) collective-permute-start(bf16[1152,128]{1,0:T(8,128)(2,1)} %get-tuple-element.138), channel_id=1, source_target_pairs={{0,16},{16,32},{32,48},{48,0},{1,17},{17,33},{33,49},{49,1},{2,18}... | collective-permute-start | bytes 884744 | tf_op jit(solution)/shard_map/ppermute | solution.py:28
  71.8 5.4 %collective-permute-start.10 = (bf16[1152,128]{1,0:T(8,128)(2,1)}, bf16[1152,128]{1,0:T(8,128)(2,1)}, u32[]{:S(2)}, u32[]{:S(2)}) collective-permute-start(bf16[1152,128]{1,0:T(8,128)(2,1)} %get-tuple-element.139), channel_id=1, source_target_pairs={{0,32},{16,48},{32,0},{48,16},{1,33},{17,49},{33,1},{49,17},{2,34}... | collective-permute-start | bytes 884744 | tf_op jit(solution)/shard_map/ppermute | solution.py:28
  77.2 2.7 %collective-permute-start.11 = (bf16[1152,128]{1,0:T(8,128)(2,1)}, bf16[1152,128]{1,0:T(8,128)(2,1)}, u32[]{:S(2)}, u32[]{:S(2)}) collective-permute-start(bf16[1152,128]{1,0:T(8,128)(2,1)} %get-tuple-element.140), channel_id=1, source_target_pairs={{0,48},{16,0},{32,16},{48,32},{1,49},{17,1},{33,17},{49,33},{2,50}... | collective-permute-start | bytes 884744 | tf_op jit(solution)/shard_map/ppermute | solution.py:28
  79.9 2.4 %collective-permute-done.12.refs_4_ = bf16[1536,256]{1,0:T(8,128)(2,1)} collective-permute-done((bf16[1536,256]{1,0:T(8,128)(2,1)S(1)}, bf16[1536,256]{1,0:T(8,128)(2,1)}, u32[]{:S(2)}, u32[]{:S(2)}) %collective-permute-start.12) | collective-permute-done | bytes 786464 | tf_op jit(solution)/shard_map/ppermute | solution.py:28
  82.3 6.2 %collective-permute-done.9 = bf16[1152,128]{1,0:T(8,128)(2,1)} collective-permute-done((bf16[1152,128]{1,0:T(8,128)(2,1)}, bf16[1152,128]{1,0:T(8,128)(2,1)}, u32[]{:S(2)}, u32[]{:S(2)}) %collective-permute-start.9) | collective-permute-done | bytes 294944 | tf_op jit(solution)/shard_map/ppermute | solution.py:28
  88.6 7.2 %collective-permute-done.10 = bf16[1152,128]{1,0:T(8,128)(2,1)} collective-permute-done((bf16[1152,128]{1,0:T(8,128)(2,1)}, bf16[1152,128]{1,0:T(8,128)(2,1)}, u32[]{:S(2)}, u32[]{:S(2)}) %collective-permute-start.10) | collective-permute-done | bytes 294944 | tf_op jit(solution)/shard_map/ppermute | solution.py:28
  95.8 7.2 %collective-permute-done.11 = bf16[1152,128]{1,0:T(8,128)(2,1)} collective-permute-done((bf16[1152,128]{1,0:T(8,128)(2,1)}, bf16[1152,128]{1,0:T(8,128)(2,1)}, u32[]{:S(2)}, u32[]{:S(2)}) %collective-permute-start.11) | collective-permute-done | bytes 294944 | tf_op jit(solution)/shard_map/ppermute | solution.py:28
  103.0 2.6 %broadcast_in_dim.81 = bf16[8,128,2048]{2,1,0:T(8,128)(2,1)} broadcast(bf16[128,2048]{1,0:T(8,128)(2,1)S(1)} %constant_dynamic-slice_fusion.1), dimensions={1,2} | broadcast | bytes 4718592 | tf_op jit(solution)/shard_map/broadcast_in_dim | solution.py:387
  105.5 4.9 %all-to-all-start.3 = ((bf16[8,128,2048]{2,1,0:T(8,128)(2,1)}), bf16[8,128,2048]{2,1,0:T(8,128)(2,1)}, u32[]{:S(2)}, u32[]{:S(2)}) async-start(bf16[8,128,2048]{2,1,0:T(8,128)(2,1)} %broadcast_in_dim.81), calls=%async_computation.3 | async-start | bytes 8388608 | tf_op jit(solution)/shard_map/all_to_all | solution.py:388
  110.7 0.7 reduce_max.9
  112.1 0.1 add_convert_fusion
  112.1 0.1 convert_element_type.26
  112.2 0.4 copy.28.refs_8_
  112.6 0.1 stack.47.ids
  112.7 0.3 fusion.9
  113.1 2.8 %fusion = (f32[1536,128]{1,0:T(8,128)S(1)}, f32[1536,128]{1,0:T(8,128)S(1)}) fusion(f32[128]{0:T(128)S(1)} %get-tuple-element.172, f32[128]{0:T(128)S(1)} %get-tuple-element.173, f32[1536]{0:T(1024)S(1)} %convert_element_type.26), kind=kLoop, calls=%fused_computation.8 | loop fusion | flops 393216 | bytes 1580032 | tf_op jit(solution)/shard_map/mul | solution.py:369
  115.9 3.2 %pack.7 = (bf16[1152,128]{1,0:T(8,128)(2,1)}, bf16[1152,128]{1,0:T(8,128)(2,1)S(1)}, bf16[1152,128]{1,0:T(8,128)(2,1)S(1)}, bf16[1152,128]{1,0:T(8,128)(2,1)S(1)}) custom-call(s32[68]{0:T(128)S(1)} %pad_add_fusion.2.offsets, bf16[8,4,2,128,128]{4,3,2,1,0:T(8,128)(2,1)} %bitcast.9.cache), custom_call_target="tpu_custom_call" | custom-call | flops 1048576 | bytes 1048576 | tf_op jit(solution)/shard_map/pack/pallas_call | solution.py:212
  119.0 1.6 collective-permute-start.16
  120.7 4.2 %collective-permute-start.17 = (bf16[1152,128]{1,0:T(8,128)(2,1)S(1)}, bf16[1152,128]{1,0:T(8,128)(2,1)S(1)}, u32[]{:S(2)}, u32[]{:S(2)}) collective-permute-start(bf16[1152,128]{1,0:T(8,128)(2,1)S(1)} %get-tuple-element.159), channel_id=1, source_target_pairs={{0,32},{16,48},{32,0},{48,16},{1,33},{17,49},{33,1},{49,17},{2,34}... | collective-permute-start | bytes 884744 | tf_op jit(solution)/shard_map/ppermute | solution.py:28
  124.9 2.6 %collective-permute-start.18 = (bf16[1152,128]{1,0:T(8,128)(2,1)S(1)}, bf16[1152,128]{1,0:T(8,128)(2,1)S(1)}, u32[]{:S(2)}, u32[]{:S(2)}) collective-permute-start(bf16[1152,128]{1,0:T(8,128)(2,1)S(1)} %get-tuple-element.160), channel_id=1, source_target_pairs={{0,48},{16,0},{32,16},{48,32},{1,49},{17,1},{33,17},{49,33},{2,50}... | collective-permute-start | bytes 884744 | tf_op jit(solution)/shard_map/ppermute | solution.py:28
  127.5 0.2 select_reduce_fusion.2
  127.7 1.1 copy-done.8
  128.8 1.1 copy-done.10
  130.0 1.0 copy-done.11
  131.0 1.0 copy-done.12
  132.1 12.2 %project.1 = (bf16[1536,256]{1,0:T(8,128)(2,1)}, f32[1536,256]{1,0:T(8,128)}, bf16[1536,128]{1,0:T(8,128)(2,1)}, bf16[1536,128]{1,0:T(8,128)(2,1)}) custom-call(s32[8]{0:T(128)S(1)} %stack.47.ids, bf16[1536,256]{1,0:T(8,128)(2,1)S(1)} %copy-done.4, bf16[1536,256]{1,0:T(8,128)(2,1)S(1)} %copy-done.8, bf16[1536,256]{1,0:T(8,128)(2,1)S(1)} %copy-done.6, ...), custom_call_target="tpu_custom_call" | custom-call | flops 1048576 | bytes 1048576 | tf_op jit(solution)/shard_map/project/pallas_call | solution.py:104
  144.2 29.9 %collective-permute-done.16 = bf16[1152,128]{1,0:T(8,128)(2,1)S(1)} collective-permute-done((bf16[1152,128]{1,0:T(8,128)(2,1)S(1)}, bf16[1152,128]{1,0:T(8,128)(2,1)S(1)}, u32[]{:S(2)}, u32[]{:S(2)}) %collective-permute-start.16) | collective-permute-done | bytes 294944 | tf_op jit(solution)/shard_map/ppermute | solution.py:28
  174.2 8.4 %collective-permute-done.17 = bf16[1152,128]{1,0:T(8,128)(2,1)S(1)} collective-permute-done((bf16[1152,128]{1,0:T(8,128)(2,1)S(1)}, bf16[1152,128]{1,0:T(8,128)(2,1)S(1)}, u32[]{:S(2)}, u32[]{:S(2)}) %collective-permute-start.17) | collective-permute-done | bytes 294944 | tf_op jit(solution)/shard_map/ppermute | solution.py:28
  182.6 10.3 %conditional.1 = (bf16[1536,256]{1,0:T(8,128)(2,1)}) conditional(s32[]{:T(128)} %convert_element_type.23, (s32[24]{0:T(128)S(1)}, s32[24]{0:T(128)S(1)}, s32[4,16]{1,0:T(4,128)S(1)}, s32[4,16]{1,0:T(4,128)S(1)}, s32[4]{0:T(128)S(1)}, /*index=5*/bf16[8,4,2,128,128]{4,3,2,1,0:T(8,128)(2,1)}, bf16[8,4,2,128,128]{4,3,2,1,0:T(8,128)(2,1)}, ...), branch_computations={%region_6.7_spmd, %region_7.8_spmd} | conditional | flops 3146060 | bytes 28314024 | solution.py:407
  182.6 10.3 %attend.3 = bf16[1536,256]{1,0:T(8,128)(2,1)} custom-call(s32[24]{0:T(128)S(1)} %add_minimum_fusion.1.starts, s32[24]{0:T(128)S(1)} %get-tuple-element.95.lengths, bf16[1536,256]{1,0:T(8,128)(2,1)} %get-tuple-element.96.q, f32[1536,256]{1,0:T(8,128)} %get-tuple-element.97.g, bf16[1536,128]{1,0:T(8,128)(2,1)} %get-tuple-element.98.k, ...), custom_call_target="tpu_custom_call" | custom-call | flops 1048576 | bytes 1048576 | tf_op jit(solution)/shard_map/cond/branch_1_fun/attend/pallas_call | solution.py:183
  192.9 0.1 collective-permute-start.19
  193.0 5.6 %all-to-all-start.2 = ((bf16[8,192,256]{2,1,0:T(8,128)(2,1)}), bf16[8,192,256]{2,1,0:T(8,128)(2,1)S(1)}, u32[]{:S(2)}, u32[]{:S(2)}) async-start(bf16[8,192,256]{2,1,0:T(8,128)(2,1)} %bitcast.22), calls=%async_computation.2 | async-start | bytes 1572864 | tf_op jit(solution)/shard_map/all_to_all | solution.py:408
  198.6 0.1 pad_add_fusion.1.place
  198.7 12.6 %all-to-all-done.2.heads = bf16[8,192,256]{2,1,0:T(8,128)(2,1)S(1)} async-done(((bf16[8,192,256]{2,1,0:T(8,128)(2,1)}), bf16[8,192,256]{2,1,0:T(8,128)(2,1)S(1)}, u32[]{:S(2)}, u32[]{:S(2)}) %all-to-all-start.2) | async-done | bytes 786464 | tf_op jit(solution)/shard_map/all_to_all | solution.py:408
  211.3 6.6 %project_out.1 = bf16[192,2048]{1,0:T(8,128)(2,1)} custom-call(s32[2]{0:T(128)S(1)} %pad_add_fusion.1.place, bf16[8,192,256]{2,1,0:T(8,128)(2,1)S(1)} %all-to-all-done.2.heads, bf16[8,128,2048]{2,1,0:T(8,128)(2,1)} %all-to-all-done.3.mine, bf16[8,128,2048]{2,1,0:T(8,128)(2,1)} %collective-permute-done.19.other), custom_call_target="tpu_custom_call" | custom-call | flops 1048576 | bytes 1048576 | tf_op jit(solution)/shard_map/project_out/pallas_call | solution.py:270
  (59 shorter events, 0.5 us)
Async XLA Ops:
  0.0 79.9 %copy-start = (bf16[256,2048]{1,0:T(8,128)(2,1)S(1)}, bf16[256,2048]{1,0:T(8,128)(2,1)}, u32[]{:S(2)}) copy-start(bf16[256,2048]{1,0:T(8,128)(2,1)} %param.23) | copy-start | bytes 3145732
  3.9 6.6 %copy-start.3 = (bf16[1536,256]{1,0:T(8,128)(2,1)S(1)}, bf16[1536,256]{1,0:T(8,128)(2,1)}, u32[]{:S(2)}) copy-start(bf16[1536,256]{1,0:T(8,128)(2,1)} %refs_0_.1) | copy-start | bytes 2359300
  3.9 32.4 %all-to-all-start = ((bf16[8,1024,128]{2,1,0:T(8,128)(2,1)}), bf16[8,1024,128]{2,1,0:T(8,128)(2,1)}, u32[]{:S(2)}, u32[]{:S(2)}) async-start(bf16[8,1024,128]{2,1,0:T(8,128)(2,1)} %bitcast.29), calls=%async_computation | async-start | bytes 4194304 | tf_op jit(solution)/shard_map/all_to_all | solution.py:289
  10.5 20.8 %collective-permute-start.7 = (bf16[1536,256]{1,0:T(8,128)(2,1)S(1)}, bf16[1536,256]{1,0:T(8,128)(2,1)S(1)}, u32[]{:S(2)}, u32[]{:S(2)}) collective-permute-start(bf16[1536,256]{1,0:T(8,128)(2,1)S(1)} %copy-done.3), channel_id=1, source_target_pairs={{0,1},{1,2},{2,3},{3,0},{4,5},{5,6},{6,7},{7,4},{8,9},{9,10},{10,1... | collective-permute-start | bytes 2359304 | tf_op jit(solution)/shard_map/ppermute | solution.py:28
  10.5 20.8 %collective-permute-start.6 = (bf16[1536,256]{1,0:T(8,128)(2,1)S(1)}, bf16[1536,256]{1,0:T(8,128)(2,1)S(1)}, u32[]{:S(2)}, u32[]{:S(2)}) collective-permute-start(bf16[1536,256]{1,0:T(8,128)(2,1)S(1)} %copy-done.3), channel_id=1, source_target_pairs={{0,4},{4,0},{1,5},{5,1},{2,6},{6,2},{3,7},{7,3},{8,12},{12,8},{9,1... | collective-permute-start | bytes 2359304 | tf_op jit(solution)/shard_map/ppermute | solution.py:28
  12.4 19.1 %collective-permute-start.8 = (bf16[1536,256]{1,0:T(8,128)(2,1)S(1)}, bf16[1536,256]{1,0:T(8,128)(2,1)}, u32[]{:S(2)}, u32[]{:S(2)}) collective-permute-start(bf16[1536,256]{1,0:T(8,128)(2,1)S(1)} %copy-done.3), channel_id=1, source_target_pairs={{0,3},{1,0},{2,1},{3,2},{4,7},{5,4},{6,5},{7,6},{8,11},{9,8},{10,9... | collective-permute-start | bytes 2359304 | tf_op jit(solution)/shard_map/ppermute | solution.py:28
  31.3 13.5 %copy-start.5 = (bf16[1536,256]{1,0:T(8,128)(2,1)}, bf16[1536,256]{1,0:T(8,128)(2,1)S(1)}, u32[]{:S(2)}) copy-start(bf16[1536,256]{1,0:T(8,128)(2,1)S(1)} %collective-permute-done.7.refs_2_) | copy-start | bytes 2359300
  31.3 14.9 %copy-start.7 = (bf16[1536,256]{1,0:T(8,128)(2,1)}, bf16[1536,256]{1,0:T(8,128)(2,1)S(1)}, u32[]{:S(2)}) copy-start(bf16[1536,256]{1,0:T(8,128)(2,1)S(1)} %collective-permute-done.6.refs_1_) | copy-start | bytes 2359300
  36.3 6.0 %copy-start.21 = (s32[768,1]{0,1:T(1,128)S(1)}, s32[768,1]{0,1:T(1,128)}, u32[]{:S(2)}) copy-start(s32[768,1]{0,1:T(1,128)} %param.26) | copy-start | bytes 9220
  36.3 7.7 %copy-start.20 = (s32[768]{0:T(1024)S(1)}, s32[768]{0:T(1024)}, u32[]{:S(2)}) copy-start(s32[768]{0:T(1024)} %param.27) | copy-start | bytes 9220
  36.3 66.6 %all-to-all-start.1 = ((bf16[8,1024,128]{2,1,0:T(8,128)(2,1)}), bf16[8,1024,128]{2,1,0:T(8,128)(2,1)}, u32[]{:S(2)}, u32[]{:S(2)}) async-start(bf16[8,1024,128]{2,1,0:T(8,128)(2,1)} %bitcast.28), calls=%async_computation.1 | async-start | bytes 4194304 | tf_op jit(solution)/shard_map/all_to_all | solution.py:289
  42.5 19.7 %collective-permute-start.13 = (bf16[1536,256]{1,0:T(8,128)(2,1)S(1)}, bf16[1536,256]{1,0:T(8,128)(2,1)S(1)}, u32[]{:S(2)}, u32[]{:S(2)}) collective-permute-start(bf16[1536,256]{1,0:T(8,128)(2,1)S(1)} %collective-permute-done.6.refs_1_), channel_id=1, source_target_pairs={{0,3},{1,0},{2,1},{3,2},{4,7},{5,4},{6,5},{7,6},{8,11},{9,8},{10,9... | collective-permute-start | bytes 2359304 | tf_op jit(solution)/shard_map/ppermute | solution.py:28
  44.8 32.4 %collective-permute-start.14 = (bf16[1536,256]{1,0:T(8,128)(2,1)S(1)}, bf16[1536,256]{1,0:T(8,128)(2,1)}, u32[]{:S(2)}, u32[]{:S(2)}) collective-permute-start(bf16[1536,256]{1,0:T(8,128)(2,1)S(1)} %collective-permute-done.7.refs_2_), channel_id=1, source_target_pairs={{0,1},{1,2},{2,3},{3,0},{4,5},{5,6},{6,7},{7,4},{8,9},{9,10},{10,1... | collective-permute-start | bytes 2359304 | tf_op jit(solution)/shard_map/ppermute | solution.py:28
  46.2 36.1 %collective-permute-start.12 = (bf16[1536,256]{1,0:T(8,128)(2,1)S(1)}, bf16[1536,256]{1,0:T(8,128)(2,1)}, u32[]{:S(2)}, u32[]{:S(2)}) collective-permute-start(bf16[1536,256]{1,0:T(8,128)(2,1)S(1)} %collective-permute-done.6.refs_1_), channel_id=1, source_target_pairs={{0,1},{1,2},{2,3},{3,0},{4,5},{5,6},{6,7},{7,4},{8,9},{9,10},{10,1... | collective-permute-start | bytes 2359304 | tf_op jit(solution)/shard_map/ppermute | solution.py:28
  62.2 43.4 %copy-start.9 = (bf16[1536,256]{1,0:T(8,128)(2,1)}, bf16[1536,256]{1,0:T(8,128)(2,1)S(1)}, u32[]{:S(2)}) copy-start(bf16[1536,256]{1,0:T(8,128)(2,1)S(1)} %collective-permute-done.13.refs_5_) | copy-start | bytes 2359300
  62.2 40.8 %collective-permute-start.15 = (bf16[1536,256]{1,0:T(8,128)(2,1)S(1)}, bf16[1536,256]{1,0:T(8,128)(2,1)}, u32[]{:S(2)}, u32[]{:S(2)}) collective-permute-start(bf16[1536,256]{1,0:T(8,128)(2,1)S(1)} %collective-permute-done.13.refs_5_), channel_id=1, source_target_pairs={{0,3},{1,0},{2,1},{3,2},{4,7},{5,4},{6,5},{7,6},{8,11},{9,8},{10,9... | collective-permute-start | bytes 2359304 | tf_op jit(solution)/shard_map/ppermute | solution.py:28
  68.6 20.0 %collective-permute-start.9 = (bf16[1152,128]{1,0:T(8,128)(2,1)}, bf16[1152,128]{1,0:T(8,128)(2,1)}, u32[]{:S(2)}, u32[]{:S(2)}) collective-permute-start(bf16[1152,128]{1,0:T(8,128)(2,1)} %get-tuple-element.138), channel_id=1, source_target_pairs={{0,16},{16,32},{32,48},{48,0},{1,17},{17,33},{33,49},{49,1},{2,18}... | collective-permute-start | bytes 884744 | tf_op jit(solution)/shard_map/ppermute | solution.py:28
  71.8 23.9 %collective-permute-start.10 = (bf16[1152,128]{1,0:T(8,128)(2,1)}, bf16[1152,128]{1,0:T(8,128)(2,1)}, u32[]{:S(2)}, u32[]{:S(2)}) collective-permute-start(bf16[1152,128]{1,0:T(8,128)(2,1)} %get-tuple-element.139), channel_id=1, source_target_pairs={{0,32},{16,48},{32,0},{48,16},{1,33},{17,49},{33,1},{49,17},{2,34}... | collective-permute-start | bytes 884744 | tf_op jit(solution)/shard_map/ppermute | solution.py:28
  77.2 25.7 %collective-permute-start.11 = (bf16[1152,128]{1,0:T(8,128)(2,1)}, bf16[1152,128]{1,0:T(8,128)(2,1)}, u32[]{:S(2)}, u32[]{:S(2)}) collective-permute-start(bf16[1152,128]{1,0:T(8,128)(2,1)} %get-tuple-element.140), channel_id=1, source_target_pairs={{0,48},{16,0},{32,16},{48,32},{1,49},{17,1},{33,17},{49,33},{2,50}... | collective-permute-start | bytes 884744 | tf_op jit(solution)/shard_map/ppermute | solution.py:28
  105.5 6.7 %copy-start.19 = (f32[2048]{0:T(1024)S(1)}, f32[2048]{0:T(1024)}, u32[]{:S(2)}) copy-start(f32[2048]{0:T(1024)} %param.16) | copy-start | bytes 24580
  105.5 87.4 %all-to-all-start.3 = ((bf16[8,128,2048]{2,1,0:T(8,128)(2,1)}), bf16[8,128,2048]{2,1,0:T(8,128)(2,1)}, u32[]{:S(2)}, u32[]{:S(2)}) async-start(bf16[8,128,2048]{2,1,0:T(8,128)(2,1)} %broadcast_in_dim.81), calls=%async_computation.3 | async-start | bytes 8388608 | tf_op jit(solution)/shard_map/all_to_all | solution.py:388
  112.6 15.0 %copy-start.1 = (bf16[2048,256]{1,0:T(8,128)(2,1)S(1)}, bf16[2048,256]{1,0:T(8,128)(2,1)}, u32[]{:S(2)}) copy-start(bf16[2048,256]{1,0:T(8,128)(2,1)} %refs_9_.1) | copy-start | bytes 3145732
  112.6 15.0 %copy-start.13 = (f32[128]{0:T(128)S(1)}, f32[128]{0:T(128)}, u32[]{:S(2)}) copy-start(f32[128]{0:T(128)} %param.21) | copy-start | bytes 1540
  112.6 15.0 %copy-start.14 = (f32[128]{0:T(128)S(1)}, f32[128]{0:T(128)}, u32[]{:S(2)}) copy-start(f32[128]{0:T(128)} %param.22) | copy-start | bytes 1540
  112.7 14.9 %copy-start.2 = (bf16[2048,256]{1,0:T(8,128)(2,1)S(1)}, bf16[2048,256]{1,0:T(8,128)(2,1)}, u32[]{:S(2)}) copy-start(bf16[2048,256]{1,0:T(8,128)(2,1)} %refs_10_.1) | copy-start | bytes 3145732
  112.7 15.0 %copy-start.4 = (bf16[1536,256]{1,0:T(8,128)(2,1)S(1)}, bf16[1536,256]{1,0:T(8,128)(2,1)}, u32[]{:S(2)}) copy-start(bf16[1536,256]{1,0:T(8,128)(2,1)} %refs_0_.1) | copy-start | bytes 2359300
  112.7 15.0 %copy-start.6 = (bf16[1536,256]{1,0:T(8,128)(2,1)S(1)}, bf16[1536,256]{1,0:T(8,128)(2,1)}, u32[]{:S(2)}) copy-start(bf16[1536,256]{1,0:T(8,128)(2,1)} %copy-done.5) | copy-start | bytes 2359300
  119.0 55.2 %collective-permute-start.16 = (bf16[1152,128]{1,0:T(8,128)(2,1)S(1)}, bf16[1152,128]{1,0:T(8,128)(2,1)S(1)}, u32[]{:S(2)}, u32[]{:S(2)}) collective-permute-start(bf16[1152,128]{1,0:T(8,128)(2,1)S(1)} %get-tuple-element.158), channel_id=1, source_target_pairs={{0,16},{16,32},{32,48},{48,0},{1,17},{17,33},{33,49},{49,1},{2,18}... | collective-permute-start | bytes 884744 | tf_op jit(solution)/shard_map/ppermute | solution.py:28
  120.7 61.9 %collective-permute-start.17 = (bf16[1152,128]{1,0:T(8,128)(2,1)S(1)}, bf16[1152,128]{1,0:T(8,128)(2,1)S(1)}, u32[]{:S(2)}, u32[]{:S(2)}) collective-permute-start(bf16[1152,128]{1,0:T(8,128)(2,1)S(1)} %get-tuple-element.159), channel_id=1, source_target_pairs={{0,32},{16,48},{32,0},{48,16},{1,33},{17,49},{33,1},{49,17},{2,34}... | collective-permute-start | bytes 884744 | tf_op jit(solution)/shard_map/ppermute | solution.py:28
  124.9 57.7 %collective-permute-start.18 = (bf16[1152,128]{1,0:T(8,128)(2,1)S(1)}, bf16[1152,128]{1,0:T(8,128)(2,1)S(1)}, u32[]{:S(2)}, u32[]{:S(2)}) collective-permute-start(bf16[1152,128]{1,0:T(8,128)(2,1)S(1)} %get-tuple-element.160), channel_id=1, source_target_pairs={{0,48},{16,0},{32,16},{48,32},{1,49},{17,1},{33,17},{49,33},{2,50}... | collective-permute-start | bytes 884744 | tf_op jit(solution)/shard_map/ppermute | solution.py:28
  127.7 1.1 copy-start.8
  128.8 1.1 copy-start.10
  130.0 1.0 copy-start.11
  131.0 1.0 copy-start.12
  192.9 18.4 %collective-permute-start.19 = (bf16[8,128,2048]{2,1,0:T(8,128)(2,1)}, bf16[8,128,2048]{2,1,0:T(8,128)(2,1)}, u32[]{:S(2)}, u32[]{:S(2)}) collective-permute-start(bf16[8,128,2048]{2,1,0:T(8,128)(2,1)} %all-to-all-done.3.mine), channel_id=1, source_target_pairs={{0,8},{8,0},{1,9},{9,1},{2,10},{10,2},{3,11},{11,3},{4,12},{12,4},... | collective-permute-start | bytes 12582920 | tf_op jit(solution)/shard_map/ppermute | solution.py:28
  193.0 18.2 %all-to-all-start.2 = ((bf16[8,192,256]{2,1,0:T(8,128)(2,1)}), bf16[8,192,256]{2,1,0:T(8,128)(2,1)S(1)}, u32[]{:S(2)}, u32[]{:S(2)}) async-start(bf16[8,192,256]{2,1,0:T(8,128)(2,1)} %bitcast.22), calls=%async_computation.2 | async-start | bytes 1572864 | tf_op jit(solution)/shard_map/all_to_all | solution.py:408

commit v6 on v5

--- a/solution.py
+++ b/solution.py
@@ -243,16 +243,34 @@
     )(cache)
 
 
-def output_kernel(place, heads, mine, other, out, joined):
+def copies_kernel(half, twin, out):
+    out[0, 0], out[0, 1] = half[...], twin[...]
+
+
+def copies(half, twin):
+    depth, columns = half.shape
+    whole = pl.BlockSpec((depth, columns), lambda i: (0, 0))
+    return pl.pallas_call(
+        copies_kernel,
+        out_shape=jax.ShapeDtypeStruct((4, 2, depth, columns), half.dtype),
+        grid=(4,),
+        in_specs=[whole, whole],
+        out_specs=pl.BlockSpec((1, 2, depth, columns), lambda i: (i, 0, 0, 0)),
+        cost_estimate=COST,
+        name="copies",
+    )(half, twin)
+
+
+def output_kernel(places, heads, mine, other, out, joined):
     count, depth = mine.shape[:2]
 
     @pl.when(pl.program_id(0) == 0)
     def _():
         for j in range(count):
             for h in range(2):
-                first = pl.multiple_of((place[1] + h) % 2 * depth, depth)
+                first = pl.multiple_of((places[count] + h) % 2 * depth, depth)
                 columns = slice((2 * j + h) * depth, (2 * j + h + 1) * depth)
-                joined[:, columns] = heads[j, :, pl.ds(first, depth)]
+                joined[:, columns] = heads[places[j], :, pl.ds(first, depth)]
 
     total = jnp.zeros(out.shape, jnp.float32)
     for j in range(count):
@@ -262,7 +280,7 @@
     out[...] = total.astype(jnp.bfloat16)
 
 
-def project_out(place, heads, mine, other):
+def project_out(places, heads, mine, other):
     blocks, rows, width = heads.shape
     depth, columns = mine.shape[1:]
     tile = 512
@@ -280,7 +298,7 @@
         compiler_params=pltpu.CompilerParams(vmem_limit_bytes=30 << 20),
         cost_estimate=COST,
         name="project_out",
-    )(place, heads, mine, other)
+    )(places, heads, mine, other)
 
 
 def across_y(slots):
@@ -372,23 +390,27 @@
     sides = (4, 4, 2, capacity, window, head_dim)
     places, starts = packing(PACKED)
     pieces = spread(span_rows)
+    depth = o_weight.shape[0] // 2
+    half = lax.dynamic_slice_in_dim(o_weight, core * depth, depth, 0)
+    half, pieces[1] = lax.optimization_barrier((half, pieces[1]))
+    twin_half = shift(half, "zl", 1)
+
     key_part = across_y(by_target(key_cache.reshape(sides)))
-    value_slots, key_part, pieces[1:4] = lax.optimization_barrier(
-        (by_target(value_cache.reshape(sides)), key_part, pieces[1:4])
+    value_slots, key_part, pieces[1:6], twin_half = lax.optimization_barrier(
+        (by_target(value_cache.reshape(sides)), key_part, pieces[1:6], twin_half)
     )
     value_part = across_y(value_slots)
     keys = across_z(pack(places, key_part, PACKED))
-
-    depth = o_weight.shape[0] // 2
-    half = lax.dynamic_slice_in_dim(o_weight, core * depth, depth, 0)
-    half, value_part, keys, pieces[4:] = lax.optimization_barrier(
-        (half, value_part, keys, pieces[4:])
-    )
-    copies = jnp.broadcast_to(half, (blocks,) + half.shape)
-    halves = lax.all_to_all(copies, TENSOR, 0, 0, tiled=True)
+    repeated, value_part, keys, pieces[6:] = lax.optimization_barrier(
+        (copies(half, twin_half), value_part, keys, pieces[6:])
+    )
+    packed_values = pack(places, value_part, PACKED)
+    repeated, packed_values = lax.optimization_barrier((repeated, packed_values))
+    halves = lax.all_to_all(repeated, "x", 0, 0, tiled=True)
+    halves = halves.reshape((blocks,) + half.shape)
     other_halves = shift(halves, "c", 1)
 
-    values = across_z(pack(places, value_part, PACKED))
+    values = across_z(packed_values)
 
     q, g, k, v = project(
         ids, pieces, norm_gain, q_weight, gate_weight, k_weight, v_weight,
@@ -408,8 +430,9 @@
     heads = lax.all_to_all(
         attended.reshape(blocks, rows // blocks, attended.shape[1]), TENSOR, 0, 0, tiled=True
     )
-    place = jnp.stack([y, core]).astype(jnp.int32)
-    return project_out(place, heads, halves, other_halves)
+    x_ids, zl_ids = jnp.arange(blocks) // 2, (lax.axis_index("zl") + jnp.arange(blocks)) % 2
+    out_places = jnp.concatenate([zl_ids * 4 + x_ids, core[None]]).astype(jnp.int32)
+    return project_out(out_places, heads, halves, other_halves)
 
 
 def solution(mesh):

time: 220 us -> 185 us (0.84)
  waiting for transfers between devices: 108 us -> 67 us
  local copies, waits for them, and re-layouts: 9.28 us -> 13.1 us
  Pallas kernels: 43.3 us -> 47 us
    ppermute x14 -> x15, waiting for transfers between devices: 90.7 us -> 49.5 us  [shift(): return lax.ppermute(value, axis, ring(lax.axis_size(axis), step))]
    unnamed x36 -> x48, local copies, waits for them, and re-layouts: 4.4 us -> 9.97 us
    all_to_all x2, waiting for transfers between devices: 4.84 us -> 0.01 us  [across_y(): flat = lax.all_to_all(flat, ('y', 'c'), 0, 0, tiled=True)]
    all_to_all x1, waiting for transfers between devices: 0.01 us -> 4.73 us  [local(): halves = lax.all_to_all(repeated, 'x', 0, 0, tiled=True)]
    pallas_call x0 -> x1, Pallas kernels: none -> 3.68 us  [copies(): pl.pallas_call(copies_kernel, out_shape=jax.ShapeDtypeStruct((4, 2, depth...]
    broadcast_in_dim x1 -> x0, local copies, waits for them, and re-layouts: 2.56 us -> none  [local(): copies = jnp.broadcast_to(half, (blocks,) + half.shape)]
    ppermute x14 -> x15, starting transfers between devices: 28.2 us -> 29.6 us  [shift(): return lax.ppermute(value, axis, ring(lax.axis_size(axis), step))]
  transfers between devices with their start and end apart: 18 -> 19, of which waited for: 11 -> 9; matrix products, arithmetic and copies ran while one was open for 3% -> 4% of each run, Pallas kernels for 15% -> 18%
where the time goes in v6:
time: 185 us; the launch traced here: 183 us
  waiting for transfers between devices  67 us (36%)
  starting transfers between devices  49.9 us (27%)
  Pallas kernels  47 us (25%)
  local copies, waits for them, and re-layouts  13.1 us (7%)
  other arithmetic  5.07 us (3%)
    ppermute x15, waiting for transfers between devices, shift(): return lax.ppermute(value, axis, ring(lax.axis_size(axis), step))  49.5 us
    ppermute x15, starting transfers between devices, shift(): return lax.ppermute(value, axis, ring(lax.axis_size(axis), step))  29.6 us
    all_to_all x1, waiting for transfers between devices, local(): lax.all_to_all(attended.reshape(blocks, rows // blocks, attended.shape[1]...  12.8 us
    pallas_call x1, Pallas kernels, project(): pl.pallas_call(project_kernel, out_shape=(jax.ShapeDtypeStruct((rows, wq....  12.1 us
    all_to_all x2, starting transfers between devices, across_y(): flat = lax.all_to_all(flat, ('y', 'c'), 0, 0, tiled=True)  11.6 us
    pallas_call x1, Pallas kernels, attend(): pl.pallas_call(attend_kernel, out_shape=jax.ShapeDtypeStruct((rows, colum...  10.3 us
    unnamed x48, local copies, waits for them, and re-layouts  9.97 us
    pallas_call x2, Pallas kernels, by_target(): pl.pallas_call(by_target_kernel, out_shape=jax.ShapeDtypeStruct((ny, nc,...  7.71 us
  transfers between devices with their start and end apart: 19, of which 9 were waited for; matrix products, arithmetic and copies ran while one was open for 4% of the time, Pallas kernels for 18%

profile of v6, /device:TPU:8, one launch (start us, length us, event | category | flops | bytes accessed | tf_op | source)
XLA Modules:
  0.0 183.0 jit_solution(14231964004224771236)
XLA Ops:
  0.0 3.9 %by_target.3 = bf16[4,2,4,2,128,128]{5,4,3,2,1,0:T(8,128)(2,1)} custom-call(bf16[4,4,2,2,128,128]{5,4,3,2,1,0:T(8,128)(2,1)} %bitcast.30), custom_call_target="tpu_custom_call" | custom-call | flops 1048576 | bytes 1048576 | tf_op jit(solution)/shard_map/by_target/pallas_call | solution.py:235
  3.9 6.6 %all-to-all-start = ((bf16[8,1024,128]{2,1,0:T(8,128)(2,1)}), bf16[8,1024,128]{2,1,0:T(8,128)(2,1)}, u32[]{:S(2)}, u32[]{:S(2)}) async-start(bf16[8,1024,128]{2,1,0:T(8,128)(2,1)} %bitcast.29), calls=%async_computation | async-start | bytes 4194304 | tf_op jit(solution)/shard_map/all_to_all | solution.py:307
  10.5 0.4 collective-permute-start.6
  10.9 1.5 collective-permute-start.7
  12.4 1.7 collective-permute-start.8
  14.1 16.0 %collective-permute-done.6.refs_1_ = bf16[1536,256]{1,0:T(8,128)(2,1)S(1)} collective-permute-done((bf16[1536,256]{1,0:T(8,128)(2,1)S(1)}, bf16[1536,256]{1,0:T(8,128)(2,1)S(1)}, u32[]{:S(2)}, u32[]{:S(2)}) %collective-permute-start.6) | collective-permute-done | bytes 786464 | tf_op jit(solution)/shard_map/ppermute | solution.py:28
  30.1 1.4 collective-permute-start.10
  31.5 0.6 collective-permute-start.9
  32.1 0.9 constant_dynamic-slice_fusion.1.half
  33.0 1.1 collective-permute-start.11
  34.1 3.8 %by_target.2 = bf16[4,2,4,2,128,128]{5,4,3,2,1,0:T(8,128)(2,1)} custom-call(bf16[4,4,2,2,128,128]{5,4,3,2,1,0:T(8,128)(2,1)} %bitcast.31), custom_call_target="tpu_custom_call" | custom-call | flops 1048576 | bytes 1048576 | tf_op jit(solution)/shard_map/by_target/pallas_call | solution.py:235
  38.0 8.0 %collective-permute-done.11.twin = bf16[128,2048]{1,0:T(8,128)(2,1)} collective-permute-done((bf16[128,2048]{1,0:T(8,128)(2,1)}, bf16[128,2048]{1,0:T(8,128)(2,1)}, u32[]{:S(2)}, u32[]{:S(2)}) %collective-permute-start.11) | collective-permute-done | bytes 524320 | tf_op jit(solution)/shard_map/ppermute | solution.py:28
  46.0 3.1 %collective-permute-done.10.refs_5_ = bf16[1536,256]{1,0:T(8,128)(2,1)} collective-permute-done((bf16[1536,256]{1,0:T(8,128)(2,1)S(1)}, bf16[1536,256]{1,0:T(8,128)(2,1)}, u32[]{:S(2)}, u32[]{:S(2)}) %collective-permute-start.10) | collective-permute-done | bytes 786464 | tf_op jit(solution)/shard_map/ppermute | solution.py:28
  49.1 2.5 %collective-permute-done.9.refs_4_ = bf16[1536,256]{1,0:T(8,128)(2,1)} collective-permute-done((bf16[1536,256]{1,0:T(8,128)(2,1)S(1)}, bf16[1536,256]{1,0:T(8,128)(2,1)}, u32[]{:S(2)}, u32[]{:S(2)}) %collective-permute-start.9) | collective-permute-done | bytes 786464 | tf_op jit(solution)/shard_map/ppermute | solution.py:28
  51.6 5.0 %all-to-all-start.1 = ((bf16[8,1024,128]{2,1,0:T(8,128)(2,1)}), bf16[8,1024,128]{2,1,0:T(8,128)(2,1)}, u32[]{:S(2)}, u32[]{:S(2)}) async-start(bf16[8,1024,128]{2,1,0:T(8,128)(2,1)} %bitcast.28), calls=%async_computation.1 | async-start | bytes 4194304 | tf_op jit(solution)/shard_map/all_to_all | solution.py:307
  56.7 0.1 add.392
  56.8 0.1 reshape.365
  57.0 0.2 convert_reduce_fusion
  57.2 0.1 reshape.366
  57.4 0.6 gather_fusion
  58.0 0.6 gather_fusion.1
  58.5 0.1 collective-permute-start.15
  58.6 3.2 %collective-permute-start.16 = (bf16[1536,256]{1,0:T(8,128)(2,1)}, bf16[1536,256]{1,0:T(8,128)(2,1)S(1)}, u32[]{:S(2)}, u32[]{:S(2)}) collective-permute-start(bf16[1536,256]{1,0:T(8,128)(2,1)} %collective-permute-done.10.refs_5_), channel_id=1, source_target_pairs={{0,3},{1,0},{2,1},{3,2},{4,7},{5,4},{6,5},{7,6},{8,11},{9,8},{10,9... | collective-permute-start | bytes 2359304 | tf_op jit(solution)/shard_map/ppermute | solution.py:28
  61.9 0.2 select_reduce_fusion.1
  62.1 0.2 reduce_window_sum.11
  62.3 0.1 min.22
  62.4 0.1 pad_add_fusion.2.offsets
  62.5 3.4 %pack.6 = (bf16[1152,128]{1,0:T(8,128)(2,1)}, bf16[1152,128]{1,0:T(8,128)(2,1)}, bf16[1152,128]{1,0:T(8,128)(2,1)}, bf16[1152,128]{1,0:T(8,128)(2,1)}) custom-call(s32[68]{0:T(128)S(1)} %pad_add_fusion.2.offsets, bf16[8,4,2,128,128]{4,3,2,1,0:T(8,128)(2,1)} %bitcast.6.cache), custom_call_target="tpu_custom_call" | custom-call | flops 1048576 | bytes 1048576 | tf_op jit(solution)/shard_map/pack/pallas_call | solution.py:212
  65.8 3.3 %collective-permute-start.12 = (bf16[1152,128]{1,0:T(8,128)(2,1)}, bf16[1152,128]{1,0:T(8,128)(2,1)}, u32[]{:S(2)}, u32[]{:S(2)}) collective-permute-start(bf16[1152,128]{1,0:T(8,128)(2,1)} %get-tuple-element.149), channel_id=1, source_target_pairs={{0,16},{16,32},{32,48},{48,0},{1,17},{17,33},{33,49},{49,1},{2,18}... | collective-permute-start | bytes 884744 | tf_op jit(solution)/shard_map/ppermute | solution.py:28
  69.1 5.0 %collective-permute-start.13 = (bf16[1152,128]{1,0:T(8,128)(2,1)}, bf16[1152,128]{1,0:T(8,128)(2,1)}, u32[]{:S(2)}, u32[]{:S(2)}) collective-permute-start(bf16[1152,128]{1,0:T(8,128)(2,1)} %get-tuple-element.150), channel_id=1, source_target_pairs={{0,32},{16,48},{32,0},{48,16},{1,33},{17,49},{33,1},{49,17},{2,34}... | collective-permute-start | bytes 884744 | tf_op jit(solution)/shard_map/ppermute | solution.py:28
  74.1 2.7 %collective-permute-start.14 = (bf16[1152,128]{1,0:T(8,128)(2,1)}, bf16[1152,128]{1,0:T(8,128)(2,1)}, u32[]{:S(2)}, u32[]{:S(2)}) collective-permute-start(bf16[1152,128]{1,0:T(8,128)(2,1)} %get-tuple-element.151), channel_id=1, source_target_pairs={{0,48},{16,0},{32,16},{48,32},{1,49},{17,1},{33,17},{49,33},{2,50}... | collective-permute-start | bytes 884744 | tf_op jit(solution)/shard_map/ppermute | solution.py:28
  76.8 3.7 %copies.1 = bf16[4,2,128,2048]{3,2,1,0:T(8,128)(2,1)} custom-call(bf16[128,2048]{1,0:T(8,128)(2,1)} %constant_dynamic-slice_fusion.1.half, bf16[128,2048]{1,0:T(8,128)(2,1)} %collective-permute-done.11.twin), custom_call_target="tpu_custom_call" | custom-call | flops 1048576 | bytes 1048576 | tf_op jit(solution)/shard_map/copies/pallas_call | solution.py:253
  80.5 3.3 %collective-permute-done.12 = bf16[1152,128]{1,0:T(8,128)(2,1)} collective-permute-done((bf16[1152,128]{1,0:T(8,128)(2,1)}, bf16[1152,128]{1,0:T(8,128)(2,1)}, u32[]{:S(2)}, u32[]{:S(2)}) %collective-permute-start.12) | collective-permute-done | bytes 294944 | tf_op jit(solution)/shard_map/ppermute | solution.py:28
  83.8 9.3 %collective-permute-done.13 = bf16[1152,128]{1,0:T(8,128)(2,1)} collective-permute-done((bf16[1152,128]{1,0:T(8,128)(2,1)}, bf16[1152,128]{1,0:T(8,128)(2,1)}, u32[]{:S(2)}, u32[]{:S(2)}) %collective-permute-start.13) | collective-permute-done | bytes 294944 | tf_op jit(solution)/shard_map/ppermute | solution.py:28
  93.0 7.4 %collective-permute-done.14 = bf16[1152,128]{1,0:T(8,128)(2,1)} collective-permute-done((bf16[1152,128]{1,0:T(8,128)(2,1)}, bf16[1152,128]{1,0:T(8,128)(2,1)}, u32[]{:S(2)}, u32[]{:S(2)}) %collective-permute-start.14) | collective-permute-done | bytes 294944 | tf_op jit(solution)/shard_map/ppermute | solution.py:28
  100.4 3.1 %pack.7 = (bf16[1152,128]{1,0:T(8,128)(2,1)}, bf16[1152,128]{1,0:T(8,128)(2,1)S(1)}, bf16[1152,128]{1,0:T(8,128)(2,1)S(1)}, bf16[1152,128]{1,0:T(8,128)(2,1)S(1)}) custom-call(s32[68]{0:T(128)S(1)} %pad_add_fusion.2.offsets, bf16[8,4,2,128,128]{4,3,2,1,0:T(8,128)(2,1)} %bitcast.8.cache), custom_call_target="tpu_custom_call" | custom-call | flops 1048576 | bytes 1048576 | tf_op jit(solution)/shard_map/pack/pallas_call | solution.py:212
  103.6 0.7 copy-done.19
  104.3 0.7 copy-done.20
  105.1 0.7 copy-done.17
  105.8 5.1 %all-to-all-start.3 = ((bf16[4,2,128,2048]{3,2,1,0:T(8,128)(2,1)}), bf16[4,2,128,2048]{3,2,1,0:T(8,128)(2,1)}, u32[]{:S(2)}, u32[]{:S(2)}) async-start(bf16[4,2,128,2048]{3,2,1,0:T(8,128)(2,1)} %copies.1), calls=%async_computation.3 | async-start | bytes 8388608 | tf_op jit(solution)/shard_map/all_to_all | solution.py:409
  111.1 0.7 reduce_max.9
  112.6 0.4 copy.28.refs_8_
  113.0 0.1 stack.35.ids
  113.1 0.3 fusion.9
  113.4 2.8 %fusion = (f32[1536,128]{1,0:T(8,128)S(1)}, f32[1536,128]{1,0:T(8,128)S(1)}) fusion(f32[128]{0:T(128)S(1)} %get-tuple-element.188, f32[128]{0:T(128)S(1)} %get-tuple-element.189, f32[1536]{0:T(1024)S(1)} %convert_element_type.26), kind=kLoop, calls=%fused_computation.8 | loop fusion | flops 393216 | bytes 1580032 | tf_op jit(solution)/shard_map/mul | solution.py:387
  116.2 1.7 collective-permute-start.17
  117.9 4.2 %collective-permute-start.18 = (bf16[1152,128]{1,0:T(8,128)(2,1)}, bf16[1152,128]{1,0:T(8,128)(2,1)S(1)}, u32[]{:S(2)}, u32[]{:S(2)}) collective-permute-start(bf16[1152,128]{1,0:T(8,128)(2,1)} %copy-done.19), channel_id=1, source_target_pairs={{0,32},{16,48},{32,0},{48,16},{1,33},{17,49},{33,1},{49,17},{2,34}... | collective-permute-start | bytes 884744 | tf_op jit(solution)/shard_map/ppermute | solution.py:28
  122.2 2.6 %collective-permute-start.19 = (bf16[1152,128]{1,0:T(8,128)(2,1)S(1)}, bf16[1152,128]{1,0:T(8,128)(2,1)S(1)}, u32[]{:S(2)}, u32[]{:S(2)}) collective-permute-start(bf16[1152,128]{1,0:T(8,128)(2,1)S(1)} %copy-done.18), channel_id=1, source_target_pairs={{0,48},{16,0},{32,16},{48,32},{1,49},{17,1},{33,17},{49,33},{2,50}... | collective-permute-start | bytes 884744 | tf_op jit(solution)/shard_map/ppermute | solution.py:28
  124.8 0.2 select_reduce_fusion.2
  125.0 1.1 copy-done.4
  126.1 1.1 copy-done.6
  127.3 1.1 copy-done.8
  128.4 1.1 copy-done.10
  129.5 1.1 copy-done.12
  130.7 1.0 copy-done.13
  131.7 1.0 copy-done.14
  132.8 12.1 %project.1 = (bf16[1536,256]{1,0:T(8,128)(2,1)}, f32[1536,256]{1,0:T(8,128)}, bf16[1536,128]{1,0:T(8,128)(2,1)}, bf16[1536,128]{1,0:T(8,128)(2,1)}) custom-call(s32[8]{0:T(128)S(1)} %stack.35.ids, bf16[1536,256]{1,0:T(8,128)(2,1)S(1)} %copy-done.4, bf16[1536,256]{1,0:T(8,128)(2,1)S(1)} %copy-done.6, bf16[1536,256]{1,0:T(8,128)(2,1)S(1)} %copy-done.8, ...), custom_call_target="tpu_custom_call" | custom-call | flops 1048576 | bytes 1048576 | tf_op jit(solution)/shard_map/project/pallas_call | solution.py:104
  144.9 10.4 %conditional.1 = (bf16[1536,256]{1,0:T(8,128)(2,1)}) conditional(s32[]{:T(128)} %convert_element_type.23, (s32[24]{0:T(128)S(1)}, s32[24]{0:T(128)S(1)}, s32[4,16]{1,0:T(4,128)S(1)}, s32[4,16]{1,0:T(4,128)S(1)}, s32[4]{0:T(128)S(1)}, /*index=5*/bf16[8,4,2,128,128]{4,3,2,1,0:T(8,128)(2,1)}, bf16[8,4,2,128,128]{4,3,2,1,0:T(8,128)(2,1)}, ...), branch_computations={%region_6.7_spmd, %region_7.8_spmd} | conditional | flops 3146060 | bytes 28314024 | solution.py:429
  144.9 10.3 %attend.3 = bf16[1536,256]{1,0:T(8,128)(2,1)} custom-call(s32[24]{0:T(128)S(1)} %add_minimum_fusion.1.starts, s32[24]{0:T(128)S(1)} %get-tuple-element.95.lengths, bf16[1536,256]{1,0:T(8,128)(2,1)} %get-tuple-element.96.q, f32[1536,256]{1,0:T(8,128)} %get-tuple-element.97.g, bf16[1536,128]{1,0:T(8,128)(2,1)} %get-tuple-element.98.k, ...), custom_call_target="tpu_custom_call" | custom-call | flops 1048576 | bytes 1048576 | tf_op jit(solution)/shard_map/cond/branch_1_fun/attend/pallas_call | solution.py:183
  155.3 4.7 %all-to-all-done.3 = bf16[4,2,128,2048]{3,2,1,0:T(8,128)(2,1)} async-done(((bf16[4,2,128,2048]{3,2,1,0:T(8,128)(2,1)}), bf16[4,2,128,2048]{3,2,1,0:T(8,128)(2,1)}, u32[]{:S(2)}, u32[]{:S(2)}) %all-to-all-start.3) | async-done | bytes 4194336 | tf_op jit(solution)/shard_map/all_to_all | solution.py:409
  160.0 3.5 %all-to-all-start.2 = ((bf16[8,192,256]{2,1,0:T(8,128)(2,1)}), bf16[8,192,256]{2,1,0:T(8,128)(2,1)S(1)}, u32[]{:S(2)}, u32[]{:S(2)}) async-start(bf16[8,192,256]{2,1,0:T(8,128)(2,1)} %bitcast.21), calls=%async_computation.2 | async-start | bytes 1572864 | tf_op jit(solution)/shard_map/all_to_all | solution.py:430
  163.6 0.1 pad_add_fusion.1.places
  163.6 12.8 %all-to-all-done.2.heads = bf16[8,192,256]{2,1,0:T(8,128)(2,1)S(1)} async-done(((bf16[8,192,256]{2,1,0:T(8,128)(2,1)}), bf16[8,192,256]{2,1,0:T(8,128)(2,1)S(1)}, u32[]{:S(2)}, u32[]{:S(2)}) %all-to-all-start.2) | async-done | bytes 786464 | tf_op jit(solution)/shard_map/all_to_all | solution.py:430
  176.4 6.6 %project_out.1 = bf16[192,2048]{1,0:T(8,128)(2,1)} custom-call(s32[9]{0:T(128)S(1)} %pad_add_fusion.1.places, bf16[8,192,256]{2,1,0:T(8,128)(2,1)S(1)} %all-to-all-done.2.heads, bf16[8,128,2048]{2,1,0:T(8,128)(2,1)} %bitcast.22.mine, bf16[8,128,2048]{2,1,0:T(8,128)(2,1)} %collective-permute-done.20.other), custom_call_target="tpu_custom_call" | custom-call | flops 1048576 | bytes 1048576 | tf_op jit(solution)/shard_map/project_out/pallas_call | solution.py:288
  (74 shorter events, 0.9 us)
Async XLA Ops:
  0.0 32.1 %copy-start = (bf16[256,2048]{1,0:T(8,128)(2,1)S(1)}, bf16[256,2048]{1,0:T(8,128)(2,1)}, u32[]{:S(2)}) copy-start(bf16[256,2048]{1,0:T(8,128)(2,1)} %param.23) | copy-start | bytes 3145732
  3.9 6.6 %copy-start.3 = (bf16[1536,256]{1,0:T(8,128)(2,1)S(1)}, bf16[1536,256]{1,0:T(8,128)(2,1)}, u32[]{:S(2)}) copy-start(bf16[1536,256]{1,0:T(8,128)(2,1)} %refs_0_.1) | copy-start | bytes 2359300
  3.9 47.7 %all-to-all-start = ((bf16[8,1024,128]{2,1,0:T(8,128)(2,1)}), bf16[8,1024,128]{2,1,0:T(8,128)(2,1)}, u32[]{:S(2)}, u32[]{:S(2)}) async-start(bf16[8,1024,128]{2,1,0:T(8,128)(2,1)} %bitcast.29), calls=%async_computation | async-start | bytes 4194304 | tf_op jit(solution)/shard_map/all_to_all | solution.py:307
  10.5 19.6 %collective-permute-start.6 = (bf16[1536,256]{1,0:T(8,128)(2,1)S(1)}, bf16[1536,256]{1,0:T(8,128)(2,1)S(1)}, u32[]{:S(2)}, u32[]{:S(2)}) collective-permute-start(bf16[1536,256]{1,0:T(8,128)(2,1)S(1)} %copy-done.3), channel_id=1, source_target_pairs={{0,4},{4,0},{1,5},{5,1},{2,6},{6,2},{3,7},{7,3},{8,12},{12,8},{9,1... | collective-permute-start | bytes 2359304 | tf_op jit(solution)/shard_map/ppermute | solution.py:28
  10.9 27.1 %collective-permute-start.7 = (bf16[1536,256]{1,0:T(8,128)(2,1)S(1)}, bf16[1536,256]{1,0:T(8,128)(2,1)S(1)}, u32[]{:S(2)}, u32[]{:S(2)}) collective-permute-start(bf16[1536,256]{1,0:T(8,128)(2,1)S(1)} %copy-done.3), channel_id=1, source_target_pairs={{0,1},{1,2},{2,3},{3,0},{4,5},{5,6},{6,7},{7,4},{8,9},{9,10},{10,1... | collective-permute-start | bytes 2359304 | tf_op jit(solution)/shard_map/ppermute | solution.py:28
  12.4 25.6 %collective-permute-start.8 = (bf16[1536,256]{1,0:T(8,128)(2,1)S(1)}, bf16[1536,256]{1,0:T(8,128)(2,1)}, u32[]{:S(2)}, u32[]{:S(2)}) collective-permute-start(bf16[1536,256]{1,0:T(8,128)(2,1)S(1)} %copy-done.3), channel_id=1, source_target_pairs={{0,3},{1,0},{2,1},{3,2},{4,7},{5,4},{6,5},{7,6},{8,11},{9,8},{10,9... | collective-permute-start | bytes 2359304 | tf_op jit(solution)/shard_map/ppermute | solution.py:28
  30.1 7.8 %copy-start.5 = (bf16[1536,256]{1,0:T(8,128)(2,1)}, bf16[1536,256]{1,0:T(8,128)(2,1)S(1)}, u32[]{:S(2)}) copy-start(bf16[1536,256]{1,0:T(8,128)(2,1)S(1)} %collective-permute-done.6.refs_1_) | copy-start | bytes 2359300
  30.1 19.0 %collective-permute-start.10 = (bf16[1536,256]{1,0:T(8,128)(2,1)S(1)}, bf16[1536,256]{1,0:T(8,128)(2,1)}, u32[]{:S(2)}, u32[]{:S(2)}) collective-permute-start(bf16[1536,256]{1,0:T(8,128)(2,1)S(1)} %collective-permute-done.6.refs_1_), channel_id=1, source_target_pairs={{0,3},{1,0},{2,1},{3,2},{4,7},{5,4},{6,5},{7,6},{8,11},{9,8},{10,9... | collective-permute-start | bytes 2359304 | tf_op jit(solution)/shard_map/ppermute | solution.py:28
  31.5 20.1 %collective-permute-start.9 = (bf16[1536,256]{1,0:T(8,128)(2,1)S(1)}, bf16[1536,256]{1,0:T(8,128)(2,1)}, u32[]{:S(2)}, u32[]{:S(2)}) collective-permute-start(bf16[1536,256]{1,0:T(8,128)(2,1)S(1)} %collective-permute-done.6.refs_1_), channel_id=1, source_target_pairs={{0,1},{1,2},{2,3},{3,0},{4,5},{5,6},{6,7},{7,4},{8,9},{9,10},{10,1... | collective-permute-start | bytes 2359304 | tf_op jit(solution)/shard_map/ppermute | solution.py:28
  33.0 13.0 %collective-permute-start.11 = (bf16[128,2048]{1,0:T(8,128)(2,1)}, bf16[128,2048]{1,0:T(8,128)(2,1)}, u32[]{:S(2)}, u32[]{:S(2)}) collective-permute-start(bf16[128,2048]{1,0:T(8,128)(2,1)} %constant_dynamic-slice_fusion.1.half), channel_id=1, source_target_pairs={{0,4},{4,0},{1,5},{5,1},{2,6},{6,2},{3,7},{7,3},{8,12},{12,8},{9,1... | collective-permute-start | bytes 1572872 | tf_op jit(solution)/shard_map/ppermute | solution.py:28
  38.0 20.6 %copy-start.7 = (bf16[1536,256]{1,0:T(8,128)(2,1)}, bf16[1536,256]{1,0:T(8,128)(2,1)S(1)}, u32[]{:S(2)}) copy-start(bf16[1536,256]{1,0:T(8,128)(2,1)S(1)} %collective-permute-done.7.refs_2_) | copy-start | bytes 2359300
  51.6 5.2 %copy-start.27 = (s32[768,1]{0,1:T(1,128)S(1)}, s32[768,1]{0,1:T(1,128)}, u32[]{:S(2)}) copy-start(s32[768,1]{0,1:T(1,128)} %param.26) | copy-start | bytes 9220
  51.6 5.6 %copy-start.26 = (s32[768]{0:T(1024)S(1)}, s32[768]{0:T(1024)}, u32[]{:S(2)}) copy-start(s32[768]{0:T(1024)} %param.27) | copy-start | bytes 9220
  51.6 48.8 %all-to-all-start.1 = ((bf16[8,1024,128]{2,1,0:T(8,128)(2,1)}), bf16[8,1024,128]{2,1,0:T(8,128)(2,1)}, u32[]{:S(2)}, u32[]{:S(2)}) async-start(bf16[8,1024,128]{2,1,0:T(8,128)(2,1)} %bitcast.28), calls=%async_computation.1 | async-start | bytes 4194304 | tf_op jit(solution)/shard_map/all_to_all | solution.py:307
  58.5 21.9 %collective-permute-start.15 = (bf16[1536,256]{1,0:T(8,128)(2,1)S(1)}, bf16[1536,256]{1,0:T(8,128)(2,1)S(1)}, u32[]{:S(2)}, u32[]{:S(2)}) collective-permute-start(bf16[1536,256]{1,0:T(8,128)(2,1)S(1)} %collective-permute-done.7.refs_2_), channel_id=1, source_target_pairs={{0,1},{1,2},{2,3},{3,0},{4,5},{5,6},{6,7},{7,4},{8,9},{9,10},{10,1... | collective-permute-start | bytes 2359304 | tf_op jit(solution)/shard_map/ppermute | solution.py:28
  58.6 41.8 %collective-permute-start.16 = (bf16[1536,256]{1,0:T(8,128)(2,1)}, bf16[1536,256]{1,0:T(8,128)(2,1)S(1)}, u32[]{:S(2)}, u32[]{:S(2)}) collective-permute-start(bf16[1536,256]{1,0:T(8,128)(2,1)} %collective-permute-done.10.refs_5_), channel_id=1, source_target_pairs={{0,3},{1,0},{2,1},{3,2},{4,7},{5,4},{6,5},{7,6},{8,11},{9,8},{10,9... | collective-permute-start | bytes 2359304 | tf_op jit(solution)/shard_map/ppermute | solution.py:28
  65.8 17.9 %collective-permute-start.12 = (bf16[1152,128]{1,0:T(8,128)(2,1)}, bf16[1152,128]{1,0:T(8,128)(2,1)}, u32[]{:S(2)}, u32[]{:S(2)}) collective-permute-start(bf16[1152,128]{1,0:T(8,128)(2,1)} %get-tuple-element.149), channel_id=1, source_target_pairs={{0,16},{16,32},{32,48},{48,0},{1,17},{17,33},{33,49},{49,1},{2,18}... | collective-permute-start | bytes 884744 | tf_op jit(solution)/shard_map/ppermute | solution.py:28
  69.1 23.9 %collective-permute-start.13 = (bf16[1152,128]{1,0:T(8,128)(2,1)}, bf16[1152,128]{1,0:T(8,128)(2,1)}, u32[]{:S(2)}, u32[]{:S(2)}) collective-permute-start(bf16[1152,128]{1,0:T(8,128)(2,1)} %get-tuple-element.150), channel_id=1, source_target_pairs={{0,32},{16,48},{32,0},{48,16},{1,33},{17,49},{33,1},{49,17},{2,34}... | collective-permute-start | bytes 884744 | tf_op jit(solution)/shard_map/ppermute | solution.py:28
  74.1 26.3 %collective-permute-start.14 = (bf16[1152,128]{1,0:T(8,128)(2,1)}, bf16[1152,128]{1,0:T(8,128)(2,1)}, u32[]{:S(2)}, u32[]{:S(2)}) collective-permute-start(bf16[1152,128]{1,0:T(8,128)(2,1)} %get-tuple-element.151), channel_id=1, source_target_pairs={{0,48},{16,0},{32,16},{48,32},{1,49},{17,1},{33,17},{49,33},{2,50}... | collective-permute-start | bytes 884744 | tf_op jit(solution)/shard_map/ppermute | solution.py:28
  80.5 24.6 %copy-start.9 = (bf16[1536,256]{1,0:T(8,128)(2,1)}, bf16[1536,256]{1,0:T(8,128)(2,1)S(1)}, u32[]{:S(2)}) copy-start(bf16[1536,256]{1,0:T(8,128)(2,1)S(1)} %collective-permute-done.15.refs_6_) | copy-start | bytes 2359300
  100.4 4.6 %copy-start.11 = (bf16[1536,256]{1,0:T(8,128)(2,1)}, bf16[1536,256]{1,0:T(8,128)(2,1)S(1)}, u32[]{:S(2)}) copy-start(bf16[1536,256]{1,0:T(8,128)(2,1)S(1)} %collective-permute-done.16.refs_7_) | copy-start | bytes 2359300
  103.6 0.7 copy-start.19
  104.3 0.7 copy-start.20
  105.1 0.7 copy-start.17
  105.1 7.6 %copy-start.25 = (f32[2048]{0:T(1024)S(1)}, f32[2048]{0:T(1024)}, u32[]{:S(2)}) copy-start(f32[2048]{0:T(1024)} %param.16) | copy-start | bytes 24580
  105.8 54.2 %all-to-all-start.3 = ((bf16[4,2,128,2048]{3,2,1,0:T(8,128)(2,1)}), bf16[4,2,128,2048]{3,2,1,0:T(8,128)(2,1)}, u32[]{:S(2)}, u32[]{:S(2)}) async-start(bf16[4,2,128,2048]{3,2,1,0:T(8,128)(2,1)} %copies.1), calls=%async_computation.3 | async-start | bytes 8388608 | tf_op jit(solution)/shard_map/all_to_all | solution.py:409
  110.8 11.3 %copy-start.18 = (bf16[1152,128]{1,0:T(8,128)(2,1)S(1)}, bf16[1152,128]{1,0:T(8,128)(2,1)}, u32[]{:S(2)}) copy-start(bf16[1152,128]{1,0:T(8,128)(2,1)} %copy-done.17) | copy-start | bytes 884740
  110.9 14.1 %copy-start.1 = (bf16[2048,256]{1,0:T(8,128)(2,1)S(1)}, bf16[2048,256]{1,0:T(8,128)(2,1)}, u32[]{:S(2)}) copy-start(bf16[2048,256]{1,0:T(8,128)(2,1)} %refs_9_.1) | copy-start | bytes 3145732
  110.9 14.1 %copy-start.15 = (f32[128]{0:T(128)S(1)}, f32[128]{0:T(128)}, u32[]{:S(2)}) copy-start(f32[128]{0:T(128)} %param.21) | copy-start | bytes 1540
  110.9 14.1 %copy-start.16 = (f32[128]{0:T(128)S(1)}, f32[128]{0:T(128)}, u32[]{:S(2)}) copy-start(f32[128]{0:T(128)} %param.22) | copy-start | bytes 1540
  113.1 11.9 %copy-start.2 = (bf16[2048,256]{1,0:T(8,128)(2,1)S(1)}, bf16[2048,256]{1,0:T(8,128)(2,1)}, u32[]{:S(2)}) copy-start(bf16[2048,256]{1,0:T(8,128)(2,1)} %refs_10_.1) | copy-start | bytes 3145732
  116.2 28.7 %collective-permute-start.17 = (bf16[1152,128]{1,0:T(8,128)(2,1)}, bf16[1152,128]{1,0:T(8,128)(2,1)S(1)}, u32[]{:S(2)}, u32[]{:S(2)}) collective-permute-start(bf16[1152,128]{1,0:T(8,128)(2,1)} %copy-done.20), channel_id=1, source_target_pairs={{0,16},{16,32},{32,48},{48,0},{1,17},{17,33},{33,49},{49,1},{2,18}... | collective-permute-start | bytes 884744 | tf_op jit(solution)/shard_map/ppermute | solution.py:28
  117.9 27.0 %collective-permute-start.18 = (bf16[1152,128]{1,0:T(8,128)(2,1)}, bf16[1152,128]{1,0:T(8,128)(2,1)S(1)}, u32[]{:S(2)}, u32[]{:S(2)}) collective-permute-start(bf16[1152,128]{1,0:T(8,128)(2,1)} %copy-done.19), channel_id=1, source_target_pairs={{0,32},{16,48},{32,0},{48,16},{1,33},{17,49},{33,1},{49,17},{2,34}... | collective-permute-start | bytes 884744 | tf_op jit(solution)/shard_map/ppermute | solution.py:28
  122.2 22.7 %collective-permute-start.19 = (bf16[1152,128]{1,0:T(8,128)(2,1)S(1)}, bf16[1152,128]{1,0:T(8,128)(2,1)S(1)}, u32[]{:S(2)}, u32[]{:S(2)}) collective-permute-start(bf16[1152,128]{1,0:T(8,128)(2,1)S(1)} %copy-done.18), channel_id=1, source_target_pairs={{0,48},{16,0},{32,16},{48,32},{1,49},{17,1},{33,17},{49,33},{2,50}... | collective-permute-start | bytes 884744 | tf_op jit(solution)/shard_map/ppermute | solution.py:28
  125.0 1.1 copy-start.4
  126.1 1.1 copy-start.6
  127.3 1.1 copy-start.8
  128.4 1.1 copy-start.10
  129.5 1.1 copy-start.12
  130.7 1.0 copy-start.13
  131.7 1.0 copy-start.14
  160.0 16.4 %collective-permute-start.20 = (bf16[8,128,2048]{2,1,0:T(8,128)(2,1)}, bf16[8,128,2048]{2,1,0:T(8,128)(2,1)}, u32[]{:S(2)}, u32[]{:S(2)}) collective-permute-start(bf16[8,128,2048]{2,1,0:T(8,128)(2,1)} %bitcast.22.mine), channel_id=1, source_target_pairs={{0,8},{8,0},{1,9},{9,1},{2,10},{10,2},{3,11},{11,3},{4,12},{12,4},... | collective-permute-start | bytes 12582920 | tf_op jit(solution)/shard_map/ppermute | solution.py:28
  160.0 16.4 %all-to-all-start.2 = ((bf16[8,192,256]{2,1,0:T(8,128)(2,1)}), bf16[8,192,256]{2,1,0:T(8,128)(2,1)S(1)}, u32[]{:S(2)}, u32[]{:S(2)}) async-start(bf16[8,192,256]{2,1,0:T(8,128)(2,1)} %bitcast.21), calls=%async_computation.2 | async-start | bytes 1572864 | tf_op jit(solution)/shard_map/all_to_all | solution.py:430

commit v7 on v6

--- a/solution.py
+++ b/solution.py
@@ -116,7 +116,6 @@
             out_specs=[tile(wq.shape[1]), tile(wg.shape[1]), tile(head), tile(head)],
             scratch_shapes=[pltpu.VMEM((depth, columns), jnp.bfloat16)],
         ),
-        compiler_params=pltpu.CompilerParams(vmem_limit_bytes=40 << 20),
         cost_estimate=COST,
         name="project",
     )(ids, *pieces, *constants, cosine, sine)
@@ -190,7 +189,6 @@
             out_specs=tile(columns),
             scratch_shapes=[store, store],
         ),
-        compiler_params=pltpu.CompilerParams(vmem_limit_bytes=40 << 20),
         cost_estimate=COST,
         name="attend",
     )(starts, lengths, q, g, k, v, *keys, *values)
@@ -219,7 +217,6 @@
             out_specs=[pl.BlockSpec((size, head), lambda i, _: (0, 0))] * 4,
             scratch_shapes=[pltpu.VMEM((size + window, head), cache.dtype)],
         ),
-        compiler_params=pltpu.CompilerParams(vmem_limit_bytes=30 << 20),
         cost_estimate=COST,
         name="pack",
     )(offsets, cache)
@@ -295,7 +292,6 @@
             out_specs=pl.BlockSpec((rows, tile), lambda i, _: (0, i)),
             scratch_shapes=[pltpu.VMEM((rows, blocks * width), jnp.bfloat16)],
         ),
-        compiler_params=pltpu.CompilerParams(vmem_limit_bytes=30 << 20),
         cost_estimate=COST,
         name="project_out",
     )(places, heads, mine, other)
@@ -401,21 +397,21 @@
     )
     value_part = across_y(value_slots)
     keys = across_z(pack(places, key_part, PACKED))
-    repeated, value_part, keys, pieces[6:] = lax.optimization_barrier(
-        (copies(half, twin_half), value_part, keys, pieces[6:])
+    q, g, k, v = project(
+        ids, pieces, norm_gain, q_weight, gate_weight, k_weight, v_weight,
+        q_norm_gain, k_norm_gain, cosine, sine,
+    )
+    repeated, value_part, q = lax.optimization_barrier(
+        (copies(half, twin_half), value_part, q)
     )
     packed_values = pack(places, value_part, PACKED)
-    repeated, packed_values = lax.optimization_barrier((repeated, packed_values))
+    repeated, packed_values, keys[1], keys[3] = lax.optimization_barrier(
+        (repeated, packed_values, keys[1], keys[3])
+    )
+    values = across_z(packed_values)
     halves = lax.all_to_all(repeated, "x", 0, 0, tiled=True)
     halves = halves.reshape((blocks,) + half.shape)
     other_halves = shift(halves, "c", 1)
-
-    values = across_z(packed_values)
-
-    q, g, k, v = project(
-        ids, pieces, norm_gain, q_weight, gate_weight, k_weight, v_weight,
-        q_norm_gain, k_norm_gain, cosine, sine,
-    )
 
     def packed(keys, values, key_part, value_part, q, g, k, v):
         return attend(starts, my_lengths, q, g, k, v, keys, values, window)

time: 185 us -> 198 us (1.070)
  other arithmetic: 5.07 us -> 12.7 us
  waiting for transfers between devices: 67 us -> 74 us
  local copies, waits for them, and re-layouts: 13.1 us -> 9.87 us
    ppermute x15, waiting for transfers between devices: 49.5 us -> 62 us  [shift(): return lax.ppermute(value, axis, ring(lax.axis_size(axis), step))]
    unnamed x48 -> x20, local copies, waits for them, and re-layouts: 9.97 us -> 1.9 us
    all_to_all x1, waiting for transfers between devices: 4.73 us -> 0.01 us  [local(): halves = lax.all_to_all(repeated, 'x', 0, 0, tiled=True)]
    pallas_call x1, Pallas kernels: 12.1 us -> 14.2 us  [project(): pl.pallas_call(project_kernel, out_shape=(jax.ShapeDtypeStruct((rows, wq....]
  transfers between devices with their start and end apart: 19 -> 19, of which waited for: 9 -> 10; matrix products, arithmetic and copies ran while one was open for 4% -> 11% of each run, Pallas kernels for 18% -> 19%
where the time goes in v7:
time: 198 us; the launch traced here: 196 us
  waiting for transfers between devices  74 us (37%)
  starting transfers between devices  50 us (25%)
  Pallas kernels  48.7 us (25%)
  other arithmetic  12.7 us (6%)
  local copies, waits for them, and re-layouts  9.87 us (5%)
    ppermute x15, waiting for transfers between devices, shift(): return lax.ppermute(value, axis, ring(lax.axis_size(axis), step))  62 us
    ppermute x15, starting transfers between devices, shift(): return lax.ppermute(value, axis, ring(lax.axis_size(axis), step))  29.7 us
    pallas_call x1, Pallas kernels, project(): pl.pallas_call(project_kernel, out_shape=(jax.ShapeDtypeStruct((rows, wq....  14.2 us
    all_to_all x1, waiting for transfers between devices, local(): lax.all_to_all(attended.reshape(blocks, rows // blocks, attended.shape[1]...  12 us
    all_to_all x2, starting transfers between devices, across_y(): flat = lax.all_to_all(flat, ('y', 'c'), 0, 0, tiled=True)  10.9 us
    pallas_call x1, Pallas kernels, attend(): pl.pallas_call(attend_kernel, out_shape=jax.ShapeDtypeStruct((rows, colum...  10.7 us
    pallas_call x2, Pallas kernels, by_target(): pl.pallas_call(by_target_kernel, out_shape=jax.ShapeDtypeStruct((ny, nc,...  7.69 us
    pallas_call x1, Pallas kernels, project_out(): pl.pallas_call(output_kernel, out_shape=jax.ShapeDtypeStruct((rows, colum...  7 us
  transfers between devices with their start and end apart: 19, of which 10 were waited for; matrix products, arithmetic and copies ran while one was open for 11% of the time, Pallas kernels for 19%

profile of v7, /device:TPU:8, one launch (start us, length us, event | category | flops | bytes accessed | tf_op | source)
XLA Modules:
  0.0 196.1 jit_solution(10694144772976483766)
XLA Ops:
  0.0 3.9 %by_target.3 = bf16[4,2,4,2,128,128]{5,4,3,2,1,0:T(8,128)(2,1)} custom-call(bf16[4,4,2,2,128,128]{5,4,3,2,1,0:T(8,128)(2,1)} %bitcast.30), custom_call_target="tpu_custom_call" | custom-call | flops 1048576 | bytes 1048576 | tf_op jit(solution)/shard_map/by_target/pallas_call | solution.py:232
  3.9 5.8 %all-to-all-start = ((bf16[8,1024,128]{2,1,0:T(8,128)(2,1)}), bf16[8,1024,128]{2,1,0:T(8,128)(2,1)S(1)}, u32[]{:S(2)}, u32[]{:S(2)}) async-start(bf16[8,1024,128]{2,1,0:T(8,128)(2,1)} %bitcast.28), calls=%async_computation | async-start | bytes 4194304 | tf_op jit(solution)/shard_map/all_to_all | solution.py:303
  9.7 1.1 collective-permute-start.6
  10.9 1.5 collective-permute-start.7
  12.3 1.7 collective-permute-start.8
  14.2 0.1 add.394
  14.4 0.1 reshape.365
  14.5 15.1 %collective-permute-done.6.refs_1_ = bf16[1536,256]{1,0:T(8,128)(2,1)} collective-permute-done((bf16[1536,256]{1,0:T(8,128)(2,1)}, bf16[1536,256]{1,0:T(8,128)(2,1)}, u32[]{:S(2)}, u32[]{:S(2)}) %collective-permute-start.6) | collective-permute-done | bytes 786464 | tf_op jit(solution)/shard_map/ppermute | solution.py:28
  29.6 2.2 %collective-permute-start.10 = (bf16[1536,256]{1,0:T(8,128)(2,1)}, bf16[1536,256]{1,0:T(8,128)(2,1)}, u32[]{:S(2)}, u32[]{:S(2)}) collective-permute-start(bf16[1536,256]{1,0:T(8,128)(2,1)} %collective-permute-done.6.refs_1_), channel_id=1, source_target_pairs={{0,3},{1,0},{2,1},{3,2},{4,7},{5,4},{6,5},{7,6},{8,11},{9,8},{10,9... | collective-permute-start | bytes 2359304 | tf_op jit(solution)/shard_map/ppermute | solution.py:28
  31.8 0.9 constant_dynamic-slice_fusion.1.half
  32.6 1.7 collective-permute-start.11
  34.4 0.2 convert_reduce_fusion
  34.6 0.1 reshape.366
  34.7 3.8 %by_target.2 = bf16[4,2,4,2,128,128]{5,4,3,2,1,0:T(8,128)(2,1)} custom-call(bf16[4,4,2,2,128,128]{5,4,3,2,1,0:T(8,128)(2,1)} %bitcast.31), custom_call_target="tpu_custom_call" | custom-call | flops 1048576 | bytes 1048576 | tf_op jit(solution)/shard_map/by_target/pallas_call | solution.py:232
  38.6 0.6 multiply_add_fusion
  39.2 6.8 %collective-permute-done.11.twin = bf16[128,2048]{1,0:T(8,128)(2,1)} collective-permute-done((bf16[128,2048]{1,0:T(8,128)(2,1)}, bf16[128,2048]{1,0:T(8,128)(2,1)}, u32[]{:S(2)}, u32[]{:S(2)}) %collective-permute-start.11) | collective-permute-done | bytes 524320 | tf_op jit(solution)/shard_map/ppermute | solution.py:28
  46.0 2.7 %collective-permute-done.10.refs_5_ = bf16[1536,256]{1,0:T(8,128)(2,1)} collective-permute-done((bf16[1536,256]{1,0:T(8,128)(2,1)}, bf16[1536,256]{1,0:T(8,128)(2,1)}, u32[]{:S(2)}, u32[]{:S(2)}) %collective-permute-start.10) | collective-permute-done | bytes 786464 | tf_op jit(solution)/shard_map/ppermute | solution.py:28
  48.7 3.3 %collective-permute-done.9.refs_4_ = bf16[1536,256]{1,0:T(8,128)(2,1)} collective-permute-done((bf16[1536,256]{1,0:T(8,128)(2,1)}, bf16[1536,256]{1,0:T(8,128)(2,1)}, u32[]{:S(2)}, u32[]{:S(2)}) %collective-permute-start.9) | collective-permute-done | bytes 786464 | tf_op jit(solution)/shard_map/ppermute | solution.py:28
  52.0 5.0 %all-to-all-start.1 = ((bf16[8,1024,128]{2,1,0:T(8,128)(2,1)}), bf16[8,1024,128]{2,1,0:T(8,128)(2,1)}, u32[]{:S(2)}, u32[]{:S(2)}) async-start(bf16[8,1024,128]{2,1,0:T(8,128)(2,1)} %bitcast.29), calls=%async_computation.1 | async-start | bytes 4194304 | tf_op jit(solution)/shard_map/all_to_all | solution.py:303
  57.0 0.6 gather_fusion
  57.6 0.6 gather_fusion.1
  58.2 0.2 select_reduce_fusion.1
  58.4 0.2 reduce_window_sum.11
  58.6 0.1 min.22
  58.7 0.5 copy-done.7
  59.3 1.4 copy.28.refs_8_
  60.7 0.6 stack.35.ids
  61.3 3.2 %collective-permute-start.13 = (bf16[1536,256]{1,0:T(8,128)(2,1)}, bf16[1536,256]{1,0:T(8,128)(2,1)}, u32[]{:S(2)}, u32[]{:S(2)}) collective-permute-start(bf16[1536,256]{1,0:T(8,128)(2,1)} %collective-permute-done.10.refs_5_), channel_id=1, source_target_pairs={{0,3},{1,0},{2,1},{3,2},{4,7},{5,4},{6,5},{7,6},{8,11},{9,8},{10,9... | collective-permute-start | bytes 2359304 | tf_op jit(solution)/shard_map/ppermute | solution.py:28
  64.5 0.5 copy-done.13
  65.1 0.6 pad_add_fusion.2.offsets
  65.6 1.9 pack.6
  67.6 3.3 %collective-permute-start.14 = (bf16[1152,128]{1,0:T(8,128)(2,1)}, bf16[1152,128]{1,0:T(8,128)(2,1)}, u32[]{:S(2)}, u32[]{:S(2)}) collective-permute-start(bf16[1152,128]{1,0:T(8,128)(2,1)} %get-tuple-element.162), channel_id=1, source_target_pairs={{0,16},{16,32},{32,48},{48,0},{1,17},{17,33},{33,49},{49,1},{2,18}... | collective-permute-start | bytes 884744 | tf_op jit(solution)/shard_map/ppermute | solution.py:28
  70.8 2.8 %collective-permute-start.15 = (bf16[1152,128]{1,0:T(8,128)(2,1)}, bf16[1152,128]{1,0:T(8,128)(2,1)}, u32[]{:S(2)}, u32[]{:S(2)}) collective-permute-start(bf16[1152,128]{1,0:T(8,128)(2,1)} %get-tuple-element.163), channel_id=1, source_target_pairs={{0,48},{16,0},{32,16},{48,32},{1,49},{17,1},{33,17},{49,33},{2,50}... | collective-permute-start | bytes 884744 | tf_op jit(solution)/shard_map/ppermute | solution.py:28
  73.6 4.3 %fusion = (f32[1536,128]{1,0:T(8,128)}, f32[1536,128]{1,0:T(8,128)}) fusion(f32[128]{0:T(128)S(1)} %get-tuple-element.182, f32[128]{0:T(128)S(1)} %get-tuple-element.183, f32[1536]{0:T(1024)S(1)} %convert_element_type.26), kind=kLoop, calls=%fused_computation.8 | loop fusion | flops 393216 | bytes 1580032 | tf_op jit(solution)/shard_map/mul | solution.py:383
  77.9 3.7 %copies.1 = bf16[4,2,128,2048]{3,2,1,0:T(8,128)(2,1)} custom-call(bf16[128,2048]{1,0:T(8,128)(2,1)} %constant_dynamic-slice_fusion.1.half, bf16[128,2048]{1,0:T(8,128)(2,1)} %collective-permute-done.11.twin), custom_call_target="tpu_custom_call" | custom-call | flops 1048576 | bytes 1048576 | tf_op jit(solution)/shard_map/copies/pallas_call | solution.py:250
  81.6 0.8 collective-permute-done.12.refs_6_
  82.4 14.2 %project.1 = (bf16[1536,256]{1,0:T(8,128)(2,1)}, f32[1536,256]{1,0:T(8,128)}, bf16[1536,128]{1,0:T(8,128)(2,1)S(1)}, bf16[1536,128]{1,0:T(8,128)(2,1)}) custom-call(s32[8]{0:T(128)} %stack.35.ids, bf16[1536,256]{1,0:T(8,128)(2,1)} %refs_0_.1, bf16[1536,256]{1,0:T(8,128)(2,1)} %collective-permute-done.6.refs_1_, ...), custom_call_target="tpu_custom_call" | custom-call | flops 1048576 | bytes 1048576 | tf_op jit(solution)/shard_map/project/pallas_call | solution.py:104
  96.6 3.4 %pack.7 = (bf16[1152,128]{1,0:T(8,128)(2,1)}, bf16[1152,128]{1,0:T(8,128)(2,1)}, bf16[1152,128]{1,0:T(8,128)(2,1)}, bf16[1152,128]{1,0:T(8,128)(2,1)}) custom-call(s32[68]{0:T(128)} %pad_add_fusion.2.offsets, bf16[8,4,2,128,128]{4,3,2,1,0:T(8,128)(2,1)} %bitcast.8.cache), custom_call_target="tpu_custom_call" | custom-call | flops 1048576 | bytes 1048576 | tf_op jit(solution)/shard_map/pack/pallas_call | solution.py:210
  100.1 4.9 %all-to-all-start.3 = ((bf16[4,2,128,2048]{3,2,1,0:T(8,128)(2,1)}), bf16[4,2,128,2048]{3,2,1,0:T(8,128)(2,1)}, u32[]{:S(2)}, u32[]{:S(2)}) async-start(bf16[4,2,128,2048]{3,2,1,0:T(8,128)(2,1)} %copies.1), calls=%async_computation.3 | async-start | bytes 8388608 | tf_op jit(solution)/shard_map/all_to_all | solution.py:412
  104.9 1.4 copy.23
  106.3 1.4 copy.22
  107.7 1.3 select_reduce_fusion
  109.0 1.4 reduce_max.9
  111.1 1.0 fusion.9
  112.1 0.7 fusion.22
  112.8 7.0 %collective-permute-start.16 = (bf16[1152,128]{1,0:T(8,128)(2,1)}, bf16[1152,128]{1,0:T(8,128)(2,1)}, u32[]{:S(2)}, u32[]{:S(2)}) collective-permute-start(bf16[1152,128]{1,0:T(8,128)(2,1)} %get-tuple-element.165), channel_id=1, source_target_pairs={{0,32},{16,48},{32,0},{48,16},{1,33},{17,49},{33,1},{49,17},{2,34}... | collective-permute-start | bytes 884744 | tf_op jit(solution)/shard_map/ppermute | solution.py:28
  119.8 1.5 collective-permute-start.17
  121.3 0.8 collective-permute-start.18
  122.1 2.8 %collective-permute-start.19 = (bf16[1152,128]{1,0:T(8,128)(2,1)}, bf16[1152,128]{1,0:T(8,128)(2,1)}, u32[]{:S(2)}, u32[]{:S(2)}) collective-permute-start(bf16[1152,128]{1,0:T(8,128)(2,1)} %get-tuple-element.170), channel_id=1, source_target_pairs={{0,48},{16,0},{32,16},{48,32},{1,49},{17,1},{33,17},{49,33},{2,50}... | collective-permute-start | bytes 884744 | tf_op jit(solution)/shard_map/ppermute | solution.py:28
  124.8 0.2 select_reduce_fusion.2
  125.0 0.6 broadcast_multiply_fusion
  125.6 9.3 %collective-permute-done.16 = bf16[1152,128]{1,0:T(8,128)(2,1)} collective-permute-done((bf16[1152,128]{1,0:T(8,128)(2,1)}, bf16[1152,128]{1,0:T(8,128)(2,1)}, u32[]{:S(2)}, u32[]{:S(2)}) %collective-permute-start.16) | collective-permute-done | bytes 294944 | tf_op jit(solution)/shard_map/ppermute | solution.py:28
  134.9 9.8 %collective-permute-done.17 = bf16[1152,128]{1,0:T(8,128)(2,1)} collective-permute-done((bf16[1152,128]{1,0:T(8,128)(2,1)}, bf16[1152,128]{1,0:T(8,128)(2,1)}, u32[]{:S(2)}, u32[]{:S(2)}) %collective-permute-start.17) | collective-permute-done | bytes 294944 | tf_op jit(solution)/shard_map/ppermute | solution.py:28
  144.7 12.5 %collective-permute-done.18 = bf16[1152,128]{1,0:T(8,128)(2,1)} collective-permute-done((bf16[1152,128]{1,0:T(8,128)(2,1)}, bf16[1152,128]{1,0:T(8,128)(2,1)}, u32[]{:S(2)}, u32[]{:S(2)}) %collective-permute-start.18) | collective-permute-done | bytes 294944 | tf_op jit(solution)/shard_map/ppermute | solution.py:28
  157.2 1.7 collective-permute-done.19
  158.9 12.0 %conditional.1 = (bf16[1536,256]{1,0:T(8,128)(2,1)}) conditional(s32[]{:T(128)} %convert_element_type.23, (s32[24]{0:T(128)S(1)}, s32[24]{0:T(128)}, s32[4,16]{1,0:T(4,128)}, s32[4,16]{1,0:T(4,128)S(1)}, s32[4]{0:T(128)}, /*index=5*/bf16[8,4,2,128,128]{4,3,2,1,0:T(8,128)(2,1)S(1)}, bf16[8,4,2,128,128]{4,3,2,1,0:T(8,128)(2,1)}, s32[24]{0:T(128)}, ...), branch_computations={%region_6.7_spmd, %region_7.8_spmd} | conditional | flops 3146060 | bytes 22023364 | solution.py:425
  158.9 1.3 add_minimum_fusion.1.starts
  160.1 10.7 %attend.3 = bf16[1536,256]{1,0:T(8,128)(2,1)} custom-call(s32[24]{0:T(128)} %add_minimum_fusion.1.starts, s32[24]{0:T(128)} %get-tuple-element.95.lengths, bf16[1536,256]{1,0:T(8,128)(2,1)} %get-tuple-element.96.q, f32[1536,256]{1,0:T(8,128)} %get-tuple-element.97.g, bf16[1536,128]{1,0:T(8,128)(2,1)S(1)} %get-tuple-element.98.k, ...), custom_call_target="tpu_custom_call" | custom-call | flops 1048576 | bytes 1048576 | tf_op jit(solution)/shard_map/cond/branch_1_fun/attend/pallas_call | solution.py:182
  170.9 0.1 collective-permute-start.20
  171.0 4.6 %all-to-all-start.2 = ((bf16[8,192,256]{2,1,0:T(8,128)(2,1)}), bf16[8,192,256]{2,1,0:T(8,128)(2,1)S(1)}, u32[]{:S(2)}, u32[]{:S(2)}) async-start(bf16[8,192,256]{2,1,0:T(8,128)(2,1)} %bitcast.21), calls=%async_computation.2 | async-start | bytes 1572864 | tf_op jit(solution)/shard_map/all_to_all | solution.py:426
  175.6 0.6 pad_add_fusion.1.places
  176.2 12.0 %all-to-all-done.2.heads = bf16[8,192,256]{2,1,0:T(8,128)(2,1)S(1)} async-done(((bf16[8,192,256]{2,1,0:T(8,128)(2,1)}), bf16[8,192,256]{2,1,0:T(8,128)(2,1)S(1)}, u32[]{:S(2)}, u32[]{:S(2)}) %all-to-all-start.2) | async-done | bytes 786464 | tf_op jit(solution)/shard_map/all_to_all | solution.py:426
  188.2 0.9 copy-done.1
  189.1 7.0 %project_out.1 = bf16[192,2048]{1,0:T(8,128)(2,1)} custom-call(s32[9]{0:T(128)} %pad_add_fusion.1.places, bf16[8,192,256]{2,1,0:T(8,128)(2,1)} %copy-done.1, bf16[8,128,2048]{2,1,0:T(8,128)(2,1)} %bitcast.22.mine, bf16[8,128,2048]{2,1,0:T(8,128)(2,1)} %collective-permute-done.20.other), custom_call_target="tpu_custom_call" | custom-call | flops 1048576 | bytes 1048576 | tf_op jit(solution)/shard_map/project_out/pallas_call | solution.py:285
  (46 shorter events, 0.6 us)
Async XLA Ops:
  0.0 31.8 %copy-start = (bf16[256,2048]{1,0:T(8,128)(2,1)S(1)}, bf16[256,2048]{1,0:T(8,128)(2,1)}, u32[]{:S(2)}) copy-start(bf16[256,2048]{1,0:T(8,128)(2,1)} %param.23) | copy-start | bytes 3145732
  3.9 10.5 %copy-start.12 = (s32[768,1]{0,1:T(1,128)S(1)}, s32[768,1]{0,1:T(1,128)}, u32[]{:S(2)}) copy-start(s32[768,1]{0,1:T(1,128)} %param.26) | copy-start | bytes 9220
  3.9 30.8 %copy-start.11 = (s32[768]{0:T(1024)S(1)}, s32[768]{0:T(1024)}, u32[]{:S(2)}) copy-start(s32[768]{0:T(1024)} %param.27) | copy-start | bytes 9220
  3.9 48.1 %all-to-all-start = ((bf16[8,1024,128]{2,1,0:T(8,128)(2,1)}), bf16[8,1024,128]{2,1,0:T(8,128)(2,1)S(1)}, u32[]{:S(2)}, u32[]{:S(2)}) async-start(bf16[8,1024,128]{2,1,0:T(8,128)(2,1)} %bitcast.28), calls=%async_computation | async-start | bytes 4194304 | tf_op jit(solution)/shard_map/all_to_all | solution.py:303
  9.7 19.9 %collective-permute-start.6 = (bf16[1536,256]{1,0:T(8,128)(2,1)}, bf16[1536,256]{1,0:T(8,128)(2,1)}, u32[]{:S(2)}, u32[]{:S(2)}) collective-permute-start(bf16[1536,256]{1,0:T(8,128)(2,1)} %refs_0_.1), channel_id=1, source_target_pairs={{0,4},{4,0},{1,5},{5,1},{2,6},{6,2},{3,7},{7,3},{8,12},{12,8},{9,1... | collective-permute-start | bytes 2359304 | tf_op jit(solution)/shard_map/ppermute | solution.py:28
  10.9 28.3 %collective-permute-start.7 = (bf16[1536,256]{1,0:T(8,128)(2,1)}, bf16[1536,256]{1,0:T(8,128)(2,1)}, u32[]{:S(2)}, u32[]{:S(2)}) collective-permute-start(bf16[1536,256]{1,0:T(8,128)(2,1)} %refs_0_.1), channel_id=1, source_target_pairs={{0,1},{1,2},{2,3},{3,0},{4,5},{5,6},{6,7},{7,4},{8,9},{9,10},{10,1... | collective-permute-start | bytes 2359304 | tf_op jit(solution)/shard_map/ppermute | solution.py:28
  12.3 26.9 %collective-permute-start.8 = (bf16[1536,256]{1,0:T(8,128)(2,1)}, bf16[1536,256]{1,0:T(8,128)(2,1)}, u32[]{:S(2)}, u32[]{:S(2)}) collective-permute-start(bf16[1536,256]{1,0:T(8,128)(2,1)} %refs_0_.1), channel_id=1, source_target_pairs={{0,3},{1,0},{2,1},{3,2},{4,7},{5,4},{6,5},{7,6},{8,11},{9,8},{10,9... | collective-permute-start | bytes 2359304 | tf_op jit(solution)/shard_map/ppermute | solution.py:28
  29.6 19.1 %collective-permute-start.10 = (bf16[1536,256]{1,0:T(8,128)(2,1)}, bf16[1536,256]{1,0:T(8,128)(2,1)}, u32[]{:S(2)}, u32[]{:S(2)}) collective-permute-start(bf16[1536,256]{1,0:T(8,128)(2,1)} %collective-permute-done.6.refs_1_), channel_id=1, source_target_pairs={{0,3},{1,0},{2,1},{3,2},{4,7},{5,4},{6,5},{7,6},{8,11},{9,8},{10,9... | collective-permute-start | bytes 2359304 | tf_op jit(solution)/shard_map/ppermute | solution.py:28
  31.8 20.2 %collective-permute-start.9 = (bf16[1536,256]{1,0:T(8,128)(2,1)}, bf16[1536,256]{1,0:T(8,128)(2,1)}, u32[]{:S(2)}, u32[]{:S(2)}) collective-permute-start(bf16[1536,256]{1,0:T(8,128)(2,1)} %collective-permute-done.6.refs_1_), channel_id=1, source_target_pairs={{0,1},{1,2},{2,3},{3,0},{4,5},{5,6},{6,7},{7,4},{8,9},{9,10},{10,1... | collective-permute-start | bytes 2359304 | tf_op jit(solution)/shard_map/ppermute | solution.py:28
  32.6 13.4 %collective-permute-start.11 = (bf16[128,2048]{1,0:T(8,128)(2,1)}, bf16[128,2048]{1,0:T(8,128)(2,1)}, u32[]{:S(2)}, u32[]{:S(2)}) collective-permute-start(bf16[128,2048]{1,0:T(8,128)(2,1)} %constant_dynamic-slice_fusion.1.half), channel_id=1, source_target_pairs={{0,4},{4,0},{1,5},{5,1},{2,6},{6,2},{3,7},{7,3},{8,12},{12,8},{9,1... | collective-permute-start | bytes 1572872 | tf_op jit(solution)/shard_map/ppermute | solution.py:28
  34.6 4.0 %copy-start.6 = (s32[32,24]{0,1:T(8,128)}, s32[32,24]{0,1:T(8,128)S(1)}, u32[]{:S(2)}) copy-start(s32[32,24]{0,1:T(8,128)S(1)} %convert_reduce_fusion) | copy-start | bytes 9220
  52.0 7.3 %copy-start.8 = (f32[2048]{0:T(1024)S(1)}, f32[2048]{0:T(1024)}, u32[]{:S(2)}) copy-start(f32[2048]{0:T(1024)} %param.16) | copy-start | bytes 24580
  52.0 44.6 %all-to-all-start.1 = ((bf16[8,1024,128]{2,1,0:T(8,128)(2,1)}), bf16[8,1024,128]{2,1,0:T(8,128)(2,1)}, u32[]{:S(2)}, u32[]{:S(2)}) async-start(bf16[8,1024,128]{2,1,0:T(8,128)(2,1)} %bitcast.29), calls=%async_computation.1 | async-start | bytes 4194304 | tf_op jit(solution)/shard_map/all_to_all | solution.py:303
  57.6 20.3 %copy-start.5 = (s32[32,24]{1,0:T(8,128)}, s32[32,24]{1,0:T(8,128)S(1)}, u32[]{:S(2)}) copy-start(s32[32,24]{1,0:T(8,128)S(1)} %add_select_fusion) | copy-start | bytes 9220
  58.6 0.6 copy-start.7
  59.2 18.7 %copy-start.9 = (s32[24]{0:T(128)}, s32[24]{0:T(128)S(1)}, u32[]{:S(2)}) copy-start(s32[24]{0:T(128)S(1)} %fusion.23) | copy-start | bytes 292
  61.3 21.1 %collective-permute-start.12 = (bf16[1536,256]{1,0:T(8,128)(2,1)}, bf16[1536,256]{1,0:T(8,128)(2,1)}, u32[]{:S(2)}, u32[]{:S(2)}) collective-permute-start(bf16[1536,256]{1,0:T(8,128)(2,1)} %collective-permute-done.7.refs_2_), channel_id=1, source_target_pairs={{0,1},{1,2},{2,3},{3,0},{4,5},{5,6},{6,7},{7,4},{8,9},{9,10},{10,1... | collective-permute-start | bytes 2359304 | tf_op jit(solution)/shard_map/ppermute | solution.py:28
  61.3 21.1 %collective-permute-start.13 = (bf16[1536,256]{1,0:T(8,128)(2,1)}, bf16[1536,256]{1,0:T(8,128)(2,1)}, u32[]{:S(2)}, u32[]{:S(2)}) collective-permute-start(bf16[1536,256]{1,0:T(8,128)(2,1)} %collective-permute-done.10.refs_5_), channel_id=1, source_target_pairs={{0,3},{1,0},{2,1},{3,2},{4,7},{5,4},{6,5},{7,6},{8,11},{9,8},{10,9... | collective-permute-start | bytes 2359304 | tf_op jit(solution)/shard_map/ppermute | solution.py:28
  64.5 0.5 copy-start.13
  67.6 32.5 %collective-permute-start.14 = (bf16[1152,128]{1,0:T(8,128)(2,1)}, bf16[1152,128]{1,0:T(8,128)(2,1)}, u32[]{:S(2)}, u32[]{:S(2)}) collective-permute-start(bf16[1152,128]{1,0:T(8,128)(2,1)} %get-tuple-element.162), channel_id=1, source_target_pairs={{0,16},{16,32},{32,48},{48,0},{1,17},{17,33},{33,49},{49,1},{2,18}... | collective-permute-start | bytes 884744 | tf_op jit(solution)/shard_map/ppermute | solution.py:28
  70.8 29.2 %collective-permute-start.15 = (bf16[1152,128]{1,0:T(8,128)(2,1)}, bf16[1152,128]{1,0:T(8,128)(2,1)}, u32[]{:S(2)}, u32[]{:S(2)}) collective-permute-start(bf16[1152,128]{1,0:T(8,128)(2,1)} %get-tuple-element.163), channel_id=1, source_target_pairs={{0,48},{16,0},{32,16},{48,32},{1,49},{17,1},{33,17},{49,33},{2,50}... | collective-permute-start | bytes 884744 | tf_op jit(solution)/shard_map/ppermute | solution.py:28
  100.1 70.8 %all-to-all-start.3 = ((bf16[4,2,128,2048]{3,2,1,0:T(8,128)(2,1)}), bf16[4,2,128,2048]{3,2,1,0:T(8,128)(2,1)}, u32[]{:S(2)}, u32[]{:S(2)}) async-start(bf16[4,2,128,2048]{3,2,1,0:T(8,128)(2,1)} %copies.1), calls=%async_computation.3 | async-start | bytes 8388608 | tf_op jit(solution)/shard_map/all_to_all | solution.py:412
  112.8 22.1 %collective-permute-start.16 = (bf16[1152,128]{1,0:T(8,128)(2,1)}, bf16[1152,128]{1,0:T(8,128)(2,1)}, u32[]{:S(2)}, u32[]{:S(2)}) collective-permute-start(bf16[1152,128]{1,0:T(8,128)(2,1)} %get-tuple-element.165), channel_id=1, source_target_pairs={{0,32},{16,48},{32,0},{48,16},{1,33},{17,49},{33,1},{49,17},{2,34}... | collective-permute-start | bytes 884744 | tf_op jit(solution)/shard_map/ppermute | solution.py:28
  119.8 24.9 %collective-permute-start.17 = (bf16[1152,128]{1,0:T(8,128)(2,1)}, bf16[1152,128]{1,0:T(8,128)(2,1)}, u32[]{:S(2)}, u32[]{:S(2)}) collective-permute-start(bf16[1152,128]{1,0:T(8,128)(2,1)} %get-tuple-element.168), channel_id=1, source_target_pairs={{0,16},{16,32},{32,48},{48,0},{1,17},{17,33},{33,49},{49,1},{2,18}... | collective-permute-start | bytes 884744 | tf_op jit(solution)/shard_map/ppermute | solution.py:28
  121.3 35.9 %collective-permute-start.18 = (bf16[1152,128]{1,0:T(8,128)(2,1)}, bf16[1152,128]{1,0:T(8,128)(2,1)}, u32[]{:S(2)}, u32[]{:S(2)}) collective-permute-start(bf16[1152,128]{1,0:T(8,128)(2,1)} %get-tuple-element.169), channel_id=1, source_target_pairs={{0,32},{16,48},{32,0},{48,16},{1,33},{17,49},{33,1},{49,17},{2,34}... | collective-permute-start | bytes 884744 | tf_op jit(solution)/shard_map/ppermute | solution.py:28
  122.1 36.8 %collective-permute-start.19 = (bf16[1152,128]{1,0:T(8,128)(2,1)}, bf16[1152,128]{1,0:T(8,128)(2,1)}, u32[]{:S(2)}, u32[]{:S(2)}) collective-permute-start(bf16[1152,128]{1,0:T(8,128)(2,1)} %get-tuple-element.170), channel_id=1, source_target_pairs={{0,48},{16,0},{32,16},{48,32},{1,49},{17,1},{33,17},{49,33},{2,50}... | collective-permute-start | bytes 884744 | tf_op jit(solution)/shard_map/ppermute | solution.py:28
  170.9 17.3 %collective-permute-start.20 = (bf16[8,128,2048]{2,1,0:T(8,128)(2,1)}, bf16[8,128,2048]{2,1,0:T(8,128)(2,1)}, u32[]{:S(2)}, u32[]{:S(2)}) collective-permute-start(bf16[8,128,2048]{2,1,0:T(8,128)(2,1)} %bitcast.22.mine), channel_id=1, source_target_pairs={{0,8},{8,0},{1,9},{9,1},{2,10},{10,2},{3,11},{11,3},{4,12},{12,4},... | collective-permute-start | bytes 12582920 | tf_op jit(solution)/shard_map/ppermute | solution.py:28
  171.0 17.2 %all-to-all-start.2 = ((bf16[8,192,256]{2,1,0:T(8,128)(2,1)}), bf16[8,192,256]{2,1,0:T(8,128)(2,1)S(1)}, u32[]{:S(2)}, u32[]{:S(2)}) async-start(bf16[8,192,256]{2,1,0:T(8,128)(2,1)} %bitcast.21), calls=%async_computation.2 | async-start | bytes 1572864 | tf_op jit(solution)/shard_map/all_to_all | solution.py:426
  188.2 0.9 copy-start.1

commit v8 on v7

--- a/solution.py
+++ b/solution.py
@@ -16,7 +16,8 @@
 ROW_TILE = 256
 BATCH = 4
 UNIT = 16
-PACKED = 72 * UNIT
+PACKED = 68 * UNIT
+LONG = pl.CostEstimate(flops=1 << 20, bytes_accessed=64 << 20, transcendentals=0)
 COST = pl.CostEstimate(flops=1 << 20, bytes_accessed=1 << 20, transcendentals=0)
 
 
@@ -189,6 +190,7 @@
             out_specs=tile(columns),
             scratch_shapes=[store, store],
         ),
+        compiler_params=pltpu.CompilerParams(vmem_limit_bytes=30 << 20),
         cost_estimate=COST,
         name="attend",
     )(starts, lengths, q, g, k, v, *keys, *values)
@@ -217,6 +219,7 @@
             out_specs=[pl.BlockSpec((size, head), lambda i, _: (0, 0))] * 4,
             scratch_shapes=[pltpu.VMEM((size + window, head), cache.dtype)],
         ),
+        compiler_params=pltpu.CompilerParams(vmem_limit_bytes=16 << 20),
         cost_estimate=COST,
         name="pack",
     )(offsets, cache)
@@ -235,7 +238,8 @@
         grid=(ny,),
         in_specs=[pl.BlockSpec((1, nz, nc, capacity, window, head), lambda i: (i, 0, 0, 0, 0, 0))],
         out_specs=pl.BlockSpec((1, nc, nz, capacity, window, head), lambda i: (i, 0, 0, 0, 0, 0)),
-        cost_estimate=COST,
+        compiler_params=pltpu.CompilerParams(vmem_limit_bytes=12 << 20),
+        cost_estimate=LONG,
         name="by_target",
     )(cache)
 
@@ -253,6 +257,7 @@
         grid=(4,),
         in_specs=[whole, whole],
         out_specs=pl.BlockSpec((1, 2, depth, columns), lambda i: (i, 0, 0, 0)),
+        compiler_params=pltpu.CompilerParams(vmem_limit_bytes=12 << 20),
         cost_estimate=COST,
         name="copies",
     )(half, twin)
@@ -292,6 +297,7 @@
             out_specs=pl.BlockSpec((rows, tile), lambda i, _: (0, i)),
             scratch_shapes=[pltpu.VMEM((rows, blocks * width), jnp.bfloat16)],
         ),
+        compiler_params=pltpu.CompilerParams(vmem_limit_bytes=30 << 20),
         cost_estimate=COST,
         name="project_out",
     )(places, heads, mine, other)
@@ -392,8 +398,8 @@
     twin_half = shift(half, "zl", 1)
 
     key_part = across_y(by_target(key_cache.reshape(sides)))
-    value_slots, key_part, pieces[1:6], twin_half = lax.optimization_barrier(
-        (by_target(value_cache.reshape(sides)), key_part, pieces[1:6], twin_half)
+    value_slots, key_part, pieces[1:6], twin_half, places, starts, fits = lax.optimization_barrier(
+        (by_target(value_cache.reshape(sides)), key_part, pieces[1:6], twin_half, places, starts, fits)
     )
     value_part = across_y(value_slots)
     keys = across_z(pack(places, key_part, PACKED))
@@ -405,9 +411,7 @@
         (copies(half, twin_half), value_part, q)
     )
     packed_values = pack(places, value_part, PACKED)
-    repeated, packed_values, keys[1], keys[3] = lax.optimization_barrier(
-        (repeated, packed_values, keys[1], keys[3])
-    )
+    repeated, packed_values, keys = lax.optimization_barrier((repeated, packed_values, keys))
     values = across_z(packed_values)
     halves = lax.all_to_all(repeated, "x", 0, 0, tiled=True)
     halves = halves.reshape((blocks,) + half.shape)

time: 198 us -> 169 us (0.85)
  waiting for transfers between devices: 74 us -> 62.5 us
  Pallas kernels: 48.7 us -> 41.5 us
  other arithmetic: 12.7 us -> 6.49 us
  starting transfers between devices: 50 us -> 47.9 us
    ppermute x15, waiting for transfers between devices: 62 us -> 42.1 us  [shift(): return lax.ppermute(value, axis, ring(lax.axis_size(axis), step))]
    all_to_all x1, waiting for transfers between devices: 0.01 us -> 7.68 us  [local(): halves = lax.all_to_all(repeated, 'x', 0, 0, tiled=True)]
    pallas_call x2, Pallas kernels: 7.69 us -> 3.82 us  [by_target(): pl.pallas_call(by_target_kernel, out_shape=jax.ShapeDtypeStruct((ny, nc,...]
    pallas_call x1, Pallas kernels: 3.71 us -> 0.33 us  [copies(): pl.pallas_call(copies_kernel, out_shape=jax.ShapeDtypeStruct((4, 2, depth...]
    unnamed x20, local copies, waits for them, and re-layouts: 1.9 us -> 4.32 us
  transfers between devices with their start and end apart: 19 -> 19, of which waited for: 10 -> 9; matrix products, arithmetic and copies ran while one was open for 11% -> 6% of each run, Pallas kernels for 19% -> 21%
where the time goes in v8:
time: 169 us; the launch traced here: 168 us
  waiting for transfers between devices  62.5 us (37%)
  starting transfers between devices  47.9 us (28%)
  Pallas kernels  41.5 us (25%)
  local copies, waits for them, and re-layouts  8.19 us (5%)
  other arithmetic  6.49 us (4%)
    ppermute x15, waiting for transfers between devices, shift(): return lax.ppermute(value, axis, ring(lax.axis_size(axis), step))  42.1 us
    ppermute x15, starting transfers between devices, shift(): return lax.ppermute(value, axis, ring(lax.axis_size(axis), step))  29.3 us
    pallas_call x1, Pallas kernels, project(): pl.pallas_call(project_kernel, out_shape=(jax.ShapeDtypeStruct((rows, wq....  14.2 us
    all_to_all x1, waiting for transfers between devices, local(): lax.all_to_all(attended.reshape(blocks, rows // blocks, attended.shape[1]...  12.8 us
    pallas_call x1, Pallas kernels, attend(): pl.pallas_call(attend_kernel, out_shape=jax.ShapeDtypeStruct((rows, colum...  10.4 us
    all_to_all x2, starting transfers between devices, across_y(): flat = lax.all_to_all(flat, ('y', 'c'), 0, 0, tiled=True)  10.1 us
    all_to_all x1, waiting for transfers between devices, local(): halves = lax.all_to_all(repeated, 'x', 0, 0, tiled=True)  7.68 us
    pallas_call x1, Pallas kernels, project_out(): pl.pallas_call(output_kernel, out_shape=jax.ShapeDtypeStruct((rows, colum...  6.63 us
  transfers between devices with their start and end apart: 19, of which 9 were waited for; matrix products, arithmetic and copies ran while one was open for 6% of the time, Pallas kernels for 21%

profile of v8, /device:TPU:8, one launch (start us, length us, event | category | flops | bytes accessed | tf_op | source)
XLA Modules:
  0.0 167.6 jit_solution(10193069273778814007)
XLA Ops:
  0.0 1.5 collective-permute-start.7
  1.5 1.9 %collective-permute-start.6 = (bf16[1536,256]{1,0:T(8,128)(2,1)}, bf16[1536,256]{1,0:T(8,128)(2,1)}, u32[]{:S(2)}, u32[]{:S(2)}) collective-permute-start(bf16[1536,256]{1,0:T(8,128)(2,1)} %refs_0_.1), channel_id=1, source_target_pairs={{0,4},{4,0},{1,5},{5,1},{2,6},{6,2},{3,7},{7,3},{8,12},{12,8},{9,1... | collective-permute-start | bytes 2359304 | tf_op jit(solution)/shard_map/ppermute | solution.py:29
  3.4 1.7 %collective-permute-start.8 = (bf16[1536,256]{1,0:T(8,128)(2,1)}, bf16[1536,256]{1,0:T(8,128)(2,1)}, u32[]{:S(2)}, u32[]{:S(2)}) collective-permute-start(bf16[1536,256]{1,0:T(8,128)(2,1)} %refs_0_.1), channel_id=1, source_target_pairs={{0,3},{1,0},{2,1},{3,2},{4,7},{5,4},{6,5},{7,6},{8,11},{9,8},{10,9... | collective-permute-start | bytes 2359304 | tf_op jit(solution)/shard_map/ppermute | solution.py:29
  5.2 1.6 copy-done.2
  6.8 1.9 %by_target.3 = bf16[4,2,4,2,128,128]{5,4,3,2,1,0:T(8,128)(2,1)} custom-call(bf16[4,4,2,2,128,128]{5,4,3,2,1,0:T(8,128)(2,1)S(1)} %bitcast.26), custom_call_target="tpu_custom_call" | custom-call | flops 1048576 | bytes 67108864 | tf_op jit(solution)/shard_map/by_target/pallas_call | solution.py:235
  8.7 5.0 %all-to-all-start = ((bf16[8,1024,128]{2,1,0:T(8,128)(2,1)}), bf16[8,1024,128]{2,1,0:T(8,128)(2,1)}, u32[]{:S(2)}, u32[]{:S(2)}) async-start(bf16[8,1024,128]{2,1,0:T(8,128)(2,1)} %bitcast.3), calls=%async_computation | async-start | bytes 4194304 | tf_op jit(solution)/shard_map/all_to_all | solution.py:309
  13.8 0.1 add_multiply_fusion
  13.8 0.1 reshape.369
  13.9 0.1 copy.22
  14.0 0.2 convert_reduce_fusion
  14.2 0.1 copy.24
  14.3 0.1 reshape.370
  14.4 0.1 iota_add_fusion
  14.5 0.1 add.382
  14.6 0.1 copy.26
  14.7 0.6 gather_fusion.1
  15.3 0.6 gather_fusion
  15.8 0.2 select_reduce_fusion.1
  16.1 0.2 reduce_window_sum.11
  16.3 0.1 min.21
  16.4 0.6 reduce_max.9
  17.7 1.9 %by_target.2 = bf16[4,2,4,2,128,128]{5,4,3,2,1,0:T(8,128)(2,1)} custom-call(bf16[4,4,2,2,128,128]{5,4,3,2,1,0:T(8,128)(2,1)S(1)} %bitcast.27), custom_call_target="tpu_custom_call" | custom-call | flops 1048576 | bytes 67108864 | tf_op jit(solution)/shard_map/by_target/pallas_call | solution.py:235
  19.6 0.2 fusion.9
  19.9 0.1 pad_add_fusion.2.offsets
  19.9 1.1 collective-permute-done.6.refs_1_
  21.0 1.7 %collective-permute-start.10 = (bf16[1536,256]{1,0:T(8,128)(2,1)}, bf16[1536,256]{1,0:T(8,128)(2,1)}, u32[]{:S(2)}, u32[]{:S(2)}) collective-permute-start(bf16[1536,256]{1,0:T(8,128)(2,1)} %collective-permute-done.6.refs_1_), channel_id=1, source_target_pairs={{0,3},{1,0},{2,1},{3,2},{4,7},{5,4},{6,5},{7,6},{8,11},{9,8},{10,9... | collective-permute-start | bytes 2359304 | tf_op jit(solution)/shard_map/ppermute | solution.py:29
  22.8 0.3 collective-permute-start.9
  23.1 1.8 %collective-permute-start.11 = (bf16[128,2048]{1,0:T(8,128)(2,1)S(1)}, bf16[128,2048]{1,0:T(8,128)(2,1)S(1)}, u32[]{:S(2)}, u32[]{:S(2)}) collective-permute-start(bf16[128,2048]{1,0:T(8,128)(2,1)S(1)} %constant_dynamic-slice_fusion.2.half), channel_id=1, source_target_pairs={{0,4},{4,0},{1,5},{5,1},{2,6},{6,2},{3,7},{7,3},{8,12},{12,8},{9,1... | collective-permute-start | bytes 1572872 | tf_op jit(solution)/shard_map/ppermute | solution.py:29
  24.9 0.2 select_reduce_fusion.2
  25.1 10.4 %collective-permute-done.11.twin = bf16[128,2048]{1,0:T(8,128)(2,1)S(1)} collective-permute-done((bf16[128,2048]{1,0:T(8,128)(2,1)S(1)}, bf16[128,2048]{1,0:T(8,128)(2,1)S(1)}, u32[]{:S(2)}, u32[]{:S(2)}) %collective-permute-start.11) | collective-permute-done | bytes 524320 | tf_op jit(solution)/shard_map/ppermute | solution.py:29
  35.5 4.3 %collective-permute-done.10.refs_5_ = bf16[1536,256]{1,0:T(8,128)(2,1)} collective-permute-done((bf16[1536,256]{1,0:T(8,128)(2,1)}, bf16[1536,256]{1,0:T(8,128)(2,1)}, u32[]{:S(2)}, u32[]{:S(2)}) %collective-permute-start.10) | collective-permute-done | bytes 786464 | tf_op jit(solution)/shard_map/ppermute | solution.py:29
  39.9 2.5 %collective-permute-done.9.refs_4_ = bf16[1536,256]{1,0:T(8,128)(2,1)} collective-permute-done((bf16[1536,256]{1,0:T(8,128)(2,1)}, bf16[1536,256]{1,0:T(8,128)(2,1)}, u32[]{:S(2)}, u32[]{:S(2)}) %collective-permute-start.9) | collective-permute-done | bytes 786464 | tf_op jit(solution)/shard_map/ppermute | solution.py:29
  42.4 5.0 %all-to-all-start.1 = ((bf16[8,1024,128]{2,1,0:T(8,128)(2,1)}), bf16[8,1024,128]{2,1,0:T(8,128)(2,1)}, u32[]{:S(2)}, u32[]{:S(2)}) async-start(bf16[8,1024,128]{2,1,0:T(8,128)(2,1)} %bitcast.7), calls=%async_computation.1 | async-start | bytes 4194304 | tf_op jit(solution)/shard_map/all_to_all | solution.py:309
  47.4 0.1 collective-permute-start.12
  47.5 3.2 %collective-permute-start.13 = (bf16[1536,256]{1,0:T(8,128)(2,1)}, bf16[1536,256]{1,0:T(8,128)(2,1)}, u32[]{:S(2)}, u32[]{:S(2)}) collective-permute-start(bf16[1536,256]{1,0:T(8,128)(2,1)} %collective-permute-done.10.refs_5_), channel_id=1, source_target_pairs={{0,3},{1,0},{2,1},{3,2},{4,7},{5,4},{6,5},{7,6},{8,11},{9,8},{10,9... | collective-permute-start | bytes 2359304 | tf_op jit(solution)/shard_map/ppermute | solution.py:29
  50.7 0.1 add_convert_fusion
  50.8 0.1 convert_element_type.26
  50.9 1.3 copy.28.refs_8_
  52.2 0.7 stack.35.ids
  52.9 3.1 %pack.7 = (bf16[1088,128]{1,0:T(8,128)(2,1)}, bf16[1088,128]{1,0:T(8,128)(2,1)S(1)}, bf16[1088,128]{1,0:T(8,128)(2,1)S(1)}, bf16[1088,128]{1,0:T(8,128)(2,1)S(1)}) custom-call(s32[68]{0:T(128)S(1)} %pad_add_fusion.2.offsets, bf16[8,4,2,128,128]{4,3,2,1,0:T(8,128)(2,1)} %bitcast.4.cache), custom_call_target="tpu_custom_call" | custom-call | flops 1048576 | bytes 1048576 | tf_op jit(solution)/shard_map/pack/pallas_call | solution.py:212
  55.9 3.3 %collective-permute-start.14 = (bf16[1088,128]{1,0:T(8,128)(2,1)S(1)}, bf16[1088,128]{1,0:T(8,128)(2,1)S(1)}, u32[]{:S(2)}, u32[]{:S(2)}) collective-permute-start(bf16[1088,128]{1,0:T(8,128)(2,1)S(1)} %get-tuple-element.160), channel_id=1, source_target_pairs={{0,16},{16,32},{32,48},{48,0},{1,17},{17,33},{33,49},{49,1},{2,18}... | collective-permute-start | bytes 835592 | tf_op jit(solution)/shard_map/ppermute | solution.py:29
  59.2 5.0 %collective-permute-start.15 = (bf16[1088,128]{1,0:T(8,128)(2,1)S(1)}, bf16[1088,128]{1,0:T(8,128)(2,1)S(1)}, u32[]{:S(2)}, u32[]{:S(2)}) collective-permute-start(bf16[1088,128]{1,0:T(8,128)(2,1)S(1)} %get-tuple-element.161), channel_id=1, source_target_pairs={{0,32},{16,48},{32,0},{48,16},{1,33},{17,49},{33,1},{49,17},{2,34}... | collective-permute-start | bytes 835592 | tf_op jit(solution)/shard_map/ppermute | solution.py:29
  64.2 2.7 %collective-permute-start.16 = (bf16[1088,128]{1,0:T(8,128)(2,1)S(1)}, bf16[1088,128]{1,0:T(8,128)(2,1)}, u32[]{:S(2)}, u32[]{:S(2)}) collective-permute-start(bf16[1088,128]{1,0:T(8,128)(2,1)S(1)} %get-tuple-element.162), channel_id=1, source_target_pairs={{0,48},{16,0},{32,16},{48,32},{1,49},{17,1},{33,17},{49,33},{2,50}... | collective-permute-start | bytes 835592 | tf_op jit(solution)/shard_map/ppermute | solution.py:29
  66.8 4.3 %fusion = (f32[1536,128]{1,0:T(8,128)}, f32[1536,128]{1,0:T(8,128)}) fusion(f32[128]{0:T(128)S(1)} %get-tuple-element.184, f32[128]{0:T(128)S(1)} %get-tuple-element.185, f32[1536]{0:T(1024)S(1)} %convert_element_type.26), kind=kLoop, calls=%fused_computation.7 | loop fusion | flops 393216 | bytes 1580032 | tf_op jit(solution)/shard_map/mul | solution.py:389
  71.1 0.3 copies.1
  71.5 1.9 %copy-done.1 = bf16[4,2,128,2048]{3,2,1,0:T(8,128)(2,1)} copy-done((bf16[4,2,128,2048]{3,2,1,0:T(8,128)(2,1)}, bf16[4,2,128,2048]{3,2,1,0:T(8,128)(2,1)S(1)}, u32[]{:S(2)}) %copy-start.1) | copy-done | bytes 4194328
  73.4 14.2 %project.1 = (bf16[1536,256]{1,0:T(8,128)(2,1)}, f32[1536,256]{1,0:T(8,128)}, bf16[1536,128]{1,0:T(8,128)(2,1)}, bf16[1536,128]{1,0:T(8,128)(2,1)}) custom-call(s32[8]{0:T(128)} %stack.35.ids, bf16[1536,256]{1,0:T(8,128)(2,1)} %refs_0_.1, bf16[1536,256]{1,0:T(8,128)(2,1)} %collective-permute-done.6.refs_1_, ...), custom_call_target="tpu_custom_call" | custom-call | flops 1048576 | bytes 1048576 | tf_op jit(solution)/shard_map/project/pallas_call | solution.py:105
  87.6 3.1 %pack.6 = (bf16[1088,128]{1,0:T(8,128)(2,1)}, bf16[1088,128]{1,0:T(8,128)(2,1)S(1)}, bf16[1088,128]{1,0:T(8,128)(2,1)S(1)}, bf16[1088,128]{1,0:T(8,128)(2,1)S(1)}) custom-call(s32[68]{0:T(128)S(1)} %pad_add_fusion.2.offsets, bf16[8,4,2,128,128]{4,3,2,1,0:T(8,128)(2,1)} %bitcast.8.cache), custom_call_target="tpu_custom_call" | custom-call | flops 1048576 | bytes 1048576 | tf_op jit(solution)/shard_map/pack/pallas_call | solution.py:212
  90.7 0.7 copy-done.8
  91.4 0.1 copy-done.9
  91.5 5.0 %all-to-all-start.3 = ((bf16[4,2,128,2048]{3,2,1,0:T(8,128)(2,1)}), bf16[4,2,128,2048]{3,2,1,0:T(8,128)(2,1)}, u32[]{:S(2)}, u32[]{:S(2)}) async-start(bf16[4,2,128,2048]{3,2,1,0:T(8,128)(2,1)} %copy-done.1), calls=%async_computation.3 | async-start | bytes 8388608 | tf_op jit(solution)/shard_map/all_to_all | solution.py:416
  96.5 0.3 collective-permute-start.17
  96.8 3.2 %collective-permute-start.18 = (bf16[1088,128]{1,0:T(8,128)(2,1)S(1)}, bf16[1088,128]{1,0:T(8,128)(2,1)}, u32[]{:S(2)}, u32[]{:S(2)}) collective-permute-start(bf16[1088,128]{1,0:T(8,128)(2,1)S(1)} %get-tuple-element.169), channel_id=1, source_target_pairs={{0,32},{16,48},{32,0},{48,16},{1,33},{17,49},{33,1},{49,17},{2,34}... | collective-permute-start | bytes 835592 | tf_op jit(solution)/shard_map/ppermute | solution.py:29
  100.0 2.7 %collective-permute-start.19 = (bf16[1088,128]{1,0:T(8,128)(2,1)S(1)}, bf16[1088,128]{1,0:T(8,128)(2,1)}, u32[]{:S(2)}, u32[]{:S(2)}) collective-permute-start(bf16[1088,128]{1,0:T(8,128)(2,1)S(1)} %get-tuple-element.170), channel_id=1, source_target_pairs={{0,48},{16,0},{32,16},{48,32},{1,49},{17,1},{33,17},{49,33},{2,50}... | collective-permute-start | bytes 835592 | tf_op jit(solution)/shard_map/ppermute | solution.py:29
  102.6 14.5 %collective-permute-done.17 = bf16[1088,128]{1,0:T(8,128)(2,1)} collective-permute-done((bf16[1088,128]{1,0:T(8,128)(2,1)S(1)}, bf16[1088,128]{1,0:T(8,128)(2,1)}, u32[]{:S(2)}, u32[]{:S(2)}) %collective-permute-start.17) | collective-permute-done | bytes 278560 | tf_op jit(solution)/shard_map/ppermute | solution.py:29
  117.2 2.2 %collective-permute-done.18 = bf16[1088,128]{1,0:T(8,128)(2,1)} collective-permute-done((bf16[1088,128]{1,0:T(8,128)(2,1)S(1)}, bf16[1088,128]{1,0:T(8,128)(2,1)}, u32[]{:S(2)}, u32[]{:S(2)}) %collective-permute-start.18) | collective-permute-done | bytes 278560 | tf_op jit(solution)/shard_map/ppermute | solution.py:29
  119.4 7.0 %collective-permute-done.19 = bf16[1088,128]{1,0:T(8,128)(2,1)} collective-permute-done((bf16[1088,128]{1,0:T(8,128)(2,1)S(1)}, bf16[1088,128]{1,0:T(8,128)(2,1)}, u32[]{:S(2)}, u32[]{:S(2)}) %collective-permute-start.19) | collective-permute-done | bytes 278560 | tf_op jit(solution)/shard_map/ppermute | solution.py:29
  126.4 10.4 %conditional.1 = (bf16[1536,256]{1,0:T(8,128)(2,1)}) conditional(s32[]{:T(128)} %convert_element_type.24, (s32[24]{0:T(128)S(1)}, s32[24]{0:T(128)S(1)}, s32[4,16]{1,0:T(4,128)S(1)}, s32[4,16]{1,0:T(4,128)S(1)}, s32[4]{0:T(128)S(1)}, /*index=5*/bf16[8,4,2,128,128]{4,3,2,1,0:T(8,128)(2,1)}, bf16[8,4,2,128,128]{4,3,2,1,0:T(8,128)(2,1)}, ...), branch_computations={%region_6.7_spmd, %region_7.8_spmd} | conditional | flops 3146060 | bytes 22022540 | solution.py:429
  126.4 10.4 %attend.3 = bf16[1536,256]{1,0:T(8,128)(2,1)} custom-call(s32[24]{0:T(128)S(1)} %get-tuple-element.84.starts, s32[24]{0:T(128)S(1)} %get-tuple-element.85.lengths, bf16[1536,256]{1,0:T(8,128)(2,1)} %get-tuple-element.86.q, f32[1536,256]{1,0:T(8,128)S(1)} %get-tuple-element.87.g, bf16[1536,128]{1,0:T(8,128)(2,1)} %get-tuple-element.88.k, ...), custom_call_target="tpu_custom_call" | custom-call | flops 1048576 | bytes 1048576 | tf_op jit(solution)/shard_map/cond/branch_1_fun/attend/pallas_call | solution.py:183
  136.8 7.7 %all-to-all-done.3 = bf16[4,2,128,2048]{3,2,1,0:T(8,128)(2,1)} async-done(((bf16[4,2,128,2048]{3,2,1,0:T(8,128)(2,1)}), bf16[4,2,128,2048]{3,2,1,0:T(8,128)(2,1)}, u32[]{:S(2)}, u32[]{:S(2)}) %all-to-all-start.3) | async-done | bytes 4194336 | tf_op jit(solution)/shard_map/all_to_all | solution.py:416
  144.5 3.5 %all-to-all-start.2 = ((bf16[8,192,256]{2,1,0:T(8,128)(2,1)}), bf16[8,192,256]{2,1,0:T(8,128)(2,1)S(1)}, u32[]{:S(2)}, u32[]{:S(2)}) async-start(bf16[8,192,256]{2,1,0:T(8,128)(2,1)} %bitcast.28), calls=%async_computation.2 | async-start | bytes 1572864 | tf_op jit(solution)/shard_map/all_to_all | solution.py:430
  148.1 0.1 pad_add_fusion.1.places
  148.2 12.8 %all-to-all-done.2.heads = bf16[8,192,256]{2,1,0:T(8,128)(2,1)S(1)} async-done(((bf16[8,192,256]{2,1,0:T(8,128)(2,1)}), bf16[8,192,256]{2,1,0:T(8,128)(2,1)S(1)}, u32[]{:S(2)}, u32[]{:S(2)}) %all-to-all-start.2) | async-done | bytes 786464 | tf_op jit(solution)/shard_map/all_to_all | solution.py:430
  160.9 6.6 %project_out.1 = bf16[192,2048]{1,0:T(8,128)(2,1)} custom-call(s32[9]{0:T(128)S(1)} %pad_add_fusion.1.places, bf16[8,192,256]{2,1,0:T(8,128)(2,1)S(1)} %all-to-all-done.2.heads, bf16[8,128,2048]{2,1,0:T(8,128)(2,1)} %bitcast.22.mine, bf16[8,128,2048]{2,1,0:T(8,128)(2,1)} %collective-permute-done.20.other), custom_call_target="tpu_custom_call" | custom-call | flops 1048576 | bytes 1048576 | tf_op jit(solution)/shard_map/project_out/pallas_call | solution.py:290
  (45 shorter events, 0.4 us)
Async XLA Ops:
  0.0 23.0 %copy-start = (bf16[256,2048]{1,0:T(8,128)(2,1)S(1)}, bf16[256,2048]{1,0:T(8,128)(2,1)}, u32[]{:S(2)}) copy-start(bf16[256,2048]{1,0:T(8,128)(2,1)} %param.23) | copy-start | bytes 3145732
  0.0 25.1 %collective-permute-start.7 = (bf16[1536,256]{1,0:T(8,128)(2,1)}, bf16[1536,256]{1,0:T(8,128)(2,1)}, u32[]{:S(2)}, u32[]{:S(2)}) collective-permute-start(bf16[1536,256]{1,0:T(8,128)(2,1)} %refs_0_.1), channel_id=1, source_target_pairs={{0,1},{1,2},{2,3},{3,0},{4,5},{5,6},{6,7},{7,4},{8,9},{9,10},{10,1... | collective-permute-start | bytes 2359304 | tf_op jit(solution)/shard_map/ppermute | solution.py:29
  1.5 19.5 %collective-permute-start.6 = (bf16[1536,256]{1,0:T(8,128)(2,1)}, bf16[1536,256]{1,0:T(8,128)(2,1)}, u32[]{:S(2)}, u32[]{:S(2)}) collective-permute-start(bf16[1536,256]{1,0:T(8,128)(2,1)} %refs_0_.1), channel_id=1, source_target_pairs={{0,4},{4,0},{1,5},{5,1},{2,6},{6,2},{3,7},{7,3},{8,12},{12,8},{9,1... | collective-permute-start | bytes 2359304 | tf_op jit(solution)/shard_map/ppermute | solution.py:29
  3.4 21.7 %collective-permute-start.8 = (bf16[1536,256]{1,0:T(8,128)(2,1)}, bf16[1536,256]{1,0:T(8,128)(2,1)}, u32[]{:S(2)}, u32[]{:S(2)}) collective-permute-start(bf16[1536,256]{1,0:T(8,128)(2,1)} %refs_0_.1), channel_id=1, source_target_pairs={{0,3},{1,0},{2,1},{3,2},{4,7},{5,4},{6,5},{7,6},{8,11},{9,8},{10,9... | collective-permute-start | bytes 2359304 | tf_op jit(solution)/shard_map/ppermute | solution.py:29
  5.2 1.6 copy-start.2
  8.7 5.2 %copy-start.12 = (s32[768,1]{0,1:T(1,128)S(1)}, s32[768,1]{0,1:T(1,128)}, u32[]{:S(2)}) copy-start(s32[768,1]{0,1:T(1,128)} %param.26) | copy-start | bytes 9220
  8.7 5.6 %copy-start.11 = (s32[768]{0:T(1024)S(1)}, s32[768]{0:T(1024)}, u32[]{:S(2)}) copy-start(s32[768]{0:T(1024)} %param.27) | copy-start | bytes 9220
  8.7 9.0 %copy-start.3 = (bf16[1,64,128,128]{3,2,1,0:T(8,128)(2,1)S(1)}, bf16[1,64,128,128]{3,2,1,0:T(8,128)(2,1)}, u32[]{:S(2)}) copy-start(bf16[1,64,128,128]{3,2,1,0:T(8,128)(2,1)} %param.25) | copy-start | bytes 6291460
  8.7 33.7 %all-to-all-start = ((bf16[8,1024,128]{2,1,0:T(8,128)(2,1)}), bf16[8,1024,128]{2,1,0:T(8,128)(2,1)}, u32[]{:S(2)}, u32[]{:S(2)}) async-start(bf16[8,1024,128]{2,1,0:T(8,128)(2,1)} %bitcast.3), calls=%async_computation | async-start | bytes 4194304 | tf_op jit(solution)/shard_map/all_to_all | solution.py:309
  21.0 18.9 %collective-permute-start.10 = (bf16[1536,256]{1,0:T(8,128)(2,1)}, bf16[1536,256]{1,0:T(8,128)(2,1)}, u32[]{:S(2)}, u32[]{:S(2)}) collective-permute-start(bf16[1536,256]{1,0:T(8,128)(2,1)} %collective-permute-done.6.refs_1_), channel_id=1, source_target_pairs={{0,3},{1,0},{2,1},{3,2},{4,7},{5,4},{6,5},{7,6},{8,11},{9,8},{10,9... | collective-permute-start | bytes 2359304 | tf_op jit(solution)/shard_map/ppermute | solution.py:29
  22.8 19.6 %collective-permute-start.9 = (bf16[1536,256]{1,0:T(8,128)(2,1)}, bf16[1536,256]{1,0:T(8,128)(2,1)}, u32[]{:S(2)}, u32[]{:S(2)}) collective-permute-start(bf16[1536,256]{1,0:T(8,128)(2,1)} %collective-permute-done.6.refs_1_), channel_id=1, source_target_pairs={{0,1},{1,2},{2,3},{3,0},{4,5},{5,6},{6,7},{7,4},{8,9},{9,10},{10,1... | collective-permute-start | bytes 2359304 | tf_op jit(solution)/shard_map/ppermute | solution.py:29
  23.1 12.5 %collective-permute-start.11 = (bf16[128,2048]{1,0:T(8,128)(2,1)S(1)}, bf16[128,2048]{1,0:T(8,128)(2,1)S(1)}, u32[]{:S(2)}, u32[]{:S(2)}) collective-permute-start(bf16[128,2048]{1,0:T(8,128)(2,1)S(1)} %constant_dynamic-slice_fusion.2.half), channel_id=1, source_target_pairs={{0,4},{4,0},{1,5},{5,1},{2,6},{6,2},{3,7},{7,3},{8,12},{12,8},{9,1... | collective-permute-start | bytes 1572872 | tf_op jit(solution)/shard_map/ppermute | solution.py:29
  42.4 8.5 %copy-start.10 = (f32[2048]{0:T(1024)S(1)}, f32[2048]{0:T(1024)}, u32[]{:S(2)}) copy-start(f32[2048]{0:T(1024)} %param.16) | copy-start | bytes 24580
  42.4 45.2 %all-to-all-start.1 = ((bf16[8,1024,128]{2,1,0:T(8,128)(2,1)}), bf16[8,1024,128]{2,1,0:T(8,128)(2,1)}, u32[]{:S(2)}, u32[]{:S(2)}) async-start(bf16[8,1024,128]{2,1,0:T(8,128)(2,1)} %bitcast.7), calls=%async_computation.1 | async-start | bytes 4194304 | tf_op jit(solution)/shard_map/all_to_all | solution.py:309
  47.4 26.0 %collective-permute-start.12 = (bf16[1536,256]{1,0:T(8,128)(2,1)}, bf16[1536,256]{1,0:T(8,128)(2,1)}, u32[]{:S(2)}, u32[]{:S(2)}) collective-permute-start(bf16[1536,256]{1,0:T(8,128)(2,1)} %collective-permute-done.7.refs_2_), channel_id=1, source_target_pairs={{0,1},{1,2},{2,3},{3,0},{4,5},{5,6},{6,7},{7,4},{8,9},{9,10},{10,1... | collective-permute-start | bytes 2359304 | tf_op jit(solution)/shard_map/ppermute | solution.py:29
  47.5 25.9 %collective-permute-start.13 = (bf16[1536,256]{1,0:T(8,128)(2,1)}, bf16[1536,256]{1,0:T(8,128)(2,1)}, u32[]{:S(2)}, u32[]{:S(2)}) collective-permute-start(bf16[1536,256]{1,0:T(8,128)(2,1)} %collective-permute-done.10.refs_5_), channel_id=1, source_target_pairs={{0,3},{1,0},{2,1},{3,2},{4,7},{5,4},{6,5},{7,6},{8,11},{9,8},{10,9... | collective-permute-start | bytes 2359304 | tf_op jit(solution)/shard_map/ppermute | solution.py:29
  55.9 34.7 %collective-permute-start.14 = (bf16[1088,128]{1,0:T(8,128)(2,1)S(1)}, bf16[1088,128]{1,0:T(8,128)(2,1)S(1)}, u32[]{:S(2)}, u32[]{:S(2)}) collective-permute-start(bf16[1088,128]{1,0:T(8,128)(2,1)S(1)} %get-tuple-element.160), channel_id=1, source_target_pairs={{0,16},{16,32},{32,48},{48,0},{1,17},{17,33},{33,49},{49,1},{2,18}... | collective-permute-start | bytes 835592 | tf_op jit(solution)/shard_map/ppermute | solution.py:29
  59.2 31.5 %collective-permute-start.15 = (bf16[1088,128]{1,0:T(8,128)(2,1)S(1)}, bf16[1088,128]{1,0:T(8,128)(2,1)S(1)}, u32[]{:S(2)}, u32[]{:S(2)}) collective-permute-start(bf16[1088,128]{1,0:T(8,128)(2,1)S(1)} %get-tuple-element.161), channel_id=1, source_target_pairs={{0,32},{16,48},{32,0},{48,16},{1,33},{17,49},{33,1},{49,17},{2,34}... | collective-permute-start | bytes 835592 | tf_op jit(solution)/shard_map/ppermute | solution.py:29
  64.2 26.5 %collective-permute-start.16 = (bf16[1088,128]{1,0:T(8,128)(2,1)S(1)}, bf16[1088,128]{1,0:T(8,128)(2,1)}, u32[]{:S(2)}, u32[]{:S(2)}) collective-permute-start(bf16[1088,128]{1,0:T(8,128)(2,1)S(1)} %get-tuple-element.162), channel_id=1, source_target_pairs={{0,48},{16,0},{32,16},{48,32},{1,49},{17,1},{33,17},{49,33},{2,50}... | collective-permute-start | bytes 835592 | tf_op jit(solution)/shard_map/ppermute | solution.py:29
  71.5 1.9 %copy-start.1 = (bf16[4,2,128,2048]{3,2,1,0:T(8,128)(2,1)}, bf16[4,2,128,2048]{3,2,1,0:T(8,128)(2,1)S(1)}, u32[]{:S(2)}) copy-start(bf16[4,2,128,2048]{3,2,1,0:T(8,128)(2,1)S(1)} %copies.1) | copy-start | bytes 12582916
  90.7 0.7 copy-start.8
  90.7 0.8 copy-start.9
  91.5 34.9 %copy-start.4 = (f32[1536,256]{1,0:T(8,128)S(1)}, f32[1536,256]{1,0:T(8,128)}, u32[]{:S(2)}) copy-start(f32[1536,256]{1,0:T(8,128)} %get-tuple-element.149) | copy-start | bytes 4718596
  91.5 53.0 %all-to-all-start.3 = ((bf16[4,2,128,2048]{3,2,1,0:T(8,128)(2,1)}), bf16[4,2,128,2048]{3,2,1,0:T(8,128)(2,1)}, u32[]{:S(2)}, u32[]{:S(2)}) async-start(bf16[4,2,128,2048]{3,2,1,0:T(8,128)(2,1)} %copy-done.1), calls=%async_computation.3 | async-start | bytes 8388608 | tf_op jit(solution)/shard_map/all_to_all | solution.py:416
  96.5 20.7 %collective-permute-start.17 = (bf16[1088,128]{1,0:T(8,128)(2,1)S(1)}, bf16[1088,128]{1,0:T(8,128)(2,1)}, u32[]{:S(2)}, u32[]{:S(2)}) collective-permute-start(bf16[1088,128]{1,0:T(8,128)(2,1)S(1)} %get-tuple-element.168), channel_id=1, source_target_pairs={{0,16},{16,32},{32,48},{48,0},{1,17},{17,33},{33,49},{49,1},{2,18}... | collective-permute-start | bytes 835592 | tf_op jit(solution)/shard_map/ppermute | solution.py:29
  96.8 22.5 %collective-permute-start.18 = (bf16[1088,128]{1,0:T(8,128)(2,1)S(1)}, bf16[1088,128]{1,0:T(8,128)(2,1)}, u32[]{:S(2)}, u32[]{:S(2)}) collective-permute-start(bf16[1088,128]{1,0:T(8,128)(2,1)S(1)} %get-tuple-element.169), channel_id=1, source_target_pairs={{0,32},{16,48},{32,0},{48,16},{1,33},{17,49},{33,1},{49,17},{2,34}... | collective-permute-start | bytes 835592 | tf_op jit(solution)/shard_map/ppermute | solution.py:29
  100.0 26.4 %collective-permute-start.19 = (bf16[1088,128]{1,0:T(8,128)(2,1)S(1)}, bf16[1088,128]{1,0:T(8,128)(2,1)}, u32[]{:S(2)}, u32[]{:S(2)}) collective-permute-start(bf16[1088,128]{1,0:T(8,128)(2,1)S(1)} %get-tuple-element.170), channel_id=1, source_target_pairs={{0,48},{16,0},{32,16},{48,32},{1,49},{17,1},{33,17},{49,33},{2,50}... | collective-permute-start | bytes 835592 | tf_op jit(solution)/shard_map/ppermute | solution.py:29
  144.5 16.4 %collective-permute-start.20 = (bf16[8,128,2048]{2,1,0:T(8,128)(2,1)}, bf16[8,128,2048]{2,1,0:T(8,128)(2,1)}, u32[]{:S(2)}, u32[]{:S(2)}) collective-permute-start(bf16[8,128,2048]{2,1,0:T(8,128)(2,1)} %bitcast.22.mine), channel_id=1, source_target_pairs={{0,8},{8,0},{1,9},{9,1},{2,10},{10,2},{3,11},{11,3},{4,12},{12,4},... | collective-permute-start | bytes 12582920 | tf_op jit(solution)/shard_map/ppermute | solution.py:29
  144.5 16.4 %all-to-all-start.2 = ((bf16[8,192,256]{2,1,0:T(8,128)(2,1)}), bf16[8,192,256]{2,1,0:T(8,128)(2,1)S(1)}, u32[]{:S(2)}, u32[]{:S(2)}) async-start(bf16[8,192,256]{2,1,0:T(8,128)(2,1)} %bitcast.28), calls=%async_computation.2 | async-start | bytes 1572864 | tf_op jit(solution)/shard_map/all_to_all | solution.py:430

commit v9 on v8

--- a/solution.py
+++ b/solution.py
@@ -100,7 +100,7 @@
     tile = lambda columns: pl.BlockSpec((ROW_TILE, columns), lambda i, _: (i, 0))
     whole = lambda a: pl.BlockSpec(a.shape, lambda i, _: (0, 0))
     q_gain, k_gain = q_gain.reshape(1, head), k_gain.reshape(1, head)
-    constants = (gain.reshape(depth, 1), wq, wg, wk, wv, q_gain, k_gain)
+    constants = (gain, wq, wg, wk, wv, q_gain, k_gain)
     columns = sum(w.shape[1] for w in (wq, wg, wk, wv))
     return pl.pallas_call(
         project_kernel,
@@ -122,27 +122,28 @@
     )(ids, *pieces, *constants, cosine, sine)
 
 
-def attend_kernel(starts, lengths, q, g, k, v, *refs):
-    key_parts, value_parts = refs[:4], refs[4:8]
-    out, keys, values = refs[8:]
+def gather_parts(parts, store):
+    size = parts[0].shape[0]
+    for j, part in enumerate(parts):
+        store[j * size : (j + 1) * size, :] = part[...]
+    slack = slice(len(parts) * size, store.shape[0])
+    store[slack, :] = jnp.zeros((store.shape[0] - len(parts) * size, store.shape[1]), store.dtype)
+
+
+def weigh_kernel(starts, lengths, q, g, k, v, *refs):
+    parts, (weights, mixed_new, factor, keys) = refs[:4], refs[4:]
     head = k.shape[1]
     span = q.shape[0] // BATCH
     shares = q.shape[1] // head
-    size = key_parts[0].shape[0]
-    window = keys.shape[0] - 4 * size
+    window = keys.shape[0] - 4 * parts[0].shape[0]
     score_scale = 1.0 / math.sqrt(head)
     contract = (((1,), (1,)), ((), ()))
 
     @pl.when(pl.program_id(0) == 0)
     def _():
-        for j in range(4):
-            keys[j * size : (j + 1) * size, :] = key_parts[j][...]
-            values[j * size : (j + 1) * size, :] = value_parts[j][...]
-        keys[4 * size :, :] = jnp.zeros((window, head), keys.dtype)
-        values[4 * size :, :] = jnp.zeros((window, head), values.dtype)
+        gather_parts(parts, keys)
 
     column = lax.broadcasted_iota(jnp.int32, (shares * span, window), 1)
-    old_row = lax.broadcasted_iota(jnp.int32, (window, head), 0)
     token = lax.broadcasted_iota(jnp.int32, (shares, span, window), 1)
     token = token.reshape(shares * span, window)
     together = window // span
@@ -154,9 +155,7 @@
         both = slice(first * span, (first + together) * span)
         own = column - (b - first) * span
         query = jnp.concatenate([q[rows, s * head : (s + 1) * head] for s in range(shares)], axis=0)
-        place = pl.ds(pl.multiple_of(starts[r], UNIT), window)
-        old_keys, old_values = keys[place, :], values[place, :]
-        old_values = jnp.where(old_row < length, old_values, jnp.zeros_like(old_values))
+        old_keys = keys[pl.ds(pl.multiple_of(starts[r], UNIT), window), :]
         old = lax.dot_general(query, old_keys, contract, preferred_element_type=jnp.float32)
         new = lax.dot_general(query, k[both, :], contract, preferred_element_type=jnp.float32)
         old = jnp.where(column < length, old * score_scale, -jnp.inf)
@@ -164,36 +163,94 @@
         row_max = jnp.max(jnp.maximum(old, new), axis=-1, keepdims=True)
         old, new = jnp.exp(old - row_max), jnp.exp(new - row_max)
         row_total = jnp.sum(old + new, axis=-1, keepdims=True)
-        mixed = jnp.dot(old.astype(jnp.bfloat16), old_values, preferred_element_type=jnp.float32)
-        mixed += jnp.dot(new.astype(jnp.bfloat16), v[both, :], preferred_element_type=jnp.float32)
-        mixed = mixed / row_total
+        weights[b * shares * span : (b + 1) * shares * span, :] = old.astype(jnp.bfloat16)
+        mixed = jnp.dot(new.astype(jnp.bfloat16), v[both, :], preferred_element_type=jnp.float32)
         for s in range(shares):
-            columns = slice(s * head, (s + 1) * head)
-            part = mixed[s * span : (s + 1) * span] * g[rows, columns]
-            out[rows, columns] = part.astype(jnp.bfloat16)
-
-
-def attend(starts, lengths, q, g, k, v, keys, values, window):
+            columns, here = slice(s * head, (s + 1) * head), slice(s * span, (s + 1) * span)
+            mixed_new[rows, columns] = mixed[here]
+            factor[rows, columns] = g[rows, columns] / row_total[here]
+
+
+def weigh(starts, lengths, q, g, k, v, keys, window):
     rows, columns = q.shape
     head = k.shape[1]
+    shares = columns // head
     step = rows // lengths.shape[0] * BATCH
     tile = lambda width: pl.BlockSpec((step, width), lambda i, *_: (i, 0))
     whole = lambda a: pl.BlockSpec(a.shape, lambda i, *_: (0, 0))
-    store = pltpu.VMEM((4 * keys[0].shape[0] + window, head), keys[0].dtype)
-    return pl.pallas_call(
-        attend_kernel,
+    return pl.pallas_call(
+        weigh_kernel,
+        out_shape=(
+            jax.ShapeDtypeStruct((shares * rows, window), jnp.bfloat16),
+            jax.ShapeDtypeStruct((rows, columns), jnp.float32),
+            jax.ShapeDtypeStruct((rows, columns), jnp.float32),
+        ),
+        grid_spec=pltpu.PrefetchScalarGridSpec(
+            num_scalar_prefetch=2,
+            grid=(rows // step,),
+            in_specs=[tile(columns)] * 2 + [tile(head)] * 2 + [whole(a) for a in keys],
+            out_specs=(
+                pl.BlockSpec((shares * step, window), lambda i, *_: (i, 0)),
+                tile(columns),
+                tile(columns),
+            ),
+            scratch_shapes=[pltpu.VMEM((4 * keys[0].shape[0] + window, head), keys[0].dtype)],
+        ),
+        compiler_params=pltpu.CompilerParams(vmem_limit_bytes=30 << 20),
+        cost_estimate=COST,
+        name="weigh",
+    )(starts, lengths, q, g, k, v, *keys)
+
+
+def mix_kernel(starts, lengths, weights, mixed_new, factor, *refs):
+    parts, (out, values) = refs[:4], refs[4:]
+    window, head = weights.shape[1], values.shape[1]
+    span = out.shape[0] // BATCH
+    shares = out.shape[1] // head
+
+    @pl.when(pl.program_id(0) == 0)
+    def _():
+        gather_parts(parts, values)
+
+    old_row = lax.broadcasted_iota(jnp.int32, (window, head), 0)
+    for b in range(BATCH):
+        r = pl.program_id(0) * BATCH + b
+        rows = slice(b * span, (b + 1) * span)
+        old_values = values[pl.ds(pl.multiple_of(starts[r], UNIT), window), :]
+        old_values = jnp.where(old_row < lengths[r], old_values, jnp.zeros_like(old_values))
+        old = weights[b * shares * span : (b + 1) * shares * span, :]
+        mixed = jnp.dot(old, old_values, preferred_element_type=jnp.float32)
+        for s in range(shares):
+            columns, here = slice(s * head, (s + 1) * head), slice(s * span, (s + 1) * span)
+            part = (mixed[here] + mixed_new[rows, columns]) * factor[rows, columns]
+            out[rows, columns] = part.astype(jnp.bfloat16)
+
+
+def mix(starts, lengths, weights, mixed_new, factor, values):
+    rows, columns = factor.shape
+    window, head = weights.shape[1], values[0].shape[1]
+    step = rows // lengths.shape[0] * BATCH
+    tile = lambda width: pl.BlockSpec((step, width), lambda i, *_: (i, 0))
+    whole = lambda a: pl.BlockSpec(a.shape, lambda i, *_: (0, 0))
+    return pl.pallas_call(
+        mix_kernel,
         out_shape=jax.ShapeDtypeStruct((rows, columns), jnp.bfloat16),
         grid_spec=pltpu.PrefetchScalarGridSpec(
             num_scalar_prefetch=2,
             grid=(rows // step,),
-            in_specs=[tile(columns)] * 2 + [tile(head)] * 2 + [whole(a) for a in keys + values],
+            in_specs=[
+                pl.BlockSpec((columns // head * step, window), lambda i, *_: (i, 0)),
+                tile(columns),
+                tile(columns),
+            ]
+            + [whole(a) for a in values],
             out_specs=tile(columns),
-            scratch_shapes=[store, store],
+            scratch_shapes=[pltpu.VMEM((4 * values[0].shape[0] + window, head), values[0].dtype)],
         ),
         compiler_params=pltpu.CompilerParams(vmem_limit_bytes=30 << 20),
         cost_estimate=COST,
-        name="attend",
-    )(starts, lengths, q, g, k, v, *keys, *values)
+        name="mix",
+    )(starts, lengths, weights, mixed_new, factor, *values)
 
 
 def pack_kernel(offsets, cache, *refs):
@@ -244,22 +301,23 @@
     )(cache)
 
 
-def copies_kernel(half, twin, out):
-    out[0, 0], out[0, 1] = half[...], twin[...]
-
-
-def copies(half, twin):
+def pair_kernel(half, twin, out):
+    out[0], out[1] = half[...], twin[...]
+
+
+def pair(half, twin):
     depth, columns = half.shape
-    whole = pl.BlockSpec((depth, columns), lambda i: (0, 0))
-    return pl.pallas_call(
-        copies_kernel,
-        out_shape=jax.ShapeDtypeStruct((4, 2, depth, columns), half.dtype),
-        grid=(4,),
-        in_specs=[whole, whole],
-        out_specs=pl.BlockSpec((1, 2, depth, columns), lambda i: (i, 0, 0, 0)),
+    tile = 512
+    part = pl.BlockSpec((depth, tile), lambda i: (0, i))
+    return pl.pallas_call(
+        pair_kernel,
+        out_shape=jax.ShapeDtypeStruct((2, depth, columns), half.dtype),
+        grid=(columns // tile,),
+        in_specs=[part, part],
+        out_specs=pl.BlockSpec((2, depth, tile), lambda i: (0, 0, i)),
         compiler_params=pltpu.CompilerParams(vmem_limit_bytes=12 << 20),
         cost_estimate=COST,
-        name="copies",
+        name="pair",
     )(half, twin)
 
 
@@ -398,35 +456,40 @@
     twin_half = shift(half, "zl", 1)
 
     key_part = across_y(by_target(key_cache.reshape(sides)))
-    value_slots, key_part, pieces[1:6], twin_half, places, starts, fits = lax.optimization_barrier(
-        (by_target(value_cache.reshape(sides)), key_part, pieces[1:6], twin_half, places, starts, fits)
-    )
+    gain = norm_gain.reshape(-1, 1)
+    tables = (ids, places, starts, fits, gain, cosine, sine)
+    value_slots, key_part, pieces[1:6], twin_half, tables = lax.optimization_barrier(
+        (by_target(value_cache.reshape(sides)), key_part, pieces[1:6], twin_half, tables)
+    )
+    ids, places, starts, fits, gain, cosine, sine = tables
     value_part = across_y(value_slots)
+    halves = lax.all_gather(pair(half, twin_half), "x").reshape((blocks,) + half.shape)
     keys = across_z(pack(places, key_part, PACKED))
+    value_part, keys[1] = lax.optimization_barrier((value_part, keys[1]))
+    packed_values, keys, pieces[6:] = lax.optimization_barrier(
+        (pack(places, value_part, PACKED), keys, pieces[6:])
+    )
+    values = across_z(packed_values)
     q, g, k, v = project(
-        ids, pieces, norm_gain, q_weight, gate_weight, k_weight, v_weight,
+        ids, pieces, gain, q_weight, gate_weight, k_weight, v_weight,
         q_norm_gain, k_norm_gain, cosine, sine,
     )
-    repeated, value_part, q = lax.optimization_barrier(
-        (copies(half, twin_half), value_part, q)
-    )
-    packed_values = pack(places, value_part, PACKED)
-    repeated, packed_values, keys = lax.optimization_barrier((repeated, packed_values, keys))
-    values = across_z(packed_values)
-    halves = lax.all_to_all(repeated, "x", 0, 0, tiled=True)
-    halves = halves.reshape((blocks,) + half.shape)
-    other_halves = shift(halves, "c", 1)
-
-    def packed(keys, values, key_part, value_part, q, g, k, v):
-        return attend(starts, my_lengths, q, g, k, v, keys, values, window)
-
-    def full(keys, values, key_part, value_part, q, g, k, v):
-        size = 8 * capacity * window
+
+    size = 8 * capacity * window
+
+    def packed(values, key_part, value_part, q, g, k, v, *weighed):
+        return mix(starts, my_lengths, *weighed, values)
+
+    def full(values, key_part, value_part, q, g, k, v, *weighed):
         places, starts = packing(size)
         keys, values = (across_z(pack(places, a, size)) for a in (key_part, value_part))
-        return attend(starts, my_lengths, q, g, k, v, keys, values, window)
-
-    attended = lax.cond(fits, packed, full, keys, values, key_part, value_part, q, g, k, v)
+        weighed = weigh(starts, my_lengths, q, g, k, v, keys, window)
+        return mix(starts, my_lengths, *weighed, values)
+
+    weighed = weigh(starts, my_lengths, q, g, k, v, keys, window)
+    halves, weighed = lax.optimization_barrier((halves, weighed))
+    other_halves = shift(halves, "c", 1)
+    attended = lax.cond(fits, packed, full, values, key_part, value_part, q, g, k, v, *weighed)
     heads = lax.all_to_all(
         attended.reshape(blocks, rows // blocks, attended.shape[1]), TENSOR, 0, 0, tiled=True
     )

time: 169 us -> 168 us (level)
  waiting for transfers between devices: 62.5 us -> 40.8 us
  between operations: 0.88 us -> 14.2 us
  Pallas kernels: 41.5 us -> 49 us
  starting transfers between devices: 47.9 us -> 46.2 us
    ppermute x15, waiting for transfers between devices: 42.1 us -> 25.2 us  [shift(): return lax.ppermute(value, axis, ring(lax.axis_size(axis), step))]
    pallas_call x2 -> x3, Pallas kernels: 10.8 us -> 18.9 us  [the longest x1 9.24 us: weigh(): pl.pallas_call(weigh_kernel, out_shape=(jax.ShapeDtypeStruct((shares * ro...]
    all_to_all x1 -> x0, waiting for transfers between devices: 7.68 us -> none  [local(): halves = lax.all_to_all(repeated, 'x', 0, 0, tiled=True)]
    all_to_all x1 -> x0, starting transfers between devices: 4.98 us -> none  [local(): halves = lax.all_to_all(repeated, 'x', 0, 0, tiled=True)]
    ppermute x15, starting transfers between devices: 29.3 us -> 32.3 us  [shift(): return lax.ppermute(value, axis, ring(lax.axis_size(axis), step))]
    all_to_all x2, waiting for transfers between devices: 0.01 us -> 2.8 us  [across_y(): flat = lax.all_to_all(flat, ('y', 'c'), 0, 0, tiled=True)]
    unnamed x20 -> x16, local copies, waits for them, and re-layouts: 4.32 us -> 4.84 us
  transfers between devices with their start and end apart: 19 -> 19, of which waited for: 9 -> 8; matrix products, arithmetic and copies ran while one was open for 6% -> 7% of each run, Pallas kernels for 21% -> 20%
where the time goes in v9:
time: 168 us; the launch traced here: 166 us
  Pallas kernels  49 us (29%)
  starting transfers between devices  46.2 us (28%)
  waiting for transfers between devices  40.8 us (24%)
  between operations  14.2 us (8%)
  local copies, waits for them, and re-layouts  9.48 us (6%)
  other arithmetic  6.49 us (4%)
    ppermute x15, starting transfers between devices, shift(): return lax.ppermute(value, axis, ring(lax.axis_size(axis), step))  32.3 us
    ppermute x15, waiting for transfers between devices, shift(): return lax.ppermute(value, axis, ring(lax.axis_size(axis), step))  25.2 us
    pallas_call x1, Pallas kernels, project(): pl.pallas_call(project_kernel, out_shape=(jax.ShapeDtypeStruct((rows, wq....  14.2 us
    all_to_all x1, waiting for transfers between devices, local(): lax.all_to_all(attended.reshape(blocks, rows // blocks, attended.shape[1]...  12.8 us
    all_to_all x2, starting transfers between devices, across_y(): flat = lax.all_to_all(flat, ('y', 'c'), 0, 0, tiled=True)  10.3 us
    pallas_call x1, Pallas kernels, weigh(): pl.pallas_call(weigh_kernel, out_shape=(jax.ShapeDtypeStruct((shares * ro...  9.24 us
    pallas_call x1, Pallas kernels, mix(): pl.pallas_call(mix_kernel, out_shape=jax.ShapeDtypeStruct((rows, columns)...  6.33 us
    pallas_call x2, Pallas kernels, pack(): pl.pallas_call(pack_kernel, out_shape=[jax.ShapeDtypeStruct((size, head),...  6.19 us
  transfers between devices with their start and end apart: 19, of which 8 were waited for; matrix products, arithmetic and copies ran while one was open for 7% of the time, Pallas kernels for 20%

profile of v9, /device:TPU:8, one launch (start us, length us, event | category | flops | bytes accessed | tf_op | source)
XLA Modules:
  0.0 166.2 jit_solution(13477038584432380952)
XLA Ops:
  6.5 1.9 %collective-permute-start.6 = (bf16[1536,256]{1,0:T(8,128)(2,1)}, bf16[1536,256]{1,0:T(8,128)(2,1)}, u32[]{:S(2)}, u32[]{:S(2)}) collective-permute-start(bf16[1536,256]{1,0:T(8,128)(2,1)} %refs_0_.1), channel_id=1, source_target_pairs={{0,4},{4,0},{1,5},{5,1},{2,6},{6,2},{3,7},{7,3},{8,12},{12,8},{9,1... | collective-permute-start | bytes 2359304 | tf_op jit(solution)/shard_map/ppermute | solution.py:29
  8.5 1.5 collective-permute-start.7
  9.9 1.7 %collective-permute-start.8 = (bf16[1536,256]{1,0:T(8,128)(2,1)}, bf16[1536,256]{1,0:T(8,128)(2,1)}, u32[]{:S(2)}, u32[]{:S(2)}) collective-permute-start(bf16[1536,256]{1,0:T(8,128)(2,1)} %refs_0_.1), channel_id=1, source_target_pairs={{0,3},{1,0},{2,1},{3,2},{4,7},{5,4},{6,5},{7,6},{8,11},{9,8},{10,9... | collective-permute-start | bytes 2359304 | tf_op jit(solution)/shard_map/ppermute | solution.py:29
  11.7 1.6 copy-done.2
  13.3 1.8 %by_target.3 = bf16[4,2,4,2,128,128]{5,4,3,2,1,0:T(8,128)(2,1)} custom-call(bf16[4,4,2,2,128,128]{5,4,3,2,1,0:T(8,128)(2,1)S(1)} %bitcast.25), custom_call_target="tpu_custom_call" | custom-call | flops 1048576 | bytes 67108864 | tf_op jit(solution)/shard_map/by_target/pallas_call | solution.py:292
  15.1 5.0 %all-to-all-start = ((bf16[8,1024,128]{2,1,0:T(8,128)(2,1)}), bf16[8,1024,128]{2,1,0:T(8,128)(2,1)}, u32[]{:S(2)}, u32[]{:S(2)}) async-start(bf16[8,1024,128]{2,1,0:T(8,128)(2,1)} %bitcast.3), calls=%async_computation | async-start | bytes 4194304 | tf_op jit(solution)/shard_map/all_to_all | solution.py:367
  20.2 0.1 reshape.370
  20.4 0.1 reshape.369
  20.5 0.1 copy.23
  20.5 0.2 convert_reduce_fusion
  20.7 0.1 copy.25
  20.8 0.3 fusion.9
  21.1 0.6 gather_fusion.1
  21.7 0.6 gather_fusion
  22.2 0.1 add_multiply_fusion
  22.3 0.1 iota_add_fusion
  22.4 0.1 add.400
  22.4 0.2 select_reduce_fusion.1
  22.7 0.2 reduce_window_sum.11
  22.9 0.2 select_reduce_fusion.2
  23.1 0.1 add_convert_fusion
  23.2 0.9 constant_dynamic-slice_fusion.2.half
  24.0 2.3 %collective-permute-done.6.refs_1_ = bf16[1536,256]{1,0:T(8,128)(2,1)} collective-permute-done((bf16[1536,256]{1,0:T(8,128)(2,1)}, bf16[1536,256]{1,0:T(8,128)(2,1)}, u32[]{:S(2)}, u32[]{:S(2)}) %collective-permute-start.6) | collective-permute-done | bytes 786464 | tf_op jit(solution)/shard_map/ppermute | solution.py:29
  26.3 1.5 collective-permute-start.9
  27.8 1.7 %collective-permute-start.10 = (bf16[1536,256]{1,0:T(8,128)(2,1)}, bf16[1536,256]{1,0:T(8,128)(2,1)}, u32[]{:S(2)}, u32[]{:S(2)}) collective-permute-start(bf16[1536,256]{1,0:T(8,128)(2,1)} %collective-permute-done.6.refs_1_), channel_id=1, source_target_pairs={{0,3},{1,0},{2,1},{3,2},{4,7},{5,4},{6,5},{7,6},{8,11},{9,8},{10,9... | collective-permute-start | bytes 2359304 | tf_op jit(solution)/shard_map/ppermute | solution.py:29
  29.6 0.1 copy.28
  29.6 0.1 min.21
  29.7 0.1 copy.27
  29.8 1.8 %collective-permute-start.11 = (bf16[128,2048]{1,0:T(8,128)(2,1)}, bf16[128,2048]{1,0:T(8,128)(2,1)}, u32[]{:S(2)}, u32[]{:S(2)}) collective-permute-start(bf16[128,2048]{1,0:T(8,128)(2,1)} %constant_dynamic-slice_fusion.2.half), channel_id=1, source_target_pairs={{0,4},{4,0},{1,5},{5,1},{2,6},{6,2},{3,7},{7,3},{8,12},{12,8},{9,1... | collective-permute-start | bytes 1572872 | tf_op jit(solution)/shard_map/ppermute | solution.py:29
  31.6 0.1 pad_add_fusion.2.offsets
  31.7 0.1 convert_element_type.25
  31.8 0.6 reduce_max.9
  33.1 0.6 stack.35.ids
  33.7 1.9 %by_target.2 = bf16[4,2,4,2,128,128]{5,4,3,2,1,0:T(8,128)(2,1)} custom-call(bf16[4,4,2,2,128,128]{5,4,3,2,1,0:T(8,128)(2,1)S(1)} %bitcast.26), custom_call_target="tpu_custom_call" | custom-call | flops 1048576 | bytes 67108864 | tf_op jit(solution)/shard_map/by_target/pallas_call | solution.py:292
  35.6 4.3 %fusion = (f32[1536,128]{1,0:T(8,128)}, f32[1536,128]{1,0:T(8,128)}) fusion(f32[128]{0:T(128)S(1)} %get-tuple-element.196, f32[128]{0:T(128)S(1)} %get-tuple-element.197, f32[1536]{0:T(1024)S(1)} %convert_element_type.25), kind=kLoop, calls=%fused_computation.7 | loop fusion | flops 393216 | bytes 1580032 | tf_op jit(solution)/shard_map/mul | solution.py:447
  39.8 2.8 %collective-permute-done.11.twin = bf16[128,2048]{1,0:T(8,128)(2,1)} collective-permute-done((bf16[128,2048]{1,0:T(8,128)(2,1)}, bf16[128,2048]{1,0:T(8,128)(2,1)}, u32[]{:S(2)}, u32[]{:S(2)}) %collective-permute-start.11) | collective-permute-done | bytes 524320 | tf_op jit(solution)/shard_map/ppermute | solution.py:29
  42.6 3.8 %collective-permute-done.9.refs_4_ = bf16[1536,256]{1,0:T(8,128)(2,1)} collective-permute-done((bf16[1536,256]{1,0:T(8,128)(2,1)}, bf16[1536,256]{1,0:T(8,128)(2,1)}, u32[]{:S(2)}, u32[]{:S(2)}) %collective-permute-start.9) | collective-permute-done | bytes 786464 | tf_op jit(solution)/shard_map/ppermute | solution.py:29
  46.4 1.0 copy-done.4
  47.5 3.4 %pair.1 = bf16[2,128,2048]{2,1,0:T(8,128)(2,1)} custom-call(bf16[128,2048]{1,0:T(8,128)(2,1)S(1)} %copy-done.4, bf16[128,2048]{1,0:T(8,128)(2,1)} %collective-permute-done.11.twin), custom_call_target="tpu_custom_call" | custom-call | flops 1048576 | bytes 1048576 | tf_op jit(solution)/shard_map/pair/pallas_call | solution.py:312
  50.9 5.3 %all-to-all-start.1 = ((bf16[8,1024,128]{2,1,0:T(8,128)(2,1)}), bf16[8,1024,128]{2,1,0:T(8,128)(2,1)}, u32[]{:S(2)}, u32[]{:S(2)}) async-start(bf16[8,1024,128]{2,1,0:T(8,128)(2,1)} %bitcast.17), calls=%async_computation.1 | async-start | bytes 4194304 | tf_op jit(solution)/shard_map/all_to_all | solution.py:367
  56.2 1.1 collective-permute-start.15
  57.3 2.1 %collective-permute-start.16 = (bf16[1536,256]{1,0:T(8,128)(2,1)}, bf16[1536,256]{1,0:T(8,128)(2,1)}, u32[]{:S(2)}, u32[]{:S(2)}) collective-permute-start(bf16[1536,256]{1,0:T(8,128)(2,1)} %collective-permute-done.10.refs_5_), channel_id=1, source_target_pairs={{0,3},{1,0},{2,1},{3,2},{4,7},{5,4},{6,5},{7,6},{8,11},{9,8},{10,9... | collective-permute-start | bytes 2359304 | tf_op jit(solution)/shard_map/ppermute | solution.py:29
  59.4 3.1 %pack.6 = (bf16[1088,128]{1,0:T(8,128)(2,1)S(1)}, bf16[1088,128]{1,0:T(8,128)(2,1)S(1)}, bf16[1088,128]{1,0:T(8,128)(2,1)}, bf16[1088,128]{1,0:T(8,128)(2,1)S(1)}) custom-call(s32[68]{0:T(128)S(1)} %pad_add_fusion.2.offsets, bf16[8,4,2,128,128]{4,3,2,1,0:T(8,128)(2,1)} %bitcast.4.cache), custom_call_target="tpu_custom_call" | custom-call | flops 1048576 | bytes 1048576 | tf_op jit(solution)/shard_map/pack/pallas_call | solution.py:269
  62.5 3.3 %collective-permute-start.12 = (bf16[1088,128]{1,0:T(8,128)(2,1)S(1)}, bf16[1088,128]{1,0:T(8,128)(2,1)S(1)}, u32[]{:S(2)}, u32[]{:S(2)}) collective-permute-start(bf16[1088,128]{1,0:T(8,128)(2,1)S(1)} %get-tuple-element.146), channel_id=1, source_target_pairs={{0,16},{16,32},{32,48},{48,0},{1,17},{17,33},{33,49},{49,1},{2,18}... | collective-permute-start | bytes 835592 | tf_op jit(solution)/shard_map/ppermute | solution.py:29
  65.8 4.7 %collective-permute-start.13 = (bf16[1088,128]{1,0:T(8,128)(2,1)}, bf16[1088,128]{1,0:T(8,128)(2,1)S(1)}, u32[]{:S(2)}, u32[]{:S(2)}) collective-permute-start(bf16[1088,128]{1,0:T(8,128)(2,1)} %get-tuple-element.154), channel_id=1, source_target_pairs={{0,32},{16,48},{32,0},{48,16},{1,33},{17,49},{33,1},{49,17},{2,34}... | collective-permute-start | bytes 835592 | tf_op jit(solution)/shard_map/ppermute | solution.py:29
  70.5 2.7 %collective-permute-start.14 = (bf16[1088,128]{1,0:T(8,128)(2,1)S(1)}, bf16[1088,128]{1,0:T(8,128)(2,1)S(1)}, u32[]{:S(2)}, u32[]{:S(2)}) collective-permute-start(bf16[1088,128]{1,0:T(8,128)(2,1)S(1)} %get-tuple-element.155), channel_id=1, source_target_pairs={{0,48},{16,0},{32,16},{48,32},{1,49},{17,1},{33,17},{49,33},{2,50}... | collective-permute-start | bytes 835592 | tf_op jit(solution)/shard_map/ppermute | solution.py:29
  73.1 6.1 %collective-permute-done.12.refs_1_ = bf16[1088,128]{1,0:T(8,128)(2,1)S(1)} collective-permute-done((bf16[1088,128]{1,0:T(8,128)(2,1)S(1)}, bf16[1088,128]{1,0:T(8,128)(2,1)S(1)}, u32[]{:S(2)}, u32[]{:S(2)}) %collective-permute-start.12) | collective-permute-done | bytes 278560 | tf_op jit(solution)/shard_map/ppermute | solution.py:29
  79.3 2.8 %all-to-all-done.1 = bf16[8,1024,128]{2,1,0:T(8,128)(2,1)} async-done(((bf16[8,1024,128]{2,1,0:T(8,128)(2,1)}), bf16[8,1024,128]{2,1,0:T(8,128)(2,1)}, u32[]{:S(2)}, u32[]{:S(2)}) %all-to-all-start.1) | async-done | bytes 2097184 | tf_op jit(solution)/shard_map/all_to_all | solution.py:367
  82.1 3.1 %pack.7 = (bf16[1088,128]{1,0:T(8,128)(2,1)}, bf16[1088,128]{1,0:T(8,128)(2,1)S(1)}, bf16[1088,128]{1,0:T(8,128)(2,1)S(1)}, bf16[1088,128]{1,0:T(8,128)(2,1)S(1)}) custom-call(s32[68]{0:T(128)S(1)} %pad_add_fusion.2.offsets, bf16[8,4,2,128,128]{4,3,2,1,0:T(8,128)(2,1)} %bitcast.18.cache), custom_call_target="tpu_custom_call" | custom-call | flops 1048576 | bytes 1048576 | tf_op jit(solution)/shard_map/pack/pallas_call | solution.py:269
  85.1 3.5 %collective-permute-done.13.refs_2_ = bf16[1088,128]{1,0:T(8,128)(2,1)S(1)} collective-permute-done((bf16[1088,128]{1,0:T(8,128)(2,1)}, bf16[1088,128]{1,0:T(8,128)(2,1)S(1)}, u32[]{:S(2)}, u32[]{:S(2)}) %collective-permute-start.13) | collective-permute-done | bytes 278560 | tf_op jit(solution)/shard_map/ppermute | solution.py:29
  88.6 6.8 %collective-permute-done.14.refs_3_ = bf16[1088,128]{1,0:T(8,128)(2,1)S(1)} collective-permute-done((bf16[1088,128]{1,0:T(8,128)(2,1)S(1)}, bf16[1088,128]{1,0:T(8,128)(2,1)S(1)}, u32[]{:S(2)}, u32[]{:S(2)}) %collective-permute-start.14) | collective-permute-done | bytes 278560 | tf_op jit(solution)/shard_map/ppermute | solution.py:29
  95.3 1.6 collective-permute-start.17
  97.0 4.2 %collective-permute-start.18 = (bf16[1088,128]{1,0:T(8,128)(2,1)S(1)}, bf16[1088,128]{1,0:T(8,128)(2,1)}, u32[]{:S(2)}, u32[]{:S(2)}) collective-permute-start(bf16[1088,128]{1,0:T(8,128)(2,1)S(1)} %get-tuple-element.179), channel_id=1, source_target_pairs={{0,32},{16,48},{32,0},{48,16},{1,33},{17,49},{33,1},{49,17},{2,34}... | collective-permute-start | bytes 835592 | tf_op jit(solution)/shard_map/ppermute | solution.py:29
  101.2 2.4 %collective-permute-start.19 = (bf16[1088,128]{1,0:T(8,128)(2,1)S(1)}, bf16[1088,128]{1,0:T(8,128)(2,1)}, u32[]{:S(2)}, u32[]{:S(2)}) collective-permute-start(bf16[1088,128]{1,0:T(8,128)(2,1)S(1)} %get-tuple-element.180), channel_id=1, source_target_pairs={{0,48},{16,0},{32,16},{48,32},{1,49},{17,1},{33,17},{49,33},{2,50}... | collective-permute-start | bytes 835592 | tf_op jit(solution)/shard_map/ppermute | solution.py:29
  103.6 1.4 copy.29.refs_8_
  105.0 14.2 %project.1 = (bf16[1536,256]{1,0:T(8,128)(2,1)}, f32[1536,256]{1,0:T(8,128)}, bf16[1536,128]{1,0:T(8,128)(2,1)S(1)}, bf16[1536,128]{1,0:T(8,128)(2,1)}) custom-call(s32[8]{0:T(128)} %stack.35.ids, bf16[1536,256]{1,0:T(8,128)(2,1)} %refs_0_.1, bf16[1536,256]{1,0:T(8,128)(2,1)} %collective-permute-done.6.refs_1_, ...), custom_call_target="tpu_custom_call" | custom-call | flops 1048576 | bytes 1048576 | tf_op jit(solution)/shard_map/project/pallas_call | solution.py:105
  119.2 9.2 %weigh.3 = (bf16[3072,128]{1,0:T(8,128)(2,1)}, f32[1536,256]{1,0:T(8,128)}, f32[1536,256]{1,0:T(8,128)}) custom-call(s32[24]{0:T(128)S(1)} %get-tuple-element.165.starts, s32[24]{0:T(128)S(1)} %get-tuple-element.195.lengths, bf16[1536,256]{1,0:T(8,128)(2,1)} %get-tuple-element.161.q, f32[1536,256]{1,0:T(8,128)} %get-tuple-element.162.g, ...), custom_call_target="tpu_custom_call" | custom-call | flops 1048576 | bytes 1048576 | tf_op jit(solution)/shard_map/weigh/pallas_call | solution.py:181
  128.4 6.4 %conditional.1 = (bf16[1536,256]{1,0:T(8,128)(2,1)}) conditional(s32[]{:T(128)} %convert_element_type.27, (s32[24]{0:T(128)S(1)}, s32[24]{0:T(128)S(1)}, s32[4,16]{1,0:T(4,128)S(1)}, s32[4,16]{1,0:T(4,128)S(1)}, s32[4]{0:T(128)S(1)}, /*index=5*/bf16[8,4,2,128,128]{4,3,2,1,0:T(8,128)(2,1)}, s32[24]{0:T(128)S(1)}, bf16[1536,256]{1,0:T(8,128)(2,1)}, ...), branch_computations={%region_6.7_spmd, %region_7.8_spmd} | conditional | flops 4194636 | bytes 27789708 | solution.py:492
  128.5 6.3 %mix.3 = bf16[1536,256]{1,0:T(8,128)(2,1)} custom-call(s32[24]{0:T(128)S(1)} %get-tuple-element.77.starts, s32[24]{0:T(128)S(1)} %get-tuple-element.78.lengths, bf16[3072,128]{1,0:T(8,128)(2,1)} %get-tuple-element.79.weights, f32[1536,256]{1,0:T(8,128)} %get-tuple-element.80.mixed_new, f32[1536,256]{1,0:T(8,128)} %get-tuple-element.81.factor, ...), custom_call_target="tpu_custom_call" | custom-call | flops 1048576 | bytes 1048576 | tf_op jit(solution)/shard_map/cond/branch_1_fun/mix/pallas_call | solution.py:235
  134.8 3.6 %all-to-all-start.2 = ((bf16[8,192,256]{2,1,0:T(8,128)(2,1)}), bf16[8,192,256]{2,1,0:T(8,128)(2,1)S(1)}, u32[]{:S(2)}, u32[]{:S(2)}) async-start(bf16[8,192,256]{2,1,0:T(8,128)(2,1)} %bitcast.21), calls=%async_computation.2 | async-start | bytes 1572864 | tf_op jit(solution)/shard_map/all_to_all | solution.py:493
  138.4 0.1 pad_add_fusion.1.places
  138.5 12.8 %all-to-all-done.2.heads = bf16[8,192,256]{2,1,0:T(8,128)(2,1)S(1)} async-done(((bf16[8,192,256]{2,1,0:T(8,128)(2,1)}), bf16[8,192,256]{2,1,0:T(8,128)(2,1)S(1)}, u32[]{:S(2)}, u32[]{:S(2)}) %all-to-all-start.2) | async-done | bytes 786464 | tf_op jit(solution)/shard_map/all_to_all | solution.py:493
  151.2 2.2 %copy-done.1 = bf16[8,128,2048]{2,1,0:T(8,128)(2,1)S(1)} copy-done((bf16[8,128,2048]{2,1,0:T(8,128)(2,1)S(1)}, bf16[8,128,2048]{2,1,0:T(8,128)(2,1)}, u32[]{:S(2)}) %copy-start.1) | copy-done | bytes 4194328
  153.4 6.0 %project_out.1 = bf16[192,2048]{1,0:T(8,128)(2,1)} custom-call(s32[9]{0:T(128)S(1)} %pad_add_fusion.1.places, bf16[8,192,256]{2,1,0:T(8,128)(2,1)S(1)} %all-to-all-done.2.heads, bf16[8,128,2048]{2,1,0:T(8,128)(2,1)S(1)} %copy-done.1, bf16[8,128,2048]{2,1,0:T(8,128)(2,1)} %collective-permute-done.20.other), custom_call_target="tpu_custom_call" | custom-call | flops 1048576 | bytes 1048576 | tf_op jit(solution)/shard_map/project_out/pallas_call | solution.py:348
  (42 shorter events, 0.3 us)
Async XLA Ops:
  6.5 16.6 %copy-start = (bf16[256,2048]{1,0:T(8,128)(2,1)S(1)}, bf16[256,2048]{1,0:T(8,128)(2,1)}, u32[]{:S(2)}) copy-start(bf16[256,2048]{1,0:T(8,128)(2,1)} %param.23) | copy-start | bytes 3145732
  6.5 19.8 %collective-permute-start.6 = (bf16[1536,256]{1,0:T(8,128)(2,1)}, bf16[1536,256]{1,0:T(8,128)(2,1)}, u32[]{:S(2)}, u32[]{:S(2)}) collective-permute-start(bf16[1536,256]{1,0:T(8,128)(2,1)} %refs_0_.1), channel_id=1, source_target_pairs={{0,4},{4,0},{1,5},{5,1},{2,6},{6,2},{3,7},{7,3},{8,12},{12,8},{9,1... | collective-permute-start | bytes 2359304 | tf_op jit(solution)/shard_map/ppermute | solution.py:29
  8.5 31.4 %collective-permute-start.7 = (bf16[1536,256]{1,0:T(8,128)(2,1)}, bf16[1536,256]{1,0:T(8,128)(2,1)}, u32[]{:S(2)}, u32[]{:S(2)}) collective-permute-start(bf16[1536,256]{1,0:T(8,128)(2,1)} %refs_0_.1), channel_id=1, source_target_pairs={{0,1},{1,2},{2,3},{3,0},{4,5},{5,6},{6,7},{7,4},{8,9},{9,10},{10,1... | collective-permute-start | bytes 2359304 | tf_op jit(solution)/shard_map/ppermute | solution.py:29
  9.9 29.9 %collective-permute-start.8 = (bf16[1536,256]{1,0:T(8,128)(2,1)}, bf16[1536,256]{1,0:T(8,128)(2,1)}, u32[]{:S(2)}, u32[]{:S(2)}) collective-permute-start(bf16[1536,256]{1,0:T(8,128)(2,1)} %refs_0_.1), channel_id=1, source_target_pairs={{0,3},{1,0},{2,1},{3,2},{4,7},{5,4},{6,5},{7,6},{8,11},{9,8},{10,9... | collective-permute-start | bytes 2359304 | tf_op jit(solution)/shard_map/ppermute | solution.py:29
  11.7 1.6 copy-start.2
  15.1 5.1 %copy-start.9 = (s32[768]{0:T(1024)S(1)}, s32[768]{0:T(1024)}, u32[]{:S(2)}) copy-start(s32[768]{0:T(1024)} %param.27) | copy-start | bytes 9220
  15.1 5.2 %copy-start.10 = (s32[768,1]{0,1:T(1,128)S(1)}, s32[768,1]{0,1:T(1,128)}, u32[]{:S(2)}) copy-start(s32[768,1]{0,1:T(1,128)} %param.26) | copy-start | bytes 9220
  15.1 18.6 %copy-start.3 = (bf16[1,64,128,128]{3,2,1,0:T(8,128)(2,1)S(1)}, bf16[1,64,128,128]{3,2,1,0:T(8,128)(2,1)}, u32[]{:S(2)}) copy-start(bf16[1,64,128,128]{3,2,1,0:T(8,128)(2,1)} %param.25) | copy-start | bytes 6291460
  15.1 31.3 %all-to-all-start = ((bf16[8,1024,128]{2,1,0:T(8,128)(2,1)}), bf16[8,1024,128]{2,1,0:T(8,128)(2,1)}, u32[]{:S(2)}, u32[]{:S(2)}) async-start(bf16[8,1024,128]{2,1,0:T(8,128)(2,1)} %bitcast.3), calls=%async_computation | async-start | bytes 4194304 | tf_op jit(solution)/shard_map/all_to_all | solution.py:367
  20.2 108.2 %all-gather.3.cloned.1.call-start = ((), (), s32[]{:S(2)}) async-start(), calls=%async_computation.3 | async-start | bytes 5242880 | tf_op jit(solution)/shard_map/all_gather | solution.py:466
  26.3 20.1 %collective-permute-start.9 = (bf16[1536,256]{1,0:T(8,128)(2,1)}, bf16[1536,256]{1,0:T(8,128)(2,1)}, u32[]{:S(2)}, u32[]{:S(2)}) collective-permute-start(bf16[1536,256]{1,0:T(8,128)(2,1)} %collective-permute-done.6.refs_1_), channel_id=1, source_target_pairs={{0,1},{1,2},{2,3},{3,0},{4,5},{5,6},{6,7},{7,4},{8,9},{9,10},{10,1... | collective-permute-start | bytes 2359304 | tf_op jit(solution)/shard_map/ppermute | solution.py:29
  27.8 18.6 %collective-permute-start.10 = (bf16[1536,256]{1,0:T(8,128)(2,1)}, bf16[1536,256]{1,0:T(8,128)(2,1)}, u32[]{:S(2)}, u32[]{:S(2)}) collective-permute-start(bf16[1536,256]{1,0:T(8,128)(2,1)} %collective-permute-done.6.refs_1_), channel_id=1, source_target_pairs={{0,3},{1,0},{2,1},{3,2},{4,7},{5,4},{6,5},{7,6},{8,11},{9,8},{10,9... | collective-permute-start | bytes 2359304 | tf_op jit(solution)/shard_map/ppermute | solution.py:29
  29.8 12.8 %collective-permute-start.11 = (bf16[128,2048]{1,0:T(8,128)(2,1)}, bf16[128,2048]{1,0:T(8,128)(2,1)}, u32[]{:S(2)}, u32[]{:S(2)}) collective-permute-start(bf16[128,2048]{1,0:T(8,128)(2,1)} %constant_dynamic-slice_fusion.2.half), channel_id=1, source_target_pairs={{0,4},{4,0},{1,5},{5,1},{2,6},{6,2},{3,7},{7,3},{8,12},{12,8},{9,1... | collective-permute-start | bytes 1572872 | tf_op jit(solution)/shard_map/ppermute | solution.py:29
  46.4 1.0 copy-start.4
  50.9 31.2 %all-to-all-start.1 = ((bf16[8,1024,128]{2,1,0:T(8,128)(2,1)}), bf16[8,1024,128]{2,1,0:T(8,128)(2,1)}, u32[]{:S(2)}, u32[]{:S(2)}) async-start(bf16[8,1024,128]{2,1,0:T(8,128)(2,1)} %bitcast.17), calls=%async_computation.1 | async-start | bytes 4194304 | tf_op jit(solution)/shard_map/all_to_all | solution.py:367
  56.2 47.4 %copy-start.8 = (f32[2048]{0:T(1024)S(1)}, f32[2048]{0:T(1024)}, u32[]{:S(2)}) copy-start(f32[2048]{0:T(1024)} %param.16) | copy-start | bytes 24580
  56.2 28.9 %collective-permute-start.15 = (bf16[1536,256]{1,0:T(8,128)(2,1)}, bf16[1536,256]{1,0:T(8,128)(2,1)}, u32[]{:S(2)}, u32[]{:S(2)}) collective-permute-start(bf16[1536,256]{1,0:T(8,128)(2,1)} %collective-permute-done.7.refs_2_), channel_id=1, source_target_pairs={{0,1},{1,2},{2,3},{3,0},{4,5},{5,6},{6,7},{7,4},{8,9},{9,10},{10,1... | collective-permute-start | bytes 2359304 | tf_op jit(solution)/shard_map/ppermute | solution.py:29
  57.3 38.0 %collective-permute-start.16 = (bf16[1536,256]{1,0:T(8,128)(2,1)}, bf16[1536,256]{1,0:T(8,128)(2,1)}, u32[]{:S(2)}, u32[]{:S(2)}) collective-permute-start(bf16[1536,256]{1,0:T(8,128)(2,1)} %collective-permute-done.10.refs_5_), channel_id=1, source_target_pairs={{0,3},{1,0},{2,1},{3,2},{4,7},{5,4},{6,5},{7,6},{8,11},{9,8},{10,9... | collective-permute-start | bytes 2359304 | tf_op jit(solution)/shard_map/ppermute | solution.py:29
  62.5 16.7 %collective-permute-start.12 = (bf16[1088,128]{1,0:T(8,128)(2,1)S(1)}, bf16[1088,128]{1,0:T(8,128)(2,1)S(1)}, u32[]{:S(2)}, u32[]{:S(2)}) collective-permute-start(bf16[1088,128]{1,0:T(8,128)(2,1)S(1)} %get-tuple-element.146), channel_id=1, source_target_pairs={{0,16},{16,32},{32,48},{48,0},{1,17},{17,33},{33,49},{49,1},{2,18}... | collective-permute-start | bytes 835592 | tf_op jit(solution)/shard_map/ppermute | solution.py:29
  65.8 22.8 %collective-permute-start.13 = (bf16[1088,128]{1,0:T(8,128)(2,1)}, bf16[1088,128]{1,0:T(8,128)(2,1)S(1)}, u32[]{:S(2)}, u32[]{:S(2)}) collective-permute-start(bf16[1088,128]{1,0:T(8,128)(2,1)} %get-tuple-element.154), channel_id=1, source_target_pairs={{0,32},{16,48},{32,0},{48,16},{1,33},{17,49},{33,1},{49,17},{2,34}... | collective-permute-start | bytes 835592 | tf_op jit(solution)/shard_map/ppermute | solution.py:29
  70.5 24.9 %collective-permute-start.14 = (bf16[1088,128]{1,0:T(8,128)(2,1)S(1)}, bf16[1088,128]{1,0:T(8,128)(2,1)S(1)}, u32[]{:S(2)}, u32[]{:S(2)}) collective-permute-start(bf16[1088,128]{1,0:T(8,128)(2,1)S(1)} %get-tuple-element.155), channel_id=1, source_target_pairs={{0,48},{16,0},{32,16},{48,32},{1,49},{17,1},{33,17},{49,33},{2,50}... | collective-permute-start | bytes 835592 | tf_op jit(solution)/shard_map/ppermute | solution.py:29
  95.3 33.1 %collective-permute-start.17 = (bf16[1088,128]{1,0:T(8,128)(2,1)S(1)}, bf16[1088,128]{1,0:T(8,128)(2,1)}, u32[]{:S(2)}, u32[]{:S(2)}) collective-permute-start(bf16[1088,128]{1,0:T(8,128)(2,1)S(1)} %get-tuple-element.178), channel_id=1, source_target_pairs={{0,16},{16,32},{32,48},{48,0},{1,17},{17,33},{33,49},{49,1},{2,18}... | collective-permute-start | bytes 835592 | tf_op jit(solution)/shard_map/ppermute | solution.py:29
  97.0 31.4 %collective-permute-start.18 = (bf16[1088,128]{1,0:T(8,128)(2,1)S(1)}, bf16[1088,128]{1,0:T(8,128)(2,1)}, u32[]{:S(2)}, u32[]{:S(2)}) collective-permute-start(bf16[1088,128]{1,0:T(8,128)(2,1)S(1)} %get-tuple-element.179), channel_id=1, source_target_pairs={{0,32},{16,48},{32,0},{48,16},{1,33},{17,49},{33,1},{49,17},{2,34}... | collective-permute-start | bytes 835592 | tf_op jit(solution)/shard_map/ppermute | solution.py:29
  101.2 27.2 %collective-permute-start.19 = (bf16[1088,128]{1,0:T(8,128)(2,1)S(1)}, bf16[1088,128]{1,0:T(8,128)(2,1)}, u32[]{:S(2)}, u32[]{:S(2)}) collective-permute-start(bf16[1088,128]{1,0:T(8,128)(2,1)S(1)} %get-tuple-element.180), channel_id=1, source_target_pairs={{0,48},{16,0},{32,16},{48,32},{1,49},{17,1},{33,17},{49,33},{2,50}... | collective-permute-start | bytes 835592 | tf_op jit(solution)/shard_map/ppermute | solution.py:29
  134.8 16.4 %collective-permute-start.20 = (bf16[8,128,2048]{2,1,0:T(8,128)(2,1)}, bf16[8,128,2048]{2,1,0:T(8,128)(2,1)}, u32[]{:S(2)}, u32[]{:S(2)}) collective-permute-start(bf16[8,128,2048]{2,1,0:T(8,128)(2,1)} %all-gather.3.cloned.1.call-done.mine), channel_id=1, source_target_pairs={{0,8},{8,0},{1,9},{9,1},{2,10},{10,2},{3,11},{11,3},{4,12},{12,4},... | collective-permute-start | bytes 12582920 | tf_op jit(solution)/shard_map/ppermute | solution.py:29
  134.8 16.4 %all-to-all-start.2 = ((bf16[8,192,256]{2,1,0:T(8,128)(2,1)}), bf16[8,192,256]{2,1,0:T(8,128)(2,1)S(1)}, u32[]{:S(2)}, u32[]{:S(2)}) async-start(bf16[8,192,256]{2,1,0:T(8,128)(2,1)} %bitcast.21), calls=%async_computation.2 | async-start | bytes 1572864 | tf_op jit(solution)/shard_map/all_to_all | solution.py:493
  151.2 2.2 %copy-start.1 = (bf16[8,128,2048]{2,1,0:T(8,128)(2,1)S(1)}, bf16[8,128,2048]{2,1,0:T(8,128)(2,1)}, u32[]{:S(2)}) copy-start(bf16[8,128,2048]{2,1,0:T(8,128)(2,1)} %all-gather.3.cloned.1.call-done.mine) | copy-start | bytes 12582916
Sparse Core Ops, SparseCore 0:
  51.0 60.2 all-gather.2

commit v10 on v9

--- a/solution.py
+++ b/solution.py
@@ -66,7 +66,8 @@
             block = pl.multiple_of(ids[j] * width, width)
             here = pl.ds(block, width)
             for w, first, last in zip((wq, wg, wk, wv), edges, edges[1:]):
-                part = w[here, :].astype(jnp.float32) * gain[here, :]
+                lanes = jnp.concatenate([gain[here, :]] * ((last - first) // head), axis=1)
+                part = w[here, :].astype(jnp.float32) * lanes
                 scaled[j * width : (j + 1) * width, first:last] = part.astype(jnp.bfloat16)
 
     total = jnp.zeros((rows, 128), jnp.float32)
@@ -456,24 +457,22 @@
     twin_half = shift(half, "zl", 1)
 
     key_part = across_y(by_target(key_cache.reshape(sides)))
-    gain = norm_gain.reshape(-1, 1)
+    gain = jnp.broadcast_to(norm_gain[:, None], (norm_gain.shape[0], head_dim))
     tables = (ids, places, starts, fits, gain, cosine, sine)
-    value_slots, key_part, pieces[1:6], twin_half, tables = lax.optimization_barrier(
-        (by_target(value_cache.reshape(sides)), key_part, pieces[1:6], twin_half, tables)
+    value_slots, key_part, pieces[1:6], both_halves, tables = lax.optimization_barrier(
+        (by_target(value_cache.reshape(sides)), key_part, pieces[1:6], pair(half, twin_half), tables)
     )
     ids, places, starts, fits, gain, cosine, sine = tables
     value_part = across_y(value_slots)
-    halves = lax.all_gather(pair(half, twin_half), "x").reshape((blocks,) + half.shape)
+    halves = lax.all_gather(both_halves, "x").reshape((blocks,) + half.shape)
     keys = across_z(pack(places, key_part, PACKED))
-    value_part, keys[1] = lax.optimization_barrier((value_part, keys[1]))
-    packed_values, keys, pieces[6:] = lax.optimization_barrier(
-        (pack(places, value_part, PACKED), keys, pieces[6:])
-    )
-    values = across_z(packed_values)
     q, g, k, v = project(
         ids, pieces, gain, q_weight, gate_weight, k_weight, v_weight,
         q_norm_gain, k_norm_gain, cosine, sine,
     )
+    value_part, keys[1], q = lax.optimization_barrier((value_part, keys[1], q))
+    packed_values, keys = lax.optimization_barrier((pack(places, value_part, PACKED), keys))
+    values = across_z(packed_values)
 
     size = 8 * capacity * window
 

time: 168 us -> 173 us (1.030)
  starting transfers between devices: 46.2 us -> 50.6 us
  waiting for transfers between devices: 40.8 us -> 43.1 us
    ppermute x15, waiting for transfers between devices: 25.2 us -> 30.5 us  [shift(): return lax.ppermute(value, axis, ring(lax.axis_size(axis), step))]
    ppermute x15, starting transfers between devices: 32.3 us -> 35.4 us  [shift(): return lax.ppermute(value, axis, ring(lax.axis_size(axis), step))]
    all_to_all x2, waiting for transfers between devices: 2.8 us -> 0.01 us  [across_y(): flat = lax.all_to_all(flat, ('y', 'c'), 0, 0, tiled=True)]
    unnamed x16 -> x18, local copies, waits for them, and re-layouts: 4.84 us -> 3.81 us
  transfers between devices with their start and end apart: 19 -> 19, of which waited for: 8 -> 9; matrix products, arithmetic and copies ran while one was open for 7% -> 6% of each run, Pallas kernels for 20% -> 21%
where the time goes in v10:
time: 173 us; the launch traced here: 171 us
  starting transfers between devices  50.6 us (29%)
  Pallas kernels  48 us (28%)
  waiting for transfers between devices  43.1 us (25%)
  between operations  14.2 us (8%)
  local copies, waits for them, and re-layouts  8.42 us (5%)
  other arithmetic  6.49 us (4%)
    ppermute x15, starting transfers between devices, shift(): return lax.ppermute(value, axis, ring(lax.axis_size(axis), step))  35.4 us
    ppermute x15, waiting for transfers between devices, shift(): return lax.ppermute(value, axis, ring(lax.axis_size(axis), step))  30.5 us
    pallas_call x1, Pallas kernels, project(): pl.pallas_call(project_kernel, out_shape=(jax.ShapeDtypeStruct((rows, wq....  13.7 us
    all_to_all x1, waiting for transfers between devices, local(): lax.all_to_all(attended.reshape(blocks, rows // blocks, attended.shape[1]...  12.6 us
    all_to_all x2, starting transfers between devices, across_y(): flat = lax.all_to_all(flat, ('y', 'c'), 0, 0, tiled=True)  10.4 us
    pallas_call x1, Pallas kernels, weigh(): pl.pallas_call(weigh_kernel, out_shape=(jax.ShapeDtypeStruct((shares * ro...  9.28 us
    pallas_call x1, Pallas kernels, mix(): pl.pallas_call(mix_kernel, out_shape=jax.ShapeDtypeStruct((rows, columns)...  6.33 us
    pallas_call x1, Pallas kernels, project_out(): pl.pallas_call(output_kernel, out_shape=jax.ShapeDtypeStruct((rows, colum...  5.99 us
  transfers between devices with their start and end apart: 19, of which 9 were waited for; matrix products, arithmetic and copies ran while one was open for 6% of the time, Pallas kernels for 21%

profile of v10, /device:TPU:8, one launch (start us, length us, event | category | flops | bytes accessed | tf_op | source)
XLA Modules:
  0.0 170.9 jit_solution(9189433353070251902)
XLA Ops:
  6.5 1.9 %collective-permute-start.6 = (bf16[1536,256]{1,0:T(8,128)(2,1)}, bf16[1536,256]{1,0:T(8,128)(2,1)}, u32[]{:S(2)}, u32[]{:S(2)}) collective-permute-start(bf16[1536,256]{1,0:T(8,128)(2,1)} %refs_0_.1), channel_id=1, source_target_pairs={{0,4},{4,0},{1,5},{5,1},{2,6},{6,2},{3,7},{7,3},{8,12},{12,8},{9,1... | collective-permute-start | bytes 2359304 | tf_op jit(solution)/shard_map/ppermute | solution.py:29
  8.5 1.5 collective-permute-start.7
  9.9 1.7 %collective-permute-start.8 = (bf16[1536,256]{1,0:T(8,128)(2,1)}, bf16[1536,256]{1,0:T(8,128)(2,1)}, u32[]{:S(2)}, u32[]{:S(2)}) collective-permute-start(bf16[1536,256]{1,0:T(8,128)(2,1)} %refs_0_.1), channel_id=1, source_target_pairs={{0,3},{1,0},{2,1},{3,2},{4,7},{5,4},{6,5},{7,6},{8,11},{9,8},{10,9... | collective-permute-start | bytes 2359304 | tf_op jit(solution)/shard_map/ppermute | solution.py:29
  11.7 1.6 copy-done.2
  13.3 1.9 %by_target.3 = bf16[4,2,4,2,128,128]{5,4,3,2,1,0:T(8,128)(2,1)} custom-call(bf16[4,4,2,2,128,128]{5,4,3,2,1,0:T(8,128)(2,1)S(1)} %bitcast.24), custom_call_target="tpu_custom_call" | custom-call | flops 1048576 | bytes 67108864 | tf_op jit(solution)/shard_map/by_target/pallas_call | solution.py:293
  15.2 5.0 %all-to-all-start = ((bf16[8,1024,128]{2,1,0:T(8,128)(2,1)}), bf16[8,1024,128]{2,1,0:T(8,128)(2,1)}, u32[]{:S(2)}, u32[]{:S(2)}) async-start(bf16[8,1024,128]{2,1,0:T(8,128)(2,1)} %bitcast.3), calls=%async_computation | async-start | bytes 4194304 | tf_op jit(solution)/shard_map/all_to_all | solution.py:368
  20.3 0.1 reshape.368
  20.5 0.1 reshape.367
  20.5 0.1 copy.20
  20.6 0.2 convert_reduce_fusion
  20.8 0.1 copy.22
  20.9 0.3 fusion.9
  21.1 0.6 gather_fusion.1
  21.7 0.6 gather_fusion
  22.3 0.1 add_multiply_fusion
  22.3 0.1 iota_add_fusion
  22.4 0.1 add.400
  22.5 0.2 select_reduce_fusion.1
  22.7 0.2 reduce_window_sum.11
  22.9 0.2 select_reduce_fusion.2
  23.2 0.1 add_convert_fusion
  23.3 0.9 constant_dynamic-slice_fusion.2.half
  24.1 2.2 %collective-permute-done.6.refs_1_ = bf16[1536,256]{1,0:T(8,128)(2,1)} collective-permute-done((bf16[1536,256]{1,0:T(8,128)(2,1)}, bf16[1536,256]{1,0:T(8,128)(2,1)}, u32[]{:S(2)}, u32[]{:S(2)}) %collective-permute-start.6) | collective-permute-done | bytes 786464 | tf_op jit(solution)/shard_map/ppermute | solution.py:29
  26.3 1.5 collective-permute-start.9
  27.8 1.7 %collective-permute-start.10 = (bf16[1536,256]{1,0:T(8,128)(2,1)}, bf16[1536,256]{1,0:T(8,128)(2,1)}, u32[]{:S(2)}, u32[]{:S(2)}) collective-permute-start(bf16[1536,256]{1,0:T(8,128)(2,1)} %collective-permute-done.6.refs_1_), channel_id=1, source_target_pairs={{0,3},{1,0},{2,1},{3,2},{4,7},{5,4},{6,5},{7,6},{8,11},{9,8},{10,9... | collective-permute-start | bytes 2359304 | tf_op jit(solution)/shard_map/ppermute | solution.py:29
  29.6 0.1 copy.25
  29.6 0.1 min.21
  29.7 0.1 copy.24
  29.8 1.8 %collective-permute-start.11 = (bf16[128,2048]{1,0:T(8,128)(2,1)}, bf16[128,2048]{1,0:T(8,128)(2,1)}, u32[]{:S(2)}, u32[]{:S(2)}) collective-permute-start(bf16[128,2048]{1,0:T(8,128)(2,1)} %constant_dynamic-slice_fusion.2.half), channel_id=1, source_target_pairs={{0,4},{4,0},{1,5},{5,1},{2,6},{6,2},{3,7},{7,3},{8,12},{12,8},{9,1... | collective-permute-start | bytes 1572872 | tf_op jit(solution)/shard_map/ppermute | solution.py:29
  31.6 0.1 pad_add_fusion.2.offsets
  31.7 0.1 convert_element_type.25
  31.8 0.6 reduce_max.9
  33.1 0.6 stack.35.ids
  33.7 1.9 %by_target.2 = bf16[4,2,4,2,128,128]{5,4,3,2,1,0:T(8,128)(2,1)} custom-call(bf16[4,4,2,2,128,128]{5,4,3,2,1,0:T(8,128)(2,1)S(1)} %bitcast.25), custom_call_target="tpu_custom_call" | custom-call | flops 1048576 | bytes 67108864 | tf_op jit(solution)/shard_map/by_target/pallas_call | solution.py:293
  35.6 4.3 %fusion = (f32[1536,128]{1,0:T(8,128)}, f32[1536,128]{1,0:T(8,128)}) fusion(f32[128]{0:T(128)S(1)} %get-tuple-element.192, f32[128]{0:T(128)S(1)} %get-tuple-element.193, f32[1536]{0:T(1024)S(1)} %convert_element_type.25), kind=kLoop, calls=%fused_computation.7 | loop fusion | flops 393216 | bytes 1580032 | tf_op jit(solution)/shard_map/mul | solution.py:448
  39.9 2.8 %collective-permute-done.11.twin = bf16[128,2048]{1,0:T(8,128)(2,1)} collective-permute-done((bf16[128,2048]{1,0:T(8,128)(2,1)}, bf16[128,2048]{1,0:T(8,128)(2,1)}, u32[]{:S(2)}, u32[]{:S(2)}) %collective-permute-start.11) | collective-permute-done | bytes 524320 | tf_op jit(solution)/shard_map/ppermute | solution.py:29
  42.6 3.3 %pair.1 = bf16[2,128,2048]{2,1,0:T(8,128)(2,1)} custom-call(bf16[128,2048]{1,0:T(8,128)(2,1)S(1)} %copy-done.4, bf16[128,2048]{1,0:T(8,128)(2,1)} %collective-permute-done.11.twin), custom_call_target="tpu_custom_call" | custom-call | flops 1048576 | bytes 1048576 | tf_op jit(solution)/shard_map/pair/pallas_call | solution.py:313
  45.9 0.5 collective-permute-done.9.refs_4_
  46.4 1.3 broadcast_in_dim.86.refs_8_
  47.8 5.3 %all-to-all-start.1 = ((bf16[8,1024,128]{2,1,0:T(8,128)(2,1)}), bf16[8,1024,128]{2,1,0:T(8,128)(2,1)}, u32[]{:S(2)}, u32[]{:S(2)}) async-start(bf16[8,1024,128]{2,1,0:T(8,128)(2,1)} %bitcast.16), calls=%async_computation.1 | async-start | bytes 4194304 | tf_op jit(solution)/shard_map/all_to_all | solution.py:368
  53.1 1.1 collective-permute-start.13
  54.2 2.2 %collective-permute-start.14 = (bf16[1536,256]{1,0:T(8,128)(2,1)}, bf16[1536,256]{1,0:T(8,128)(2,1)}, u32[]{:S(2)}, u32[]{:S(2)}) collective-permute-start(bf16[1536,256]{1,0:T(8,128)(2,1)} %collective-permute-done.10.refs_5_), channel_id=1, source_target_pairs={{0,3},{1,0},{2,1},{3,2},{4,7},{5,4},{6,5},{7,6},{8,11},{9,8},{10,9... | collective-permute-start | bytes 2359304 | tf_op jit(solution)/shard_map/ppermute | solution.py:29
  56.4 2.4 %pack.6 = (bf16[1088,128]{1,0:T(8,128)(2,1)S(1)}, bf16[1088,128]{1,0:T(8,128)(2,1)S(1)}, bf16[1088,128]{1,0:T(8,128)(2,1)S(1)}, bf16[1088,128]{1,0:T(8,128)(2,1)S(1)}) custom-call(s32[68]{0:T(128)S(1)} %pad_add_fusion.2.offsets, bf16[8,4,2,128,128]{4,3,2,1,0:T(8,128)(2,1)} %bitcast.4.cache), custom_call_target="tpu_custom_call" | custom-call | flops 1048576 | bytes 1048576 | tf_op jit(solution)/shard_map/pack/pallas_call | solution.py:270
  58.8 3.3 %collective-permute-start.12 = (bf16[1088,128]{1,0:T(8,128)(2,1)S(1)}, bf16[1088,128]{1,0:T(8,128)(2,1)S(1)}, u32[]{:S(2)}, u32[]{:S(2)}) collective-permute-start(bf16[1088,128]{1,0:T(8,128)(2,1)S(1)} %get-tuple-element.139), channel_id=1, source_target_pairs={{0,16},{16,32},{32,48},{48,0},{1,17},{17,33},{33,49},{49,1},{2,18}... | collective-permute-start | bytes 835592 | tf_op jit(solution)/shard_map/ppermute | solution.py:29
  62.1 4.6 %collective-permute-start.15 = (bf16[1088,128]{1,0:T(8,128)(2,1)S(1)}, bf16[1088,128]{1,0:T(8,128)(2,1)S(1)}, u32[]{:S(2)}, u32[]{:S(2)}) collective-permute-start(bf16[1088,128]{1,0:T(8,128)(2,1)S(1)} %get-tuple-element.163), channel_id=1, source_target_pairs={{0,32},{16,48},{32,0},{48,16},{1,33},{17,49},{33,1},{49,17},{2,34}... | collective-permute-start | bytes 835592 | tf_op jit(solution)/shard_map/ppermute | solution.py:29
  66.8 2.7 %collective-permute-start.16 = (bf16[1088,128]{1,0:T(8,128)(2,1)S(1)}, bf16[1088,128]{1,0:T(8,128)(2,1)S(1)}, u32[]{:S(2)}, u32[]{:S(2)}) collective-permute-start(bf16[1088,128]{1,0:T(8,128)(2,1)S(1)} %get-tuple-element.164), channel_id=1, source_target_pairs={{0,48},{16,0},{32,16},{48,32},{1,49},{17,1},{33,17},{49,33},{2,50}... | collective-permute-start | bytes 835592 | tf_op jit(solution)/shard_map/ppermute | solution.py:29
  69.4 12.5 %collective-permute-done.13.refs_6_ = bf16[1536,256]{1,0:T(8,128)(2,1)} collective-permute-done((bf16[1536,256]{1,0:T(8,128)(2,1)}, bf16[1536,256]{1,0:T(8,128)(2,1)}, u32[]{:S(2)}, u32[]{:S(2)}) %collective-permute-start.13) | collective-permute-done | bytes 786464 | tf_op jit(solution)/shard_map/ppermute | solution.py:29
  82.0 1.4 collective-permute-done.14.refs_7_
  83.3 13.7 %project.1 = (bf16[1536,256]{1,0:T(8,128)(2,1)}, f32[1536,256]{1,0:T(8,128)}, bf16[1536,128]{1,0:T(8,128)(2,1)}, bf16[1536,128]{1,0:T(8,128)(2,1)}) custom-call(s32[8]{0:T(128)} %stack.35.ids, bf16[1536,256]{1,0:T(8,128)(2,1)} %refs_0_.1, bf16[1536,256]{1,0:T(8,128)(2,1)} %collective-permute-done.6.refs_1_, ...), custom_call_target="tpu_custom_call" | custom-call | flops 1048576 | bytes 1048576 | tf_op jit(solution)/shard_map/project/pallas_call | solution.py:106
  97.0 3.2 %pack.7 = (bf16[1088,128]{1,0:T(8,128)(2,1)}, bf16[1088,128]{1,0:T(8,128)(2,1)}, bf16[1088,128]{1,0:T(8,128)(2,1)S(1)}, bf16[1088,128]{1,0:T(8,128)(2,1)S(1)}) custom-call(s32[68]{0:T(128)S(1)} %pad_add_fusion.2.offsets, bf16[8,4,2,128,128]{4,3,2,1,0:T(8,128)(2,1)} %bitcast.17.cache), custom_call_target="tpu_custom_call" | custom-call | flops 1048576 | bytes 1048576 | tf_op jit(solution)/shard_map/pack/pallas_call | solution.py:270
  100.2 4.0 %collective-permute-start.17 = (bf16[1088,128]{1,0:T(8,128)(2,1)}, bf16[1088,128]{1,0:T(8,128)(2,1)}, u32[]{:S(2)}, u32[]{:S(2)}) collective-permute-start(bf16[1088,128]{1,0:T(8,128)(2,1)} %get-tuple-element.176), channel_id=1, source_target_pairs={{0,16},{16,32},{32,48},{48,0},{1,17},{17,33},{33,49},{49,1},{2,18}... | collective-permute-start | bytes 835592 | tf_op jit(solution)/shard_map/ppermute | solution.py:29
  104.3 5.3 %collective-permute-start.18 = (bf16[1088,128]{1,0:T(8,128)(2,1)S(1)}, bf16[1088,128]{1,0:T(8,128)(2,1)}, u32[]{:S(2)}, u32[]{:S(2)}) collective-permute-start(bf16[1088,128]{1,0:T(8,128)(2,1)S(1)} %get-tuple-element.177), channel_id=1, source_target_pairs={{0,32},{16,48},{32,0},{48,16},{1,33},{17,49},{33,1},{49,17},{2,34}... | collective-permute-start | bytes 835592 | tf_op jit(solution)/shard_map/ppermute | solution.py:29
  109.6 1.9 %collective-permute-start.19 = (bf16[1088,128]{1,0:T(8,128)(2,1)S(1)}, bf16[1088,128]{1,0:T(8,128)(2,1)}, u32[]{:S(2)}, u32[]{:S(2)}) collective-permute-start(bf16[1088,128]{1,0:T(8,128)(2,1)S(1)} %get-tuple-element.178), channel_id=1, source_target_pairs={{0,48},{16,0},{32,16},{48,32},{1,49},{17,1},{33,17},{49,33},{2,50}... | collective-permute-start | bytes 835592 | tf_op jit(solution)/shard_map/ppermute | solution.py:29
  111.5 9.3 %weigh.3 = (bf16[3072,128]{1,0:T(8,128)(2,1)}, f32[1536,256]{1,0:T(8,128)}, f32[1536,256]{1,0:T(8,128)}) custom-call(s32[24]{0:T(128)S(1)} %get-tuple-element.155.starts, s32[24]{0:T(128)S(1)} %fusion.23.lengths, bf16[1536,256]{1,0:T(8,128)(2,1)} %get-tuple-element.150.q, f32[1536,256]{1,0:T(8,128)} %get-tuple-element.151.g, ...), custom_call_target="tpu_custom_call" | custom-call | flops 1048576 | bytes 1048576 | tf_op jit(solution)/shard_map/weigh/pallas_call | solution.py:182
  120.8 1.0 collective-permute-done.17
  121.8 5.9 %collective-permute-done.18 = bf16[1088,128]{1,0:T(8,128)(2,1)} collective-permute-done((bf16[1088,128]{1,0:T(8,128)(2,1)S(1)}, bf16[1088,128]{1,0:T(8,128)(2,1)}, u32[]{:S(2)}, u32[]{:S(2)}) %collective-permute-start.18) | collective-permute-done | bytes 278560 | tf_op jit(solution)/shard_map/ppermute | solution.py:29
  127.7 4.3 %collective-permute-done.19 = bf16[1088,128]{1,0:T(8,128)(2,1)} collective-permute-done((bf16[1088,128]{1,0:T(8,128)(2,1)S(1)}, bf16[1088,128]{1,0:T(8,128)(2,1)}, u32[]{:S(2)}, u32[]{:S(2)}) %collective-permute-start.19) | collective-permute-done | bytes 278560 | tf_op jit(solution)/shard_map/ppermute | solution.py:29
  132.0 6.3 %conditional.1 = (bf16[1536,256]{1,0:T(8,128)(2,1)}) conditional(s32[]{:T(128)} %convert_element_type.27, (s32[24]{0:T(128)S(1)}, s32[24]{0:T(128)S(1)}, s32[4,16]{1,0:T(4,128)S(1)}, s32[4,16]{1,0:T(4,128)S(1)}, s32[4]{0:T(128)S(1)}, /*index=5*/bf16[8,4,2,128,128]{4,3,2,1,0:T(8,128)(2,1)}, s32[24]{0:T(128)S(1)}, bf16[1536,256]{1,0:T(8,128)(2,1)S(1)}, ...), branch_computations={%region_6.7_spmd, %region_7.8_spmd} | conditional | flops 4194636 | bytes 26216844 | solution.py:491
  132.0 6.3 %mix.3 = bf16[1536,256]{1,0:T(8,128)(2,1)} custom-call(s32[24]{0:T(128)S(1)} %get-tuple-element.77.starts, s32[24]{0:T(128)S(1)} %get-tuple-element.78.lengths, bf16[3072,128]{1,0:T(8,128)(2,1)} %get-tuple-element.79.weights, f32[1536,256]{1,0:T(8,128)} %get-tuple-element.80.mixed_new, f32[1536,256]{1,0:T(8,128)} %get-tuple-element.81.factor, ...), custom_call_target="tpu_custom_call" | custom-call | flops 1048576 | bytes 1048576 | tf_op jit(solution)/shard_map/cond/branch_1_fun/mix/pallas_call | solution.py:236
  138.3 4.9 %all-to-all-start.2 = ((bf16[8,192,256]{2,1,0:T(8,128)(2,1)}), bf16[8,192,256]{2,1,0:T(8,128)(2,1)S(1)}, u32[]{:S(2)}, u32[]{:S(2)}) async-start(bf16[8,192,256]{2,1,0:T(8,128)(2,1)} %bitcast.20), calls=%async_computation.2 | async-start | bytes 1572864 | tf_op jit(solution)/shard_map/all_to_all | solution.py:492
  143.2 0.1 pad_add_fusion.1.places
  143.3 12.6 %all-to-all-done.2.heads = bf16[8,192,256]{2,1,0:T(8,128)(2,1)S(1)} async-done(((bf16[8,192,256]{2,1,0:T(8,128)(2,1)}), bf16[8,192,256]{2,1,0:T(8,128)(2,1)S(1)}, u32[]{:S(2)}, u32[]{:S(2)}) %all-to-all-start.2) | async-done | bytes 786464 | tf_op jit(solution)/shard_map/all_to_all | solution.py:492
  155.8 2.2 %copy-done.1 = bf16[8,128,2048]{2,1,0:T(8,128)(2,1)S(1)} copy-done((bf16[8,128,2048]{2,1,0:T(8,128)(2,1)S(1)}, bf16[8,128,2048]{2,1,0:T(8,128)(2,1)}, u32[]{:S(2)}) %copy-start.1) | copy-done | bytes 4194328
  158.0 6.0 %project_out.1 = bf16[192,2048]{1,0:T(8,128)(2,1)} custom-call(s32[9]{0:T(128)S(1)} %pad_add_fusion.1.places, bf16[8,192,256]{2,1,0:T(8,128)(2,1)S(1)} %all-to-all-done.2.heads, bf16[8,128,2048]{2,1,0:T(8,128)(2,1)S(1)} %copy-done.1, bf16[8,128,2048]{2,1,0:T(8,128)(2,1)} %collective-permute-done.20.other), custom_call_target="tpu_custom_call" | custom-call | flops 1048576 | bytes 1048576 | tf_op jit(solution)/shard_map/project_out/pallas_call | solution.py:349
  (45 shorter events, 0.3 us)
Async XLA Ops:
  6.5 16.7 %copy-start = (bf16[256,2048]{1,0:T(8,128)(2,1)S(1)}, bf16[256,2048]{1,0:T(8,128)(2,1)}, u32[]{:S(2)}) copy-start(bf16[256,2048]{1,0:T(8,128)(2,1)} %param.23) | copy-start | bytes 3145732
  6.5 19.8 %collective-permute-start.6 = (bf16[1536,256]{1,0:T(8,128)(2,1)}, bf16[1536,256]{1,0:T(8,128)(2,1)}, u32[]{:S(2)}, u32[]{:S(2)}) collective-permute-start(bf16[1536,256]{1,0:T(8,128)(2,1)} %refs_0_.1), channel_id=1, source_target_pairs={{0,4},{4,0},{1,5},{5,1},{2,6},{6,2},{3,7},{7,3},{8,12},{12,8},{9,1... | collective-permute-start | bytes 2359304 | tf_op jit(solution)/shard_map/ppermute | solution.py:29
  8.5 37.5 %collective-permute-start.7 = (bf16[1536,256]{1,0:T(8,128)(2,1)}, bf16[1536,256]{1,0:T(8,128)(2,1)}, u32[]{:S(2)}, u32[]{:S(2)}) collective-permute-start(bf16[1536,256]{1,0:T(8,128)(2,1)} %refs_0_.1), channel_id=1, source_target_pairs={{0,1},{1,2},{2,3},{3,0},{4,5},{5,6},{6,7},{7,4},{8,9},{9,10},{10,1... | collective-permute-start | bytes 2359304 | tf_op jit(solution)/shard_map/ppermute | solution.py:29
  9.9 36.0 %collective-permute-start.8 = (bf16[1536,256]{1,0:T(8,128)(2,1)}, bf16[1536,256]{1,0:T(8,128)(2,1)}, u32[]{:S(2)}, u32[]{:S(2)}) collective-permute-start(bf16[1536,256]{1,0:T(8,128)(2,1)} %refs_0_.1), channel_id=1, source_target_pairs={{0,3},{1,0},{2,1},{3,2},{4,7},{5,4},{6,5},{7,6},{8,11},{9,8},{10,9... | collective-permute-start | bytes 2359304 | tf_op jit(solution)/shard_map/ppermute | solution.py:29
  11.7 1.6 copy-start.2
  15.2 5.1 %copy-start.10 = (s32[768]{0:T(1024)S(1)}, s32[768]{0:T(1024)}, u32[]{:S(2)}) copy-start(s32[768]{0:T(1024)} %param.27) | copy-start | bytes 9220
  15.2 5.3 %copy-start.11 = (s32[768,1]{0,1:T(1,128)S(1)}, s32[768,1]{0,1:T(1,128)}, u32[]{:S(2)}) copy-start(s32[768,1]{0,1:T(1,128)} %param.26) | copy-start | bytes 9220
  15.2 18.5 %copy-start.3 = (bf16[1,64,128,128]{3,2,1,0:T(8,128)(2,1)S(1)}, bf16[1,64,128,128]{3,2,1,0:T(8,128)(2,1)}, u32[]{:S(2)}) copy-start(bf16[1,64,128,128]{3,2,1,0:T(8,128)(2,1)} %param.25) | copy-start | bytes 6291460
  15.2 31.3 %all-to-all-start = ((bf16[8,1024,128]{2,1,0:T(8,128)(2,1)}), bf16[8,1024,128]{2,1,0:T(8,128)(2,1)}, u32[]{:S(2)}, u32[]{:S(2)}) async-start(bf16[8,1024,128]{2,1,0:T(8,128)(2,1)} %bitcast.3), calls=%async_computation | async-start | bytes 4194304 | tf_op jit(solution)/shard_map/all_to_all | solution.py:368
  20.2 100.6 %all-gather.3.cloned.1.call-start = ((), (), s32[]{:S(2)}) async-start(), calls=%async_computation.3 | async-start | bytes 5242880 | tf_op jit(solution)/shard_map/all_gather | solution.py:467
  26.3 20.1 %collective-permute-start.9 = (bf16[1536,256]{1,0:T(8,128)(2,1)}, bf16[1536,256]{1,0:T(8,128)(2,1)}, u32[]{:S(2)}, u32[]{:S(2)}) collective-permute-start(bf16[1536,256]{1,0:T(8,128)(2,1)} %collective-permute-done.6.refs_1_), channel_id=1, source_target_pairs={{0,1},{1,2},{2,3},{3,0},{4,5},{5,6},{6,7},{7,4},{8,9},{9,10},{10,1... | collective-permute-start | bytes 2359304 | tf_op jit(solution)/shard_map/ppermute | solution.py:29
  27.8 18.6 %collective-permute-start.10 = (bf16[1536,256]{1,0:T(8,128)(2,1)}, bf16[1536,256]{1,0:T(8,128)(2,1)}, u32[]{:S(2)}, u32[]{:S(2)}) collective-permute-start(bf16[1536,256]{1,0:T(8,128)(2,1)} %collective-permute-done.6.refs_1_), channel_id=1, source_target_pairs={{0,3},{1,0},{2,1},{3,2},{4,7},{5,4},{6,5},{7,6},{8,11},{9,8},{10,9... | collective-permute-start | bytes 2359304 | tf_op jit(solution)/shard_map/ppermute | solution.py:29
  29.8 12.8 %collective-permute-start.11 = (bf16[128,2048]{1,0:T(8,128)(2,1)}, bf16[128,2048]{1,0:T(8,128)(2,1)}, u32[]{:S(2)}, u32[]{:S(2)}) collective-permute-start(bf16[128,2048]{1,0:T(8,128)(2,1)} %constant_dynamic-slice_fusion.2.half), channel_id=1, source_target_pairs={{0,4},{4,0},{1,5},{5,1},{2,6},{6,2},{3,7},{7,3},{8,12},{12,8},{9,1... | collective-permute-start | bytes 1572872 | tf_op jit(solution)/shard_map/ppermute | solution.py:29
  33.7 8.9 %copy-start.4 = (bf16[128,2048]{1,0:T(8,128)(2,1)S(1)}, bf16[128,2048]{1,0:T(8,128)(2,1)}, u32[]{:S(2)}) copy-start(bf16[128,2048]{1,0:T(8,128)(2,1)} %constant_dynamic-slice_fusion.2.half) | copy-start | bytes 1572868
  35.6 10.8 %copy-start.9 = (f32[2048]{0:T(1024)S(1)}, f32[2048]{0:T(1024)}, u32[]{:S(2)}) copy-start(f32[2048]{0:T(1024)} %param.16) | copy-start | bytes 24580
  47.8 49.2 %all-to-all-start.1 = ((bf16[8,1024,128]{2,1,0:T(8,128)(2,1)}), bf16[8,1024,128]{2,1,0:T(8,128)(2,1)}, u32[]{:S(2)}, u32[]{:S(2)}) async-start(bf16[8,1024,128]{2,1,0:T(8,128)(2,1)} %bitcast.16), calls=%async_computation.1 | async-start | bytes 4194304 | tf_op jit(solution)/shard_map/all_to_all | solution.py:368
  53.1 28.8 %collective-permute-start.13 = (bf16[1536,256]{1,0:T(8,128)(2,1)}, bf16[1536,256]{1,0:T(8,128)(2,1)}, u32[]{:S(2)}, u32[]{:S(2)}) collective-permute-start(bf16[1536,256]{1,0:T(8,128)(2,1)} %collective-permute-done.7.refs_2_), channel_id=1, source_target_pairs={{0,1},{1,2},{2,3},{3,0},{4,5},{5,6},{6,7},{7,4},{8,9},{9,10},{10,1... | collective-permute-start | bytes 2359304 | tf_op jit(solution)/shard_map/ppermute | solution.py:29
  54.2 29.1 %collective-permute-start.14 = (bf16[1536,256]{1,0:T(8,128)(2,1)}, bf16[1536,256]{1,0:T(8,128)(2,1)}, u32[]{:S(2)}, u32[]{:S(2)}) collective-permute-start(bf16[1536,256]{1,0:T(8,128)(2,1)} %collective-permute-done.10.refs_5_), channel_id=1, source_target_pairs={{0,3},{1,0},{2,1},{3,2},{4,7},{5,4},{6,5},{7,6},{8,11},{9,8},{10,9... | collective-permute-start | bytes 2359304 | tf_op jit(solution)/shard_map/ppermute | solution.py:29
  58.8 38.2 %collective-permute-start.12 = (bf16[1088,128]{1,0:T(8,128)(2,1)S(1)}, bf16[1088,128]{1,0:T(8,128)(2,1)S(1)}, u32[]{:S(2)}, u32[]{:S(2)}) collective-permute-start(bf16[1088,128]{1,0:T(8,128)(2,1)S(1)} %get-tuple-element.139), channel_id=1, source_target_pairs={{0,16},{16,32},{32,48},{48,0},{1,17},{17,33},{33,49},{49,1},{2,18}... | collective-permute-start | bytes 835592 | tf_op jit(solution)/shard_map/ppermute | solution.py:29
  62.1 38.1 %collective-permute-start.15 = (bf16[1088,128]{1,0:T(8,128)(2,1)S(1)}, bf16[1088,128]{1,0:T(8,128)(2,1)S(1)}, u32[]{:S(2)}, u32[]{:S(2)}) collective-permute-start(bf16[1088,128]{1,0:T(8,128)(2,1)S(1)} %get-tuple-element.163), channel_id=1, source_target_pairs={{0,32},{16,48},{32,0},{48,16},{1,33},{17,49},{33,1},{49,17},{2,34}... | collective-permute-start | bytes 835592 | tf_op jit(solution)/shard_map/ppermute | solution.py:29
  66.8 33.5 %collective-permute-start.16 = (bf16[1088,128]{1,0:T(8,128)(2,1)S(1)}, bf16[1088,128]{1,0:T(8,128)(2,1)S(1)}, u32[]{:S(2)}, u32[]{:S(2)}) collective-permute-start(bf16[1088,128]{1,0:T(8,128)(2,1)S(1)} %get-tuple-element.164), channel_id=1, source_target_pairs={{0,48},{16,0},{32,16},{48,32},{1,49},{17,1},{33,17},{49,33},{2,50}... | collective-permute-start | bytes 835592 | tf_op jit(solution)/shard_map/ppermute | solution.py:29
  100.2 21.5 %collective-permute-start.17 = (bf16[1088,128]{1,0:T(8,128)(2,1)}, bf16[1088,128]{1,0:T(8,128)(2,1)}, u32[]{:S(2)}, u32[]{:S(2)}) collective-permute-start(bf16[1088,128]{1,0:T(8,128)(2,1)} %get-tuple-element.176), channel_id=1, source_target_pairs={{0,16},{16,32},{32,48},{48,0},{1,17},{17,33},{33,49},{49,1},{2,18}... | collective-permute-start | bytes 835592 | tf_op jit(solution)/shard_map/ppermute | solution.py:29
  104.3 23.4 %collective-permute-start.18 = (bf16[1088,128]{1,0:T(8,128)(2,1)S(1)}, bf16[1088,128]{1,0:T(8,128)(2,1)}, u32[]{:S(2)}, u32[]{:S(2)}) collective-permute-start(bf16[1088,128]{1,0:T(8,128)(2,1)S(1)} %get-tuple-element.177), channel_id=1, source_target_pairs={{0,32},{16,48},{32,0},{48,16},{1,33},{17,49},{33,1},{49,17},{2,34}... | collective-permute-start | bytes 835592 | tf_op jit(solution)/shard_map/ppermute | solution.py:29
  109.6 22.4 %collective-permute-start.19 = (bf16[1088,128]{1,0:T(8,128)(2,1)S(1)}, bf16[1088,128]{1,0:T(8,128)(2,1)}, u32[]{:S(2)}, u32[]{:S(2)}) collective-permute-start(bf16[1088,128]{1,0:T(8,128)(2,1)S(1)} %get-tuple-element.178), channel_id=1, source_target_pairs={{0,48},{16,0},{32,16},{48,32},{1,49},{17,1},{33,17},{49,33},{2,50}... | collective-permute-start | bytes 835592 | tf_op jit(solution)/shard_map/ppermute | solution.py:29
  111.5 20.4 %copy-start.6 = (bf16[1536,256]{1,0:T(8,128)(2,1)S(1)}, bf16[1536,256]{1,0:T(8,128)(2,1)}, u32[]{:S(2)}) copy-start(bf16[1536,256]{1,0:T(8,128)(2,1)} %get-tuple-element.150.q) | copy-start | bytes 2359300
  138.3 17.6 %collective-permute-start.20 = (bf16[8,128,2048]{2,1,0:T(8,128)(2,1)}, bf16[8,128,2048]{2,1,0:T(8,128)(2,1)}, u32[]{:S(2)}, u32[]{:S(2)}) collective-permute-start(bf16[8,128,2048]{2,1,0:T(8,128)(2,1)} %all-gather.3.cloned.1.call-done.mine), channel_id=1, source_target_pairs={{0,8},{8,0},{1,9},{9,1},{2,10},{10,2},{3,11},{11,3},{4,12},{12,4},... | collective-permute-start | bytes 12582920 | tf_op jit(solution)/shard_map/ppermute | solution.py:29
  138.3 17.5 %all-to-all-start.2 = ((bf16[8,192,256]{2,1,0:T(8,128)(2,1)}), bf16[8,192,256]{2,1,0:T(8,128)(2,1)S(1)}, u32[]{:S(2)}, u32[]{:S(2)}) async-start(bf16[8,192,256]{2,1,0:T(8,128)(2,1)} %bitcast.20), calls=%async_computation.2 | async-start | bytes 1572864 | tf_op jit(solution)/shard_map/all_to_all | solution.py:492
  155.8 2.2 %copy-start.1 = (bf16[8,128,2048]{2,1,0:T(8,128)(2,1)S(1)}, bf16[8,128,2048]{2,1,0:T(8,128)(2,1)}, u32[]{:S(2)}) copy-start(bf16[8,128,2048]{2,1,0:T(8,128)(2,1)} %all-gather.3.cloned.1.call-done.mine) | copy-start | bytes 12582916
Sparse Core Ops, SparseCore 0:
  47.9 60.2 all-gather.2

commit v11 on v10

--- a/solution.py
+++ b/solution.py
@@ -302,23 +302,22 @@
     )(cache)
 
 
-def pair_kernel(half, twin, out):
-    out[0], out[1] = half[...], twin[...]
-
-
-def pair(half, twin):
+def copies_kernel(half, twin, out):
+    out[0, 0], out[0, 1] = half[...], twin[...]
+
+
+def copies(half, twin):
     depth, columns = half.shape
-    tile = 512
-    part = pl.BlockSpec((depth, tile), lambda i: (0, i))
-    return pl.pallas_call(
-        pair_kernel,
-        out_shape=jax.ShapeDtypeStruct((2, depth, columns), half.dtype),
-        grid=(columns // tile,),
-        in_specs=[part, part],
-        out_specs=pl.BlockSpec((2, depth, tile), lambda i: (0, 0, i)),
+    whole = pl.BlockSpec((depth, columns), lambda i: (0, 0))
+    return pl.pallas_call(
+        copies_kernel,
+        out_shape=jax.ShapeDtypeStruct((4, 2, depth, columns), half.dtype),
+        grid=(4,),
+        in_specs=[whole, whole],
+        out_specs=pl.BlockSpec((1, 2, depth, columns), lambda i: (i, 0, 0, 0)),
         compiler_params=pltpu.CompilerParams(vmem_limit_bytes=12 << 20),
         cost_estimate=COST,
-        name="pair",
+        name="copies",
     )(half, twin)
 
 
@@ -459,20 +458,24 @@
     key_part = across_y(by_target(key_cache.reshape(sides)))
     gain = jnp.broadcast_to(norm_gain[:, None], (norm_gain.shape[0], head_dim))
     tables = (ids, places, starts, fits, gain, cosine, sine)
-    value_slots, key_part, pieces[1:6], both_halves, tables = lax.optimization_barrier(
-        (by_target(value_cache.reshape(sides)), key_part, pieces[1:6], pair(half, twin_half), tables)
+    value_slots, key_part, pieces[1:6], repeated, tables = lax.optimization_barrier(
+        (by_target(value_cache.reshape(sides)), key_part, pieces[1:6], copies(half, twin_half), tables)
     )
     ids, places, starts, fits, gain, cosine, sine = tables
     value_part = across_y(value_slots)
-    halves = lax.all_gather(both_halves, "x").reshape((blocks,) + half.shape)
     keys = across_z(pack(places, key_part, PACKED))
+    value_part, keys[1], keys[3], pieces[6:], repeated = lax.optimization_barrier(
+        (value_part, keys[1], keys[3], pieces[6:], repeated)
+    )
+    halves = lax.all_to_all(repeated, "x", 0, 0, tiled=True).reshape((blocks,) + half.shape)
+    packed_values, pieces[0] = lax.optimization_barrier(
+        (pack(places, value_part, PACKED), pieces[0])
+    )
+    values = across_z(packed_values)
     q, g, k, v = project(
         ids, pieces, gain, q_weight, gate_weight, k_weight, v_weight,
         q_norm_gain, k_norm_gain, cosine, sine,
     )
-    value_part, keys[1], q = lax.optimization_barrier((value_part, keys[1], q))
-    packed_values, keys = lax.optimization_barrier((pack(places, value_part, PACKED), keys))
-    values = across_z(packed_values)
 
     size = 8 * capacity * window
 
@@ -486,9 +489,9 @@
         return mix(starts, my_lengths, *weighed, values)
 
     weighed = weigh(starts, my_lengths, q, g, k, v, keys, window)
-    halves, weighed = lax.optimization_barrier((halves, weighed))
+    attended = lax.cond(fits, packed, full, values, key_part, value_part, q, g, k, v, *weighed)
+    halves, attended = lax.optimization_barrier((halves, attended))
     other_halves = shift(halves, "c", 1)
-    attended = lax.cond(fits, packed, full, values, key_part, value_part, q, g, k, v, *weighed)
     heads = lax.all_to_all(
         attended.reshape(blocks, rows // blocks, attended.shape[1]), TENSOR, 0, 0, tiled=True
     )

time: 173 us -> 154 us (0.89)
  between operations: 14.2 us -> 0.86 us
  waiting for transfers between devices: 43.1 us -> 38.7 us
  Pallas kernels: 48 us -> 45.5 us
    ppermute x15, waiting for transfers between devices: 30.5 us -> 25 us  [shift(): return lax.ppermute(value, axis, ring(lax.axis_size(axis), step))]
    all_to_all x0 -> x1, starting transfers between devices: none -> 4.87 us  [local(): lax.all_to_all(repeated, 'x', 0, 0, tiled=True)]
    ppermute x15, starting transfers between devices: 35.4 us -> 30.5 us  [shift(): return lax.ppermute(value, axis, ring(lax.axis_size(axis), step))]
    pallas_call x1, Pallas kernels: 3.3 us -> 0.33 us  [copies(): pl.pallas_call(copies_kernel, out_shape=jax.ShapeDtypeStruct((4, 2, depth...]
  transfers between devices with their start and end apart: 19 -> 19, of which waited for: 9 -> 8; matrix products, arithmetic and copies ran while one was open for 6% -> 6% of each run, Pallas kernels for 21% -> 26%
where the time goes in v11:
time: 154 us; the launch traced here: 151 us
  starting transfers between devices  50.7 us (33%)
  Pallas kernels  45.5 us (30%)
  waiting for transfers between devices  38.7 us (25%)
  local copies, waits for them, and re-layouts  8.91 us (6%)
  other arithmetic  6.56 us (4%)
    ppermute x15, starting transfers between devices, shift(): return lax.ppermute(value, axis, ring(lax.axis_size(axis), step))  30.5 us
    ppermute x15, waiting for transfers between devices, shift(): return lax.ppermute(value, axis, ring(lax.axis_size(axis), step))  25 us
    pallas_call x1, Pallas kernels, project(): pl.pallas_call(project_kernel, out_shape=(jax.ShapeDtypeStruct((rows, wq....  13.6 us
    all_to_all x1, waiting for transfers between devices, local(): lax.all_to_all(attended.reshape(blocks, rows // blocks, attended.shape[1]...  12.5 us
    all_to_all x2, starting transfers between devices, across_y(): flat = lax.all_to_all(flat, ('y', 'c'), 0, 0, tiled=True)  10.6 us
    pallas_call x1, Pallas kernels, weigh(): pl.pallas_call(weigh_kernel, out_shape=(jax.ShapeDtypeStruct((shares * ro...  9.28 us
    pallas_call x1, Pallas kernels, project_out(): pl.pallas_call(output_kernel, out_shape=jax.ShapeDtypeStruct((rows, colum...  6.64 us
    pallas_call x1, Pallas kernels, mix(): pl.pallas_call(mix_kernel, out_shape=jax.ShapeDtypeStruct((rows, columns)...  6.34 us
  transfers between devices with their start and end apart: 19, of which 8 were waited for; matrix products, arithmetic and copies ran while one was open for 6% of the time, Pallas kernels for 26%

profile of v11, /device:TPU:8, one launch (start us, length us, event | category | flops | bytes accessed | tf_op | source)
XLA Modules:
  0.0 151.2 jit_solution(5483516406826077297)
XLA Ops:
  0.0 1.9 %collective-permute-start.6 = (bf16[1536,256]{1,0:T(8,128)(2,1)}, bf16[1536,256]{1,0:T(8,128)(2,1)S(1)}, u32[]{:S(2)}, u32[]{:S(2)}) collective-permute-start(bf16[1536,256]{1,0:T(8,128)(2,1)} %refs_0_), channel_id=1, source_target_pairs={{0,4},{4,0},{1,5},{5,1},{2,6},{6,2},{3,7},{7,3},{8,12},{12,8},{9,1... | collective-permute-start | bytes 2359304 | tf_op jit(solution)/shard_map/ppermute | solution.py:29
  1.9 1.5 collective-permute-start.7
  3.4 1.7 %collective-permute-start.8 = (bf16[1536,256]{1,0:T(8,128)(2,1)}, bf16[1536,256]{1,0:T(8,128)(2,1)}, u32[]{:S(2)}, u32[]{:S(2)}) collective-permute-start(bf16[1536,256]{1,0:T(8,128)(2,1)} %refs_0_), channel_id=1, source_target_pairs={{0,3},{1,0},{2,1},{3,2},{4,7},{5,4},{6,5},{7,6},{8,11},{9,8},{10,9... | collective-permute-start | bytes 2359304 | tf_op jit(solution)/shard_map/ppermute | solution.py:29
  5.2 1.6 %copy-done.2 = bf16[1,64,128,128]{3,2,1,0:T(8,128)(2,1)S(1)} copy-done((bf16[1,64,128,128]{3,2,1,0:T(8,128)(2,1)S(1)}, bf16[1,64,128,128]{3,2,1,0:T(8,128)(2,1)}, u32[]{:S(2)}) %copy-start.2) | copy-done | bytes 2097176
  6.8 1.9 %by_target.3 = bf16[4,2,4,2,128,128]{5,4,3,2,1,0:T(8,128)(2,1)} custom-call(bf16[4,4,2,2,128,128]{5,4,3,2,1,0:T(8,128)(2,1)S(1)} %bitcast.25), custom_call_target="tpu_custom_call" | custom-call | flops 1048576 | bytes 67108864 | tf_op jit(solution)/shard_map/by_target/pallas_call | solution.py:293
  8.6 5.0 %all-to-all-start = ((bf16[8,1024,128]{2,1,0:T(8,128)(2,1)}), bf16[8,1024,128]{2,1,0:T(8,128)(2,1)}, u32[]{:S(2)}, u32[]{:S(2)}) async-start(bf16[8,1024,128]{2,1,0:T(8,128)(2,1)} %bitcast.3), calls=%async_computation | async-start | bytes 4194304 | tf_op jit(solution)/shard_map/all_to_all | solution.py:367
  13.7 0.1 reshape.368
  13.9 0.1 reshape.367
  14.0 0.1 copy.20
  14.1 0.2 convert_reduce_fusion
  14.2 0.1 copy.22
  14.3 0.3 fusion.9
  14.6 0.6 gather_fusion.1
  15.2 0.6 gather_fusion
  15.7 0.1 add_multiply_fusion
  15.8 0.1 iota_add_fusion
  15.9 0.1 add.400
  15.9 0.2 select_reduce_fusion.1
  16.2 0.2 reduce_window_sum.11
  16.4 0.2 select_reduce_fusion.2
  16.6 0.1 add_convert_fusion
  16.7 2.9 %collective-permute-done.6.refs_1_ = bf16[1536,256]{1,0:T(8,128)(2,1)S(1)} collective-permute-done((bf16[1536,256]{1,0:T(8,128)(2,1)}, bf16[1536,256]{1,0:T(8,128)(2,1)S(1)}, u32[]{:S(2)}, u32[]{:S(2)}) %collective-permute-start.6) | collective-permute-done | bytes 786464 | tf_op jit(solution)/shard_map/ppermute | solution.py:29
  19.7 1.5 collective-permute-start.9
  21.2 1.7 %collective-permute-start.10 = (bf16[1536,256]{1,0:T(8,128)(2,1)S(1)}, bf16[1536,256]{1,0:T(8,128)(2,1)}, u32[]{:S(2)}, u32[]{:S(2)}) collective-permute-start(bf16[1536,256]{1,0:T(8,128)(2,1)S(1)} %collective-permute-done.6.refs_1_), channel_id=1, source_target_pairs={{0,3},{1,0},{2,1},{3,2},{4,7},{5,4},{6,5},{7,6},{8,11},{9,8},{10,9... | collective-permute-start | bytes 2359304 | tf_op jit(solution)/shard_map/ppermute | solution.py:29
  22.9 0.1 copy.25
  23.0 0.1 min.21
  23.2 1.8 %collective-permute-start.11 = (bf16[128,2048]{1,0:T(8,128)(2,1)S(1)}, bf16[128,2048]{1,0:T(8,128)(2,1)S(1)}, u32[]{:S(2)}, u32[]{:S(2)}) collective-permute-start(bf16[128,2048]{1,0:T(8,128)(2,1)S(1)} %constant_dynamic-slice_fusion.2.half), channel_id=1, source_target_pairs={{0,4},{4,0},{1,5},{5,1},{2,6},{6,2},{3,7},{7,3},{8,12},{12,8},{9,1... | collective-permute-start | bytes 1572872 | tf_op jit(solution)/shard_map/ppermute | solution.py:29
  25.0 0.1 pad_add_fusion.2.offsets
  25.1 0.1 convert_element_type.25
  25.2 0.6 reduce_max.9
  26.4 0.6 stack.35.ids
  27.1 1.6 %copy-done.3 = bf16[1,64,128,128]{3,2,1,0:T(8,128)(2,1)S(1)} copy-done((bf16[1,64,128,128]{3,2,1,0:T(8,128)(2,1)S(1)}, bf16[1,64,128,128]{3,2,1,0:T(8,128)(2,1)}, u32[]{:S(2)}) %copy-start.3) | copy-done | bytes 2097176
  28.7 1.9 %by_target.2 = bf16[4,2,4,2,128,128]{5,4,3,2,1,0:T(8,128)(2,1)} custom-call(bf16[4,4,2,2,128,128]{5,4,3,2,1,0:T(8,128)(2,1)S(1)} %bitcast.26), custom_call_target="tpu_custom_call" | custom-call | flops 1048576 | bytes 67108864 | tf_op jit(solution)/shard_map/by_target/pallas_call | solution.py:293
  30.6 4.3 %fusion = (f32[1536,128]{1,0:T(8,128)}, f32[1536,128]{1,0:T(8,128)}) fusion(f32[128]{0:T(128)S(1)} %get-tuple-element.190, f32[128]{0:T(128)S(1)} %get-tuple-element.191, f32[1536]{0:T(1024)S(1)} %convert_element_type.25), kind=kLoop, calls=%fused_computation.7 | loop fusion | flops 393216 | bytes 1580032 | tf_op jit(solution)/shard_map/mul | solution.py:447
  34.9 0.8 collective-permute-done.11.twin
  35.8 0.3 copies.1
  36.1 1.9 %copy-done.1 = bf16[4,2,128,2048]{3,2,1,0:T(8,128)(2,1)} copy-done((bf16[4,2,128,2048]{3,2,1,0:T(8,128)(2,1)}, bf16[4,2,128,2048]{3,2,1,0:T(8,128)(2,1)S(1)}, u32[]{:S(2)}) %copy-start.1) | copy-done | bytes 4194328
  38.1 1.6 %collective-permute-done.9.refs_4_ = bf16[1536,256]{1,0:T(8,128)(2,1)} collective-permute-done((bf16[1536,256]{1,0:T(8,128)(2,1)S(1)}, bf16[1536,256]{1,0:T(8,128)(2,1)}, u32[]{:S(2)}, u32[]{:S(2)}) %collective-permute-start.9) | collective-permute-done | bytes 786464 | tf_op jit(solution)/shard_map/ppermute | solution.py:29
  39.7 1.3 broadcast_in_dim.86.refs_8_
  41.0 5.5 %all-to-all-start.1 = ((bf16[8,1024,128]{2,1,0:T(8,128)(2,1)}), bf16[8,1024,128]{2,1,0:T(8,128)(2,1)}, u32[]{:S(2)}, u32[]{:S(2)}) async-start(bf16[8,1024,128]{2,1,0:T(8,128)(2,1)} %bitcast.16), calls=%async_computation.1 | async-start | bytes 4194304 | tf_op jit(solution)/shard_map/all_to_all | solution.py:367
  46.5 0.9 collective-permute-start.14
  47.4 2.3 %collective-permute-start.15 = (bf16[1536,256]{1,0:T(8,128)(2,1)}, bf16[1536,256]{1,0:T(8,128)(2,1)}, u32[]{:S(2)}, u32[]{:S(2)}) collective-permute-start(bf16[1536,256]{1,0:T(8,128)(2,1)} %collective-permute-done.10.refs_5_), channel_id=1, source_target_pairs={{0,3},{1,0},{2,1},{3,2},{4,7},{5,4},{6,5},{7,6},{8,11},{9,8},{10,9... | collective-permute-start | bytes 2359304 | tf_op jit(solution)/shard_map/ppermute | solution.py:29
  49.8 2.4 %pack.6 = (bf16[1088,128]{1,0:T(8,128)(2,1)S(1)}, bf16[1088,128]{1,0:T(8,128)(2,1)S(1)}, bf16[1088,128]{1,0:T(8,128)(2,1)S(1)}, bf16[1088,128]{1,0:T(8,128)(2,1)S(1)}) custom-call(s32[68]{0:T(128)S(1)} %pad_add_fusion.2.offsets, bf16[8,4,2,128,128]{4,3,2,1,0:T(8,128)(2,1)} %bitcast.4.cache), custom_call_target="tpu_custom_call" | custom-call | flops 1048576 | bytes 1048576 | tf_op jit(solution)/shard_map/pack/pallas_call | solution.py:270
  52.2 3.3 %collective-permute-start.12 = (bf16[1088,128]{1,0:T(8,128)(2,1)S(1)}, bf16[1088,128]{1,0:T(8,128)(2,1)S(1)}, u32[]{:S(2)}, u32[]{:S(2)}) collective-permute-start(bf16[1088,128]{1,0:T(8,128)(2,1)S(1)} %get-tuple-element.136), channel_id=1, source_target_pairs={{0,16},{16,32},{32,48},{48,0},{1,17},{17,33},{33,49},{49,1},{2,18}... | collective-permute-start | bytes 835592 | tf_op jit(solution)/shard_map/ppermute | solution.py:29
  55.6 2.2 %collective-permute-start.13 = (bf16[1088,128]{1,0:T(8,128)(2,1)S(1)}, bf16[1088,128]{1,0:T(8,128)(2,1)S(1)}, u32[]{:S(2)}, u32[]{:S(2)}) collective-permute-start(bf16[1088,128]{1,0:T(8,128)(2,1)S(1)} %get-tuple-element.137), channel_id=1, source_target_pairs={{0,48},{16,0},{32,16},{48,32},{1,49},{17,1},{33,17},{49,33},{2,50}... | collective-permute-start | bytes 835592 | tf_op jit(solution)/shard_map/ppermute | solution.py:29
  57.8 9.8 %collective-permute-done.14.refs_6_ = bf16[1536,256]{1,0:T(8,128)(2,1)S(1)} collective-permute-done((bf16[1536,256]{1,0:T(8,128)(2,1)}, bf16[1536,256]{1,0:T(8,128)(2,1)S(1)}, u32[]{:S(2)}, u32[]{:S(2)}) %collective-permute-start.14) | collective-permute-done | bytes 786464 | tf_op jit(solution)/shard_map/ppermute | solution.py:29
  67.6 3.7 %collective-permute-done.13.refs_3_ = bf16[1088,128]{1,0:T(8,128)(2,1)S(1)} collective-permute-done((bf16[1088,128]{1,0:T(8,128)(2,1)S(1)}, bf16[1088,128]{1,0:T(8,128)(2,1)S(1)}, u32[]{:S(2)}, u32[]{:S(2)}) %collective-permute-start.13) | collective-permute-done | bytes 278560 | tf_op jit(solution)/shard_map/ppermute | solution.py:29
  71.2 1.2 all-to-all-done.1
  72.4 4.9 %all-to-all-start.2 = ((bf16[4,2,128,2048]{3,2,1,0:T(8,128)(2,1)}), bf16[4,2,128,2048]{3,2,1,0:T(8,128)(2,1)}, u32[]{:S(2)}, u32[]{:S(2)}) async-start(bf16[4,2,128,2048]{3,2,1,0:T(8,128)(2,1)} %copy-done.1), calls=%async_computation.2 | async-start | bytes 8388608 | tf_op jit(solution)/shard_map/all_to_all | solution.py:470
  77.3 6.4 %collective-permute-start.16 = (bf16[1088,128]{1,0:T(8,128)(2,1)S(1)}, bf16[1088,128]{1,0:T(8,128)(2,1)S(1)}, u32[]{:S(2)}, u32[]{:S(2)}) collective-permute-start(bf16[1088,128]{1,0:T(8,128)(2,1)S(1)} %get-tuple-element.165), channel_id=1, source_target_pairs={{0,32},{16,48},{32,0},{48,16},{1,33},{17,49},{33,1},{49,17},{2,34}... | collective-permute-start | bytes 835592 | tf_op jit(solution)/shard_map/ppermute | solution.py:29
  83.7 3.0 %pack.7 = (bf16[1088,128]{1,0:T(8,128)(2,1)}, bf16[1088,128]{1,0:T(8,128)(2,1)S(1)}, bf16[1088,128]{1,0:T(8,128)(2,1)S(1)}, bf16[1088,128]{1,0:T(8,128)(2,1)S(1)}) custom-call(s32[68]{0:T(128)S(1)} %pad_add_fusion.2.offsets, bf16[8,4,2,128,128]{4,3,2,1,0:T(8,128)(2,1)} %bitcast.17.cache), custom_call_target="tpu_custom_call" | custom-call | flops 1048576 | bytes 1048576 | tf_op jit(solution)/shard_map/pack/pallas_call | solution.py:270
  86.7 1.5 collective-permute-start.17
  88.2 1.4 collective-permute-start.18
  89.6 2.1 %collective-permute-start.19 = (bf16[1088,128]{1,0:T(8,128)(2,1)S(1)}, bf16[1088,128]{1,0:T(8,128)(2,1)}, u32[]{:S(2)}, u32[]{:S(2)}) collective-permute-start(bf16[1088,128]{1,0:T(8,128)(2,1)S(1)} %get-tuple-element.173), channel_id=1, source_target_pairs={{0,48},{16,0},{32,16},{48,32},{1,49},{17,1},{33,17},{49,33},{2,50}... | collective-permute-start | bytes 835592 | tf_op jit(solution)/shard_map/ppermute | solution.py:29
  91.8 13.6 %project.1 = (bf16[1536,256]{1,0:T(8,128)(2,1)}, f32[1536,256]{1,0:T(8,128)}, bf16[1536,128]{1,0:T(8,128)(2,1)}, bf16[1536,128]{1,0:T(8,128)(2,1)}) custom-call(s32[8]{0:T(128)} %stack.35.ids, bf16[1536,256]{1,0:T(8,128)(2,1)} %refs_0_, bf16[1536,256]{1,0:T(8,128)(2,1)} %copy-done.8, bf16[1536,256]{1,0:T(8,128)(2,1)} %collective-permute-done.7.refs_2_, ...), custom_call_target="tpu_custom_call" | custom-call | flops 1048576 | bytes 1048576 | tf_op jit(solution)/shard_map/project/pallas_call | solution.py:106
  105.4 9.3 %weigh.3 = (bf16[3072,128]{1,0:T(8,128)(2,1)}, f32[1536,256]{1,0:T(8,128)}, f32[1536,256]{1,0:T(8,128)}) custom-call(s32[24]{0:T(128)S(1)} %get-tuple-element.162.starts, s32[24]{0:T(128)S(1)} %get-tuple-element.189.lengths, bf16[1536,256]{1,0:T(8,128)(2,1)} %get-tuple-element.158.q, f32[1536,256]{1,0:T(8,128)} %get-tuple-element.159.g, ...), custom_call_target="tpu_custom_call" | custom-call | flops 1048576 | bytes 1048576 | tf_op jit(solution)/shard_map/weigh/pallas_call | solution.py:182
  114.6 6.1 %collective-permute-done.19 = bf16[1088,128]{1,0:T(8,128)(2,1)} collective-permute-done((bf16[1088,128]{1,0:T(8,128)(2,1)S(1)}, bf16[1088,128]{1,0:T(8,128)(2,1)}, u32[]{:S(2)}, u32[]{:S(2)}) %collective-permute-start.19) | collective-permute-done | bytes 278560 | tf_op jit(solution)/shard_map/ppermute | solution.py:29
  120.8 6.3 %conditional.1 = (bf16[1536,256]{1,0:T(8,128)(2,1)}) conditional(s32[]{:T(128)} %convert_element_type.27, (s32[24]{0:T(128)S(1)}, s32[24]{0:T(128)S(1)}, s32[4,16]{1,0:T(4,128)S(1)}, s32[4,16]{1,0:T(4,128)S(1)}, s32[4]{0:T(128)S(1)}, /*index=5*/bf16[8,4,2,128,128]{4,3,2,1,0:T(8,128)(2,1)}, s32[24]{0:T(128)S(1)}, bf16[1536,256]{1,0:T(8,128)(2,1)}, ...), branch_computations={%region_6.7_spmd, %region_7.8_spmd} | conditional | flops 4194636 | bytes 29362600 | solution.py:492
  120.8 6.3 %mix.3 = bf16[1536,256]{1,0:T(8,128)(2,1)} custom-call(s32[24]{0:T(128)S(1)} %get-tuple-element.77.starts, s32[24]{0:T(128)S(1)} %get-tuple-element.78.lengths, bf16[3072,128]{1,0:T(8,128)(2,1)} %get-tuple-element.79.weights, f32[1536,256]{1,0:T(8,128)} %get-tuple-element.80.mixed_new, f32[1536,256]{1,0:T(8,128)} %get-tuple-element.81.factor, ...), custom_call_target="tpu_custom_call" | custom-call | flops 1048576 | bytes 1048576 | tf_op jit(solution)/shard_map/cond/branch_1_fun/mix/pallas_call | solution.py:236
  127.1 0.1 collective-permute-start.20
  127.2 4.7 %all-to-all-start.3 = ((bf16[8,192,256]{2,1,0:T(8,128)(2,1)}), bf16[8,192,256]{2,1,0:T(8,128)(2,1)S(1)}, u32[]{:S(2)}, u32[]{:S(2)}) async-start(bf16[8,192,256]{2,1,0:T(8,128)(2,1)} %bitcast.21), calls=%async_computation.3 | async-start | bytes 1572864 | tf_op jit(solution)/shard_map/all_to_all | solution.py:495
  131.9 0.1 pad_add_fusion.1.places
  132.0 12.5 %all-to-all-done.3.heads = bf16[8,192,256]{2,1,0:T(8,128)(2,1)S(1)} async-done(((bf16[8,192,256]{2,1,0:T(8,128)(2,1)}), bf16[8,192,256]{2,1,0:T(8,128)(2,1)S(1)}, u32[]{:S(2)}, u32[]{:S(2)}) %all-to-all-start.3) | async-done | bytes 786464 | tf_op jit(solution)/shard_map/all_to_all | solution.py:495
  144.6 6.6 %project_out.1 = bf16[192,2048]{1,0:T(8,128)(2,1)} custom-call(s32[9]{0:T(128)S(1)} %pad_add_fusion.1.places, bf16[8,192,256]{2,1,0:T(8,128)(2,1)S(1)} %all-to-all-done.3.heads, bf16[8,128,2048]{2,1,0:T(8,128)(2,1)} %bitcast.18.mine, bf16[8,128,2048]{2,1,0:T(8,128)(2,1)} %collective-permute-done.20.other), custom_call_target="tpu_custom_call" | custom-call | flops 1048576 | bytes 1048576 | tf_op jit(solution)/shard_map/project_out/pallas_call | solution.py:348
  (43 shorter events, 0.4 us)
Async XLA Ops:
  0.0 16.7 %copy-start = (bf16[256,2048]{1,0:T(8,128)(2,1)S(1)}, bf16[256,2048]{1,0:T(8,128)(2,1)}, u32[]{:S(2)}) copy-start(bf16[256,2048]{1,0:T(8,128)(2,1)} %param.23) | copy-start | bytes 3145732
  0.0 19.7 %collective-permute-start.6 = (bf16[1536,256]{1,0:T(8,128)(2,1)}, bf16[1536,256]{1,0:T(8,128)(2,1)S(1)}, u32[]{:S(2)}, u32[]{:S(2)}) collective-permute-start(bf16[1536,256]{1,0:T(8,128)(2,1)} %refs_0_), channel_id=1, source_target_pairs={{0,4},{4,0},{1,5},{5,1},{2,6},{6,2},{3,7},{7,3},{8,12},{12,8},{9,1... | collective-permute-start | bytes 2359304 | tf_op jit(solution)/shard_map/ppermute | solution.py:29
  1.9 36.1 %collective-permute-start.7 = (bf16[1536,256]{1,0:T(8,128)(2,1)}, bf16[1536,256]{1,0:T(8,128)(2,1)}, u32[]{:S(2)}, u32[]{:S(2)}) collective-permute-start(bf16[1536,256]{1,0:T(8,128)(2,1)} %refs_0_), channel_id=1, source_target_pairs={{0,1},{1,2},{2,3},{3,0},{4,5},{5,6},{6,7},{7,4},{8,9},{9,10},{10,1... | collective-permute-start | bytes 2359304 | tf_op jit(solution)/shard_map/ppermute | solution.py:29
  3.4 34.7 %collective-permute-start.8 = (bf16[1536,256]{1,0:T(8,128)(2,1)}, bf16[1536,256]{1,0:T(8,128)(2,1)}, u32[]{:S(2)}, u32[]{:S(2)}) collective-permute-start(bf16[1536,256]{1,0:T(8,128)(2,1)} %refs_0_), channel_id=1, source_target_pairs={{0,3},{1,0},{2,1},{3,2},{4,7},{5,4},{6,5},{7,6},{8,11},{9,8},{10,9... | collective-permute-start | bytes 2359304 | tf_op jit(solution)/shard_map/ppermute | solution.py:29
  5.2 1.6 %copy-start.2 = (bf16[1,64,128,128]{3,2,1,0:T(8,128)(2,1)S(1)}, bf16[1,64,128,128]{3,2,1,0:T(8,128)(2,1)}, u32[]{:S(2)}) copy-start(bf16[1,64,128,128]{3,2,1,0:T(8,128)(2,1)} %param.24) | copy-start | bytes 6291460
  8.6 5.1 %copy-start.11 = (s32[768]{0:T(1024)S(1)}, s32[768]{0:T(1024)}, u32[]{:S(2)}) copy-start(s32[768]{0:T(1024)} %param.27) | copy-start | bytes 9220
  8.6 5.2 %copy-start.12 = (s32[768,1]{0,1:T(1,128)S(1)}, s32[768,1]{0,1:T(1,128)}, u32[]{:S(2)}) copy-start(s32[768,1]{0,1:T(1,128)} %param.26) | copy-start | bytes 9220
  8.6 31.1 %all-to-all-start = ((bf16[8,1024,128]{2,1,0:T(8,128)(2,1)}), bf16[8,1024,128]{2,1,0:T(8,128)(2,1)}, u32[]{:S(2)}, u32[]{:S(2)}) async-start(bf16[8,1024,128]{2,1,0:T(8,128)(2,1)} %bitcast.3), calls=%async_computation | async-start | bytes 4194304 | tf_op jit(solution)/shard_map/all_to_all | solution.py:367
  19.7 10.9 %copy-start.8 = (bf16[1536,256]{1,0:T(8,128)(2,1)}, bf16[1536,256]{1,0:T(8,128)(2,1)S(1)}, u32[]{:S(2)}) copy-start(bf16[1536,256]{1,0:T(8,128)(2,1)S(1)} %collective-permute-done.6.refs_1_) | copy-start | bytes 2359300
  19.7 20.0 %collective-permute-start.9 = (bf16[1536,256]{1,0:T(8,128)(2,1)S(1)}, bf16[1536,256]{1,0:T(8,128)(2,1)}, u32[]{:S(2)}, u32[]{:S(2)}) collective-permute-start(bf16[1536,256]{1,0:T(8,128)(2,1)S(1)} %collective-permute-done.6.refs_1_), channel_id=1, source_target_pairs={{0,1},{1,2},{2,3},{3,0},{4,5},{5,6},{6,7},{7,4},{8,9},{9,10},{10,1... | collective-permute-start | bytes 2359304 | tf_op jit(solution)/shard_map/ppermute | solution.py:29
  21.2 18.5 %collective-permute-start.10 = (bf16[1536,256]{1,0:T(8,128)(2,1)S(1)}, bf16[1536,256]{1,0:T(8,128)(2,1)}, u32[]{:S(2)}, u32[]{:S(2)}) collective-permute-start(bf16[1536,256]{1,0:T(8,128)(2,1)S(1)} %collective-permute-done.6.refs_1_), channel_id=1, source_target_pairs={{0,3},{1,0},{2,1},{3,2},{4,7},{5,4},{6,5},{7,6},{8,11},{9,8},{10,9... | collective-permute-start | bytes 2359304 | tf_op jit(solution)/shard_map/ppermute | solution.py:29
  23.2 12.6 %collective-permute-start.11 = (bf16[128,2048]{1,0:T(8,128)(2,1)S(1)}, bf16[128,2048]{1,0:T(8,128)(2,1)S(1)}, u32[]{:S(2)}, u32[]{:S(2)}) collective-permute-start(bf16[128,2048]{1,0:T(8,128)(2,1)S(1)} %constant_dynamic-slice_fusion.2.half), channel_id=1, source_target_pairs={{0,4},{4,0},{1,5},{5,1},{2,6},{6,2},{3,7},{7,3},{8,12},{12,8},{9,1... | collective-permute-start | bytes 1572872 | tf_op jit(solution)/shard_map/ppermute | solution.py:29
  27.1 1.6 %copy-start.3 = (bf16[1,64,128,128]{3,2,1,0:T(8,128)(2,1)S(1)}, bf16[1,64,128,128]{3,2,1,0:T(8,128)(2,1)}, u32[]{:S(2)}) copy-start(bf16[1,64,128,128]{3,2,1,0:T(8,128)(2,1)} %param.25) | copy-start | bytes 6291460
  34.9 4.8 %copy-start.10 = (f32[2048]{0:T(1024)S(1)}, f32[2048]{0:T(1024)}, u32[]{:S(2)}) copy-start(f32[2048]{0:T(1024)} %param.16) | copy-start | bytes 24580
  36.1 1.9 %copy-start.1 = (bf16[4,2,128,2048]{3,2,1,0:T(8,128)(2,1)}, bf16[4,2,128,2048]{3,2,1,0:T(8,128)(2,1)S(1)}, u32[]{:S(2)}) copy-start(bf16[4,2,128,2048]{3,2,1,0:T(8,128)(2,1)S(1)} %copies.1) | copy-start | bytes 12582916
  41.0 31.4 %all-to-all-start.1 = ((bf16[8,1024,128]{2,1,0:T(8,128)(2,1)}), bf16[8,1024,128]{2,1,0:T(8,128)(2,1)}, u32[]{:S(2)}, u32[]{:S(2)}) async-start(bf16[8,1024,128]{2,1,0:T(8,128)(2,1)} %bitcast.16), calls=%async_computation.1 | async-start | bytes 4194304 | tf_op jit(solution)/shard_map/all_to_all | solution.py:367
  46.5 21.0 %collective-permute-start.14 = (bf16[1536,256]{1,0:T(8,128)(2,1)}, bf16[1536,256]{1,0:T(8,128)(2,1)S(1)}, u32[]{:S(2)}, u32[]{:S(2)}) collective-permute-start(bf16[1536,256]{1,0:T(8,128)(2,1)} %collective-permute-done.7.refs_2_), channel_id=1, source_target_pairs={{0,1},{1,2},{2,3},{3,0},{4,5},{5,6},{6,7},{7,4},{8,9},{9,10},{10,1... | collective-permute-start | bytes 2359304 | tf_op jit(solution)/shard_map/ppermute | solution.py:29
  47.4 23.8 %collective-permute-start.15 = (bf16[1536,256]{1,0:T(8,128)(2,1)}, bf16[1536,256]{1,0:T(8,128)(2,1)}, u32[]{:S(2)}, u32[]{:S(2)}) collective-permute-start(bf16[1536,256]{1,0:T(8,128)(2,1)} %collective-permute-done.10.refs_5_), channel_id=1, source_target_pairs={{0,3},{1,0},{2,1},{3,2},{4,7},{5,4},{6,5},{7,6},{8,11},{9,8},{10,9... | collective-permute-start | bytes 2359304 | tf_op jit(solution)/shard_map/ppermute | solution.py:29
  52.2 15.3 %collective-permute-start.12 = (bf16[1088,128]{1,0:T(8,128)(2,1)S(1)}, bf16[1088,128]{1,0:T(8,128)(2,1)S(1)}, u32[]{:S(2)}, u32[]{:S(2)}) collective-permute-start(bf16[1088,128]{1,0:T(8,128)(2,1)S(1)} %get-tuple-element.136), channel_id=1, source_target_pairs={{0,16},{16,32},{32,48},{48,0},{1,17},{17,33},{33,49},{49,1},{2,18}... | collective-permute-start | bytes 835592 | tf_op jit(solution)/shard_map/ppermute | solution.py:29
  55.6 15.7 %collective-permute-start.13 = (bf16[1088,128]{1,0:T(8,128)(2,1)S(1)}, bf16[1088,128]{1,0:T(8,128)(2,1)S(1)}, u32[]{:S(2)}, u32[]{:S(2)}) collective-permute-start(bf16[1088,128]{1,0:T(8,128)(2,1)S(1)} %get-tuple-element.137), channel_id=1, source_target_pairs={{0,48},{16,0},{32,16},{48,32},{1,49},{17,1},{33,17},{49,33},{2,50}... | collective-permute-start | bytes 835592 | tf_op jit(solution)/shard_map/ppermute | solution.py:29
  67.5 3.7 %copy-start.9 = (bf16[1536,256]{1,0:T(8,128)(2,1)}, bf16[1536,256]{1,0:T(8,128)(2,1)S(1)}, u32[]{:S(2)}) copy-start(bf16[1536,256]{1,0:T(8,128)(2,1)S(1)} %collective-permute-done.14.refs_6_) | copy-start | bytes 2359300
  72.4 54.7 %all-to-all-start.2 = ((bf16[4,2,128,2048]{3,2,1,0:T(8,128)(2,1)}), bf16[4,2,128,2048]{3,2,1,0:T(8,128)(2,1)}, u32[]{:S(2)}, u32[]{:S(2)}) async-start(bf16[4,2,128,2048]{3,2,1,0:T(8,128)(2,1)} %copy-done.1), calls=%async_computation.2 | async-start | bytes 8388608 | tf_op jit(solution)/shard_map/all_to_all | solution.py:470
  77.3 28.1 %collective-permute-start.16 = (bf16[1088,128]{1,0:T(8,128)(2,1)S(1)}, bf16[1088,128]{1,0:T(8,128)(2,1)S(1)}, u32[]{:S(2)}, u32[]{:S(2)}) collective-permute-start(bf16[1088,128]{1,0:T(8,128)(2,1)S(1)} %get-tuple-element.165), channel_id=1, source_target_pairs={{0,32},{16,48},{32,0},{48,16},{1,33},{17,49},{33,1},{49,17},{2,34}... | collective-permute-start | bytes 835592 | tf_op jit(solution)/shard_map/ppermute | solution.py:29
  86.7 27.9 %collective-permute-start.17 = (bf16[1088,128]{1,0:T(8,128)(2,1)S(1)}, bf16[1088,128]{1,0:T(8,128)(2,1)}, u32[]{:S(2)}, u32[]{:S(2)}) collective-permute-start(bf16[1088,128]{1,0:T(8,128)(2,1)S(1)} %get-tuple-element.171), channel_id=1, source_target_pairs={{0,16},{16,32},{32,48},{48,0},{1,17},{17,33},{33,49},{49,1},{2,18}... | collective-permute-start | bytes 835592 | tf_op jit(solution)/shard_map/ppermute | solution.py:29
  88.2 26.5 %collective-permute-start.18 = (bf16[1088,128]{1,0:T(8,128)(2,1)S(1)}, bf16[1088,128]{1,0:T(8,128)(2,1)}, u32[]{:S(2)}, u32[]{:S(2)}) collective-permute-start(bf16[1088,128]{1,0:T(8,128)(2,1)S(1)} %get-tuple-element.172), channel_id=1, source_target_pairs={{0,32},{16,48},{32,0},{48,16},{1,33},{17,49},{33,1},{49,17},{2,34}... | collective-permute-start | bytes 835592 | tf_op jit(solution)/shard_map/ppermute | solution.py:29
  89.6 31.1 %collective-permute-start.19 = (bf16[1088,128]{1,0:T(8,128)(2,1)S(1)}, bf16[1088,128]{1,0:T(8,128)(2,1)}, u32[]{:S(2)}, u32[]{:S(2)}) collective-permute-start(bf16[1088,128]{1,0:T(8,128)(2,1)S(1)} %get-tuple-element.173), channel_id=1, source_target_pairs={{0,48},{16,0},{32,16},{48,32},{1,49},{17,1},{33,17},{49,33},{2,50}... | collective-permute-start | bytes 835592 | tf_op jit(solution)/shard_map/ppermute | solution.py:29
  127.1 17.5 %collective-permute-start.20 = (bf16[8,128,2048]{2,1,0:T(8,128)(2,1)}, bf16[8,128,2048]{2,1,0:T(8,128)(2,1)}, u32[]{:S(2)}, u32[]{:S(2)}) collective-permute-start(bf16[8,128,2048]{2,1,0:T(8,128)(2,1)} %bitcast.18.mine), channel_id=1, source_target_pairs={{0,8},{8,0},{1,9},{9,1},{2,10},{10,2},{3,11},{11,3},{4,12},{12,4},... | collective-permute-start | bytes 12582920 | tf_op jit(solution)/shard_map/ppermute | solution.py:29
  127.2 17.4 %all-to-all-start.3 = ((bf16[8,192,256]{2,1,0:T(8,128)(2,1)}), bf16[8,192,256]{2,1,0:T(8,128)(2,1)S(1)}, u32[]{:S(2)}, u32[]{:S(2)}) async-start(bf16[8,192,256]{2,1,0:T(8,128)(2,1)} %bitcast.21), calls=%async_computation.3 | async-start | bytes 1572864 | tf_op jit(solution)/shard_map/all_to_all | solution.py:495

commit v12 on v11

--- a/solution.py
+++ b/solution.py
@@ -15,8 +15,9 @@
 TENSOR = ("zl", "x")
 ROW_TILE = 256
 BATCH = 4
+MIX_BATCH = 8
 UNIT = 16
-PACKED = 68 * UNIT
+PACKED = 66 * UNIT
 LONG = pl.CostEstimate(flops=1 << 20, bytes_accessed=64 << 20, transcendentals=0)
 COST = pl.CostEstimate(flops=1 << 20, bytes_accessed=1 << 20, transcendentals=0)
 
@@ -206,7 +207,7 @@
 def mix_kernel(starts, lengths, weights, mixed_new, factor, *refs):
     parts, (out, values) = refs[:4], refs[4:]
     window, head = weights.shape[1], values.shape[1]
-    span = out.shape[0] // BATCH
+    span = out.shape[0] // MIX_BATCH
     shares = out.shape[1] // head
 
     @pl.when(pl.program_id(0) == 0)
@@ -214,8 +215,8 @@
         gather_parts(parts, values)
 
     old_row = lax.broadcasted_iota(jnp.int32, (window, head), 0)
-    for b in range(BATCH):
-        r = pl.program_id(0) * BATCH + b
+    for b in range(MIX_BATCH):
+        r = pl.program_id(0) * MIX_BATCH + b
         rows = slice(b * span, (b + 1) * span)
         old_values = values[pl.ds(pl.multiple_of(starts[r], UNIT), window), :]
         old_values = jnp.where(old_row < lengths[r], old_values, jnp.zeros_like(old_values))
@@ -230,7 +231,7 @@
 def mix(starts, lengths, weights, mixed_new, factor, values):
     rows, columns = factor.shape
     window, head = weights.shape[1], values[0].shape[1]
-    step = rows // lengths.shape[0] * BATCH
+    step = rows // lengths.shape[0] * MIX_BATCH
     tile = lambda width: pl.BlockSpec((step, width), lambda i, *_: (i, 0))
     whole = lambda a: pl.BlockSpec(a.shape, lambda i, *_: (0, 0))
     return pl.pallas_call(
@@ -452,11 +453,11 @@
     pieces = spread(span_rows)
     depth = o_weight.shape[0] // 2
     half = lax.dynamic_slice_in_dim(o_weight, core * depth, depth, 0)
-    half, pieces[1] = lax.optimization_barrier((half, pieces[1]))
+    gain = jnp.broadcast_to(norm_gain[:, None], (norm_gain.shape[0], head_dim))
+    half, pieces[1], gain = lax.optimization_barrier((half, pieces[1], gain))
     twin_half = shift(half, "zl", 1)
 
     key_part = across_y(by_target(key_cache.reshape(sides)))
-    gain = jnp.broadcast_to(norm_gain[:, None], (norm_gain.shape[0], head_dim))
     tables = (ids, places, starts, fits, gain, cosine, sine)
     value_slots, key_part, pieces[1:6], repeated, tables = lax.optimization_barrier(
         (by_target(value_cache.reshape(sides)), key_part, pieces[1:6], copies(half, twin_half), tables)

time: 154 us -> 151 us (0.981)
  Pallas kernels: 45.5 us -> 43.5 us
    ppermute x15, waiting for transfers between devices: 25 us -> 22.5 us  [shift(): return lax.ppermute(value, axis, ring(lax.axis_size(axis), step))]
  transfers between devices with their start and end apart: 19 -> 19, of which waited for: 8 -> 10; matrix products, arithmetic and copies ran while one was open for 6% -> 7% of each run, Pallas kernels for 26% -> 25%
where the time goes in v12:
time: 151 us; the launch traced here: 148 us
  starting transfers between devices  49.7 us (33%)
  Pallas kernels  43.5 us (29%)
  waiting for transfers between devices  38.4 us (25%)
  local copies, waits for them, and re-layouts  8.97 us (6%)
  other arithmetic  6.56 us (4%)
    ppermute x15, starting transfers between devices, shift(): return lax.ppermute(value, axis, ring(lax.axis_size(axis), step))  30.7 us
    ppermute x15, waiting for transfers between devices, shift(): return lax.ppermute(value, axis, ring(lax.axis_size(axis), step))  22.5 us
    pallas_call x1, Pallas kernels, project(): pl.pallas_call(project_kernel, out_shape=(jax.ShapeDtypeStruct((rows, wq....  13.6 us
    all_to_all x1, waiting for transfers between devices, local(): lax.all_to_all(attended.reshape(blocks, rows // blocks, attended.shape[1]...  12.8 us
    all_to_all x2, starting transfers between devices, across_y(): flat = lax.all_to_all(flat, ('y', 'c'), 0, 0, tiled=True)  10.6 us
    pallas_call x1, Pallas kernels, weigh(): pl.pallas_call(weigh_kernel, out_shape=(jax.ShapeDtypeStruct((shares * ro...  9.28 us
    pallas_call x1, Pallas kernels, project_out(): pl.pallas_call(output_kernel, out_shape=jax.ShapeDtypeStruct((rows, colum...  6.64 us
    unnamed x18, local copies, waits for them, and re-layouts  5.13 us
  transfers between devices with their start and end apart: 19, of which 10 were waited for; matrix products, arithmetic and copies ran while one was open for 7% of the time, Pallas kernels for 25%

profile of v12, /device:TPU:8, one launch (start us, length us, event | category | flops | bytes accessed | tf_op | source)
XLA Modules:
  0.0 148.0 jit_solution(15138729887306270097)
XLA Ops:
  0.0 1.9 %collective-permute-start.6 = (bf16[1536,256]{1,0:T(8,128)(2,1)}, bf16[1536,256]{1,0:T(8,128)(2,1)S(1)}, u32[]{:S(2)}, u32[]{:S(2)}) collective-permute-start(bf16[1536,256]{1,0:T(8,128)(2,1)} %refs_0_), channel_id=1, source_target_pairs={{0,4},{4,0},{1,5},{5,1},{2,6},{6,2},{3,7},{7,3},{8,12},{12,8},{9,1... | collective-permute-start | bytes 2359304 | tf_op jit(solution)/shard_map/ppermute | solution.py:30
  1.9 1.5 %collective-permute-start.7 = (bf16[1536,256]{1,0:T(8,128)(2,1)}, bf16[1536,256]{1,0:T(8,128)(2,1)}, u32[]{:S(2)}, u32[]{:S(2)}) collective-permute-start(bf16[1536,256]{1,0:T(8,128)(2,1)} %refs_0_), channel_id=1, source_target_pairs={{0,1},{1,2},{2,3},{3,0},{4,5},{5,6},{6,7},{7,4},{8,9},{9,10},{10,1... | collective-permute-start | bytes 2359304 | tf_op jit(solution)/shard_map/ppermute | solution.py:30
  3.4 1.7 %collective-permute-start.8 = (bf16[1536,256]{1,0:T(8,128)(2,1)}, bf16[1536,256]{1,0:T(8,128)(2,1)}, u32[]{:S(2)}, u32[]{:S(2)}) collective-permute-start(bf16[1536,256]{1,0:T(8,128)(2,1)} %refs_0_), channel_id=1, source_target_pairs={{0,3},{1,0},{2,1},{3,2},{4,7},{5,4},{6,5},{7,6},{8,11},{9,8},{10,9... | collective-permute-start | bytes 2359304 | tf_op jit(solution)/shard_map/ppermute | solution.py:30
  5.2 1.6 %copy-done.2 = bf16[1,64,128,128]{3,2,1,0:T(8,128)(2,1)S(1)} copy-done((bf16[1,64,128,128]{3,2,1,0:T(8,128)(2,1)S(1)}, bf16[1,64,128,128]{3,2,1,0:T(8,128)(2,1)}, u32[]{:S(2)}) %copy-start.2) | copy-done | bytes 2097176
  6.8 1.9 %by_target.3 = bf16[4,2,4,2,128,128]{5,4,3,2,1,0:T(8,128)(2,1)} custom-call(bf16[4,4,2,2,128,128]{5,4,3,2,1,0:T(8,128)(2,1)S(1)} %bitcast.25), custom_call_target="tpu_custom_call" | custom-call | flops 1048576 | bytes 67108864 | tf_op jit(solution)/shard_map/by_target/pallas_call | solution.py:294
  8.6 5.0 %all-to-all-start = ((bf16[8,1024,128]{2,1,0:T(8,128)(2,1)}), bf16[8,1024,128]{2,1,0:T(8,128)(2,1)}, u32[]{:S(2)}, u32[]{:S(2)}) async-start(bf16[8,1024,128]{2,1,0:T(8,128)(2,1)} %bitcast.3), calls=%async_computation | async-start | bytes 4194304 | tf_op jit(solution)/shard_map/all_to_all | solution.py:368
  13.7 0.1 reshape.368
  13.9 0.1 reshape.367
  14.0 0.1 copy.20
  14.1 0.2 convert_reduce_fusion
  14.2 0.1 copy.22
  14.3 0.3 fusion.9
  14.6 0.6 gather_fusion.1
  15.2 0.6 gather_fusion
  15.7 0.1 add_multiply_fusion
  15.8 0.1 iota_add_fusion
  15.9 0.1 add.400
  16.0 0.2 select_reduce_fusion.1
  16.2 0.2 reduce_window_sum.11
  16.4 0.2 select_reduce_fusion.2
  16.6 0.1 add_convert_fusion
  16.7 2.9 %collective-permute-done.6.refs_1_ = bf16[1536,256]{1,0:T(8,128)(2,1)S(1)} collective-permute-done((bf16[1536,256]{1,0:T(8,128)(2,1)}, bf16[1536,256]{1,0:T(8,128)(2,1)S(1)}, u32[]{:S(2)}, u32[]{:S(2)}) %collective-permute-start.6) | collective-permute-done | bytes 786464 | tf_op jit(solution)/shard_map/ppermute | solution.py:30
  19.7 1.5 %collective-permute-start.9 = (bf16[1536,256]{1,0:T(8,128)(2,1)S(1)}, bf16[1536,256]{1,0:T(8,128)(2,1)}, u32[]{:S(2)}, u32[]{:S(2)}) collective-permute-start(bf16[1536,256]{1,0:T(8,128)(2,1)S(1)} %collective-permute-done.6.refs_1_), channel_id=1, source_target_pairs={{0,1},{1,2},{2,3},{3,0},{4,5},{5,6},{6,7},{7,4},{8,9},{9,10},{10,1... | collective-permute-start | bytes 2359304 | tf_op jit(solution)/shard_map/ppermute | solution.py:30
  21.2 1.7 %collective-permute-start.10 = (bf16[1536,256]{1,0:T(8,128)(2,1)S(1)}, bf16[1536,256]{1,0:T(8,128)(2,1)}, u32[]{:S(2)}, u32[]{:S(2)}) collective-permute-start(bf16[1536,256]{1,0:T(8,128)(2,1)S(1)} %collective-permute-done.6.refs_1_), channel_id=1, source_target_pairs={{0,3},{1,0},{2,1},{3,2},{4,7},{5,4},{6,5},{7,6},{8,11},{9,8},{10,9... | collective-permute-start | bytes 2359304 | tf_op jit(solution)/shard_map/ppermute | solution.py:30
  23.0 0.1 min.21
  23.2 1.3 broadcast_in_dim.51.refs_8_
  24.5 1.7 %collective-permute-start.11 = (bf16[128,2048]{1,0:T(8,128)(2,1)S(1)}, bf16[128,2048]{1,0:T(8,128)(2,1)S(1)}, u32[]{:S(2)}, u32[]{:S(2)}) collective-permute-start(bf16[128,2048]{1,0:T(8,128)(2,1)S(1)} %constant_dynamic-slice_fusion.2.half), channel_id=1, source_target_pairs={{0,4},{4,0},{1,5},{5,1},{2,6},{6,2},{3,7},{7,3},{8,12},{12,8},{9,1... | collective-permute-start | bytes 1572872 | tf_op jit(solution)/shard_map/ppermute | solution.py:30
  26.2 0.1 pad_add_fusion.2.offsets
  26.3 0.1 convert_element_type.25
  26.4 0.6 reduce_max.9
  27.7 0.7 stack.35.ids
  28.4 1.6 %copy-done.3 = bf16[1,64,128,128]{3,2,1,0:T(8,128)(2,1)S(1)} copy-done((bf16[1,64,128,128]{3,2,1,0:T(8,128)(2,1)S(1)}, bf16[1,64,128,128]{3,2,1,0:T(8,128)(2,1)}, u32[]{:S(2)}) %copy-start.3) | copy-done | bytes 2097176
  29.9 1.9 %by_target.2 = bf16[4,2,4,2,128,128]{5,4,3,2,1,0:T(8,128)(2,1)} custom-call(bf16[4,4,2,2,128,128]{5,4,3,2,1,0:T(8,128)(2,1)S(1)} %bitcast.26), custom_call_target="tpu_custom_call" | custom-call | flops 1048576 | bytes 67108864 | tf_op jit(solution)/shard_map/by_target/pallas_call | solution.py:294
  31.9 4.3 %fusion = (f32[1536,128]{1,0:T(8,128)}, f32[1536,128]{1,0:T(8,128)}) fusion(f32[128]{0:T(128)S(1)} %get-tuple-element.192, f32[128]{0:T(128)S(1)} %get-tuple-element.193, f32[1536]{0:T(1024)S(1)} %convert_element_type.25), kind=kLoop, calls=%fused_computation.7 | loop fusion | flops 393216 | bytes 1580032 | tf_op jit(solution)/shard_map/mul | solution.py:448
  36.2 0.8 collective-permute-done.11.twin
  37.0 0.3 copies.1
  37.4 1.9 %copy-done.1 = bf16[4,2,128,2048]{3,2,1,0:T(8,128)(2,1)} copy-done((bf16[4,2,128,2048]{3,2,1,0:T(8,128)(2,1)}, bf16[4,2,128,2048]{3,2,1,0:T(8,128)(2,1)S(1)}, u32[]{:S(2)}) %copy-start.1) | copy-done | bytes 4194328
  39.3 0.4 collective-permute-done.9.refs_4_
  39.7 5.5 %all-to-all-start.1 = ((bf16[8,1024,128]{2,1,0:T(8,128)(2,1)}), bf16[8,1024,128]{2,1,0:T(8,128)(2,1)}, u32[]{:S(2)}, u32[]{:S(2)}) async-start(bf16[8,1024,128]{2,1,0:T(8,128)(2,1)} %bitcast.16), calls=%async_computation.1 | async-start | bytes 4194304 | tf_op jit(solution)/shard_map/all_to_all | solution.py:368
  45.2 0.9 collective-permute-start.14
  46.1 2.4 %collective-permute-start.15 = (bf16[1536,256]{1,0:T(8,128)(2,1)}, bf16[1536,256]{1,0:T(8,128)(2,1)}, u32[]{:S(2)}, u32[]{:S(2)}) collective-permute-start(bf16[1536,256]{1,0:T(8,128)(2,1)} %collective-permute-done.10.refs_5_), channel_id=1, source_target_pairs={{0,3},{1,0},{2,1},{3,2},{4,7},{5,4},{6,5},{7,6},{8,11},{9,8},{10,9... | collective-permute-start | bytes 2359304 | tf_op jit(solution)/shard_map/ppermute | solution.py:30
  48.5 2.4 %pack.6 = (bf16[1056,128]{1,0:T(8,128)(2,1)S(1)}, bf16[1056,128]{1,0:T(8,128)(2,1)S(1)}, bf16[1056,128]{1,0:T(8,128)(2,1)S(1)}, bf16[1056,128]{1,0:T(8,128)(2,1)S(1)}) custom-call(s32[68]{0:T(128)S(1)} %pad_add_fusion.2.offsets, bf16[8,4,2,128,128]{4,3,2,1,0:T(8,128)(2,1)} %bitcast.4.cache), custom_call_target="tpu_custom_call" | custom-call | flops 1048576 | bytes 1048576 | tf_op jit(solution)/shard_map/pack/pallas_call | solution.py:271
  50.9 3.3 %collective-permute-start.12 = (bf16[1056,128]{1,0:T(8,128)(2,1)S(1)}, bf16[1056,128]{1,0:T(8,128)(2,1)S(1)}, u32[]{:S(2)}, u32[]{:S(2)}) collective-permute-start(bf16[1056,128]{1,0:T(8,128)(2,1)S(1)} %get-tuple-element.138), channel_id=1, source_target_pairs={{0,16},{16,32},{32,48},{48,0},{1,17},{17,33},{33,49},{49,1},{2,18}... | collective-permute-start | bytes 811016 | tf_op jit(solution)/shard_map/ppermute | solution.py:30
  54.2 2.2 %collective-permute-start.13 = (bf16[1056,128]{1,0:T(8,128)(2,1)S(1)}, bf16[1056,128]{1,0:T(8,128)(2,1)S(1)}, u32[]{:S(2)}, u32[]{:S(2)}) collective-permute-start(bf16[1056,128]{1,0:T(8,128)(2,1)S(1)} %get-tuple-element.139), channel_id=1, source_target_pairs={{0,48},{16,0},{32,16},{48,32},{1,49},{17,1},{33,17},{49,33},{2,50}... | collective-permute-start | bytes 811016 | tf_op jit(solution)/shard_map/ppermute | solution.py:30
  56.5 9.8 %collective-permute-done.14.refs_6_ = bf16[1536,256]{1,0:T(8,128)(2,1)S(1)} collective-permute-done((bf16[1536,256]{1,0:T(8,128)(2,1)}, bf16[1536,256]{1,0:T(8,128)(2,1)S(1)}, u32[]{:S(2)}, u32[]{:S(2)}) %collective-permute-start.14) | collective-permute-done | bytes 786464 | tf_op jit(solution)/shard_map/ppermute | solution.py:30
  66.2 3.3 %collective-permute-done.13.refs_3_ = bf16[1056,128]{1,0:T(8,128)(2,1)S(1)} collective-permute-done((bf16[1056,128]{1,0:T(8,128)(2,1)S(1)}, bf16[1056,128]{1,0:T(8,128)(2,1)S(1)}, u32[]{:S(2)}, u32[]{:S(2)}) %collective-permute-start.13) | collective-permute-done | bytes 270368 | tf_op jit(solution)/shard_map/ppermute | solution.py:30
  69.6 1.5 %all-to-all-done.1 = bf16[8,1024,128]{2,1,0:T(8,128)(2,1)} async-done(((bf16[8,1024,128]{2,1,0:T(8,128)(2,1)}), bf16[8,1024,128]{2,1,0:T(8,128)(2,1)}, u32[]{:S(2)}, u32[]{:S(2)}) %all-to-all-start.1) | async-done | bytes 2097184 | tf_op jit(solution)/shard_map/all_to_all | solution.py:368
  71.1 4.9 %all-to-all-start.2 = ((bf16[4,2,128,2048]{3,2,1,0:T(8,128)(2,1)}), bf16[4,2,128,2048]{3,2,1,0:T(8,128)(2,1)}, u32[]{:S(2)}, u32[]{:S(2)}) async-start(bf16[4,2,128,2048]{3,2,1,0:T(8,128)(2,1)} %copy-done.1), calls=%async_computation.2 | async-start | bytes 8388608 | tf_op jit(solution)/shard_map/all_to_all | solution.py:471
  76.0 6.4 %collective-permute-start.16 = (bf16[1056,128]{1,0:T(8,128)(2,1)S(1)}, bf16[1056,128]{1,0:T(8,128)(2,1)S(1)}, u32[]{:S(2)}, u32[]{:S(2)}) collective-permute-start(bf16[1056,128]{1,0:T(8,128)(2,1)S(1)} %get-tuple-element.167), channel_id=1, source_target_pairs={{0,32},{16,48},{32,0},{48,16},{1,33},{17,49},{33,1},{49,17},{2,34}... | collective-permute-start | bytes 811016 | tf_op jit(solution)/shard_map/ppermute | solution.py:30
  82.4 2.4 %pack.7 = (bf16[1056,128]{1,0:T(8,128)(2,1)S(1)}, bf16[1056,128]{1,0:T(8,128)(2,1)S(1)}, bf16[1056,128]{1,0:T(8,128)(2,1)S(1)}, bf16[1056,128]{1,0:T(8,128)(2,1)S(1)}) custom-call(s32[68]{0:T(128)S(1)} %pad_add_fusion.2.offsets, bf16[8,4,2,128,128]{4,3,2,1,0:T(8,128)(2,1)} %bitcast.17.cache), custom_call_target="tpu_custom_call" | custom-call | flops 1048576 | bytes 1048576 | tf_op jit(solution)/shard_map/pack/pallas_call | solution.py:271
  84.8 1.6 %collective-permute-start.17 = (bf16[1056,128]{1,0:T(8,128)(2,1)S(1)}, bf16[1056,128]{1,0:T(8,128)(2,1)}, u32[]{:S(2)}, u32[]{:S(2)}) collective-permute-start(bf16[1056,128]{1,0:T(8,128)(2,1)S(1)} %get-tuple-element.173), channel_id=1, source_target_pairs={{0,16},{16,32},{32,48},{48,0},{1,17},{17,33},{33,49},{49,1},{2,18}... | collective-permute-start | bytes 811016 | tf_op jit(solution)/shard_map/ppermute | solution.py:30
  86.3 1.4 collective-permute-start.18
  87.8 2.4 %collective-permute-start.19 = (bf16[1056,128]{1,0:T(8,128)(2,1)S(1)}, bf16[1056,128]{1,0:T(8,128)(2,1)}, u32[]{:S(2)}, u32[]{:S(2)}) collective-permute-start(bf16[1056,128]{1,0:T(8,128)(2,1)S(1)} %get-tuple-element.175), channel_id=1, source_target_pairs={{0,48},{16,0},{32,16},{48,32},{1,49},{17,1},{33,17},{49,33},{2,50}... | collective-permute-start | bytes 811016 | tf_op jit(solution)/shard_map/ppermute | solution.py:30
  90.2 13.6 %project.1 = (bf16[1536,256]{1,0:T(8,128)(2,1)}, f32[1536,256]{1,0:T(8,128)}, bf16[1536,128]{1,0:T(8,128)(2,1)}, bf16[1536,128]{1,0:T(8,128)(2,1)}) custom-call(s32[8]{0:T(128)} %stack.35.ids, bf16[1536,256]{1,0:T(8,128)(2,1)} %refs_0_, bf16[1536,256]{1,0:T(8,128)(2,1)} %copy-done.8, bf16[1536,256]{1,0:T(8,128)(2,1)} %collective-permute-done.7.refs_2_, ...), custom_call_target="tpu_custom_call" | custom-call | flops 1048576 | bytes 1048576 | tf_op jit(solution)/shard_map/project/pallas_call | solution.py:107
  103.8 9.3 %weigh.3 = (bf16[3072,128]{1,0:T(8,128)(2,1)}, f32[1536,256]{1,0:T(8,128)}, f32[1536,256]{1,0:T(8,128)}) custom-call(s32[24]{0:T(128)S(1)} %get-tuple-element.164.starts, s32[24]{0:T(128)S(1)} %get-tuple-element.191.lengths, bf16[1536,256]{1,0:T(8,128)(2,1)} %get-tuple-element.160.q, f32[1536,256]{1,0:T(8,128)} %get-tuple-element.161.g, ...), custom_call_target="tpu_custom_call" | custom-call | flops 1048576 | bytes 1048576 | tf_op jit(solution)/shard_map/weigh/pallas_call | solution.py:183
  113.1 3.9 %collective-permute-done.18 = bf16[1056,128]{1,0:T(8,128)(2,1)} collective-permute-done((bf16[1056,128]{1,0:T(8,128)(2,1)S(1)}, bf16[1056,128]{1,0:T(8,128)(2,1)}, u32[]{:S(2)}, u32[]{:S(2)}) %collective-permute-start.18) | collective-permute-done | bytes 270368 | tf_op jit(solution)/shard_map/ppermute | solution.py:30
  116.9 1.5 collective-permute-done.19
  118.4 5.0 %conditional.1 = (bf16[1536,256]{1,0:T(8,128)(2,1)}) conditional(s32[]{:T(128)} %convert_element_type.27, (s32[24]{0:T(128)S(1)}, s32[24]{0:T(128)S(1)}, s32[4,16]{1,0:T(4,128)S(1)}, s32[4,16]{1,0:T(4,128)S(1)}, s32[4]{0:T(128)S(1)}, /*index=5*/bf16[8,4,2,128,128]{4,3,2,1,0:T(8,128)(2,1)}, s32[24]{0:T(128)S(1)}, bf16[1536,256]{1,0:T(8,128)(2,1)}, ...), branch_computations={%region_6.7_spmd, %region_7.8_spmd} | conditional | flops 4194636 | bytes 29362600 | solution.py:493
  118.4 5.0 %mix.3 = bf16[1536,256]{1,0:T(8,128)(2,1)} custom-call(s32[24]{0:T(128)S(1)} %get-tuple-element.77.starts, s32[24]{0:T(128)S(1)} %get-tuple-element.78.lengths, bf16[3072,128]{1,0:T(8,128)(2,1)} %get-tuple-element.79.weights, f32[1536,256]{1,0:T(8,128)} %get-tuple-element.80.mixed_new, f32[1536,256]{1,0:T(8,128)} %get-tuple-element.81.factor, ...), custom_call_target="tpu_custom_call" | custom-call | flops 1048576 | bytes 1048576 | tf_op jit(solution)/shard_map/cond/branch_1_fun/mix/pallas_call | solution.py:237
  123.4 1.5 %all-to-all-done.2 = bf16[4,2,128,2048]{3,2,1,0:T(8,128)(2,1)} async-done(((bf16[4,2,128,2048]{3,2,1,0:T(8,128)(2,1)}), bf16[4,2,128,2048]{3,2,1,0:T(8,128)(2,1)}, u32[]{:S(2)}, u32[]{:S(2)}) %all-to-all-start.2) | async-done | bytes 4194336 | tf_op jit(solution)/shard_map/all_to_all | solution.py:471
  124.9 3.5 %all-to-all-start.3 = ((bf16[8,192,256]{2,1,0:T(8,128)(2,1)}), bf16[8,192,256]{2,1,0:T(8,128)(2,1)S(1)}, u32[]{:S(2)}, u32[]{:S(2)}) async-start(bf16[8,192,256]{2,1,0:T(8,128)(2,1)} %bitcast.21), calls=%async_computation.3 | async-start | bytes 1572864 | tf_op jit(solution)/shard_map/all_to_all | solution.py:496
  128.5 0.1 pad_add_fusion.1.places
  128.6 12.8 %all-to-all-done.3.heads = bf16[8,192,256]{2,1,0:T(8,128)(2,1)S(1)} async-done(((bf16[8,192,256]{2,1,0:T(8,128)(2,1)}), bf16[8,192,256]{2,1,0:T(8,128)(2,1)S(1)}, u32[]{:S(2)}, u32[]{:S(2)}) %all-to-all-start.3) | async-done | bytes 786464 | tf_op jit(solution)/shard_map/all_to_all | solution.py:496
  141.3 6.6 %project_out.1 = bf16[192,2048]{1,0:T(8,128)(2,1)} custom-call(s32[9]{0:T(128)S(1)} %pad_add_fusion.1.places, bf16[8,192,256]{2,1,0:T(8,128)(2,1)S(1)} %all-to-all-done.3.heads, bf16[8,128,2048]{2,1,0:T(8,128)(2,1)} %bitcast.18.mine, bf16[8,128,2048]{2,1,0:T(8,128)(2,1)} %collective-permute-done.20.other), custom_call_target="tpu_custom_call" | custom-call | flops 1048576 | bytes 1048576 | tf_op jit(solution)/shard_map/project_out/pallas_call | solution.py:349
  (43 shorter events, 0.4 us)
Async XLA Ops:
  0.0 16.7 %copy-start = (bf16[256,2048]{1,0:T(8,128)(2,1)S(1)}, bf16[256,2048]{1,0:T(8,128)(2,1)}, u32[]{:S(2)}) copy-start(bf16[256,2048]{1,0:T(8,128)(2,1)} %param.23) | copy-start | bytes 3145732
  0.0 19.7 %collective-permute-start.6 = (bf16[1536,256]{1,0:T(8,128)(2,1)}, bf16[1536,256]{1,0:T(8,128)(2,1)S(1)}, u32[]{:S(2)}, u32[]{:S(2)}) collective-permute-start(bf16[1536,256]{1,0:T(8,128)(2,1)} %refs_0_), channel_id=1, source_target_pairs={{0,4},{4,0},{1,5},{5,1},{2,6},{6,2},{3,7},{7,3},{8,12},{12,8},{9,1... | collective-permute-start | bytes 2359304 | tf_op jit(solution)/shard_map/ppermute | solution.py:30
  1.9 37.4 %collective-permute-start.7 = (bf16[1536,256]{1,0:T(8,128)(2,1)}, bf16[1536,256]{1,0:T(8,128)(2,1)}, u32[]{:S(2)}, u32[]{:S(2)}) collective-permute-start(bf16[1536,256]{1,0:T(8,128)(2,1)} %refs_0_), channel_id=1, source_target_pairs={{0,1},{1,2},{2,3},{3,0},{4,5},{5,6},{6,7},{7,4},{8,9},{9,10},{10,1... | collective-permute-start | bytes 2359304 | tf_op jit(solution)/shard_map/ppermute | solution.py:30
  3.4 35.9 %collective-permute-start.8 = (bf16[1536,256]{1,0:T(8,128)(2,1)}, bf16[1536,256]{1,0:T(8,128)(2,1)}, u32[]{:S(2)}, u32[]{:S(2)}) collective-permute-start(bf16[1536,256]{1,0:T(8,128)(2,1)} %refs_0_), channel_id=1, source_target_pairs={{0,3},{1,0},{2,1},{3,2},{4,7},{5,4},{6,5},{7,6},{8,11},{9,8},{10,9... | collective-permute-start | bytes 2359304 | tf_op jit(solution)/shard_map/ppermute | solution.py:30
  5.2 1.6 %copy-start.2 = (bf16[1,64,128,128]{3,2,1,0:T(8,128)(2,1)S(1)}, bf16[1,64,128,128]{3,2,1,0:T(8,128)(2,1)}, u32[]{:S(2)}) copy-start(bf16[1,64,128,128]{3,2,1,0:T(8,128)(2,1)} %param.24) | copy-start | bytes 6291460
  8.6 5.1 %copy-start.11 = (s32[768]{0:T(1024)S(1)}, s32[768]{0:T(1024)}, u32[]{:S(2)}) copy-start(s32[768]{0:T(1024)} %param.27) | copy-start | bytes 9220
  8.6 5.2 %copy-start.12 = (s32[768,1]{0,1:T(1,128)S(1)}, s32[768,1]{0,1:T(1,128)}, u32[]{:S(2)}) copy-start(s32[768,1]{0,1:T(1,128)} %param.26) | copy-start | bytes 9220
  8.6 14.5 %copy-start.10 = (f32[2048]{0:T(1024)S(1)}, f32[2048]{0:T(1024)}, u32[]{:S(2)}) copy-start(f32[2048]{0:T(1024)} %param.16) | copy-start | bytes 24580
  8.6 31.1 %all-to-all-start = ((bf16[8,1024,128]{2,1,0:T(8,128)(2,1)}), bf16[8,1024,128]{2,1,0:T(8,128)(2,1)}, u32[]{:S(2)}, u32[]{:S(2)}) async-start(bf16[8,1024,128]{2,1,0:T(8,128)(2,1)} %bitcast.3), calls=%async_computation | async-start | bytes 4194304 | tf_op jit(solution)/shard_map/all_to_all | solution.py:368
  19.7 12.2 %copy-start.8 = (bf16[1536,256]{1,0:T(8,128)(2,1)}, bf16[1536,256]{1,0:T(8,128)(2,1)S(1)}, u32[]{:S(2)}) copy-start(bf16[1536,256]{1,0:T(8,128)(2,1)S(1)} %collective-permute-done.6.refs_1_) | copy-start | bytes 2359300
  19.7 20.0 %collective-permute-start.9 = (bf16[1536,256]{1,0:T(8,128)(2,1)S(1)}, bf16[1536,256]{1,0:T(8,128)(2,1)}, u32[]{:S(2)}, u32[]{:S(2)}) collective-permute-start(bf16[1536,256]{1,0:T(8,128)(2,1)S(1)} %collective-permute-done.6.refs_1_), channel_id=1, source_target_pairs={{0,1},{1,2},{2,3},{3,0},{4,5},{5,6},{6,7},{7,4},{8,9},{9,10},{10,1... | collective-permute-start | bytes 2359304 | tf_op jit(solution)/shard_map/ppermute | solution.py:30
  21.2 18.5 %collective-permute-start.10 = (bf16[1536,256]{1,0:T(8,128)(2,1)S(1)}, bf16[1536,256]{1,0:T(8,128)(2,1)}, u32[]{:S(2)}, u32[]{:S(2)}) collective-permute-start(bf16[1536,256]{1,0:T(8,128)(2,1)S(1)} %collective-permute-done.6.refs_1_), channel_id=1, source_target_pairs={{0,3},{1,0},{2,1},{3,2},{4,7},{5,4},{6,5},{7,6},{8,11},{9,8},{10,9... | collective-permute-start | bytes 2359304 | tf_op jit(solution)/shard_map/ppermute | solution.py:30
  24.5 12.5 %collective-permute-start.11 = (bf16[128,2048]{1,0:T(8,128)(2,1)S(1)}, bf16[128,2048]{1,0:T(8,128)(2,1)S(1)}, u32[]{:S(2)}, u32[]{:S(2)}) collective-permute-start(bf16[128,2048]{1,0:T(8,128)(2,1)S(1)} %constant_dynamic-slice_fusion.2.half), channel_id=1, source_target_pairs={{0,4},{4,0},{1,5},{5,1},{2,6},{6,2},{3,7},{7,3},{8,12},{12,8},{9,1... | collective-permute-start | bytes 1572872 | tf_op jit(solution)/shard_map/ppermute | solution.py:30
  28.4 1.6 %copy-start.3 = (bf16[1,64,128,128]{3,2,1,0:T(8,128)(2,1)S(1)}, bf16[1,64,128,128]{3,2,1,0:T(8,128)(2,1)}, u32[]{:S(2)}) copy-start(bf16[1,64,128,128]{3,2,1,0:T(8,128)(2,1)} %param.25) | copy-start | bytes 6291460
  37.4 1.9 %copy-start.1 = (bf16[4,2,128,2048]{3,2,1,0:T(8,128)(2,1)}, bf16[4,2,128,2048]{3,2,1,0:T(8,128)(2,1)S(1)}, u32[]{:S(2)}) copy-start(bf16[4,2,128,2048]{3,2,1,0:T(8,128)(2,1)S(1)} %copies.1) | copy-start | bytes 12582916
  39.7 31.4 %all-to-all-start.1 = ((bf16[8,1024,128]{2,1,0:T(8,128)(2,1)}), bf16[8,1024,128]{2,1,0:T(8,128)(2,1)}, u32[]{:S(2)}, u32[]{:S(2)}) async-start(bf16[8,1024,128]{2,1,0:T(8,128)(2,1)} %bitcast.16), calls=%async_computation.1 | async-start | bytes 4194304 | tf_op jit(solution)/shard_map/all_to_all | solution.py:368
  45.2 21.0 %collective-permute-start.14 = (bf16[1536,256]{1,0:T(8,128)(2,1)}, bf16[1536,256]{1,0:T(8,128)(2,1)S(1)}, u32[]{:S(2)}, u32[]{:S(2)}) collective-permute-start(bf16[1536,256]{1,0:T(8,128)(2,1)} %collective-permute-done.7.refs_2_), channel_id=1, source_target_pairs={{0,1},{1,2},{2,3},{3,0},{4,5},{5,6},{6,7},{7,4},{8,9},{9,10},{10,1... | collective-permute-start | bytes 2359304 | tf_op jit(solution)/shard_map/ppermute | solution.py:30
  46.1 23.5 %collective-permute-start.15 = (bf16[1536,256]{1,0:T(8,128)(2,1)}, bf16[1536,256]{1,0:T(8,128)(2,1)}, u32[]{:S(2)}, u32[]{:S(2)}) collective-permute-start(bf16[1536,256]{1,0:T(8,128)(2,1)} %collective-permute-done.10.refs_5_), channel_id=1, source_target_pairs={{0,3},{1,0},{2,1},{3,2},{4,7},{5,4},{6,5},{7,6},{8,11},{9,8},{10,9... | collective-permute-start | bytes 2359304 | tf_op jit(solution)/shard_map/ppermute | solution.py:30
  50.9 15.3 %collective-permute-start.12 = (bf16[1056,128]{1,0:T(8,128)(2,1)S(1)}, bf16[1056,128]{1,0:T(8,128)(2,1)S(1)}, u32[]{:S(2)}, u32[]{:S(2)}) collective-permute-start(bf16[1056,128]{1,0:T(8,128)(2,1)S(1)} %get-tuple-element.138), channel_id=1, source_target_pairs={{0,16},{16,32},{32,48},{48,0},{1,17},{17,33},{33,49},{49,1},{2,18}... | collective-permute-start | bytes 811016 | tf_op jit(solution)/shard_map/ppermute | solution.py:30
  54.2 15.3 %collective-permute-start.13 = (bf16[1056,128]{1,0:T(8,128)(2,1)S(1)}, bf16[1056,128]{1,0:T(8,128)(2,1)S(1)}, u32[]{:S(2)}, u32[]{:S(2)}) collective-permute-start(bf16[1056,128]{1,0:T(8,128)(2,1)S(1)} %get-tuple-element.139), channel_id=1, source_target_pairs={{0,48},{16,0},{32,16},{48,32},{1,49},{17,1},{33,17},{49,33},{2,50}... | collective-permute-start | bytes 811016 | tf_op jit(solution)/shard_map/ppermute | solution.py:30
  66.2 3.3 %copy-start.9 = (bf16[1536,256]{1,0:T(8,128)(2,1)}, bf16[1536,256]{1,0:T(8,128)(2,1)S(1)}, u32[]{:S(2)}) copy-start(bf16[1536,256]{1,0:T(8,128)(2,1)S(1)} %collective-permute-done.14.refs_6_) | copy-start | bytes 2359300
  71.1 53.8 %all-to-all-start.2 = ((bf16[4,2,128,2048]{3,2,1,0:T(8,128)(2,1)}), bf16[4,2,128,2048]{3,2,1,0:T(8,128)(2,1)}, u32[]{:S(2)}, u32[]{:S(2)}) async-start(bf16[4,2,128,2048]{3,2,1,0:T(8,128)(2,1)} %copy-done.1), calls=%async_computation.2 | async-start | bytes 8388608 | tf_op jit(solution)/shard_map/all_to_all | solution.py:471
  76.0 27.8 %collective-permute-start.16 = (bf16[1056,128]{1,0:T(8,128)(2,1)S(1)}, bf16[1056,128]{1,0:T(8,128)(2,1)S(1)}, u32[]{:S(2)}, u32[]{:S(2)}) collective-permute-start(bf16[1056,128]{1,0:T(8,128)(2,1)S(1)} %get-tuple-element.167), channel_id=1, source_target_pairs={{0,32},{16,48},{32,0},{48,16},{1,33},{17,49},{33,1},{49,17},{2,34}... | collective-permute-start | bytes 811016 | tf_op jit(solution)/shard_map/ppermute | solution.py:30
  84.8 28.3 %collective-permute-start.17 = (bf16[1056,128]{1,0:T(8,128)(2,1)S(1)}, bf16[1056,128]{1,0:T(8,128)(2,1)}, u32[]{:S(2)}, u32[]{:S(2)}) collective-permute-start(bf16[1056,128]{1,0:T(8,128)(2,1)S(1)} %get-tuple-element.173), channel_id=1, source_target_pairs={{0,16},{16,32},{32,48},{48,0},{1,17},{17,33},{33,49},{49,1},{2,18}... | collective-permute-start | bytes 811016 | tf_op jit(solution)/shard_map/ppermute | solution.py:30
  86.3 30.6 %collective-permute-start.18 = (bf16[1056,128]{1,0:T(8,128)(2,1)S(1)}, bf16[1056,128]{1,0:T(8,128)(2,1)}, u32[]{:S(2)}, u32[]{:S(2)}) collective-permute-start(bf16[1056,128]{1,0:T(8,128)(2,1)S(1)} %get-tuple-element.174), channel_id=1, source_target_pairs={{0,32},{16,48},{32,0},{48,16},{1,33},{17,49},{33,1},{49,17},{2,34}... | collective-permute-start | bytes 811016 | tf_op jit(solution)/shard_map/ppermute | solution.py:30
  87.8 30.6 %collective-permute-start.19 = (bf16[1056,128]{1,0:T(8,128)(2,1)S(1)}, bf16[1056,128]{1,0:T(8,128)(2,1)}, u32[]{:S(2)}, u32[]{:S(2)}) collective-permute-start(bf16[1056,128]{1,0:T(8,128)(2,1)S(1)} %get-tuple-element.175), channel_id=1, source_target_pairs={{0,48},{16,0},{32,16},{48,32},{1,49},{17,1},{33,17},{49,33},{2,50}... | collective-permute-start | bytes 811016 | tf_op jit(solution)/shard_map/ppermute | solution.py:30
  124.9 16.4 %collective-permute-start.20 = (bf16[8,128,2048]{2,1,0:T(8,128)(2,1)}, bf16[8,128,2048]{2,1,0:T(8,128)(2,1)}, u32[]{:S(2)}, u32[]{:S(2)}) collective-permute-start(bf16[8,128,2048]{2,1,0:T(8,128)(2,1)} %bitcast.18.mine), channel_id=1, source_target_pairs={{0,8},{8,0},{1,9},{9,1},{2,10},{10,2},{3,11},{11,3},{4,12},{12,4},... | collective-permute-start | bytes 12582920 | tf_op jit(solution)/shard_map/ppermute | solution.py:30
  124.9 16.4 %all-to-all-start.3 = ((bf16[8,192,256]{2,1,0:T(8,128)(2,1)}), bf16[8,192,256]{2,1,0:T(8,128)(2,1)S(1)}, u32[]{:S(2)}, u32[]{:S(2)}) async-start(bf16[8,192,256]{2,1,0:T(8,128)(2,1)} %bitcast.21), calls=%async_computation.3 | async-start | bytes 1572864 | tf_op jit(solution)/shard_map/all_to_all | solution.py:496
